TPU v7x, 32 devices: a whole 2x2x4 slice. The times are simulated.
32 devices in a mesh: seq: 8 (over y, x, core), mp: 4 (over z).
Axes of the slice: x: 2, y: 2, z: 4, core: 2. Of those that a mesh axis runs over, the one named last changes fastest.
Arguments:
- stream: float32 [4096, 2048], P('seq', 'mp'), may hold values from -6 to 6
- doc_starts: int32 [4096], P('seq'), may hold values 0 or 1
- gain_first: float32 [2048], replicated, may hold values from 0.5 to 1.5
- proj_inner: bfloat16 [2048, 2560], P(None, 'mp'), may hold values from -0.125 to 0.125
- proj_gate: bfloat16 [2048, 2560], P(None, 'mp'), may hold values from -0.125 to 0.125
- conv_weight: float32 [4, 2560], P(None, 'mp'), may hold values from -3 to 3
- conv_bias: float32 [2560], P('mp'), may hold values from -3 to 3
- gate_recur: bfloat16 [16, 160, 160], P('mp'), may hold values from -0.5 to 0.5
- gate_input: bfloat16 [16, 160, 160], P('mp'), may hold values from -0.5 to 0.5
- bias_recur: float32 [2560], P('mp'), may hold values from -3 to 3
- bias_input: float32 [2560], P('mp'), may hold values from -3 to 3
- decay_param: float32 [2560], P('mp'), may hold values from 3.4 to 15, as said below
- proj_out: bfloat16 [2560, 2048], P('mp'), may hold values from -0.25 to 0.25
- gain_second: float32 [2048], replicated, may hold values from 0.5 to 1.5
- mlp_gate: bfloat16 [2048, 6144], P(None, 'mp'), may hold values from -0.125 to 0.125
- mlp_up: bfloat16 [2048, 6144], P(None, 'mp'), may hold values from -0.125 to 0.125
- mlp_down: bfloat16 [6144, 2048], P('mp'), may hold values from -0.15625 to 0.15625
- cotangent: float32 [4096, 2048], P('seq', 'mp'), may hold values from -6 to 6
Outputs:
- output: float32 [4096, 2048], P('seq', 'mp')
- grad_stream: float32 [4096, 2048], P('seq', 'mp')
- grad_gain_first: float32 [2048], replicated
- grad_proj_inner: float32 [2048, 2560], P('seq', 'mp')
- grad_proj_gate: float32 [2048, 2560], P('seq', 'mp')
- grad_conv_weight: float32 [4, 2560], P(None, 'mp')
- grad_conv_bias: float32 [2560], P('mp')
- grad_gate_recur: float32 [16, 160, 160], P('mp')
- grad_gate_input: float32 [16, 160, 160], P('mp')
- grad_bias_recur: float32 [2560], P('mp')
- grad_bias_input: float32 [2560], P('mp')
- grad_decay: float32 [2560], P('mp')
- grad_proj_out: float32 [2560, 2048], P(('mp', 'seq'))
- grad_gain_second: float32 [2048], replicated
- grad_mlp_gate: float32 [2048, 6144], P('seq', 'mp')
- grad_mlp_up: float32 [2048, 6144], P('seq', 'mp')
- grad_mlp_down: float32 [6144, 2048], P(('mp', 'seq'))
Inputs may be any that keep to these rules, and one draw needn't show every extreme that they name: decay_param is -log(exp(q) - 1) for a per-channel rate q between 0.05 / 4096 and 0.03. `doc_starts`: a 1 marks the first token of a document.
All inputs are finite; a program needn't handle non-finite values. No bound on the sum of `doc_starts` on one device may be relied on, other than what follows from the above.
Results may differ from a plain program's by a relative error of at most 0.0089.
Values sent between devices are 32-bit elements; how exact they have to be, the bound alone decides.
No kernel may reach another device: no remote copies, remote signals or barrier semaphores. Data moves between devices by JAX's collectives and lax.ppermute only.
A program may use at most 256 MiB of HBM per device.

v0:
```python
from functools import partial

import jax
import jax.numpy as jnp
from jax import lax
from jax.sharding import PartitionSpec as P

recur_scale = 8.0
norm_eps = 1e-06


def passed_along(value, axis, steps):
    count = lax.axis_size(axis)
    first, last = (max(0, -steps), min(count, count - steps))
    return lax.ppermute(value, axis, [(source, source + steps) for source in range(first, last)])


def carried_in(value, axis, join, neutral, backward):
    count, mine = (lax.axis_size(axis), lax.axis_index(axis))
    pieces = jax.tree.map(lambda part: lax.all_gather(part, axis), value)
    if backward:
        pieces = jax.tree.map(lambda part: part[::-1], pieces)
        mine = count - 1 - mine
    running = jax.tree.map(
        lambda part, zero: jnp.full_like(part, 0) + jnp.asarray(zero, part.dtype), value, neutral
    )

    def turn(position, running):
        longer = join(running, jax.tree.map(lambda part: part[position], pieces))
        return jax.tree.map(lambda new, old: jnp.where(position < mine, new, old), longer, running)

    return lax.fori_loop(0, count - 1, turn, running)


def norm_rows(rows, gain):
    return rows * lax.rsqrt(jnp.mean(rows * rows, axis=-1, keepdims=True) + norm_eps) * gain


def matmul(left, right):
    return jnp.dot(left, right, preferred_element_type=jnp.float32)


def matmul_nt(left, right):
    return lax.dot_general(
        left, right, (((1,), (1,)), ((), ())), preferred_element_type=jnp.float32
    )


def matmul_tn(left, right):
    return lax.dot_general(
        left, right, (((0,), (0,)), ((), ())), preferred_element_type=jnp.float32
    )


def block_apply(values, weights):
    count = values.shape[0]
    groups = weights.shape[0]
    width = weights.shape[1]
    split = values.reshape(count, groups, width)
    mixed = jnp.einsum("tbi,bio->tbo", split, weights, preferred_element_type=jnp.float32)
    return mixed.reshape(count, groups * width)


def block_back(grads, weights):
    count = grads.shape[0]
    groups = weights.shape[0]
    width = weights.shape[1]
    split = grads.reshape(count, groups, width)
    mixed = jnp.einsum("tbo,bio->tbi", split, weights, preferred_element_type=jnp.float32)
    return mixed.reshape(count, groups * width)


def block_grad(values, grads, groups):
    count = values.shape[0]
    width = values.shape[1] // groups
    left = values.reshape(count, groups, width)
    right = grads.reshape(count, groups, width)
    return jnp.einsum("tbi,tbo->bio", left, right, preferred_element_type=jnp.float32)


def link(earlier, later):
    return (later[0] * earlier[0], later[0] * earlier[1] + later[1])


def local_scan(starts, conv_out, recur_pre, input_pre, decay):
    recur = jax.nn.sigmoid(recur_pre)
    entry = jax.nn.sigmoid(input_pre)
    log_decay = -recur_scale * recur * jax.nn.softplus(-decay)
    factor = starts + (1.0 - starts) * jnp.sqrt(-jnp.expm1(2.0 * log_decay))
    carry = jnp.exp(log_decay) * (1.0 - starts)
    fresh = factor * entry * conv_out
    return lax.associative_scan(link, (carry, fresh), axis=0)


def body(
    stream,
    doc_starts,
    gain_first,
    proj_inner,
    proj_gate,
    conv_weight,
    conv_bias,
    gate_recur,
    gate_input,
    bias_recur,
    bias_input,
    decay_param,
    proj_out,
    gain_second,
    mlp_gate,
    mlp_up,
    mlp_down,
    cotangent,
):
    count = stream.shape[0]
    own_width = stream.shape[1]
    inner_width = proj_inner.shape[1]
    ffn_width = mlp_gate.shape[1]
    groups = gate_recur.shape[0]
    lag = conv_weight.shape[0] - 1
    column = lax.axis_index("mp") * own_width
    rows_full = lax.all_gather(stream, "mp", axis=1, tiled=True)
    first_norm, first_back = jax.vjp(norm_rows, rows_full, gain_first)
    first_low = first_norm.astype(jnp.bfloat16)
    inner = matmul(first_low, proj_inner)
    gate_pre = matmul(first_low, proj_gate)
    starts = doc_starts.astype(jnp.float32)[:, None]
    keep = 1.0 - starts
    tail_keep = jnp.concatenate([keep[count - lag + 1 :], jnp.ones((1, 1), jnp.float32)], 0)
    tail_mask = jnp.flip(jnp.cumprod(jnp.flip(tail_keep, 0), 0), 0)
    prior = passed_along(inner[count - lag :] * tail_mask, "seq", 1)
    ext_inner = jnp.concatenate([prior, inner], 0)
    ext_keep = jnp.concatenate([jnp.ones((lag, 1), jnp.float32), keep], 0)
    valid = jnp.ones((count, 1), jnp.float32)
    valids = []
    conv_out = conv_weight[0] * inner
    for k in range(1, lag + 1):
        valid = valid * ext_keep[lag - k + 1 : lag - k + 1 + count]
        valids.append(valid)
        conv_out = conv_out + conv_weight[k] * ext_inner[lag - k : lag - k + count] * valid
    conv_out = conv_out + conv_bias
    conv_low = conv_out.astype(jnp.bfloat16)
    recur_pre = block_apply(conv_low, gate_recur) + bias_recur
    input_pre = block_apply(conv_low, gate_input) + bias_input
    scan_fn = partial(local_scan, starts)
    (span, partial_state), scan_back = jax.vjp(scan_fn, conv_out, recur_pre, input_pre, decay_param)
    identity = (jnp.ones((inner_width,), jnp.float32), jnp.zeros((inner_width,), jnp.float32))
    entering = carried_in(
        (span[count - 1], partial_state[count - 1]), "seq", link, identity, False
    )[1]
    states = span * entering + partial_state
    gated, gelu_back = jax.vjp(jax.nn.gelu, gate_pre)
    mixed_low = (gated * states).astype(jnp.bfloat16)
    branch = lax.psum(matmul(mixed_low, proj_out), "mp")
    resid = rows_full + branch
    second_norm, second_back = jax.vjp(norm_rows, resid, gain_second)
    second_low = second_norm.astype(jnp.bfloat16)
    ffn_gate = matmul(second_low, mlp_gate)
    ffn_up = matmul(second_low, mlp_up)
    ffn_act, act_back = jax.vjp(jax.nn.gelu, ffn_gate)
    hidden_low = (ffn_act * ffn_up).astype(jnp.bfloat16)
    mlp_own = lax.psum_scatter(matmul(hidden_low, mlp_down), "mp", scatter_dimension=1, tiled=True)
    output = lax.dynamic_slice_in_dim(resid, column, own_width, 1) + mlp_own
    cot_full = lax.all_gather(cotangent, "mp", axis=1, tiled=True)
    cot_low = cot_full.astype(jnp.bfloat16)
    d_hidden = matmul_nt(cot_low, mlp_down)
    d_gate_ffn = act_back(d_hidden * ffn_up)[0]
    d_pair_low = jnp.concatenate([d_gate_ffn, d_hidden * ffn_act], 1).astype(jnp.bfloat16)
    d_second_part = matmul_nt(d_pair_low[:, :ffn_width], mlp_gate) + matmul_nt(
        d_pair_low[:, ffn_width:], mlp_up
    )
    d_second = lax.psum(d_second_part, "mp")
    d_resid_norm, d_gain_second = second_back(d_second)
    d_resid = cot_full + d_resid_norm
    branch_low = d_resid.astype(jnp.bfloat16)
    d_mixed = matmul_nt(branch_low, proj_out)
    d_states = d_mixed * gated
    d_gate_low = gelu_back(d_mixed * states)[0].astype(jnp.bfloat16)
    outgoing = jnp.sum(d_states * span, axis=0)
    incoming = carried_in((span[count - 1], outgoing), "seq", link, identity, True)[1]
    d_total = d_states.at[count - 1].add(incoming)
    d_conv_direct, d_recur, d_input, d_decay = scan_back((d_total * entering, d_total))
    d_recur_low = d_recur.astype(jnp.bfloat16)
    d_input_low = d_input.astype(jnp.bfloat16)
    d_conv = (
        d_conv_direct + block_back(d_recur_low, gate_recur) + block_back(d_input_low, gate_input)
    )
    grad_gate_recur = block_grad(conv_low, d_recur_low, groups)
    grad_gate_input = block_grad(conv_low, d_input_low, groups)
    grad_bias_recur = jnp.sum(d_recur_low.astype(jnp.float32), axis=0)
    grad_bias_input = jnp.sum(d_input_low.astype(jnp.float32), axis=0)
    ext_grad = (
        jnp.zeros((count + lag, inner_width), jnp.float32).at[lag:].add(conv_weight[0] * d_conv)
    )
    conv_terms = [jnp.sum(d_conv * inner, axis=0)]
    for k in range(1, lag + 1):
        weighted = d_conv * valids[k - 1]
        ext_grad = ext_grad.at[lag - k : lag - k + count].add(conv_weight[k] * weighted)
        conv_terms.append(jnp.sum(weighted * ext_inner[lag - k : lag - k + count], axis=0))
    grad_conv_weight = jnp.stack(conv_terms, 0)
    grad_conv_bias = jnp.sum(d_conv, axis=0)
    returned = passed_along(ext_grad[:lag], "seq", -1)
    d_inner = ext_grad[lag:].at[count - lag :].add(returned * tail_mask)
    d_inner_low = d_inner.astype(jnp.bfloat16)
    first_pair_low = jnp.concatenate([d_inner_low, d_gate_low], 1)
    d_first_part = matmul_nt(d_inner_low, proj_inner) + matmul_nt(d_gate_low, proj_gate)
    d_first = lax.psum(d_first_part, "mp")
    d_rows_norm, d_gain_first = first_back(d_first)
    grad_stream = lax.dynamic_slice_in_dim(d_resid + d_rows_norm, column, own_width, 1)
    small = lax.psum(
        (
            d_gain_first,
            d_gain_second,
            grad_conv_weight,
            grad_conv_bias,
            grad_gate_recur,
            grad_gate_input,
            grad_bias_recur,
            grad_bias_input,
            d_decay,
        ),
        "seq",
    )
    grad_first, grad_out, grad_pair, grad_down = (
        lax.psum_scatter(
            matmul_tn(first_low, first_pair_low), "seq", scatter_dimension=0, tiled=True
        ),
        lax.psum_scatter(matmul_tn(mixed_low, branch_low), "seq", scatter_dimension=0, tiled=True),
        lax.psum_scatter(matmul_tn(second_low, d_pair_low), "seq", scatter_dimension=0, tiled=True),
        lax.psum_scatter(matmul_tn(hidden_low, cot_low), "seq", scatter_dimension=0, tiled=True),
    )
    return (
        output,
        grad_stream,
        small[0],
        grad_first[:, :inner_width],
        grad_first[:, inner_width:],
        small[2],
        small[3],
        small[4],
        small[5],
        small[6],
        small[7],
        small[8],
        grad_out,
        small[1],
        grad_pair[:, :ffn_width],
        grad_pair[:, ffn_width:],
        grad_down,
    )


def solution(mesh):
    in_specs = (
        P("seq", "mp"),
        P("seq"),
        P(),
        P(None, "mp"),
        P(None, "mp"),
        P(None, "mp"),
        P("mp"),
        P("mp", None, None),
        P("mp", None, None),
        P("mp"),
        P("mp"),
        P("mp"),
        P("mp", None),
        P(),
        P(None, "mp"),
        P(None, "mp"),
        P("mp", None),
        P("seq", "mp"),
    )
    out_specs = (
        P("seq", "mp"),
        P("seq", "mp"),
        P(),
        P("seq", "mp"),
        P("seq", "mp"),
        P(None, "mp"),
        P("mp"),
        P("mp", None, None),
        P("mp", None, None),
        P("mp"),
        P("mp"),
        P("mp"),
        P(("mp", "seq"), None),
        P(),
        P("seq", "mp"),
        P("seq", "mp"),
        P(("mp", "seq"), None),
    )
    return jax.shard_map(body, mesh=mesh, in_specs=in_specs, out_specs=out_specs, check_vma=False)
```

profile of v0, /device:TPU:0, one launch (start us, length us, event | category | flops | bytes accessed | tf_op | source)
XLA Modules:
  0.0 1586.6 jit_solution(3280703168751612168)
XLA Ops:
  10.0 83.1 %all-gather.7.cloned.1.call-done = f32[512,2048]{1,0:T(8,128)} async-done(((f32[512,512]{1,0:T(8,128)}), f32[512,2048]{1,0:T(8,128)}) %all-gather.7.cloned.1.call-update) | async-done | bytes 4194320 | tf_op jit(solution)/shard_map/all_gather | solution.py:122
  103.9 5.4 fusion.68
  121.4 4.7 exponential_multiply_fusion
  130.3 4.5 slice.593
  134.8 4.3 slice.592
  144.1 4.3 slice.675
  219.0 4.8 pad.543
  226.0 4.8 pad.561
  234.6 4.8 pad.560
  240.2 12.3 all-gather.2
  255.1 4.8 pad.542
  260.7 8.3 all-gather.1
  269.6 5.7 while.34
  275.2 7.2 multiply_convert_fusion.4
  287.9 152.0 %all-reduce.129.cloned.1.call-done = f32[512,2048]{1,0:T(8,128)} async-done(((f32[512,2048]{1,0:T(8,128)}), f32[512,2048]{1,0:T(8,128)}) %all-reduce.129.cloned.1.call-update) | async-done | bytes 4194320 | tf_op jit(solution)/shard_map/psum | solution.py:154
  446.0 10.0 fusion.115
  456.0 5.1 fusion.114
  461.2 60.2 %all-gather.9.cloned.1.call-done = f32[512,2048]{1,0:T(8,128)} async-done(((f32[512,512]{1,0:T(8,128)}), f32[512,2048]{1,0:T(8,128)}) %all-gather.9.cloned.1.call-update) | async-done | bytes 4194320 | tf_op jit(solution)/shard_map/all_gather | solution.py:164
  521.4 12.5 multiply_convert_fusion.2
  533.9 6.7 fusion.117
  540.6 7.9 convolution_add_fusion.1
  551.2 9.5 fusion.116
  560.8 141.4 %all-reduce.131.cloned.1.call-done = f32[512,2048]{1,0:T(8,128)} async-done(((f32[512,2048]{1,0:T(8,128)}), f32[512,2048]{1,0:T(8,128)}) %all-reduce.131.cloned.1.call-update) | async-done | bytes 4194320 | tf_op jit(solution)/shard_map/psum | solution.py:172
  702.2 5.2 multiply_reduce_fusion
  712.3 7.2 multiply_reduce_fusion.11
  719.5 9.0 all-gather.3
  731.8 5.7 while.35
  759.6 4.3 slice.681
  876.2 4.9 pad.680
  886.4 5.1 pad.621
  891.5 4.9 pad.681
  899.5 5.9 multiply_reduce_fusion.6
  922.1 6.3 multiply_reduce_fusion.9
  931.3 4.4 scatter-add.24
  938.7 4.4 scatter-add.25
  952.3 6.8 convolution_add_fusion
  959.2 8.6 fusion.25
  967.8 14.4 fusion.8
  987.9 6.0 fusion.30
  994.0 10.6 fusion.34
  1007.4 106.2 %all-reduce.133.cloned.1.call-done = f32[512,2048]{1,0:T(8,128)} async-done(((f32[512,2048]{1,0:T(8,128)}), f32[512,2048]{1,0:T(8,128)}) %all-reduce.133.cloned.1.call-update) | async-done | bytes 4194320 | tf_op jit(solution)/shard_map/psum | solution.py:207
  1113.6 6.4 multiply_reduce_fusion.1
  1120.1 25.1 %all-reduce.122 = (f32[2048]{0:T(1024)}, f32[4,640]{1,0:T(4,128)}, f32[640]{0:T(1024)}, f32[640]{0:T(1024)}, f32[640]{0:T(1024)}, /*index=5*/f32[640]{0:T(1024)}, f32[2048]{0:T(1024)}) all-reduce(f32[2048]{0:T(1024)S(1)} %get-tuple-element.317, f32[4,640]{1,0:T(4,128)S(1)} %pad_maximum_fusion.15, ...), channel_id=1, replica_groups=mesh['seq'=8,'mp'=4] {'seq'}, use_global_device_ids=true, to_apply=%region_15.16 | all-reduce | flops 9216 | bytes 73728 | tf_op jit(solution)/shard_map/psum | solution.py:210
  1148.2 49.5 %reduce-scatter.8.cloned.1.call-done = f32[256,1280]{1,0:T(8,128)} async-done(((f32[2048,1280]{1,0:T(8,128)}), f32[256,1280]{1,0:T(8,128)}) %reduce-scatter.8.cloned.1.call-update) | async-done | bytes 1310736 | tf_op jit(solution)/shard_map/reduce_scatter | solution.py:225
  1200.1 158.1 %reduce-scatter.12.cloned.1.call-done = f32[256,3072]{1,0:T(8,128)} async-done(((f32[2048,3072]{1,0:T(8,128)}), f32[256,3072]{1,0:T(8,128)}) %reduce-scatter.12.cloned.1.call-update) | async-done | bytes 3145744 | tf_op jit(solution)/shard_map/reduce_scatter | solution.py:229
  1362.0 58.5 %all-reduce.135.cloned.1.call-done = (f32[4,160,160]{2,1,0:T(8,128)}, f32[4,160,160]{2,1,0:T(8,128)}) async-done(((f32[4,160,160]{2,1,0:T(8,128)}, f32[4,160,160]{2,1,0:T(8,128)}), (f32[4,160,160]{2,1,0:T(8,128)}, f32[4,160,160]{2,1,0:T(8,128)})) %all-reduce.135.cloned.1.call-update) | async-done | bytes 819216 | tf_op jit(solution)/shard_map/psum | solution.py:210
  1420.5 60.0 %reduce-scatter.10.cloned.1.call-done = f32[80,2048]{1,0:T(8,128)} async-done(((f32[640,2048]{1,0:T(8,128)}), f32[80,2048]{1,0:T(8,128)}) %reduce-scatter.10.cloned.1.call-update) | async-done | bytes 655376 | tf_op jit(solution)/shard_map/reduce_scatter | solution.py:228
  1480.4 96.5 %reduce-scatter.14.cloned.1.call-done = f32[192,2048]{1,0:T(8,128)} async-done(((f32[1536,2048]{1,0:T(8,128)}), f32[192,2048]{1,0:T(8,128)}) %reduce-scatter.14.cloned.1.call-update) | async-done | bytes 1572880 | tf_op jit(solution)/shard_map/reduce_scatter | solution.py:230
  (794 shorter events, 342.6 us)
Async XLA Ops:
  7.2 268.0 %copy-start = (bf16[2048,640]{1,0:T(8,128)(2,1)S(1)}, bf16[2048,640]{1,0:T(8,128)(2,1)}, u32[]{:S(2)}) copy-start(bf16[2048,640]{1,0:T(8,128)(2,1)} %param.38) | copy-start | bytes 7864324
  7.2 85.9 %all-gather.7.cloned.1.call-start = ((), (), s32[]{:S(2)}) async-start(), calls=%async_computation.5 | async-start | bytes 5242880 | tf_op jit(solution)/shard_map/all_gather | solution.py:122
  7.9 432.0 %all-reduce.129.cloned.1.call-start = ((), (), s32[]{:S(2)}) async-start(), calls=%async_computation.6 | async-start | bytes 8388608 | tf_op jit(solution)/shard_map/psum | solution.py:154
  8.7 112.7 %copy-start.115 = (f32[512]{0:T(512)}, f32[512]{0:T(512)S(1)}, u32[]{:S(2)}) copy-start(f32[512]{0:T(512)S(1)} %broadcast_subtract_fusion) | copy-start | bytes 6148
  9.2 90.9 %copy-start.180 = (f32[3,1]{0,1:T(1,128)}, f32[3,1]{0,1:T(1,128)S(1)}, u32[]{:S(2)}) copy-start(f32[3,1]{0,1:T(1,128)S(1)} %rev.14) | copy-start | bytes 40
  9.3 94.6 %copy-start.160 = (f32[512,1]{0,1:T(1,128)}, f32[512,1]{0,1:T(1,128)S(1)}, u32[]{:S(2)}) copy-start(f32[512,1]{0,1:T(1,128)S(1)} %get-tuple-element.399) | copy-start | bytes 6148
  9.3 94.6 %copy-start.162 = (f32[512,1]{0,1:T(1,128)}, f32[512,1]{0,1:T(1,128)S(1)}, u32[]{:S(2)}) copy-start(f32[512,1]{0,1:T(1,128)S(1)} %get-tuple-element.400) | copy-start | bytes 6148
  9.3 86.5 %copy-start.164 = (f32[2048]{0:T(1024)S(1)}, f32[2048]{0:T(1024)}, u32[]{:S(2)}) copy-start(f32[2048]{0:T(1024)} %param.36) | copy-start | bytes 24580
  10.0 111.4 %copy-start.117 = (f32[640]{0:T(1024)}, f32[640]{0:T(1024)S(1)}, u32[]{:S(2)}) copy-start(f32[640]{0:T(1024)S(1)} %broadcast_multiply_fusion.3) | copy-start | bytes 7684
  101.3 2.6 collective-permute-start
  103.4 18.0 %copy-start.166 = (f32[512]{0:T(512)}, f32[512]{0:T(512)S(1)}, u32[]{:S(2)}) copy-start(f32[512]{0:T(512)S(1)} %convert_element_type.44) | copy-start | bytes 6148
  130.3 22.3 %copy-start.17 = (f32[256,640]{1,0:T(8,128)}, f32[256,640]{1,0:T(8,128)S(1)}, u32[]{:S(2)}) copy-start(f32[256,640]{1,0:T(8,128)S(1)} %slice.594) | copy-start | bytes 1966084
  155.0 9.3 copy-start.28
  189.9 9.7 copy-start.22
  287.1 234.2 %all-gather.9.cloned.1.call-start = ((), (), s32[]{:S(2)}) async-start(), calls=%async_computation.8 | async-start | bytes 5242880 | tf_op jit(solution)/shard_map/all_gather | solution.py:164
  287.8 156.1 %copy-start.129 = (f32[2048]{0:T(1024)S(1)}, f32[2048]{0:T(1024)}, u32[]{:S(2)}) copy-start(f32[2048]{0:T(1024)} %param.47) | copy-start | bytes 24580
  287.9 414.3 %all-reduce.131.cloned.1.call-start = ((), (), s32[]{:S(2)}) async-start(), calls=%async_computation.9 | async-start | bytes 8388608 | tf_op jit(solution)/shard_map/psum | solution.py:172
  443.9 12.1 slice-start.14
  446.0 10.0 copy-start.46
  446.0 10.0 slice-start.15
  548.5 456.2 %reduce-scatter.6.cloned.1.call-start = ((), (), s32[]{:S(2)}) async-start(), calls=%async_computation.7 | async-start | bytes 5242880 | tf_op jit(solution)/shard_map/reduce_scatter | solution.py:162
  560.7 141.5 %copy-start.170 = (f32[512]{0:T(512)S(1)}, f32[512]{0:T(512)}, u32[]{:S(2)}) copy-start(f32[512]{0:T(512)} %copy-done.169) | copy-start | bytes 6148
  560.7 552.9 %all-reduce.133.cloned.1.call-start = ((), (), s32[]{:S(2)}) async-start(), calls=%async_computation.10 | async-start | bytes 8388608 | tf_op jit(solution)/shard_map/psum | solution.py:207
  803.1 14.4 copy-start.36
  804.7 11.1 copy-start.114
  807.3 10.2 copy-start.119
  808.1 9.4 copy-start.120
  826.8 11.4 copy-start.64
  829.5 12.3 copy-start.92
  830.8 12.4 copy-start.49
  830.8 12.4 copy-start.51
  830.8 12.4 slice-start.6
  830.8 12.4 slice-start.7
  845.2 9.5 copy-start.70
  846.7 9.5 copy-start.33
  846.7 9.5 slice-start.4
  846.7 9.5 slice-start.5
  946.2 5.3 collective-permute-start.1
  959.1 238.6 %reduce-scatter.8.cloned.1.call-start = ((), (), s32[]{:S(2)}) async-start(), calls=%async_computation.11 | async-start | bytes 11796480 | tf_op jit(solution)/shard_map/reduce_scatter | solution.py:225
  967.7 390.5 %reduce-scatter.12.cloned.1.call-start = ((), (), s32[]{:S(2)}) async-start(), calls=%async_computation.13 | async-start | bytes 28311552 | tf_op jit(solution)/shard_map/reduce_scatter | solution.py:229
  982.2 438.3 %all-reduce.135.cloned.1.call-start = ((), (), s32[]{:S(2)}) async-start(), calls=%async_computation.15 | async-start | bytes 2621440 | tf_op jit(solution)/shard_map/psum | solution.py:210
  986.8 493.6 %reduce-scatter.10.cloned.1.call-start = ((), (), s32[]{:S(2)}) async-start(), calls=%async_computation.12 | async-start | bytes 5898240 | tf_op jit(solution)/shard_map/reduce_scatter | solution.py:228
  993.9 583.0 %reduce-scatter.14.cloned.1.call-start = ((), (), s32[]{:S(2)}) async-start(), calls=%async_computation.14 | async-start | bytes 14155776 | tf_op jit(solution)/shard_map/reduce_scatter | solution.py:230
  1004.7 108.9 %copy-start.159 = (f32[512]{0:T(512)S(1)}, f32[512]{0:T(512)}, u32[]{:S(2)}) copy-start(f32[512]{0:T(512)} %copy-done.158) | copy-start | bytes 6148
  1004.7 108.9 %copy-start.165 = (f32[2048]{0:T(1024)S(1)}, f32[2048]{0:T(1024)}, u32[]{:S(2)}) copy-start(f32[2048]{0:T(1024)} %param.36) | copy-start | bytes 24580
  1007.4 112.6 %copy-start.168 = (f32[2048]{0:T(1024)S(1)}, f32[2048]{0:T(1024)}, u32[]{:S(2)}) copy-start(f32[2048]{0:T(1024)} %get-tuple-element.315) | copy-start | bytes 24580
  1007.4 137.7 %copy-start.173 = (f32[512]{0:T(512)S(1)}, f32[512]{0:T(512)}, u32[]{:S(2)}) copy-start(f32[512]{0:T(512)} %copy-done.172) | copy-start | bytes 6148
  1420.5 158.5 %copy-start.72 = (f32[4,160,160]{2,1,0:T(8,128)S(1)}, f32[4,160,160]{2,1,0:T(8,128)}, u32[]{:S(2)}) copy-start(f32[4,160,160]{2,1,0:T(8,128)} %get-tuple-element.666) | copy-start | bytes 1228804
  (167 other events, 667.3 us)
Sparse Core Ops, SparseCore 0:
  9.6 83.4 all-gather.6
  287.2 152.6 all-reduce.128
  441.5 79.7 all-gather.8
  548.6 153.4 all-reduce.130
  704.3 75.7 reduce-scatter.5
  959.2 154.3 all-reduce.132
  1117.1 80.5 reduce-scatter.7
  1201.3 156.8 reduce-scatter.11
  1362.6 57.8 all-reduce.134
  1424.7 55.7 reduce-scatter.9
  1484.5 92.3 reduce-scatter.13
where the time goes:
time: 1600 us; the launch traced here: 1590 us
  waiting for transfers between devices  967 us (60%)
  local copies, waits for them, and re-layouts  262 us (16%)
  other arithmetic  146 us (9%)
  matrix products  136 us (8%)
  blocking collectives  54.6 us (3%)
  between operations  16.9 us (1%)
    reduce_scatter x1, waiting for transfers between devices, body(): lax.psum_scatter(matmul_tn(second_low, d_pair_low), 'seq', scatter_dimens...  158 us
    psum x1, waiting for transfers between devices, body(): branch = lax.psum(matmul(mixed_low, proj_out), 'mp')  152 us
    psum x1, waiting for transfers between devices, body(): d_second = lax.psum(d_second_part, 'mp')  141 us
    pad x94, local copies, waits for them, and re-layouts, local_scan(): return lax.associative_scan(link, (carry, fresh), axis=0)  112 us
    psum x1, waiting for transfers between devices, body(): d_first = lax.psum(d_first_part, 'mp')  106 us
    reduce_scatter x1, waiting for transfers between devices, body(): lax.psum_scatter(matmul_tn(hidden_low, cot_low), 'seq', scatter_dimension...  96.5 us
    all_gather x1, waiting for transfers between devices, body(): rows_full = lax.all_gather(stream, 'mp', axis=1, tiled=True)  83.1 us
    slice x92, local copies, waits for them, and re-layouts, local_scan(): return lax.associative_scan(link, (carry, fresh), axis=0)  81.5 us
  transfers between devices with their start and end apart: 13, of which 11 were waited for; matrix products, arithmetic and copies ran while one was open for 21% of the time, Pallas kernels for 0%

commit v1 on v0

v1 whole, which is shorter than its diff:
```python
from functools import partial

import jax
import jax.numpy as jnp
from jax import lax
from jax.experimental import pallas as pl
from jax.experimental.pallas import tpu as pltpu
from jax.sharding import PartitionSpec as P

recur_scale = 8.0
norm_eps = 1e-06
bf16 = jnp.bfloat16
f32 = jnp.float32
LANES = 128
SUB = 8
ROWS = 32
VMEM_LIMIT = 50 * 1024 * 1024


def matmul(left, right):
    return jnp.dot(left, right, preferred_element_type=f32)


def matmul_nt(left, right):
    return lax.dot_general(left, right, (((1,), (1,)), ((), ())), preferred_element_type=f32)


def matmul_tn(left, right):
    return lax.dot_general(left, right, (((0,), (0,)), ((), ())), preferred_element_type=f32)


PAIRS = ((0, 1), (1, 0), (2, 3), (3, 2))
MIDDLE = ((1, 2), (2, 1))
OUTWARD = ((1, 0), (2, 3))
INWARD = ((0, 1), (3, 2))
CROSS = ((0, 2), (2, 0), (1, 3), (3, 1))


def over_mp(value, pairs):
    return lax.ppermute(value, "mp", list(pairs))


def line_places():
    mine = lax.axis_index("mp")
    half = mine >> 1
    return mine, mine ^ 1, 2 - half, 3 - 3 * half


def line_gather(own):
    beside = over_mp(own, PAIRS)
    near_in = over_mp(own, MIDDLE)
    near_out = over_mp(near_in, OUTWARD)
    far_in = over_mp(beside, MIDDLE)
    far_out = over_mp(far_in, OUTWARD)
    return own, beside, near_in + near_out, far_in + far_out


def line_scatter(piece):
    mine, beside, near, far = line_places()
    far_part = piece(far)
    far_one = over_mp(far_part, INWARD)
    far_two = over_mp(far_part + far_one, MIDDLE)
    near_part = piece(near)
    near_one = over_mp(near_part, INWARD)
    near_two = over_mp(near_part + near_one, MIDDLE)
    last = over_mp(piece(beside) + far_two, PAIRS)
    return piece(mine) + near_two + last


def line_sum(value):
    value = value + over_mp(value, PAIRS)
    return value + over_mp(value, CROSS)


def assemble(pieces, width, turn):
    rows, own_width = pieces[0].shape
    whole = jnp.zeros((rows, width), bf16)
    for piece, place in zip(pieces, line_places()):
        start = place * own_width
        whole = lax.dynamic_update_slice(whole, turn(piece, start).astype(bf16), (0, start))
    return whole


def wide(value, width):
    return jnp.concatenate([value] * (width // LANES), axis=-1)


def neg_expm1(x, e):
    poly = 1.0 / 40320.0
    for term in (5040.0, 720.0, 120.0, 24.0, 6.0, 2.0, 1.0):
        poly = poly * x + 1.0 / term
    return jnp.where(x > -0.5, -x * poly, 1.0 - e)


def gelu_parts(x):
    scale = 0.7978845608028654
    cube = 0.044715
    squared = x * x
    t = jnp.tanh(scale * (x + cube * x * squared))
    half = 0.5 * (1.0 + t)
    slope = half + 0.5 * x * (1.0 - t * t) * scale * (1.0 + 3.0 * cube * squared)
    return half * x, slope


def group_scan(a, b):
    place = lax.broadcasted_iota(jnp.int32, a.shape, 1)
    for k in (1, 2, 4):
        fits = place >= k
        b = jnp.where(fits, a * pltpu.roll(b, k, 1) + b, b)
        a = jnp.where(fits, a * pltpu.roll(a, k, 1), a)
    return a, b


def group_scan_back(a, b):
    place = lax.broadcasted_iota(jnp.int32, a.shape, 1)
    for k in (1, 2, 4):
        fits = place < SUB - k
        b = jnp.where(fits, a * pltpu.roll(b, SUB - k, 1) + b, b)
        a = jnp.where(fits, a * pltpu.roll(a, SUB - k, 1), a)
    return a, b


def forward_kernel(
    inner_ref, halo_ref, valid_ref, row_ref, gate_ref,
    conv_ref, low_ref, rg_ref, ig_ref, alpha_ref, factor_ref, part_ref, span_ref, last_ref,
    ext_ref, pre_ref,
):
    count, width = inner_ref.shape
    ext_ref[pl.ds(0, SUB), :] = halo_ref[...]

    def fill(i, _):
        r = pl.multiple_of(i * ROWS, ROWS)
        ext_ref[pl.ds(r + SUB, ROWS), :] = inner_ref[pl.ds(r, ROWS), :]
        return 0

    lax.fori_loop(0, count // ROWS, fill, 0)

    def convolve(i, _):
        r = pl.multiple_of(i * ROWS, ROWS)
        window = ext_ref[pl.ds(r, ROWS + SUB), :]
        total = row_ref[0:1, :] * window[SUB:]
        for k in range(1, 4):
            valid = wide(valid_ref[k, pl.ds(r, ROWS), :], width)
            total = total + row_ref[k : k + 1, :] * window[SUB - k : SUB - k + ROWS] * valid
        total = total + row_ref[4:5, :]
        conv_ref[pl.ds(r, ROWS), :] = total
        low_ref[pl.ds(r, ROWS), :] = total.astype(bf16)
        return 0

    lax.fori_loop(0, count // ROWS, convolve, 0)
    pre_ref[...] = jnp.dot(low_ref[...], gate_ref[...], preferred_element_type=f32)

    def scan(i, carry):
        r = pl.multiple_of(i * ROWS, ROWS)
        here = pl.ds(r, ROWS)
        rg = jax.nn.sigmoid(pre_ref[here, :width] + row_ref[5:6, :])
        ig = jax.nn.sigmoid(pre_ref[here, width:] + row_ref[6:7, :])
        log_a = row_ref[7:8, :] * rg
        keep = wide(valid_ref[0, here, :], width)
        a = jnp.exp(log_a)
        root = jnp.sqrt(neg_expm1(2.0 * log_a, a * a))
        factor = (1.0 - keep) + keep * root
        alpha = a * keep
        beta = factor * ig * conv_ref[here, :]
        rg_ref[here, :] = rg
        ig_ref[here, :] = ig
        alpha_ref[here, :] = alpha
        factor_ref[here, :] = factor
        groups = (ROWS // SUB, SUB, width)
        a3, b3 = group_scan(alpha.reshape(groups), beta.reshape(groups))
        state, product = carry
        for g in range(ROWS // SUB):
            part = b3[g] + a3[g] * state
            span = a3[g] * product
            part_ref[pl.ds(r + g * SUB, SUB), :] = part
            span_ref[pl.ds(r + g * SUB, SUB), :] = span
            state, product = part[SUB - 1 : SUB, :], span[SUB - 1 : SUB, :]
        return state, product

    zero = jnp.zeros((1, width), f32)
    state, product = lax.fori_loop(0, count // ROWS, scan, (zero, zero + 1.0))
    last_ref[...] = jnp.concatenate([product, state, jnp.zeros((SUB - 2, width), f32)], 0)


def state_kernel(
    mine_ref, ends_ref, part_ref, span_ref, gate_ref, states_ref, mixed_ref, enter_ref
):
    devices = ends_ref.shape[0]
    width = part_ref.shape[1]
    entering = jnp.zeros((1, width), f32)
    for d in range(devices):
        ends = ends_ref[d]
        entering = jnp.where(d < mine_ref[0], ends[0:1, :] * entering + ends[1:2, :], entering)
    states = span_ref[...] * entering + part_ref[...]
    states_ref[...] = states
    mixed_ref[...] = (gelu_parts(gate_ref[...])[0] * states).astype(bf16)
    enter_ref[...] = jnp.broadcast_to(entering, enter_ref.shape)


def turn_kernel(
    dmixed_ref, gate_ref, states_ref, span_ref, dstates_ref, dgate_ref, out_ref
):
    act, slope = gelu_parts(gate_ref[...])
    dmixed = dmixed_ref[...]
    dstates = dmixed * act
    dstates_ref[...] = dstates
    dgate_ref[...] = (dmixed * states_ref[...] * slope).astype(bf16)

    @pl.when(pl.program_id(0) == 0)
    def _():
        out_ref[...] = jnp.zeros_like(out_ref)

    out_ref[...] += jnp.sum(
        (dstates * span_ref[...]).reshape(-1, SUB, dstates.shape[1]), axis=0
    )


def backward_kernel(
    mine_ref, ends_ref, dstates_ref, alpha_ref, states_ref, enter_ref, conv_ref, rg_ref, ig_ref,
    factor_ref, valid_ref, inner_ref, halo_ref, row_ref, gate_ref,
    dinner_ref, tail_ref, head_ref, drec_ref, sums_ref,
    dconv_ref, ext_ref,
):
    devices = ends_ref.shape[0]
    count, width = alpha_ref.shape
    blocks = count // ROWS
    incoming = jnp.zeros((1, width), f32)
    for d in reversed(range(devices)):
        ends = ends_ref[d]
        incoming = jnp.where(d > mine_ref[0], ends[0:1, :] * incoming + ends[1:2, :], incoming)
    dconv_ref[pl.ds(0, SUB), :] = jnp.zeros((SUB, width), f32)
    dconv_ref[pl.ds(count + SUB, SUB), :] = jnp.zeros((SUB, width), f32)
    ext_ref[pl.ds(0, SUB), :] = halo_ref[...]
    groups = (ROWS // SUB, SUB, width)
    place = lax.broadcasted_iota(jnp.int32, (SUB, width), 0)

    def fold(value):
        return jnp.sum(value.reshape(groups), axis=0)

    def back(step, carry):
        flow, decay, bias_r, bias_i = carry
        i = blocks - 1 - step
        r = pl.multiple_of(i * ROWS, ROWS)
        here = pl.ds(r, ROWS)
        ext_ref[pl.ds(r + SUB, ROWS), :] = inner_ref[here, :]
        alpha = alpha_ref[here, :]
        dstates = dstates_ref[here, :]
        a3, b3 = group_scan_back(alpha.reshape(groups), (alpha * dstates).reshape(groups))
        d3 = dstates.reshape(groups)
        totals = [None] * (ROWS // SUB)
        for g in reversed(range(ROWS // SUB)):
            flows = b3[g] + a3[g] * flow
            later = jnp.where(place == SUB - 1, flow, pltpu.roll(flows, SUB - 1, 0))
            totals[g] = d3[g] + later
            flow = flows[0:1, :]
        total = jnp.concatenate(totals, 0)
        before = pl.multiple_of(jnp.maximum(r - SUB, 0), SUB)
        first = jnp.where(i == 0, enter_ref[...], states_ref[pl.ds(before, SUB), :])
        window = jnp.concatenate([first, states_ref[here, :]], 0)
        prior = window[SUB - 1 : SUB - 1 + ROWS]
        rg = rg_ref[here, :]
        ig = ig_ref[here, :]
        factor = factor_ref[here, :]
        conv = conv_ref[here, :]
        gain = total * factor
        dconv_ref[pl.ds(r + SUB, ROWS), :] = gain * ig
        dinput = (gain * conv * ig * (1.0 - ig)).astype(bf16)
        dlog = alpha * (total * prior - total * ig * conv * alpha / factor)
        drecur = (dlog * row_ref[7:8, :] * rg * (1.0 - rg)).astype(bf16)
        drec_ref[here, :width] = drecur
        drec_ref[here, width:] = dinput
        return (
            flow,
            decay + fold(dlog * rg),
            bias_r + fold(drecur.astype(f32)),
            bias_i + fold(dinput.astype(f32)),
        )

    zero = jnp.zeros((SUB, width), f32)
    _, decay, bias_r, bias_i = lax.fori_loop(0, blocks, back, (incoming, zero, zero, zero))
    dconv_ref[pl.ds(SUB, count), :] += lax.dot_general(
        drec_ref[...], gate_ref[...], (((1,), (1,)), ((), ())), preferred_element_type=f32
    )

    def spread_back(window, r, rows):
        total = row_ref[0:1, :] * window[:rows]
        for k in range(1, 4):
            valid = wide(valid_ref[k, pl.ds(r, rows + SUB), :], width)
            total = total + row_ref[k : k + 1, :] * (window * valid)[k : k + rows]
        return total

    head_ref[...] = spread_back(dconv_ref[pl.ds(0, 2 * SUB), :], 0, SUB)

    def finish(i, carry):
        r = pl.multiple_of(i * ROWS, ROWS)
        window = dconv_ref[pl.ds(r + SUB, ROWS + SUB), :]
        total = spread_back(window, r + SUB, ROWS)
        dinner_ref[pl.ds(r, ROWS), :] = total.astype(bf16)

        @pl.when(i == blocks - 1)
        def _():
            tail_ref[...] = total[ROWS - 2 * SUB :]

        dconv = window[:ROWS]
        inputs = ext_ref[pl.ds(r, ROWS + SUB), :]
        sums = [fold(dconv * inputs[SUB:])]
        for k in range(1, 4):
            valid = wide(valid_ref[k, pl.ds(r + SUB, ROWS), :], width)
            sums.append(fold(dconv * valid * inputs[SUB - k : SUB - k + ROWS]))
        sums.append(fold(dconv))
        return tuple(c + s for c, s in zip(carry, sums))

    sums = lax.fori_loop(0, blocks, finish, (zero,) * 5)
    sums_ref[...] = jnp.concatenate(
        [jnp.sum(s, axis=0, keepdims=True) for s in (*sums, bias_r, bias_i, decay)], 0
    )


def vmem(count=1):
    return [pl.BlockSpec(memory_space=pltpu.VMEM)] * count


def shape(dims, kind=f32):
    return jax.ShapeDtypeStruct(dims, kind)


def cost(flops, moved, special=0):
    return pl.CostEstimate(flops=flops, bytes_accessed=moved, transcendentals=special)


def run_forward(inner, halo, valid, rows, gates):
    count, width = inner.shape
    full = shape((count, width))
    return pl.pallas_call(
        forward_kernel,
        out_shape=(full, shape((count, width), bf16)) + (full,) * 6 + (shape((SUB, width)),),
        in_specs=vmem(5),
        out_specs=tuple(vmem(9)),
        scratch_shapes=[
            pltpu.VMEM((count + SUB, width), f32),
            pltpu.VMEM((count, 2 * width), f32),
        ],
        compiler_params=pltpu.CompilerParams(vmem_limit_bytes=VMEM_LIMIT),
        cost_estimate=cost(4 * count * width * width, 36 * count * width, 5 * count * width),
        name="recurrence_forward",
    )(inner, halo, valid, rows, gates)


def run_states(mine, ends, part, span, gate_pre):
    count, width = part.shape
    block = count // 4
    tile = pl.BlockSpec((block, width), lambda i: (i, 0))
    return pl.pallas_call(
        state_kernel,
        grid=(4,),
        out_shape=(
            shape((count, width)), shape((count, width), bf16), shape((SUB, width)),
        ),
        in_specs=[
            pl.BlockSpec(memory_space=pltpu.SMEM),
            pl.BlockSpec(ends.shape, lambda i: (0, 0, 0)),
            tile, tile, tile,
        ],
        out_specs=(tile, tile, pl.BlockSpec((SUB, width), lambda i: (0, 0))),
        compiler_params=pltpu.CompilerParams(vmem_limit_bytes=VMEM_LIMIT),
        cost_estimate=cost(20 * count * width, 18 * count * width, count * width),
        name="recurrence_states",
    )(mine, ends, part, span, gate_pre)


def run_turn(dmixed, gate_pre, states, span):
    count, width = dmixed.shape
    block = count // 4
    tile = pl.BlockSpec((block, width), lambda i: (i, 0))
    return pl.pallas_call(
        turn_kernel,
        grid=(4,),
        out_shape=(
            shape((count, width)), shape((count, width), bf16), shape((SUB, width)),
        ),
        in_specs=[tile] * 4,
        out_specs=(tile, tile, pl.BlockSpec((SUB, width), lambda i: (0, 0))),
        compiler_params=pltpu.CompilerParams(vmem_limit_bytes=VMEM_LIMIT),
        cost_estimate=cost(30 * count * width, 22 * count * width, count * width),
        name="recurrence_turn",
    )(dmixed, gate_pre, states, span)


def run_backward(mine, ends, dstates, saved, enter, valid, inner, halo, rows, gates):
    count, width = dstates.shape
    return pl.pallas_call(
        backward_kernel,
        out_shape=(
            shape((count, width), bf16), shape((2 * SUB, width)), shape((SUB, width)),
            shape((count, 2 * width), bf16), shape((SUB, width)),
        ),
        in_specs=[pl.BlockSpec(memory_space=pltpu.SMEM)] + vmem(14),
        out_specs=tuple(vmem(5)),
        scratch_shapes=[
            pltpu.VMEM((count + 2 * SUB, width), f32),
            pltpu.VMEM((count + SUB, width), f32),
        ],
        compiler_params=pltpu.CompilerParams(vmem_limit_bytes=VMEM_LIMIT),
        cost_estimate=cost(4 * count * width * width, 40 * count * width, count * width),
        name="recurrence_backward",
    )(
        mine, ends, dstates, saved["alpha"], saved["states"], enter, saved["conv"], saved["rg"],
        saved["ig"], saved["factor"], valid, inner, halo, rows, gates,
    )


def block_diagonal(weights):
    groups, width, _ = weights.shape
    rows = [
        jnp.pad(weights[b], ((0, 0), (b * width, (groups - 1 - b) * width))) for b in range(groups)
    ]
    return jnp.concatenate(rows, 0)


def diagonal_blocks(whole, groups):
    width = whole.shape[0] // groups
    return jnp.stack(
        [
            whole[b * width : (b + 1) * width, b * width : (b + 1) * width]
            for b in range(groups)
        ],
        0,
    )


def row_scale(squares, features):
    return lax.rsqrt(squares / features + norm_eps)[:, None]


def body(
    stream, doc_starts, gain_first, proj_inner, proj_gate, conv_weight, conv_bias, gate_recur,
    gate_input, bias_recur, bias_input, decay_param, proj_out, gain_second, mlp_gate, mlp_up,
    mlp_down, cotangent,
):
    count, own_width = stream.shape
    features = gain_first.shape[0]
    inner_width = proj_inner.shape[1]
    ffn_width = mlp_gate.shape[1]
    groups = gate_recur.shape[0]
    devices = lax.axis_size("seq")
    seq_at = lax.axis_index("seq").astype(jnp.int32).reshape(1)
    column = lax.axis_index("mp") * own_width
    own_first = lax.dynamic_slice_in_dim(gain_first, column, own_width)
    own_second = lax.dynamic_slice_in_dim(gain_second, column, own_width)
    onward = [(s, s + 1) for s in range(devices - 1)]
    backward = [(s + 1, s) for s in range(devices - 1)]

    stream_pieces = line_gather(stream)
    first_scale = row_scale(line_sum(jnp.sum(stream * stream, axis=1)), features)
    starts_row = jnp.zeros((own_width,), f32).at[:SUB].set(doc_starts[count - SUB :].astype(f32))
    payload = jnp.concatenate(
        [stream[count - SUB :], jnp.broadcast_to(starts_row, (SUB, own_width))], 0
    )
    payload = lax.ppermute(payload, "seq", onward)
    before = lax.all_gather(payload, "mp", axis=1, tiled=True)
    halo_rows = before[:SUB]
    halo_scale = row_scale(jnp.sum(halo_rows * halo_rows, axis=1), features)
    halo_low = (halo_rows * halo_scale * gain_first).astype(bf16)
    keep_ext = jnp.concatenate([1.0 - before[SUB, :SUB], 1.0 - doc_starts.astype(f32)], 0)
    reach = [keep_ext[SUB:]]
    for k in range(1, 4):
        reach.append(
            (reach[-1] if k > 1 else 1.0) * keep_ext[SUB - k + 1 : SUB - k + 1 + count]
        )
    valid = jnp.broadcast_to(jnp.stack(reach, 0)[:, :, None], (4, count, LANES))
    valid_pad = jnp.pad(valid, ((0, 0), (SUB, SUB), (0, 0)))
    rows = jnp.stack(
        [
            conv_weight[0], conv_weight[1], conv_weight[2], conv_weight[3], conv_bias, bias_recur,
            bias_input, -recur_scale * jax.nn.softplus(-decay_param),
        ],
        0,
    )
    gates = jnp.concatenate([block_diagonal(gate_recur), block_diagonal(gate_input)], 1)

    def first_turn(piece, start):
        return piece * first_scale * lax.dynamic_slice_in_dim(gain_first, start, own_width)

    first_low = assemble(stream_pieces, features, first_turn)
    inner = matmul(first_low, proj_inner)
    halo = matmul(halo_low, proj_inner)
    conv, conv_low, rg, ig, alpha, factor, part, span, last = run_forward(
        inner, halo, valid, rows, gates
    )
    gate_pre = matmul(first_low, proj_gate)
    ends = lax.all_gather(last, "seq")
    states, mixed_low, enter = run_states(seq_at, ends, part, span, gate_pre)

    branch = matmul(mixed_low, proj_out)
    own_resid = stream + line_scatter(
        lambda place: lax.dynamic_slice_in_dim(branch, place * own_width, own_width, 1)
    )
    cot_pieces = line_gather(cotangent)
    cot_low = assemble(cot_pieces, features, lambda piece, start: piece)

    resid_pieces = line_gather(own_resid)
    second_scale = row_scale(line_sum(jnp.sum(own_resid * own_resid, axis=1)), features)

    def second_turn(piece, start):
        return piece * second_scale * lax.dynamic_slice_in_dim(gain_second, start, own_width)

    second_low = assemble(resid_pieces, features, second_turn)
    ffn_weight = jnp.concatenate([mlp_gate, mlp_up], 1)
    ffn = matmul(second_low, ffn_weight)
    act, slope = gelu_parts(ffn[:, :ffn_width])
    ffn_up = ffn[:, ffn_width:]
    hidden_low = (act * ffn_up).astype(bf16)
    d_hidden = matmul_nt(cot_low, mlp_down)
    d_pair_low = jnp.concatenate([d_hidden * ffn_up * slope, d_hidden * act], 1).astype(bf16)
    d_second_part = matmul_nt(d_pair_low, ffn_weight)
    own_d_second = line_scatter(
        lambda place: lax.dynamic_slice_in_dim(d_second_part, place * own_width, own_width, 1)
    )
    second_product = d_second_part * second_low.astype(f32)
    second_mean = line_sum(jnp.sum(second_product, axis=1)) / features
    d_gain_second = jnp.sum(second_product, axis=0) / gain_second
    own_d_resid = (
        cotangent
        + second_scale * (own_second * own_d_second)
        - own_resid * (second_scale * second_scale * second_mean[:, None])
    )
    branch_pieces = line_gather(own_d_resid)
    branch_low = assemble(branch_pieces, features, lambda piece, start: piece)

    mlp_part = matmul(hidden_low, mlp_down)
    output = own_resid + line_scatter(
        lambda place: lax.dynamic_slice_in_dim(mlp_part, place * own_width, own_width, 1)
    )

    d_mixed = matmul_nt(branch_low, proj_out)
    d_states, d_gate_low, outgoing = run_turn(d_mixed, gate_pre, states, span)
    leaving = jnp.stack([last[0], jnp.sum(outgoing, axis=0)], 0)
    back_ends = lax.all_gather(leaving, "seq")
    saved = dict(alpha=alpha, states=states, conv=conv, rg=rg, ig=ig, factor=factor)
    d_inner_low, tail, head, d_rec_low, sums = run_backward(
        seq_at, back_ends, d_states, saved, enter, valid_pad, inner, halo, rows, gates
    )
    returned = lax.ppermute(head, "seq", backward)
    tail = tail + jnp.concatenate([jnp.zeros_like(returned), returned], 0)
    d_inner_low = lax.dynamic_update_slice(d_inner_low, tail.astype(bf16), (count - 2 * SUB, 0))

    d_first_part = matmul_nt(d_inner_low, proj_inner) + matmul_nt(d_gate_low, proj_gate)
    own_d_first = line_scatter(
        lambda place: lax.dynamic_slice_in_dim(d_first_part, place * own_width, own_width, 1)
    )
    first_product = d_first_part * first_low.astype(f32)
    first_mean = line_sum(jnp.sum(first_product, axis=1)) / features
    d_gain_first = jnp.sum(first_product, axis=0) / gain_first
    grad_stream = (
        own_d_resid
        + first_scale * (own_first * own_d_first)
        - stream * (first_scale * first_scale * first_mean[:, None])
    )

    d_gains = lax.psum((d_gain_first, d_gain_second), ("seq", "mp"))
    gate_grads = matmul_tn(conv_low, d_rec_low)
    sums, grad_gate_recur, grad_gate_input = lax.psum(
        (
            sums,
            diagonal_blocks(gate_grads[:, :inner_width], groups),
            diagonal_blocks(gate_grads[:, inner_width:], groups),
        ),
        "seq",
    )
    grad_decay = sums[7] * (recur_scale * jax.nn.sigmoid(-decay_param))

    def over_seq(value):
        return lax.psum_scatter(value, "seq", scatter_dimension=0, tiled=True)

    grad_down = over_seq(matmul_tn(hidden_low, cot_low))
    grad_pair = over_seq(matmul_tn(second_low, d_pair_low))
    grad_out = over_seq(matmul_tn(mixed_low, branch_low))
    grad_gate = over_seq(matmul_tn(first_low, d_gate_low))
    grad_inner = over_seq(matmul_tn(first_low, d_inner_low))
    return (
        output,
        grad_stream,
        d_gains[0],
        grad_inner,
        grad_gate,
        sums[:4],
        sums[4],
        grad_gate_recur,
        grad_gate_input,
        sums[5],
        sums[6],
        grad_decay,
        grad_out,
        d_gains[1],
        grad_pair[:, :ffn_width],
        grad_pair[:, ffn_width:],
        grad_down,
    )


def solution(mesh):
    in_specs = (
        P("seq", "mp"),
        P("seq"),
        P(),
        P(None, "mp"),
        P(None, "mp"),
        P(None, "mp"),
        P("mp"),
        P("mp", None, None),
        P("mp", None, None),
        P("mp"),
        P("mp"),
        P("mp"),
        P("mp", None),
        P(),
        P(None, "mp"),
        P(None, "mp"),
        P("mp", None),
        P("seq", "mp"),
    )
    out_specs = (
        P("seq", "mp"),
        P("seq", "mp"),
        P(),
        P("seq", "mp"),
        P("seq", "mp"),
        P(None, "mp"),
        P("mp"),
        P("mp", None, None),
        P("mp", None, None),
        P("mp"),
        P("mp"),
        P("mp"),
        P(("mp", "seq"), None),
        P(),
        P("seq", "mp"),
        P("seq", "mp"),
        P(("mp", "seq"), None),
    )
    return jax.shard_map(body, mesh=mesh, in_specs=in_specs, out_specs=out_specs, check_vma=False)
```

time: 1600 us -> 936 us (0.58)
  waiting for transfers between devices: 967 us -> 520 us
  local copies, waits for them, and re-layouts: 262 us -> 26.9 us
  other arithmetic: 146 us -> 32.7 us
  starting transfers between devices: 3.64 us -> 98.5 us
  blocking collectives: 54.6 us -> 115 us
  matrix products: 136 us -> 89 us
  Pallas kernels: 0 us -> 28.4 us
    psum x4 -> x1, waiting for transfers between devices: 458 us -> 0.01 us  [body(): lax.psum((sums, diagonal_blocks(gate_grads[:, :inner_width], groups), dia...]
    ppermute x2 -> x50, waiting for transfers between devices: 0.5 us -> 416 us  [the longest x48 415 us: over_mp(): return lax.ppermute(value, 'mp', list(pairs))]
    reduce_scatter x5, waiting for transfers between devices: 364 us -> 103 us  [over_seq(): return lax.psum_scatter(value, 'seq', scatter_dimension=0, tiled=True)]
    all_gather x2 -> x0, waiting for transfers between devices: 143 us -> none  [the longest x1 83.1 us: body(): rows_full = lax.all_gather(stream, 'mp', axis=1, tiled=True)]
    pad x94 -> x1, local copies, waits for them, and re-layouts: 112 us -> 1.05 us  [body(): valid_pad = jnp.pad(valid, ((0, 0), (SUB, SUB), (0, 0)))]
    ppermute x2 -> x50, starting transfers between devices: 3.19 us -> 97.9 us  [the longest x48 95.3 us: over_mp(): return lax.ppermute(value, 'mp', list(pairs))]
    slice x97 -> x4, local copies, waits for them, and re-layouts: 84.1 us -> 1.95 us  [the longest x1 0.72 us: body(): stream[count - SUB:]]
    psum x1 -> x2, blocking collectives: 25.1 us -> 64.3 us  [the longest x1 38.6 us: body(): d_gains = lax.psum((d_gain_first, d_gain_second), ('seq', 'mp'))]
  transfers between devices with their start and end apart: 13 -> 56, of which waited for: 11 -> 30; matrix products, arithmetic and copies ran while one was open for 21% -> 11% of each run, Pallas kernels for 0% -> 2%
where the time goes in v1:
time: 936 us; the launch traced here: 927 us
  waiting for transfers between devices  520 us (56%)
  blocking collectives  115 us (12%)
  starting transfers between devices  98.5 us (11%)
  matrix products  89 us (10%)
  other arithmetic  32.7 us (3%)
  Pallas kernels  28.4 us (3%)
  local copies, waits for them, and re-layouts  26.9 us (3%)
  between operations  15.9 us (2%)
    ppermute x48, waiting for transfers between devices, over_mp(): return lax.ppermute(value, 'mp', list(pairs))  415 us
    reduce_scatter x5, waiting for transfers between devices, over_seq(): return lax.psum_scatter(value, 'seq', scatter_dimension=0, tiled=True)  103 us
    ppermute x48, starting transfers between devices, over_mp(): return lax.ppermute(value, 'mp', list(pairs))  95.3 us
    dot_general x6, matrix products, matmul_tn(): lax.dot_general(left, right, (((0,), (0,)), ((), ())), preferred_element_...  40.4 us
    psum x1, blocking collectives, body(): d_gains = lax.psum((d_gain_first, d_gain_second), ('seq', 'mp'))  38.6 us
    all_gather x1, blocking collectives, body(): before = lax.all_gather(payload, 'mp', axis=1, tiled=True)  32.8 us
    dot_general x5, matrix products, matmul_nt(): lax.dot_general(left, right, (((1,), (1,)), ((), ())), preferred_element_...  25.8 us
    psum x1, blocking collectives, body(): lax.psum((sums, diagonal_blocks(gate_grads[:, :inner_width], groups), dia...  25.7 us
  transfers between devices with their start and end apart: 56, of which 30 were waited for; matrix products, arithmetic and copies ran while one was open for 11% of the time, Pallas kernels for 2%

profile of v1, /device:TPU:0, one launch (start us, length us, event | category | flops | bytes accessed | tf_op | source)
XLA Modules:
  0.0 926.5 jit_solution(8423000917269574392)
XLA Ops:
  20.9 8.4 fusion.31.gate_ref
  29.4 4.5 collective-permute-done
  39.6 32.8 %all_gather.15 = f32[16,2048]{1,0:T(8,128)S(1)} all-gather(f32[16,512]{1,0:T(8,128)S(1)} %collective-permute-done.7), channel_id=1, replica_groups=mesh['seq'=8,'mp'=4] {'mp'}, dimensions={1}, use_global_device_ids=true | all-gather | bytes 163840 | tf_op jit(solution)/shard_map/all_gather | solution.py:460
  77.2 23.5 %collective-permute-done.4 = f32[512,512]{1,0:T(8,128)S(1)} collective-permute-done((f32[512,512]{1,0:T(8,128)}, f32[512,512]{1,0:T(8,128)S(1)}, u32[]{:S(2)}, u32[]{:S(2)}) %collective-permute-start.4) | collective-permute-done | bytes 1048608 | tf_op jit(solution)/shard_map/ppermute | solution.py:40
  102.0 15.1 %collective-permute-done.6 = f32[512,512]{1,0:T(8,128)S(1)} collective-permute-done((f32[512,512]{1,0:T(8,128)S(1)}, f32[512,512]{1,0:T(8,128)S(1)}, u32[]{:S(2)}, u32[]{:S(2)}) %collective-permute-start.6) | collective-permute-done | bytes 1048608 | tf_op jit(solution)/shard_map/ppermute | solution.py:40
  120.6 11.4 %recurrence_forward.1 = (f32[512,640]{1,0:T(8,128)S(1)}, bf16[512,640]{1,0:T(8,128)(2,1)S(1)}, f32[512,640]{1,0:T(8,128)}, f32[512,640]{1,0:T(8,128)}, f32[512,6...) custom-call(f32[512,640]{1,0:T(8,128)} %fusion.63.inner_ref, ...), custom_call_target="tpu_custom_call" | custom-call | flops 838860800 | bytes 11796480 | tf_op jit(solution)/shard_map/recurrence_forward/pallas_call | solution.py:334
  132.9 9.3 all-gather
  153.4 21.7 %collective-permute-done.10 = f32[512,512]{1,0:T(8,128)S(1)} collective-permute-done((f32[512,512]{1,0:T(8,128)S(1)}, f32[512,512]{1,0:T(8,128)S(1)}, u32[]{:S(2)}, u32[]{:S(2)}) %collective-permute-start.10) | collective-permute-done | bytes 1048608 | tf_op jit(solution)/shard_map/ppermute | solution.py:40
  176.0 4.3 collective-permute-start.25
  180.3 17.2 %collective-permute-done.8 = f32[512,512]{1,0:T(8,128)S(1)} collective-permute-done((f32[512,512]{1,0:T(8,128)S(1)}, f32[512,512]{1,0:T(8,128)S(1)}, u32[]{:S(2)}, u32[]{:S(2)}) %collective-permute-start.8) | collective-permute-done | bytes 1048608 | tf_op jit(solution)/shard_map/ppermute | solution.py:40
  198.9 5.4 collective-permute-start.12
  205.9 14.1 %collective-permute-done.25 = f32[512,512]{1,0:T(8,128)} collective-permute-done((f32[512,512]{1,0:T(8,128)S(1)}, f32[512,512]{1,0:T(8,128)}, u32[]{:S(2)}, u32[]{:S(2)}) %collective-permute-start.25) | collective-permute-done | bytes 1048608 | tf_op jit(solution)/shard_map/ppermute | solution.py:40
  220.8 21.3 %collective-permute-done.12 = f32[512,512]{1,0:T(8,128)S(1)} collective-permute-done((f32[512,512]{1,0:T(8,128)S(1)}, f32[512,512]{1,0:T(8,128)S(1)}, u32[]{:S(2)}, u32[]{:S(2)}) %collective-permute-start.12) | collective-permute-done | bytes 1048608 | tf_op jit(solution)/shard_map/ppermute | solution.py:40
  252.0 17.1 %collective-permute-done.15 = f32[512,512]{1,0:T(8,128)} collective-permute-done((f32[512,512]{1,0:T(8,128)S(1)}, f32[512,512]{1,0:T(8,128)}, u32[]{:S(2)}, u32[]{:S(2)}) %collective-permute-start.15) | collective-permute-done | bytes 1048608 | tf_op jit(solution)/shard_map/ppermute | solution.py:40
  274.3 7.5 collective-permute-start.13
  283.1 8.4 collective-permute-done.27
  292.9 21.1 %collective-permute-done.13 = f32[512]{0:T(512)S(1)} collective-permute-done((f32[512]{0:T(512)S(1)}, f32[512]{0:T(512)S(1)}, u32[]{:S(2)}, u32[]{:S(2)}) %collective-permute-start.13) | collective-permute-done | bytes 2080 | tf_op jit(solution)/shard_map/ppermute | solution.py:40
  321.0 15.5 %collective-permute-done.17 = f32[512,512]{1,0:T(8,128)S(1)} collective-permute-done((f32[512,512]{1,0:T(8,128)S(1)}, f32[512,512]{1,0:T(8,128)S(1)}, u32[]{:S(2)}, u32[]{:S(2)}) %collective-permute-start.17) | collective-permute-done | bytes 1048608 | tf_op jit(solution)/shard_map/ppermute | solution.py:40
  336.7 21.4 %collective-permute-done.19 = f32[512,512]{1,0:T(8,128)S(1)} collective-permute-done((f32[512,512]{1,0:T(8,128)S(1)}, f32[512,512]{1,0:T(8,128)S(1)}, u32[]{:S(2)}, u32[]{:S(2)}) %collective-permute-start.19) | collective-permute-done | bytes 1048608 | tf_op jit(solution)/shard_map/ppermute | solution.py:40
  358.3 8.6 fusion.66
  366.9 8.3 multiply_convert_fusion.1
  376.9 11.9 %fusion.27 = f32[2048,3072]{1,0:T(8,128)} fusion(bf16[512,2048]{1,0:T(8,128)(2,1)S(1)} %fusion.47, bf16[512,1536]{1,0:T(8,128)(2,1)S(1)} %get-tuple-element.88, bf16[512,1536]{1,0:T(8,128)(2,1)S(1)} %get-tuple-element.87), kind=kOutput, calls=%fused_computation.45 | convolution fusion | flops 6448742400 | bytes 30408704 | tf_op jit(solution)/shard_map/dot_general | solution.py:29
  389.0 11.7 %fusion.23 = (f32[2048]{0:T(1024)S(1)}, f32[512]{0:T(512)S(1)}, f32[512,2048]{1,0:T(8,128)S(1)}) fusion(bf16[512,2048]{1,0:T(8,128)(2,1)} %copy-done.26, bf16[2048,3072]{1,0:T(8,128)(2,1)} %constant_dynamic-update-slice_fusion, bf16[512,1536]{1,0:T(8,128)(2,1)} %copy-done.46, bf16[512,1536]{1,0:T(8,128)(2,1)} %copy-done.45), kind=kOutput, calls=%fused_computation.41 | convolution fusion | flops 6452934144 | bytes 22030336 | tf_op jit(solution)/shard_map/dot_general | solution.py:25
  403.6 22.2 %collective-permute-done.32 = f32[512,512]{1,0:T(8,128)S(1)} collective-permute-done((f32[512,512]{1,0:T(8,128)S(1)}, f32[512,512]{1,0:T(8,128)S(1)}, u32[]{:S(2)}, u32[]{:S(2)}) %collective-permute-start.32) | collective-permute-done | bytes 1048608 | tf_op jit(solution)/shard_map/ppermute | solution.py:40
  426.7 19.5 %collective-permute-done.30 = f32[512,512]{1,0:T(8,128)S(1)} collective-permute-done((f32[512,512]{1,0:T(8,128)S(1)}, f32[512,512]{1,0:T(8,128)S(1)}, u32[]{:S(2)}, u32[]{:S(2)}) %collective-permute-start.30) | collective-permute-done | bytes 1048608 | tf_op jit(solution)/shard_map/ppermute | solution.py:40
  447.5 4.3 collective-permute-start.34
  451.9 21.7 %collective-permute-done.35 = f32[512]{0:T(512)S(1)} collective-permute-done((f32[512]{0:T(512)S(1)}, f32[512]{0:T(512)S(1)}, u32[]{:S(2)}, u32[]{:S(2)}) %collective-permute-start.35) | collective-permute-done | bytes 2080 | tf_op jit(solution)/shard_map/ppermute | solution.py:40
  481.3 19.3 %collective-permute-done.37 = f32[512,512]{1,0:T(8,128)S(1)} collective-permute-done((f32[512,512]{1,0:T(8,128)S(1)}, f32[512,512]{1,0:T(8,128)S(1)}, u32[]{:S(2)}, u32[]{:S(2)}) %collective-permute-start.37) | collective-permute-done | bytes 1048608 | tf_op jit(solution)/shard_map/ppermute | solution.py:40
  505.1 19.4 %collective-permute-done.39 = f32[512,512]{1,0:T(8,128)S(1)} collective-permute-done((f32[512,512]{1,0:T(8,128)S(1)}, f32[512,512]{1,0:T(8,128)S(1)}, u32[]{:S(2)}, u32[]{:S(2)}) %collective-permute-start.39) | collective-permute-done | bytes 1048608 | tf_op jit(solution)/shard_map/ppermute | solution.py:40
  524.7 23.5 %collective-permute-done.41 = f32[512,512]{1,0:T(8,128)S(1)} collective-permute-done((f32[512,512]{1,0:T(8,128)S(1)}, f32[512,512]{1,0:T(8,128)S(1)}, u32[]{:S(2)}, u32[]{:S(2)}) %collective-permute-start.41) | collective-permute-done | bytes 1048608 | tf_op jit(solution)/shard_map/ppermute | solution.py:40
  555.5 9.1 all-gather.2.ends_ref
  565.8 10.7 %recurrence_backward.1 = (bf16[512,640]{1,0:T(8,128)(2,1)S(1)}, f32[16,640]{1,0:T(8,128)S(1)}, f32[8,640]{1,0:T(8,128)S(1)}, bf16[512,1280]{1,0:T(8,128)(2,1)S(1)}, f32[8,640]{1,0:T(8,128)S(1)}) custom-call(s32[1]{0:T(128)} %bitcast.mine_ref, f32[8,2,640]{2,1,0:T(2,128)S(1)} %all-gather.2.ends_ref, f32[512,640]{1,0:T(8,128)} %copy-done.6, ...), custom_call_target="tpu_custom_call" | custom-call | flops 838860800 | bytes 13107200 | tf_op jit(solution)/shard_map/recurrence_backward/pallas_call | solution.py:391
  580.0 5.9 fusion.71
  585.9 5.7 fusion.73
  594.8 5.8 fusion.70
  600.7 10.1 %fusion.74 = f32[1536,2048]{1,0:T(8,128)} fusion(bf16[512,1536]{1,0:T(8,128)(2,1)} %get-tuple-element.89, bf16[512,2048]{1,0:T(8,128)(2,1)} %copy-done.25), kind=kOutput, calls=%fused_computation.169 | convolution fusion | flops 3221225472 | bytes 16252928 | tf_op jit(solution)/shard_map/dot_general | solution.py:29
  610.8 6.1 fusion.67
  626.3 14.8 %collective-permute-done.22 = f32[512,512]{1,0:T(8,128)S(1)} collective-permute-done((f32[512,512]{1,0:T(8,128)S(1)}, f32[512,512]{1,0:T(8,128)S(1)}, u32[]{:S(2)}, u32[]{:S(2)}) %collective-permute-start.22) | collective-permute-done | bytes 1048608 | tf_op jit(solution)/shard_map/ppermute | solution.py:40
  642.0 7.1 collective-permute-start.43
  649.1 14.4 %collective-permute-done.45 = f32[512,512]{1,0:T(8,128)S(1)} collective-permute-done((f32[512,512]{1,0:T(8,128)S(1)}, f32[512,512]{1,0:T(8,128)S(1)}, u32[]{:S(2)}, u32[]{:S(2)}) %collective-permute-start.45) | collective-permute-done | bytes 1048608 | tf_op jit(solution)/shard_map/ppermute | solution.py:40
  664.5 21.5 %collective-permute-done.20 = f32[512,512]{1,0:T(8,128)S(1)} collective-permute-done((f32[512,512]{1,0:T(8,128)S(1)}, f32[512,512]{1,0:T(8,128)S(1)}, u32[]{:S(2)}, u32[]{:S(2)}) %collective-permute-start.20) | collective-permute-done | bytes 1048608 | tf_op jit(solution)/shard_map/ppermute | solution.py:40
  687.2 5.2 collective-permute-start.24
  692.4 16.1 %collective-permute-done.43 = f32[512,512]{1,0:T(8,128)S(1)} collective-permute-done((f32[512,512]{1,0:T(8,128)S(1)}, f32[512,512]{1,0:T(8,128)S(1)}, u32[]{:S(2)}, u32[]{:S(2)}) %collective-permute-start.43) | collective-permute-done | bytes 1048608 | tf_op jit(solution)/shard_map/ppermute | solution.py:40
  716.7 14.2 %collective-permute-done.24 = f32[512,512]{1,0:T(8,128)S(1)} collective-permute-done((f32[512,512]{1,0:T(8,128)S(1)}, f32[512,512]{1,0:T(8,128)S(1)}, u32[]{:S(2)}, u32[]{:S(2)}) %collective-permute-start.24) | collective-permute-done | bytes 1048608 | tf_op jit(solution)/shard_map/ppermute | solution.py:40
  732.4 25.7 %psum.36 = f32[8,640]{1,0:T(8,128)S(1)} all-reduce(f32[8,640]{1,0:T(8,128)S(1)} %get-tuple-element.66), channel_id=1, replica_groups=mesh['seq'=8,'mp'=4] {'seq'}, use_global_device_ids=true, to_apply=%region_10.11 | all-reduce | flops 5120 | bytes 40960 | tf_op jit(solution)/shard_map/psum | solution.py:562
  765.6 38.6 %all-reduce.11 = (f32[2048]{0:T(1024)}, f32[2048]{0:T(1024)}) all-reduce(f32[2048]{0:T(1024)S(1)} %div.29, f32[2048]{0:T(1024)S(1)} %div.31), channel_id=1, replica_groups=mesh['seq'=8,'mp'=4] {'seq','mp'}, use_global_device_ids=true, to_apply=%region_7.8 | all-reduce | flops 4096 | bytes 32768 | tf_op jit(solution)/shard_map/psum | solution.py:560
  812.0 6.9 reduce-scatter.6.cloned.1.call-done
  818.9 96.4 %reduce-scatter.14.cloned.1.call-done = f32[192,2048]{1,0:T(8,128)} async-done(((f32[1536,2048]{1,0:T(8,128)}), f32[192,2048]{1,0:T(8,128)}) %reduce-scatter.14.cloned.1.call-update) | async-done | bytes 1572880 | tf_op jit(solution)/shard_map/reduce_scatter | solution.py:573
  (295 shorter events, 146.2 us)
Async XLA Ops:
  7.3 800.7 %reduce-scatter.12.cloned.1.call-start = ((), (), s32[]{:S(2)}) async-start(), calls=%async_computation.8 | async-start | bytes 28311552 | tf_op jit(solution)/shard_map/reduce_scatter | solution.py:573
  7.3 31.1 %collective-permute-start.2 = (f32[512,512]{1,0:T(8,128)}, f32[512,512]{1,0:T(8,128)}, u32[]{:S(2)}, u32[]{:S(2)}) collective-permute-start(f32[512,512]{1,0:T(8,128)} %param.20), channel_id=1, source_target_pairs={{0,1},{1,0},{2,3},{3,2},{4,5},{5,4},{6,7},{7,6},{8,9},{9,8},{10,11... | collective-permute-start | bytes 3145736 | tf_op jit(solution)/shard_map/ppermute | solution.py:40
  10.4 62.0 %collective-permute-start.3 = (f32[512,512]{1,0:T(8,128)}, f32[512,512]{1,0:T(8,128)}, u32[]{:S(2)}, u32[]{:S(2)}) collective-permute-start(f32[512,512]{1,0:T(8,128)} %param.20), channel_id=1, source_target_pairs={{1,2},{2,1},{5,6},{6,5},{9,10},{10,9},{13,14},{14,13},{17,18},{18,... | collective-permute-start | bytes 3145736 | tf_op jit(solution)/shard_map/ppermute | solution.py:40
  18.4 21.2 %collective-permute-start.7 = (f32[16,512]{1,0:T(8,128)S(1)}, f32[16,512]{1,0:T(8,128)S(1)}, u32[]{:S(2)}, u32[]{:S(2)}) collective-permute-start(f32[16,512]{1,0:T(8,128)S(1)} %pad_maximum_fusion.5), channel_id=1, source_target_pairs={{0,4},{4,8},{8,12},{12,16},{16,20},{20,24},{24,28},{1,5},{5,9},{9,... | collective-permute-start | bytes 98312 | tf_op jit(solution)/shard_map/ppermute | solution.py:459
  38.4 35.5 %collective-permute-start.5 = (f32[512,512]{1,0:T(8,128)}, f32[512,512]{1,0:T(8,128)S(1)}, u32[]{:S(2)}, u32[]{:S(2)}) collective-permute-start(f32[512,512]{1,0:T(8,128)} %collective-permute-done.2), channel_id=1, source_target_pairs={{1,2},{2,1},{5,6},{6,5},{9,10},{10,9},{13,14},{14,13},{17,18},{18,... | collective-permute-start | bytes 3145736 | tf_op jit(solution)/shard_map/ppermute | solution.py:40
  72.4 28.2 %collective-permute-start.4 = (f32[512,512]{1,0:T(8,128)}, f32[512,512]{1,0:T(8,128)S(1)}, u32[]{:S(2)}, u32[]{:S(2)}) collective-permute-start(f32[512,512]{1,0:T(8,128)} %collective-permute-done.3), channel_id=1, source_target_pairs={{1,0},{2,3},{5,4},{6,7},{9,8},{10,11},{13,12},{14,15},{17,16},{18,... | collective-permute-start | bytes 3145736 | tf_op jit(solution)/shard_map/ppermute | solution.py:40
  74.0 43.2 %collective-permute-start.6 = (f32[512,512]{1,0:T(8,128)S(1)}, f32[512,512]{1,0:T(8,128)S(1)}, u32[]{:S(2)}, u32[]{:S(2)}) collective-permute-start(f32[512,512]{1,0:T(8,128)S(1)} %collective-permute-done.5), channel_id=1, source_target_pairs={{1,0},{2,3},{5,4},{6,7},{9,8},{10,11},{13,12},{14,15},{17,16},{18,... | collective-permute-start | bytes 3145736 | tf_op jit(solution)/shard_map/ppermute | solution.py:40
  150.0 25.1 %collective-permute-start.10 = (f32[512,512]{1,0:T(8,128)S(1)}, f32[512,512]{1,0:T(8,128)S(1)}, u32[]{:S(2)}, u32[]{:S(2)}) collective-permute-start(f32[512,512]{1,0:T(8,128)S(1)} %get-tuple-element.97), channel_id=1, source_target_pairs={{0,1},{3,2},{4,5},{7,6},{8,9},{11,10},{12,13},{15,14},{16,17},{19,... | collective-permute-start | bytes 3145736 | tf_op jit(solution)/shard_map/ppermute | solution.py:40
  151.7 45.9 %collective-permute-start.8 = (f32[512,512]{1,0:T(8,128)S(1)}, f32[512,512]{1,0:T(8,128)S(1)}, u32[]{:S(2)}, u32[]{:S(2)}) collective-permute-start(f32[512,512]{1,0:T(8,128)S(1)} %get-tuple-element.96), channel_id=1, source_target_pairs={{0,1},{3,2},{4,5},{7,6},{8,9},{11,10},{12,13},{15,14},{16,17},{19,... | collective-permute-start | bytes 3145736 | tf_op jit(solution)/shard_map/ppermute | solution.py:40
  175.3 23.4 %collective-permute-start.11 = (f32[512,512]{1,0:T(8,128)S(1)}, f32[512,512]{1,0:T(8,128)S(1)}, u32[]{:S(2)}, u32[]{:S(2)}) collective-permute-start(f32[512,512]{1,0:T(8,128)S(1)} %add.265), channel_id=1, source_target_pairs={{1,2},{2,1},{5,6},{6,5},{9,10},{10,9},{13,14},{14,13},{17,18},{18,... | collective-permute-start | bytes 3145736 | tf_op jit(solution)/shard_map/ppermute | solution.py:40
  176.0 44.0 %collective-permute-start.25 = (f32[512,512]{1,0:T(8,128)S(1)}, f32[512,512]{1,0:T(8,128)}, u32[]{:S(2)}, u32[]{:S(2)}) collective-permute-start(f32[512,512]{1,0:T(8,128)S(1)} %copy-done.21), channel_id=1, source_target_pairs={{0,1},{1,0},{2,3},{3,2},{4,5},{5,4},{6,7},{7,6},{8,9},{9,8},{10,11... | collective-permute-start | bytes 3145736 | tf_op jit(solution)/shard_map/ppermute | solution.py:40
  197.8 23.0 %collective-permute-start.9 = (f32[512,512]{1,0:T(8,128)S(1)}, f32[512,512]{1,0:T(8,128)S(1)}, u32[]{:S(2)}, u32[]{:S(2)}) collective-permute-start(f32[512,512]{1,0:T(8,128)S(1)} %add.263), channel_id=1, source_target_pairs={{1,2},{2,1},{5,6},{6,5},{9,10},{10,9},{13,14},{14,13},{17,18},{18,... | collective-permute-start | bytes 3145736 | tf_op jit(solution)/shard_map/ppermute | solution.py:40
  198.9 43.2 %collective-permute-start.12 = (f32[512,512]{1,0:T(8,128)S(1)}, f32[512,512]{1,0:T(8,128)S(1)}, u32[]{:S(2)}, u32[]{:S(2)}) collective-permute-start(f32[512,512]{1,0:T(8,128)S(1)} %dynamic-slice_add_fusion.3), channel_id=1, source_target_pairs={{0,1},{1,0},{2,3},{3,2},{4,5},{5,4},{6,7},{7,6},{8,9},{9,8},{10,11... | collective-permute-start | bytes 3145736 | tf_op jit(solution)/shard_map/ppermute | solution.py:40
  204.2 43.9 %collective-permute-start.26 = (f32[512,512]{1,0:T(8,128)S(1)}, f32[512,512]{1,0:T(8,128)}, u32[]{:S(2)}, u32[]{:S(2)}) collective-permute-start(f32[512,512]{1,0:T(8,128)S(1)} %copy-done.21), channel_id=1, source_target_pairs={{1,2},{2,1},{5,6},{6,5},{9,10},{10,9},{13,14},{14,13},{17,18},{18,... | collective-permute-start | bytes 3145736 | tf_op jit(solution)/shard_map/ppermute | solution.py:40
  220.0 30.7 %collective-permute-start.28 = (f32[512,512]{1,0:T(8,128)}, f32[512,512]{1,0:T(8,128)S(1)}, u32[]{:S(2)}, u32[]{:S(2)}) collective-permute-start(f32[512,512]{1,0:T(8,128)} %collective-permute-done.25), channel_id=1, source_target_pairs={{1,2},{2,1},{5,6},{6,5},{9,10},{10,9},{13,14},{14,13},{17,18},{18,... | collective-permute-start | bytes 3145736 | tf_op jit(solution)/shard_map/ppermute | solution.py:40
  242.5 26.6 %collective-permute-start.15 = (f32[512,512]{1,0:T(8,128)S(1)}, f32[512,512]{1,0:T(8,128)}, u32[]{:S(2)}, u32[]{:S(2)}) collective-permute-start(f32[512,512]{1,0:T(8,128)S(1)} %get-tuple-element.84), channel_id=1, source_target_pairs={{0,1},{1,0},{2,3},{3,2},{4,5},{5,4},{6,7},{7,6},{8,9},{9,8},{10,11... | collective-permute-start | bytes 3145736 | tf_op jit(solution)/shard_map/ppermute | solution.py:40
  248.1 43.4 %collective-permute-start.27 = (f32[512,512]{1,0:T(8,128)}, f32[512,512]{1,0:T(8,128)S(1)}, u32[]{:S(2)}, u32[]{:S(2)}) collective-permute-start(f32[512,512]{1,0:T(8,128)} %collective-permute-done.26), channel_id=1, source_target_pairs={{1,0},{2,3},{5,4},{6,7},{9,8},{10,11},{13,12},{14,15},{17,16},{18,... | collective-permute-start | bytes 3145736 | tf_op jit(solution)/shard_map/ppermute | solution.py:40
  249.5 32.3 %collective-permute-start.16 = (f32[512,512]{1,0:T(8,128)S(1)}, f32[512,512]{1,0:T(8,128)S(1)}, u32[]{:S(2)}, u32[]{:S(2)}) collective-permute-start(f32[512,512]{1,0:T(8,128)S(1)} %get-tuple-element.84), channel_id=1, source_target_pairs={{1,2},{2,1},{5,6},{6,5},{9,10},{10,9},{13,14},{14,13},{17,18},{18,... | collective-permute-start | bytes 3145736 | tf_op jit(solution)/shard_map/ppermute | solution.py:40
  250.7 64.6 %collective-permute-start.29 = (f32[512,512]{1,0:T(8,128)S(1)}, f32[512,512]{1,0:T(8,128)S(1)}, u32[]{:S(2)}, u32[]{:S(2)}) collective-permute-start(f32[512,512]{1,0:T(8,128)S(1)} %collective-permute-done.28), channel_id=1, source_target_pairs={{1,0},{2,3},{5,4},{6,7},{9,8},{10,11},{13,12},{14,15},{17,16},{18,... | collective-permute-start | bytes 3145736 | tf_op jit(solution)/shard_map/ppermute | solution.py:40
  269.1 44.9 %collective-permute-start.18 = (f32[512,512]{1,0:T(8,128)}, f32[512,512]{1,0:T(8,128)S(1)}, u32[]{:S(2)}, u32[]{:S(2)}) collective-permute-start(f32[512,512]{1,0:T(8,128)} %collective-permute-done.15), channel_id=1, source_target_pairs={{1,2},{2,1},{5,6},{6,5},{9,10},{10,9},{13,14},{14,13},{17,18},{18,... | collective-permute-start | bytes 3145736 | tf_op jit(solution)/shard_map/ppermute | solution.py:40
  274.3 39.7 %collective-permute-start.13 = (f32[512]{0:T(512)S(1)}, f32[512]{0:T(512)S(1)}, u32[]{:S(2)}, u32[]{:S(2)}) collective-permute-start(f32[512]{0:T(512)S(1)} %get-tuple-element.83), channel_id=1, source_target_pairs={{0,1},{1,0},{2,3},{3,2},{4,5},{5,4},{6,7},{7,6},{8,9},{9,8},{10,11... | collective-permute-start | bytes 6152 | tf_op jit(solution)/shard_map/ppermute | solution.py:40
  281.8 54.7 %collective-permute-start.17 = (f32[512,512]{1,0:T(8,128)S(1)}, f32[512,512]{1,0:T(8,128)S(1)}, u32[]{:S(2)}, u32[]{:S(2)}) collective-permute-start(f32[512,512]{1,0:T(8,128)S(1)} %collective-permute-done.16), channel_id=1, source_target_pairs={{1,0},{2,3},{5,4},{6,7},{9,8},{10,11},{13,12},{14,15},{17,16},{18,... | collective-permute-start | bytes 3145736 | tf_op jit(solution)/shard_map/ppermute | solution.py:40
  314.0 44.1 %collective-permute-start.19 = (f32[512,512]{1,0:T(8,128)S(1)}, f32[512,512]{1,0:T(8,128)S(1)}, u32[]{:S(2)}, u32[]{:S(2)}) collective-permute-start(f32[512,512]{1,0:T(8,128)S(1)} %collective-permute-done.18), channel_id=1, source_target_pairs={{1,0},{2,3},{5,4},{6,7},{9,8},{10,11},{13,12},{14,15},{17,16},{18,... | collective-permute-start | bytes 3145736 | tf_op jit(solution)/shard_map/ppermute | solution.py:40
  388.8 423.2 %all-reduce.15.cloned.1.call-start = ((), (), s32[]{:S(2)}) async-start(), calls=%async_computation.10 | async-start | bytes 2621440 | tf_op jit(solution)/shard_map/psum | solution.py:562
  400.9 24.9 %collective-permute-start.32 = (f32[512,512]{1,0:T(8,128)S(1)}, f32[512,512]{1,0:T(8,128)S(1)}, u32[]{:S(2)}, u32[]{:S(2)}) collective-permute-start(f32[512,512]{1,0:T(8,128)S(1)} %get-tuple-element.93), channel_id=1, source_target_pairs={{0,1},{3,2},{4,5},{7,6},{8,9},{11,10},{12,13},{15,14},{16,17},{19,... | collective-permute-start | bytes 3145736 | tf_op jit(solution)/shard_map/ppermute | solution.py:40
  402.3 44.0 %collective-permute-start.30 = (f32[512,512]{1,0:T(8,128)S(1)}, f32[512,512]{1,0:T(8,128)S(1)}, u32[]{:S(2)}, u32[]{:S(2)}) collective-permute-start(f32[512,512]{1,0:T(8,128)S(1)} %get-tuple-element.92), channel_id=1, source_target_pairs={{0,1},{3,2},{4,5},{7,6},{8,9},{11,10},{12,13},{15,14},{16,17},{19,... | collective-permute-start | bytes 3145736 | tf_op jit(solution)/shard_map/ppermute | solution.py:40
  426.0 21.3 %collective-permute-start.33 = (f32[512,512]{1,0:T(8,128)S(1)}, f32[512,512]{1,0:T(8,128)S(1)}, u32[]{:S(2)}, u32[]{:S(2)}) collective-permute-start(f32[512,512]{1,0:T(8,128)S(1)} %add.288), channel_id=1, source_target_pairs={{1,2},{2,1},{5,6},{6,5},{9,10},{10,9},{13,14},{14,13},{17,18},{18,... | collective-permute-start | bytes 3145736 | tf_op jit(solution)/shard_map/ppermute | solution.py:40
  446.4 31.7 %collective-permute-start.31 = (f32[512,512]{1,0:T(8,128)S(1)}, f32[512,512]{1,0:T(8,128)S(1)}, u32[]{:S(2)}, u32[]{:S(2)}) collective-permute-start(f32[512,512]{1,0:T(8,128)S(1)} %add.286), channel_id=1, source_target_pairs={{1,2},{2,1},{5,6},{6,5},{9,10},{10,9},{13,14},{14,13},{17,18},{18,... | collective-permute-start | bytes 3145736 | tf_op jit(solution)/shard_map/ppermute | solution.py:40
  447.5 30.6 %collective-permute-start.34 = (f32[512,512]{1,0:T(8,128)S(1)}, f32[512,512]{1,0:T(8,128)S(1)}, u32[]{:S(2)}, u32[]{:S(2)}) collective-permute-start(f32[512,512]{1,0:T(8,128)S(1)} %dynamic-slice_add_fusion.1), channel_id=1, source_target_pairs={{0,1},{1,0},{2,3},{3,2},{4,5},{5,4},{6,7},{7,6},{8,9},{9,8},{10,11... | collective-permute-start | bytes 3145736 | tf_op jit(solution)/shard_map/ppermute | solution.py:40
  451.9 21.8 %collective-permute-start.35 = (f32[512]{0:T(512)S(1)}, f32[512]{0:T(512)S(1)}, u32[]{:S(2)}, u32[]{:S(2)}) collective-permute-start(f32[512]{0:T(512)S(1)} %get-tuple-element.70), channel_id=1, source_target_pairs={{0,1},{1,0},{2,3},{3,2},{4,5},{5,4},{6,7},{7,6},{8,9},{9,8},{10,11... | collective-permute-start | bytes 6152 | tf_op jit(solution)/shard_map/ppermute | solution.py:40
  478.8 21.9 %collective-permute-start.37 = (f32[512,512]{1,0:T(8,128)S(1)}, f32[512,512]{1,0:T(8,128)S(1)}, u32[]{:S(2)}, u32[]{:S(2)}) collective-permute-start(f32[512,512]{1,0:T(8,128)S(1)} %get-tuple-element.82), channel_id=1, source_target_pairs={{0,1},{1,0},{2,3},{3,2},{4,5},{5,4},{6,7},{7,6},{8,9},{9,8},{10,11... | collective-permute-start | bytes 3145736 | tf_op jit(solution)/shard_map/ppermute | solution.py:40
  501.4 23.1 %collective-permute-start.39 = (f32[512,512]{1,0:T(8,128)S(1)}, f32[512,512]{1,0:T(8,128)S(1)}, u32[]{:S(2)}, u32[]{:S(2)}) collective-permute-start(f32[512,512]{1,0:T(8,128)S(1)} %collective-permute-done.38), channel_id=1, source_target_pairs={{1,0},{2,3},{5,4},{6,7},{9,8},{10,11},{13,12},{14,15},{17,16},{18,... | collective-permute-start | bytes 3145736 | tf_op jit(solution)/shard_map/ppermute | solution.py:40
  502.7 45.5 %collective-permute-start.41 = (f32[512,512]{1,0:T(8,128)S(1)}, f32[512,512]{1,0:T(8,128)S(1)}, u32[]{:S(2)}, u32[]{:S(2)}) collective-permute-start(f32[512,512]{1,0:T(8,128)S(1)} %collective-permute-done.40), channel_id=1, source_target_pairs={{1,0},{2,3},{5,4},{6,7},{9,8},{10,11},{13,12},{14,15},{17,16},{18,... | collective-permute-start | bytes 3145736 | tf_op jit(solution)/shard_map/ppermute | solution.py:40
  579.7 232.3 %reduce-scatter.8.cloned.1.call-start = ((), (), s32[]{:S(2)}) async-start(), calls=%async_computation.6 | async-start | bytes 5898240 | tf_op jit(solution)/shard_map/reduce_scatter | solution.py:573
  585.9 226.1 %reduce-scatter.10.cloned.1.call-start = ((), (), s32[]{:S(2)}) async-start(), calls=%async_computation.7 | async-start | bytes 5898240 | tf_op jit(solution)/shard_map/reduce_scatter | solution.py:573
  591.6 227.3 %reduce-scatter.6.cloned.1.call-start = ((), (), s32[]{:S(2)}) async-start(), calls=%async_computation.5 | async-start | bytes 5898240 | tf_op jit(solution)/shard_map/reduce_scatter | solution.py:573
  600.6 314.7 %reduce-scatter.14.cloned.1.call-start = ((), (), s32[]{:S(2)}) async-start(), calls=%async_computation.9 | async-start | bytes 14155776 | tf_op jit(solution)/shard_map/reduce_scatter | solution.py:573
  617.2 23.9 %collective-permute-start.22 = (f32[512,512]{1,0:T(8,128)S(1)}, f32[512,512]{1,0:T(8,128)S(1)}, u32[]{:S(2)}, u32[]{:S(2)}) collective-permute-start(f32[512,512]{1,0:T(8,128)S(1)} %get-tuple-element.95), channel_id=1, source_target_pairs={{0,1},{3,2},{4,5},{7,6},{8,9},{11,10},{12,13},{15,14},{16,17},{19,... | collective-permute-start | bytes 3145736 | tf_op jit(solution)/shard_map/ppermute | solution.py:40
  623.6 40.0 %collective-permute-start.45 = (f32[512,512]{1,0:T(8,128)S(1)}, f32[512,512]{1,0:T(8,128)S(1)}, u32[]{:S(2)}, u32[]{:S(2)}) collective-permute-start(f32[512,512]{1,0:T(8,128)S(1)} %get-tuple-element.91), channel_id=1, source_target_pairs={{0,1},{3,2},{4,5},{7,6},{8,9},{11,10},{12,13},{15,14},{16,17},{19,... | collective-permute-start | bytes 3145736 | tf_op jit(solution)/shard_map/ppermute | solution.py:40
  624.9 61.1 %collective-permute-start.20 = (f32[512,512]{1,0:T(8,128)S(1)}, f32[512,512]{1,0:T(8,128)S(1)}, u32[]{:S(2)}, u32[]{:S(2)}) collective-permute-start(f32[512,512]{1,0:T(8,128)S(1)} %get-tuple-element.94), channel_id=1, source_target_pairs={{0,1},{3,2},{4,5},{7,6},{8,9},{11,10},{12,13},{15,14},{16,17},{19,... | collective-permute-start | bytes 3145736 | tf_op jit(solution)/shard_map/ppermute | solution.py:40
  641.3 45.7 %collective-permute-start.23 = (f32[512,512]{1,0:T(8,128)S(1)}, f32[512,512]{1,0:T(8,128)S(1)}, u32[]{:S(2)}, u32[]{:S(2)}) collective-permute-start(f32[512,512]{1,0:T(8,128)S(1)} %add.278), channel_id=1, source_target_pairs={{1,2},{2,1},{5,6},{6,5},{9,10},{10,9},{13,14},{14,13},{17,18},{18,... | collective-permute-start | bytes 3145736 | tf_op jit(solution)/shard_map/ppermute | solution.py:40
  642.0 66.5 %collective-permute-start.43 = (f32[512,512]{1,0:T(8,128)S(1)}, f32[512,512]{1,0:T(8,128)S(1)}, u32[]{:S(2)}, u32[]{:S(2)}) collective-permute-start(f32[512,512]{1,0:T(8,128)S(1)} %get-tuple-element.90), channel_id=1, source_target_pairs={{0,1},{3,2},{4,5},{7,6},{8,9},{11,10},{12,13},{15,14},{16,17},{19,... | collective-permute-start | bytes 3145736 | tf_op jit(solution)/shard_map/ppermute | solution.py:40
  663.7 47.6 %collective-permute-start.46 = (f32[512,512]{1,0:T(8,128)S(1)}, f32[512,512]{1,0:T(8,128)S(1)}, u32[]{:S(2)}, u32[]{:S(2)}) collective-permute-start(f32[512,512]{1,0:T(8,128)S(1)} %add.300), channel_id=1, source_target_pairs={{1,2},{2,1},{5,6},{6,5},{9,10},{10,9},{13,14},{14,13},{17,18},{18,... | collective-permute-start | bytes 3145736 | tf_op jit(solution)/shard_map/ppermute | solution.py:40
  686.2 30.5 %collective-permute-start.21 = (f32[512,512]{1,0:T(8,128)S(1)}, f32[512,512]{1,0:T(8,128)S(1)}, u32[]{:S(2)}, u32[]{:S(2)}) collective-permute-start(f32[512,512]{1,0:T(8,128)S(1)} %add.276), channel_id=1, source_target_pairs={{1,2},{2,1},{5,6},{6,5},{9,10},{10,9},{13,14},{14,13},{17,18},{18,... | collective-permute-start | bytes 3145736 | tf_op jit(solution)/shard_map/ppermute | solution.py:40
  687.2 43.8 %collective-permute-start.24 = (f32[512,512]{1,0:T(8,128)S(1)}, f32[512,512]{1,0:T(8,128)S(1)}, u32[]{:S(2)}, u32[]{:S(2)}) collective-permute-start(f32[512,512]{1,0:T(8,128)S(1)} %dynamic-slice_add_fusion.2), channel_id=1, source_target_pairs={{0,1},{1,0},{2,3},{3,2},{4,5},{5,4},{6,7},{7,6},{8,9},{9,8},{10,11... | collective-permute-start | bytes 3145736 | tf_op jit(solution)/shard_map/ppermute | solution.py:40
  709.6 94.6 %collective-permute-start.44 = (f32[512,512]{1,0:T(8,128)}, f32[512,512]{1,0:T(8,128)}, u32[]{:S(2)}, u32[]{:S(2)}) collective-permute-start(f32[512,512]{1,0:T(8,128)} %add.298), channel_id=1, source_target_pairs={{1,2},{2,1},{5,6},{6,5},{9,10},{10,9},{13,14},{14,13},{17,18},{18,... | collective-permute-start | bytes 3145736 | tf_op jit(solution)/shard_map/ppermute | solution.py:40
  712.5 91.7 %collective-permute-start.47 = (f32[512,512]{1,0:T(8,128)}, f32[512,512]{1,0:T(8,128)}, u32[]{:S(2)}, u32[]{:S(2)}) collective-permute-start(f32[512,512]{1,0:T(8,128)} %dynamic-slice_add_fusion), channel_id=1, source_target_pairs={{0,1},{1,0},{2,3},{3,2},{4,5},{5,4},{6,7},{7,6},{8,9},{9,8},{10,11... | collective-permute-start | bytes 3145736 | tf_op jit(solution)/shard_map/ppermute | solution.py:40
  762.7 41.5 %collective-permute-start.49 = (f32[512]{0:T(512)S(1)}, f32[512]{0:T(512)S(1)}, u32[]{:S(2)}, u32[]{:S(2)}) collective-permute-start(f32[512]{0:T(512)S(1)} %add.304), channel_id=1, source_target_pairs={{0,2},{2,0},{1,3},{3,1},{4,6},{6,4},{5,7},{7,5},{8,10},{10,8},{9,1... | collective-permute-start | bytes 6152 | tf_op jit(solution)/shard_map/ppermute | solution.py:40
  (61 other events, 1523.4 us)
Sparse Core Ops, SparseCore 0:
  388.9 155.0 reduce-scatter.11
  579.9 56.8 all-reduce.14
  641.1 55.7 reduce-scatter.7
  700.7 56.7 reduce-scatter.9
  761.7 57.1 reduce-scatter.5
  822.8 92.3 reduce-scatter.13

commit v2 on v1

--- a/solution.py
+++ b/solution.py
@@ -46,30 +46,79 @@
     return mine, mine ^ 1, 2 - half, 3 - 3 * half
 
 
-def line_gather(own):
-    beside = over_mp(own, PAIRS)
-    near_in = over_mp(own, MIDDLE)
-    near_out = over_mp(near_in, OUTWARD)
-    far_in = over_mp(beside, MIDDLE)
-    far_out = over_mp(far_in, OUTWARD)
-    return own, beside, near_in + near_out, far_in + far_out
-
-
-def line_scatter(piece):
-    mine, beside, near, far = line_places()
-    far_part = piece(far)
-    far_one = over_mp(far_part, INWARD)
-    far_two = over_mp(far_part + far_one, MIDDLE)
-    near_part = piece(near)
-    near_one = over_mp(near_part, INWARD)
-    near_two = over_mp(near_part + near_one, MIDDLE)
-    last = over_mp(piece(beside) + far_two, PAIRS)
-    return piece(mine) + near_two + last
+def after(value, *needed):
+    return lax.optimization_barrier((value, needed))[0]
+
+
+class LineGather:
+    def __init__(self, own):
+        self.own = own
+
+    def first(self, *needed):
+        own = after(self.own, *needed)
+        self.beside, self.near_in = over_mp(own, PAIRS), over_mp(own, MIDDLE)
+        return self.beside, self.near_in
+
+    def second(self, *needed):
+        near, beside = after((self.near_in, self.beside), *needed)
+        self.near_out, self.far_in = over_mp(near, OUTWARD), over_mp(beside, MIDDLE)
+        return self.near_out, self.far_in
+
+    def third(self, *needed):
+        far, _ = after((self.far_in, self.near_out), *needed)
+        self.far_out = over_mp(far, OUTWARD)
+        return self.far_out
+
+    def pieces(self):
+        return self.own, self.beside, self.near_in + self.near_out, self.far_in + self.far_out
+
+
+class LineScatter:
+    def __init__(self, whole, width):
+        self.whole, self.width = whole, width
+        self.mine, self.beside, self.near, self.far = line_places()
+
+    def piece(self, place):
+        return lax.dynamic_slice_in_dim(self.whole, place * self.width, self.width, 1)
+
+    def first(self, *needed):
+        self.far_one = over_mp(after(self.piece(self.far), *needed), INWARD)
+        return self.far_one
+
+    def second(self, *needed):
+        far, near = after(
+            (self.piece(self.far) + self.far_one, self.piece(self.near)), *needed
+        )
+        self.far_two, self.near_one = over_mp(far, MIDDLE), over_mp(near, INWARD)
+        return self.far_two, self.near_one
+
+    def third(self, *needed):
+        near, last = after(
+            (self.piece(self.near) + self.near_one, self.piece(self.beside) + self.far_two), *needed
+        )
+        self.near_two, self.last = over_mp(near, MIDDLE), over_mp(last, PAIRS)
+        return self.near_two, self.last
+
+    def result(self):
+        return self.piece(self.mine) + self.near_two + self.last
 
 
 def line_sum(value):
     value = value + over_mp(value, PAIRS)
     return value + over_mp(value, CROSS)
+
+
+def swapped(value, axis, bit):
+    count = lax.axis_size(axis)
+    return lax.ppermute(value, axis, [(d, d ^ bit) for d in range(count)])
+
+
+def sum_over(value, axis):
+    bit = 1
+    while bit < lax.axis_size(axis):
+        value = value + swapped(value, axis, bit)
+        bit *= 2
+    return value
 
 
 def assemble(pieces, width, turn):
@@ -140,7 +189,7 @@
         window = ext_ref[pl.ds(r, ROWS + SUB), :]
         total = row_ref[0:1, :] * window[SUB:]
         for k in range(1, 4):
-            valid = wide(valid_ref[k, pl.ds(r, ROWS), :], width)
+            valid = wide(valid_ref[k, pl.ds(r + SUB, ROWS), :], width)
             total = total + row_ref[k : k + 1, :] * window[SUB - k : SUB - k + ROWS] * valid
         total = total + row_ref[4:5, :]
         conv_ref[pl.ds(r, ROWS), :] = total
@@ -156,7 +205,7 @@
         rg = jax.nn.sigmoid(pre_ref[here, :width] + row_ref[5:6, :])
         ig = jax.nn.sigmoid(pre_ref[here, width:] + row_ref[6:7, :])
         log_a = row_ref[7:8, :] * rg
-        keep = wide(valid_ref[0, here, :], width)
+        keep = wide(valid_ref[0, pl.ds(r + SUB, ROWS), :], width)
         a = jnp.exp(log_a)
         root = jnp.sqrt(neg_expm1(2.0 * log_a, a * a))
         factor = (1.0 - keep) + keep * root
@@ -324,8 +373,8 @@
     return jax.ShapeDtypeStruct(dims, kind)
 
 
-def cost(flops, moved, special=0):
-    return pl.CostEstimate(flops=flops, bytes_accessed=moved, transcendentals=special)
+def small_cost():
+    return pl.CostEstimate(flops=1000, bytes_accessed=1000, transcendentals=0)
 
 
 def run_forward(inner, halo, valid, rows, gates):
@@ -341,7 +390,7 @@
             pltpu.VMEM((count, 2 * width), f32),
         ],
         compiler_params=pltpu.CompilerParams(vmem_limit_bytes=VMEM_LIMIT),
-        cost_estimate=cost(4 * count * width * width, 36 * count * width, 5 * count * width),
+        cost_estimate=small_cost(),
         name="recurrence_forward",
     )(inner, halo, valid, rows, gates)
 
@@ -363,7 +412,7 @@
         ],
         out_specs=(tile, tile, pl.BlockSpec((SUB, width), lambda i: (0, 0))),
         compiler_params=pltpu.CompilerParams(vmem_limit_bytes=VMEM_LIMIT),
-        cost_estimate=cost(20 * count * width, 18 * count * width, count * width),
+        cost_estimate=small_cost(),
         name="recurrence_states",
     )(mine, ends, part, span, gate_pre)
 
@@ -381,7 +430,7 @@
         in_specs=[tile] * 4,
         out_specs=(tile, tile, pl.BlockSpec((SUB, width), lambda i: (0, 0))),
         compiler_params=pltpu.CompilerParams(vmem_limit_bytes=VMEM_LIMIT),
-        cost_estimate=cost(30 * count * width, 22 * count * width, count * width),
+        cost_estimate=small_cost(),
         name="recurrence_turn",
     )(dmixed, gate_pre, states, span)
 
@@ -401,12 +450,84 @@
             pltpu.VMEM((count + SUB, width), f32),
         ],
         compiler_params=pltpu.CompilerParams(vmem_limit_bytes=VMEM_LIMIT),
-        cost_estimate=cost(4 * count * width * width, 40 * count * width, count * width),
+        cost_estimate=small_cost(),
         name="recurrence_backward",
     )(
         mine, ends, dstates, saved["alpha"], saved["states"], enter, saved["conv"], saved["rg"],
         saved["ig"], saved["factor"], valid, inner, halo, rows, gates,
     )
+
+
+def columns_product_kernel(ring_ref, left_ref, *refs):
+    out_ref = refs[-1]
+    left = left_ref[...].T
+    start = 0
+    for right_ref in refs[:-1]:
+        width = right_ref.shape[1]
+        out_ref[:, start : start + width] = jnp.dot(
+            left, right_ref[...], preferred_element_type=f32
+        )
+        start += width
+
+
+def ring_order():
+    devices = lax.axis_size("seq")
+    return [0, 1, 3, 2, 6, 7, 5, 4] if devices == 8 else list(range(devices))
+
+
+def ring_scatter(value):
+    return lax.psum_scatter(
+        value, "seq", scatter_dimension=0, axis_index_groups=[ring_order()], tiled=True
+    )
+
+
+def columns_product(left, rights):
+    rows, columns = left.shape
+    width = sum(right.shape[1] for right in rights)
+    ring = ring_order()
+    block = columns // len(ring)
+    if block % LANES:
+        whole = matmul_tn(left, jnp.concatenate(rights, 1)).reshape(len(ring), block, width)
+        return jnp.concatenate([whole[d] for d in ring], 0)
+    return pl.pallas_call(
+        columns_product_kernel,
+        grid_spec=pltpu.PrefetchScalarGridSpec(
+            num_scalar_prefetch=1,
+            grid=(len(ring),),
+            in_specs=[pl.BlockSpec((rows, block), lambda j, ring: (0, ring[j]))]
+            + [pl.BlockSpec(right.shape, lambda j, ring: (0, 0)) for right in rights],
+            out_specs=pl.BlockSpec((block, width), lambda j, ring: (j, 0)),
+        ),
+        out_shape=shape((columns, width)),
+        compiler_params=pltpu.CompilerParams(vmem_limit_bytes=VMEM_LIMIT),
+        cost_estimate=small_cost(),
+        name="columns_product",
+    )(jnp.array(ring, jnp.int32), left, *rights)
+
+
+def rows_product_kernel(left_ref, right_ref, out_ref, whole_ref, *, ring):
+    whole_ref[...] = jnp.dot(left_ref[...].T, right_ref[...], preferred_element_type=f32)
+    block = out_ref.shape[0] // len(ring)
+    for j, d in enumerate(ring):
+        out_ref[j * block : (j + 1) * block, :] = whole_ref[d * block : (d + 1) * block, :]
+
+
+def rows_product(left, right, width):
+    rows, columns = left.shape
+    return pl.pallas_call(
+        partial(rows_product_kernel, ring=ring_order()),
+        grid=(right.shape[1] // width,),
+        in_specs=[
+            pl.BlockSpec(left.shape, lambda n: (0, 0)),
+            pl.BlockSpec((rows, width), lambda n: (0, n)),
+        ],
+        out_specs=pl.BlockSpec((columns, width), lambda n: (0, n)),
+        scratch_shapes=[pltpu.VMEM((columns, width), f32)],
+        out_shape=shape((columns, right.shape[1])),
+        compiler_params=pltpu.CompilerParams(vmem_limit_bytes=VMEM_LIMIT),
+        cost_estimate=small_cost(),
+        name="rows_product",
+    )(left, right)
 
 
 def block_diagonal(weights):
@@ -450,25 +571,20 @@
     onward = [(s, s + 1) for s in range(devices - 1)]
     backward = [(s + 1, s) for s in range(devices - 1)]
 
-    stream_pieces = line_gather(stream)
+
+    first = LineGather(stream)
+    first.first()
     first_scale = row_scale(line_sum(jnp.sum(stream * stream, axis=1)), features)
-    starts_row = jnp.zeros((own_width,), f32).at[:SUB].set(doc_starts[count - SUB :].astype(f32))
-    payload = jnp.concatenate(
-        [stream[count - SUB :], jnp.broadcast_to(starts_row, (SUB, own_width))], 0
-    )
-    payload = lax.ppermute(payload, "seq", onward)
-    before = lax.all_gather(payload, "mp", axis=1, tiled=True)
-    halo_rows = before[:SUB]
-    halo_scale = row_scale(jnp.sum(halo_rows * halo_rows, axis=1), features)
-    halo_low = (halo_rows * halo_scale * gain_first).astype(bf16)
-    keep_ext = jnp.concatenate([1.0 - before[SUB, :SUB], 1.0 - doc_starts.astype(f32)], 0)
+    starts = doc_starts.astype(f32)
+    starts_before = lax.ppermute(starts[count - SUB :], "seq", onward)
+    keep_ext = 1.0 - jnp.concatenate([starts_before, starts], 0)
     reach = [keep_ext[SUB:]]
     for k in range(1, 4):
         reach.append(
             (reach[-1] if k > 1 else 1.0) * keep_ext[SUB - k + 1 : SUB - k + 1 + count]
         )
     valid = jnp.broadcast_to(jnp.stack(reach, 0)[:, :, None], (4, count, LANES))
-    valid_pad = jnp.pad(valid, ((0, 0), (SUB, SUB), (0, 0)))
+    valid = jnp.pad(valid, ((0, 0), (SUB, SUB), (0, 0)))
     rows = jnp.stack(
         [
             conv_weight[0], conv_weight[1], conv_weight[2], conv_weight[3], conv_bias, bias_recur,
@@ -477,121 +593,162 @@
         0,
     )
     gates = jnp.concatenate([block_diagonal(gate_recur), block_diagonal(gate_input)], 1)
+    first.second()
+    first.third(gates, valid)
 
     def first_turn(piece, start):
         return piece * first_scale * lax.dynamic_slice_in_dim(gain_first, start, own_width)
 
-    first_low = assemble(stream_pieces, features, first_turn)
+    first_low = assemble(first.pieces(), features, first_turn)
+    cot = LineGather(cotangent)
+    cot.first(first.far_out)
     inner = matmul(first_low, proj_inner)
-    halo = matmul(halo_low, proj_inner)
+    halo = lax.ppermute(inner[count - SUB :], "seq", onward)
+    gate_pre = matmul(after(first_low, inner), proj_gate)
+    halo = after(halo, gate_pre)
     conv, conv_low, rg, ig, alpha, factor, part, span, last = run_forward(
         inner, halo, valid, rows, gates
     )
-    gate_pre = matmul(first_low, proj_gate)
-    ends = lax.all_gather(last, "seq")
+    ends = after(lax.all_gather(last, "seq"), cot.beside, cot.near_in)
+    cot.second()
     states, mixed_low, enter = run_states(seq_at, ends, part, span, gate_pre)
 
-    branch = matmul(mixed_low, proj_out)
-    own_resid = stream + line_scatter(
-        lambda place: lax.dynamic_slice_in_dim(branch, place * own_width, own_width, 1)
-    )
-    cot_pieces = line_gather(cotangent)
-    cot_low = assemble(cot_pieces, features, lambda piece, start: piece)
-
-    resid_pieces = line_gather(own_resid)
+    branch = LineScatter(matmul(mixed_low, proj_out), own_width)
+    branch.first()
+    branch.second(cot.far_in, cot.near_out)
+    cot.third()
+    ffn_weight = jnp.concatenate(after((mlp_gate, mlp_up), branch.far_one), 1)
+    branch.third(cot.far_out, ffn_weight)
+    cot_low = assemble(cot.pieces(), features, lambda piece, start: piece)
+    d_hidden = matmul_nt(cot_low, mlp_down)
+    own_resid = stream + branch.result()
+
+    second = LineGather(own_resid)
+    second.first()
     second_scale = row_scale(line_sum(jnp.sum(own_resid * own_resid, axis=1)), features)
+    second.second(d_hidden)
+    second.third()
 
     def second_turn(piece, start):
         return piece * second_scale * lax.dynamic_slice_in_dim(gain_second, start, own_width)
 
-    second_low = assemble(resid_pieces, features, second_turn)
-    ffn_weight = jnp.concatenate([mlp_gate, mlp_up], 1)
+    second_low = assemble(second.pieces(), features, second_turn)
     ffn = matmul(second_low, ffn_weight)
     act, slope = gelu_parts(ffn[:, :ffn_width])
     ffn_up = ffn[:, ffn_width:]
     hidden_low = (act * ffn_up).astype(bf16)
-    d_hidden = matmul_nt(cot_low, mlp_down)
     d_pair_low = jnp.concatenate([d_hidden * ffn_up * slope, d_hidden * act], 1).astype(bf16)
     d_second_part = matmul_nt(d_pair_low, ffn_weight)
-    own_d_second = line_scatter(
-        lambda place: lax.dynamic_slice_in_dim(d_second_part, place * own_width, own_width, 1)
-    )
-    second_product = d_second_part * second_low.astype(f32)
+
+    turned = LineScatter(d_second_part, own_width)
+    turned.first()
+    whole_down = rows_product(after(hidden_low, d_second_part), cot_low, own_width)
+    whole_pair = columns_product(after(second_low, d_second_part), [d_pair_low])
+    turned.second(whole_down, whole_pair)
+    grad_down = ring_scatter(whole_down)
+    grad_pair = ring_scatter(whole_pair)
+    second_product = after(d_second_part, turned.far_one) * second_low.astype(f32)
     second_mean = line_sum(jnp.sum(second_product, axis=1)) / features
     d_gain_second = jnp.sum(second_product, axis=0) / gain_second
+    turned.third(d_gain_second, second_mean)
+    mlp_part = matmul(after(hidden_low, turned.far_two, turned.near_one), mlp_down)
+    own_d_second = turned.result()
     own_d_resid = (
         cotangent
         + second_scale * (own_second * own_d_second)
         - own_resid * (second_scale * second_scale * second_mean[:, None])
     )
-    branch_pieces = line_gather(own_d_resid)
-    branch_low = assemble(branch_pieces, features, lambda piece, start: piece)
-
-    mlp_part = matmul(hidden_low, mlp_down)
-    output = own_resid + line_scatter(
-        lambda place: lax.dynamic_slice_in_dim(mlp_part, place * own_width, own_width, 1)
-    )
-
-    d_mixed = matmul_nt(branch_low, proj_out)
+    gathered = LineGather(own_d_resid)
+    gathered.first(mlp_part)
+    gathered.second()
+    sent = LineScatter(mlp_part, own_width)
+    sent.first(gathered.near_in, gathered.beside)
+    gathered.third(sent.far_one, grad_down)
+    sent.second(gathered.near_out)
+    branch_low = assemble(gathered.pieces(), features, lambda piece, start: piece)
+
+    d_mixed = matmul_nt(after(branch_low, sent.far_two, sent.near_one), proj_out)
     d_states, d_gate_low, outgoing = run_turn(d_mixed, gate_pre, states, span)
     leaving = jnp.stack([last[0], jnp.sum(outgoing, axis=0)], 0)
     back_ends = lax.all_gather(leaving, "seq")
+    sent.third()
     saved = dict(alpha=alpha, states=states, conv=conv, rg=rg, ig=ig, factor=factor)
     d_inner_low, tail, head, d_rec_low, sums = run_backward(
-        seq_at, back_ends, d_states, saved, enter, valid_pad, inner, halo, rows, gates
+        seq_at, back_ends, d_states, saved, enter, valid, inner, halo, rows, gates
     )
     returned = lax.ppermute(head, "seq", backward)
+    d_first_gate = matmul_nt(after(d_gate_low, head), proj_gate)
+    returned = after(returned, d_first_gate, sent.last, sent.near_two)
     tail = tail + jnp.concatenate([jnp.zeros_like(returned), returned], 0)
     d_inner_low = lax.dynamic_update_slice(d_inner_low, tail.astype(bf16), (count - 2 * SUB, 0))
-
-    d_first_part = matmul_nt(d_inner_low, proj_inner) + matmul_nt(d_gate_low, proj_gate)
-    own_d_first = line_scatter(
-        lambda place: lax.dynamic_slice_in_dim(d_first_part, place * own_width, own_width, 1)
-    )
-    first_product = d_first_part * first_low.astype(f32)
-    first_mean = line_sum(jnp.sum(first_product, axis=1)) / features
-    d_gain_first = jnp.sum(first_product, axis=0) / gain_first
+    d_first_part = matmul_nt(d_inner_low, proj_inner) + d_first_gate
+
+    final = LineScatter(d_first_part, own_width)
+    final.first(grad_pair)
+    whole_first = columns_product(
+        after(first_low, d_first_part), [d_inner_low, d_gate_low]
+    )
+    grad_first = ring_scatter(whole_first)
+    first_product = after(d_first_part, whole_first) * first_low.astype(f32)
+    first_mean = jnp.sum(first_product, axis=1)
+    gains = jnp.stack([jnp.sum(first_product, axis=0) / gain_first, d_gain_second], 0)
+    gate_grads = matmul_tn(conv_low, after(d_rec_low, whole_first))
+    block_width = inner_width // groups
+    small = jnp.concatenate(
+        [
+            jnp.concatenate(
+                [
+                    diagonal_blocks(gate_grads[:, :inner_width], groups),
+                    diagonal_blocks(gate_grads[:, inner_width:], groups),
+                ],
+                2,
+            ).reshape(inner_width, 2 * block_width),
+            sums.reshape(-1, 2 * block_width),
+        ],
+        0,
+    )
+    whole_out = rows_product(after(mixed_low, whole_first), branch_low, 2 * own_width)
+    grad_out = ring_scatter(whole_out)
+    final.second(small, gains, first_mean, whole_out)
+    small = small + swapped(small, "seq", 1)
+    gains = sum_over(gains, "mp")
+    first_mean = line_sum(first_mean) / features
+    output = own_resid + sent.result()
+    final.third(output, first_mean, small, gains)
+    bit = 2
+    while bit < devices:
+        small = small + swapped(small, "seq", bit)
+        bit *= 2
+    gains = sum_over(gains, "seq")
+    own_d_first = final.result()
     grad_stream = (
         own_d_resid
         + first_scale * (own_first * own_d_first)
         - stream * (first_scale * first_scale * first_mean[:, None])
     )
-
-    d_gains = lax.psum((d_gain_first, d_gain_second), ("seq", "mp"))
-    gate_grads = matmul_tn(conv_low, d_rec_low)
-    sums, grad_gate_recur, grad_gate_input = lax.psum(
-        (
-            sums,
-            diagonal_blocks(gate_grads[:, :inner_width], groups),
-            diagonal_blocks(gate_grads[:, inner_width:], groups),
-        ),
-        "seq",
-    )
+    sums = small[inner_width:].reshape(SUB, inner_width)
+    grad_gates = [
+        small[:inner_width, g * block_width : (g + 1) * block_width].reshape(
+            groups, block_width, block_width
+        )
+        for g in range(2)
+    ]
     grad_decay = sums[7] * (recur_scale * jax.nn.sigmoid(-decay_param))
-
-    def over_seq(value):
-        return lax.psum_scatter(value, "seq", scatter_dimension=0, tiled=True)
-
-    grad_down = over_seq(matmul_tn(hidden_low, cot_low))
-    grad_pair = over_seq(matmul_tn(second_low, d_pair_low))
-    grad_out = over_seq(matmul_tn(mixed_low, branch_low))
-    grad_gate = over_seq(matmul_tn(first_low, d_gate_low))
-    grad_inner = over_seq(matmul_tn(first_low, d_inner_low))
     return (
         output,
         grad_stream,
-        d_gains[0],
-        grad_inner,
-        grad_gate,
+        gains[0],
+        grad_first[:, :inner_width],
+        grad_first[:, inner_width:],
         sums[:4],
         sums[4],
-        grad_gate_recur,
-        grad_gate_input,
+        grad_gates[0],
+        grad_gates[1],
         sums[5],
         sums[6],
         grad_decay,
         grad_out,
-        d_gains[1],
+        gains[1],
         grad_pair[:, :ffn_width],
         grad_pair[:, ffn_width:],
         grad_down,

time: 936 us -> 699 us (0.75)
  waiting for transfers between devices: 520 us -> 287 us
  blocking collectives: 115 us -> 19.5 us
  starting transfers between devices: 98.5 us -> 149 us
  matrix products: 89 us -> 49.3 us
  other arithmetic: 32.7 us -> 70 us
  Pallas kernels: 28.4 us -> 61.1 us
  local copies, waits for them, and re-layouts: 26.9 us -> 43.4 us
    ppermute x48, waiting for transfers between devices: 415 us -> 245 us  [over_mp(): return lax.ppermute(value, 'mp', list(pairs))]
    reduce_scatter x5 -> x4, waiting for transfers between devices: 103 us -> 0.01 us  [ring_scatter(): lax.psum_scatter(value, 'seq', scatter_dimension=0, axis_index_groups=[ri...]
    psum x2 -> x0, blocking collectives: 64.3 us -> none  [the longest x1 38.6 us: body(): d_gains = lax.psum((d_gain_first, d_gain_second), ('seq', 'mp'))]
    ppermute x48, starting transfers between devices: 95.3 us -> 138 us  [over_mp(): return lax.ppermute(value, 'mp', list(pairs))]
    ppermute x1 -> x10, waiting for transfers between devices: 0.01 us -> 41.4 us  [the longest x8 41.4 us: swapped(): return lax.ppermute(value, axis, [(d, d ^ bit) for d in range(count)])]
    dot_general x6 -> x1, matrix products: 40.4 us -> 2.5 us  [matmul_tn(): lax.dot_general(left, right, (((0,), (0,)), ((), ())), preferred_element_...]
    pallas_call x0 -> x4, Pallas kernels: none -> 33.2 us  [the longest x2 23 us: columns_product(): pl.pallas_call(columns_product_kernel, grid_spec=pltpu.PrefetchScalarGrid...]
    all_gather x2 -> x1, blocking collectives: 42 us -> 11 us  [body(): ends = after(lax.all_gather(last, 'seq'), cot.beside, cot.near_in)]
  transfers between devices with their start and end apart: 56 -> 63, of which waited for: 30 -> 25; matrix products, arithmetic and copies ran while one was open for 11% -> 19% of each run, Pallas kernels for 2% -> 8%
where the time goes in v2:
time: 699 us; the launch traced here: 694 us
  waiting for transfers between devices  287 us (41%)
  starting transfers between devices  149 us (21%)
  other arithmetic  70 us (10%)
  Pallas kernels  61.1 us (9%)
  matrix products  49.3 us (7%)
  local copies, waits for them, and re-layouts  43.4 us (6%)
  blocking collectives  19.5 us (3%)
  between operations  15.3 us (2%)
    ppermute x48, waiting for transfers between devices, over_mp(): return lax.ppermute(value, 'mp', list(pairs))  245 us
    ppermute x48, starting transfers between devices, over_mp(): return lax.ppermute(value, 'mp', list(pairs))  138 us
    ppermute x8, waiting for transfers between devices, swapped(): return lax.ppermute(value, axis, [(d, d ^ bit) for d in range(count)])  41.4 us
    dot_general x5, matrix products, matmul_nt(): lax.dot_general(left, right, (((1,), (1,)), ((), ())), preferred_element_...  27.9 us
    pallas_call x2, Pallas kernels, columns_product(): pl.pallas_call(columns_product_kernel, grid_spec=pltpu.PrefetchScalarGrid...  23 us
    dot_general x5, matrix products, matmul(): return jnp.dot(left, right, preferred_element_type=f32)  18.9 us
    dynamic_update_slice x16, other arithmetic, assemble(): lax.dynamic_update_slice(whole, turn(piece, start).astype(bf16), (0, start))  17.3 us
    unnamed x145, local copies, waits for them, and re-layouts  15.6 us
  transfers between devices with their start and end apart: 63, of which 25 were waited for; matrix products, arithmetic and copies ran while one was open for 19% of the time, Pallas kernels for 8%

profile of v2, /device:TPU:0, one launch (start us, length us, event | category | flops | bytes accessed | tf_op | source)
XLA Modules:
  0.0 694.0 jit_solution(15020287055881217515)
XLA Ops:
  20.1 13.7 %collective-permute-done.2 = f32[512,512]{1,0:T(8,128)} collective-permute-done((f32[512,512]{1,0:T(8,128)}, f32[512,512]{1,0:T(8,128)}, u32[]{:S(2)}, u32[]{:S(2)}) %collective-permute-start.2) | collective-permute-done | bytes 1048608 | tf_op jit(solution)/shard_map/ppermute | solution.py:40
  36.8 8.4 %fusion.29.gate_ref = bf16[640,1280]{1,0:T(8,128)(2,1)} fusion(bf16[160,160]{1,0:T(8,128)(2,1)S(1)} %get-tuple-element.236, bf16[160,160]{1,0:T(8,128)(2,1)S(1)} %get-tuple-element.237, bf16[160,160]{1,0:T(8,128)(2,1)S(1)} %get-tuple-element.235, bf16[160,160]{1,0:T(8,128)(2,1)S(1)} %get-tuple-element.234, bf16[160,160]{1,0:T(8,128)(2,1)S(1)} %get-tuple-element.250, ...), kind=kLoop, calls=%fused_computation.47 | loop fusion | flops 40960000 | bytes 2048000 | tf_op jit(solution)/shard_map/concatenate | solution.py:595
  46.9 7.5 %collective-permute-start.1 = (f32[512]{0:T(512)S(1)}, f32[512]{0:T(512)S(1)}, u32[]{:S(2)}, u32[]{:S(2)}) collective-permute-start(f32[512]{0:T(512)S(1)} %add.261), channel_id=1, source_target_pairs={{0,2},{2,0},{1,3},{3,1},{4,6},{6,4},{5,7},{7,5},{8,10},{10,8},{9,1... | collective-permute-start | bytes 6152 | tf_op jit(solution)/shard_map/ppermute | solution.py:40
  54.4 8.1 %collective-permute-done.4 = f32[512,512]{1,0:T(8,128)} collective-permute-done((f32[512,512]{1,0:T(8,128)}, f32[512,512]{1,0:T(8,128)}, u32[]{:S(2)}, u32[]{:S(2)}) %collective-permute-start.4) | collective-permute-done | bytes 1048608 | tf_op jit(solution)/shard_map/ppermute | solution.py:40
  70.4 19.7 %collective-permute-done.7 = f32[512,512]{1,0:T(8,128)} collective-permute-done((f32[512,512]{1,0:T(8,128)}, f32[512,512]{1,0:T(8,128)}, u32[]{:S(2)}, u32[]{:S(2)}) %collective-permute-start.7) | collective-permute-done | bytes 1048608 | tf_op jit(solution)/shard_map/ppermute | solution.py:40
  100.8 10.9 %recurrence_forward.1 = (f32[512,640]{1,0:T(8,128)S(1)}, bf16[512,640]{1,0:T(8,128)(2,1)S(1)}, f32[512,640]{1,0:T(8,128)}, f32[512,640]{1,0:T(8,128)}, f32[512,6...) custom-call(f32[512,640]{1,0:T(8,128)} %copy-done.35, ...), custom_call_target="tpu_custom_call" | custom-call | flops 1000 | bytes 1000 | tf_op jit(solution)/shard_map/recurrence_forward/pallas_call | solution.py:383
  112.8 11.0 %all-gather = f32[64,640]{1,0:T(8,128)S(1)} all-gather(f32[8,640]{1,0:T(8,128)S(1)} %get-tuple-element.90), channel_id=2, replica_groups=mesh['seq'=8,'mp'=4] {'seq'}, dimensions={0}, use_global_device_ids=true | all-gather | bytes 184320 | tf_op jit(solution)/shard_map/all_gather | solution.py:612
  133.0 7.0 %collective-permute-start.11 = (f32[512,512]{1,0:T(8,128)S(1)}, f32[512,512]{1,0:T(8,128)S(1)}, u32[]{:S(2)}, u32[]{:S(2)}) collective-permute-start(f32[512,512]{1,0:T(8,128)S(1)} %get-tuple-element.210), channel_id=1, source_target_pairs={{0,1},{3,2},{4,5},{7,6},{8,9},{11,10},{12,13},{15,14},{16,17},{19,... | collective-permute-start | bytes 3145736 | tf_op jit(solution)/shard_map/ppermute | solution.py:40
  140.0 11.5 %collective-permute-done.13 = f32[512,512]{1,0:T(8,128)} collective-permute-done((f32[512,512]{1,0:T(8,128)}, f32[512,512]{1,0:T(8,128)}, u32[]{:S(2)}, u32[]{:S(2)}) %collective-permute-start.13) | collective-permute-done | bytes 1048608 | tf_op jit(solution)/shard_map/ppermute | solution.py:40
  152.7 9.5 %collective-permute-done.11 = f32[512,512]{1,0:T(8,128)S(1)} collective-permute-done((f32[512,512]{1,0:T(8,128)S(1)}, f32[512,512]{1,0:T(8,128)S(1)}, u32[]{:S(2)}, u32[]{:S(2)}) %collective-permute-start.11) | collective-permute-done | bytes 1048608 | tf_op jit(solution)/shard_map/ppermute | solution.py:40
  163.4 13.9 %collective-permute-start.15 = (f32[512,512]{1,0:T(8,128)}, f32[512,512]{1,0:T(8,128)}, u32[]{:S(2)}, u32[]{:S(2)}) collective-permute-start(f32[512,512]{1,0:T(8,128)} %add.271), channel_id=1, source_target_pairs={{1,2},{2,1},{5,6},{6,5},{9,10},{10,9},{13,14},{14,13},{17,18},{18,... | collective-permute-start | bytes 3145736 | tf_op jit(solution)/shard_map/ppermute | solution.py:40
  177.4 6.9 collective-permute-start.14
  190.8 13.7 %collective-permute-done.14 = f32[512,512]{1,0:T(8,128)} collective-permute-done((f32[512,512]{1,0:T(8,128)S(1)}, f32[512,512]{1,0:T(8,128)}, u32[]{:S(2)}, u32[]{:S(2)}) %collective-permute-start.14) | collective-permute-done | bytes 1048608 | tf_op jit(solution)/shard_map/ppermute | solution.py:40
  208.2 4.8 collective-permute-start.18
  216.3 17.5 %collective-permute-done.18 = f32[512,512]{1,0:T(8,128)S(1)} collective-permute-done((f32[512,512]{1,0:T(8,128)S(1)}, f32[512,512]{1,0:T(8,128)S(1)}, u32[]{:S(2)}, u32[]{:S(2)}) %collective-permute-start.18) | collective-permute-done | bytes 1048608 | tf_op jit(solution)/shard_map/ppermute | solution.py:40
  238.9 5.8 fusion.65
  244.6 11.5 %collective-permute-done.21 = f32[512,512]{1,0:T(8,128)S(1)} collective-permute-done((f32[512,512]{1,0:T(8,128)S(1)}, f32[512,512]{1,0:T(8,128)S(1)}, u32[]{:S(2)}, u32[]{:S(2)}) %collective-permute-start.21) | collective-permute-done | bytes 1048608 | tf_op jit(solution)/shard_map/ppermute | solution.py:40
  258.2 5.8 collective-permute-start.19
  264.0 15.6 %collective-permute-done.19 = f32[512]{0:T(512)S(1)} collective-permute-done((f32[512]{0:T(512)S(1)}, f32[512]{0:T(512)S(1)}, u32[]{:S(2)}, u32[]{:S(2)}) %collective-permute-start.19) | collective-permute-done | bytes 2080 | tf_op jit(solution)/shard_map/ppermute | solution.py:40
  285.0 17.4 %collective-permute-done.25 = f32[512,512]{1,0:T(8,128)S(1)} collective-permute-done((f32[512,512]{1,0:T(8,128)S(1)}, f32[512,512]{1,0:T(8,128)S(1)}, u32[]{:S(2)}, u32[]{:S(2)}) %collective-permute-start.25) | collective-permute-done | bytes 1048608 | tf_op jit(solution)/shard_map/ppermute | solution.py:40
  302.6 6.8 fusion.66
  311.9 12.8 %fusion.54 = f32[512,2048]{1,0:T(8,128)} fusion(bf16[2048,3072]{1,0:T(8,128)(2,1)} %constant_dynamic-update-slice_fusion, bf16[512,1536]{1,0:T(8,128)(2,1)S(1)} %get-tuple-element.202, bf16[512,1536]{1,0:T(8,128)(2,1)S(1)} %get-tuple-element.201), kind=kOutput, calls=%fused_computation.141 | convolution fusion | flops 6448742400 | bytes 19922944 | tf_op jit(solution)/shard_map/dot_general | solution.py:25
  324.8 6.7 rows_product.2
  331.6 4.0 pad_maximum_fusion.refs_0_
  335.6 14.9 %columns_product.2 = f32[2048,3072]{1,0:T(8,128)} custom-call(s32[8]{0:T(128)S(1)} %copy-done.23, bf16[512,2048]{1,0:T(8,128)(2,1)S(1)} %copy-done.2, bf16[512,3072]{1,0:T(8,128)(2,1)} %pad_maximum_fusion.refs_0_), custom_call_target="tpu_custom_call" | custom-call | flops 1000 | bytes 1000 | tf_op jit(solution)/shard_map/columns_product/pallas_call | solution.py:492
  353.9 18.2 %collective-permute-done.26 = f32[512,512]{1,0:T(8,128)S(1)} collective-permute-done((f32[512,512]{1,0:T(8,128)S(1)}, f32[512,512]{1,0:T(8,128)S(1)}, u32[]{:S(2)}, u32[]{:S(2)}) %collective-permute-start.26) | collective-permute-done | bytes 1048608 | tf_op jit(solution)/shard_map/ppermute | solution.py:40
  372.3 4.8 collective-permute-start.28
  380.0 13.0 %collective-permute-done.29 = f32[512]{0:T(512)S(1)} collective-permute-done((f32[512]{0:T(512)S(1)}, f32[512]{0:T(512)S(1)}, u32[]{:S(2)}, u32[]{:S(2)}) %collective-permute-start.29) | collective-permute-done | bytes 2080 | tf_op jit(solution)/shard_map/ppermute | solution.py:40
  398.9 4.5 collective-permute-start.32
  403.5 5.6 fusion.67
  409.1 12.1 %collective-permute-done.32 = f32[512,512]{1,0:T(8,128)S(1)} collective-permute-done((f32[512,512]{1,0:T(8,128)S(1)}, f32[512,512]{1,0:T(8,128)S(1)}, u32[]{:S(2)}, u32[]{:S(2)}) %collective-permute-start.32) | collective-permute-done | bytes 1048608 | tf_op jit(solution)/shard_map/ppermute | solution.py:40
  422.6 5.1 collective-permute-start.34
  428.9 17.8 %collective-permute-done.34 = f32[512,512]{1,0:T(8,128)S(1)} collective-permute-done((f32[512,512]{1,0:T(8,128)S(1)}, f32[512,512]{1,0:T(8,128)S(1)}, u32[]{:S(2)}, u32[]{:S(2)}) %collective-permute-start.34) | collective-permute-done | bytes 1048608 | tf_op jit(solution)/shard_map/ppermute | solution.py:40
  446.7 4.4 collective-permute-start.35
  454.1 15.2 %collective-permute-done.35 = f32[512,512]{1,0:T(8,128)S(1)} collective-permute-done((f32[512,512]{1,0:T(8,128)S(1)}, f32[512,512]{1,0:T(8,128)S(1)}, u32[]{:S(2)}, u32[]{:S(2)}) %collective-permute-start.35) | collective-permute-done | bytes 1048608 | tf_op jit(solution)/shard_map/ppermute | solution.py:40
  471.5 4.5 collective-permute-start.37
  483.6 3.9 collective-permute-done.37
  494.7 7.4 %collective-permute-start.40 = (f32[512,512]{1,0:T(8,128)}, f32[512,512]{1,0:T(8,128)}, u32[]{:S(2)}, u32[]{:S(2)}) collective-permute-start(f32[512,512]{1,0:T(8,128)} %dynamic-slice_add_fusion.1), channel_id=1, source_target_pairs={{0,1},{1,0},{2,3},{3,2},{4,5},{5,4},{6,7},{7,6},{8,9},{9,8},{10,11... | collective-permute-start | bytes 3145736 | tf_op jit(solution)/shard_map/ppermute | solution.py:40
  512.2 8.5 %all-gather.2.ends_ref = f32[8,2,640]{2,1,0:T(2,128)S(1)} all-gather(f32[1,2,640]{2,1,0:T(2,128)S(1)} %maximum_bitcast_fusion), channel_id=3, replica_groups=mesh['seq'=8,'mp'=4] {'seq'}, dimensions={0}, use_global_device_ids=true | all-gather | bytes 46080 | tf_op jit(solution)/shard_map/all_gather | solution.py:673
  521.9 10.9 %recurrence_backward.1 = (bf16[512,640]{1,0:T(8,128)(2,1)S(1)}, f32[16,640]{1,0:T(8,128)S(1)}, f32[8,640]{1,0:T(8,128)S(1)}, bf16[512,1280]{1,0:T(8,128)(2,1)S(1)}, f32[8,640]{1,0:T(8,128)S(1)}) custom-call(s32[1]{0:T(128)} %bitcast.mine_ref, f32[8,2,640]{2,1,0:T(2,128)S(1)} %all-gather.2.ends_ref, f32[512,640]{1,0:T(8,128)} %copy-done.16, ...), custom_call_target="tpu_custom_call" | custom-call | flops 1000 | bytes 1000 | tf_op jit(solution)/shard_map/recurrence_backward/pallas_call | solution.py:440
  538.2 3.8 convolution_add_fusion
  542.0 8.1 %columns_product.3 = f32[2048,1280]{1,0:T(8,128)} custom-call(s32[8]{0:T(128)S(1)} %copy-done.23, bf16[512,2048]{1,0:T(8,128)(2,1)S(1)} %copy-done.5, bf16[512,640]{1,0:T(8,128)(2,1)S(1)} %fusion.50.refs_0_, bf16[512,640]{1,0:T(8,128)(2,1)S(1)} %copy-done.22), custom_call_target="tpu_custom_call" | custom-call | flops 1000 | bytes 1000 | tf_op jit(solution)/shard_map/columns_product/pallas_call | solution.py:492
  573.9 3.8 collective-permute-start.44
  577.8 23.1 %collective-permute-done.51 = f32[2,2048]{1,0:T(2,128)S(1)} collective-permute-done((f32[2,2048]{1,0:T(2,128)S(1)}, f32[2,2048]{1,0:T(2,128)S(1)}, u32[]{:S(2)}, u32[]{:S(2)}) %collective-permute-start.51) | collective-permute-done | bytes 16416 | tf_op jit(solution)/shard_map/ppermute | solution.py:113
  618.6 4.6 collective-permute-start.45
  623.2 18.3 %collective-permute-done.56 = f32[2,2048]{1,0:T(2,128)S(1)} collective-permute-done((f32[2,2048]{1,0:T(2,128)S(1)}, f32[2,2048]{1,0:T(2,128)S(1)}, u32[]{:S(2)}, u32[]{:S(2)}) %collective-permute-start.56) | collective-permute-done | bytes 16416 | tf_op jit(solution)/shard_map/ppermute | solution.py:113
  664.9 4.0 fusion.55
  668.9 15.2 %collective-permute-done.53 = f32[512,512]{1,0:T(8,128)} collective-permute-done((f32[512,512]{1,0:T(8,128)}, f32[512,512]{1,0:T(8,128)}, u32[]{:S(2)}, u32[]{:S(2)}) %collective-permute-start.53) | collective-permute-done | bytes 1048608 | tf_op jit(solution)/shard_map/ppermute | solution.py:40
  (362 shorter events, 196.4 us)
Async XLA Ops:
  7.2 470.4 %reduce-scatter.5.cloned.1.call-start = ((), (), s32[]{:S(2)}) async-start(), calls=%async_computation.4 | async-start | bytes 14155776 | tf_op jit(solution)/shard_map/reduce_scatter | solution.py:479
  7.3 26.6 %collective-permute-start.2 = (f32[512,512]{1,0:T(8,128)}, f32[512,512]{1,0:T(8,128)}, u32[]{:S(2)}, u32[]{:S(2)}) collective-permute-start(f32[512,512]{1,0:T(8,128)} %param.20), channel_id=1, source_target_pairs={{0,1},{1,0},{2,3},{3,2},{4,5},{5,4},{6,7},{7,6},{8,9},{9,8},{10,11... | collective-permute-start | bytes 3145736 | tf_op jit(solution)/shard_map/ppermute | solution.py:40
  10.4 23.5 %collective-permute-start.3 = (f32[512,512]{1,0:T(8,128)}, f32[512,512]{1,0:T(8,128)}, u32[]{:S(2)}, u32[]{:S(2)}) collective-permute-start(f32[512,512]{1,0:T(8,128)} %param.20), channel_id=1, source_target_pairs={{1,2},{2,1},{5,6},{6,5},{9,10},{10,9},{13,14},{14,13},{17,18},{18,... | collective-permute-start | bytes 3145736 | tf_op jit(solution)/shard_map/ppermute | solution.py:40
  12.7 32.5 %collective-permute-start.6 = (f32[8]{0:T(128)S(1)}, f32[8]{0:T(128)S(1)}, u32[]{:S(2)}, u32[]{:S(2)}) collective-permute-start(f32[8]{0:T(128)S(1)} %slice.148), channel_id=1, source_target_pairs={{0,4},{4,8},{8,12},{12,16},{16,20},{20,24},{24,28},{1,5},{5,9},{9,... | collective-permute-start | bytes 104 | tf_op jit(solution)/shard_map/ppermute | solution.py:579
  15.6 31.3 %collective-permute-start = (f32[512]{0:T(512)S(1)}, f32[512]{0:T(512)S(1)}, u32[]{:S(2)}, u32[]{:S(2)}) collective-permute-start(f32[512]{0:T(512)S(1)} %multiply_reduce_fusion.1), channel_id=1, source_target_pairs={{0,1},{1,0},{2,3},{3,2},{4,5},{5,4},{6,7},{7,6},{8,9},{9,8},{10,11... | collective-permute-start | bytes 6152 | tf_op jit(solution)/shard_map/ppermute | solution.py:40
  33.9 28.6 %collective-permute-start.4 = (f32[512,512]{1,0:T(8,128)}, f32[512,512]{1,0:T(8,128)}, u32[]{:S(2)}, u32[]{:S(2)}) collective-permute-start(f32[512,512]{1,0:T(8,128)} %collective-permute-done.3), channel_id=1, source_target_pairs={{1,0},{2,3},{5,4},{6,7},{9,8},{10,11},{13,12},{14,15},{17,16},{18,... | collective-permute-start | bytes 3145736 | tf_op jit(solution)/shard_map/ppermute | solution.py:40
  35.1 27.3 %collective-permute-start.5 = (f32[512,512]{1,0:T(8,128)}, f32[512,512]{1,0:T(8,128)}, u32[]{:S(2)}, u32[]{:S(2)}) collective-permute-start(f32[512,512]{1,0:T(8,128)} %collective-permute-done.2), channel_id=1, source_target_pairs={{1,2},{2,1},{5,6},{6,5},{9,10},{10,9},{13,14},{14,13},{17,18},{18,... | collective-permute-start | bytes 3145736 | tf_op jit(solution)/shard_map/ppermute | solution.py:40
  46.9 19.7 %collective-permute-start.1 = (f32[512]{0:T(512)S(1)}, f32[512]{0:T(512)S(1)}, u32[]{:S(2)}, u32[]{:S(2)}) collective-permute-start(f32[512]{0:T(512)S(1)} %add.261), channel_id=1, source_target_pairs={{0,2},{2,0},{1,3},{3,1},{4,6},{6,4},{5,7},{7,5},{8,10},{10,8},{9,1... | collective-permute-start | bytes 6152 | tf_op jit(solution)/shard_map/ppermute | solution.py:40
  62.5 27.7 %collective-permute-start.7 = (f32[512,512]{1,0:T(8,128)}, f32[512,512]{1,0:T(8,128)}, u32[]{:S(2)}, u32[]{:S(2)}) collective-permute-start(f32[512,512]{1,0:T(8,128)} %collective-permute-done.5), channel_id=1, source_target_pairs={{1,0},{2,3},{5,4},{6,7},{9,8},{10,11},{13,12},{14,15},{17,16},{18,... | collective-permute-start | bytes 3145736 | tf_op jit(solution)/shard_map/ppermute | solution.py:40
  90.1 33.7 %collective-permute-start.10 = (f32[512,512]{1,0:T(8,128)S(1)}, f32[512,512]{1,0:T(8,128)}, u32[]{:S(2)}, u32[]{:S(2)}) collective-permute-start(f32[512,512]{1,0:T(8,128)S(1)} %copy-done.40), channel_id=1, source_target_pairs={{1,2},{2,1},{5,6},{6,5},{9,10},{10,9},{13,14},{14,13},{17,18},{18,... | collective-permute-start | bytes 3145736 | tf_op jit(solution)/shard_map/ppermute | solution.py:40
  91.8 32.1 %collective-permute-start.9 = (f32[512,512]{1,0:T(8,128)S(1)}, f32[512,512]{1,0:T(8,128)}, u32[]{:S(2)}, u32[]{:S(2)}) collective-permute-start(f32[512,512]{1,0:T(8,128)S(1)} %copy-done.40), channel_id=1, source_target_pairs={{0,1},{1,0},{2,3},{3,2},{4,5},{5,4},{6,7},{7,6},{8,9},{9,8},{10,11... | collective-permute-start | bytes 3145736 | tf_op jit(solution)/shard_map/ppermute | solution.py:40
  123.8 27.6 %collective-permute-start.13 = (f32[512,512]{1,0:T(8,128)}, f32[512,512]{1,0:T(8,128)}, u32[]{:S(2)}, u32[]{:S(2)}) collective-permute-start(f32[512,512]{1,0:T(8,128)} %collective-permute-done.10), channel_id=1, source_target_pairs={{1,0},{2,3},{5,4},{6,7},{9,8},{10,11},{13,12},{14,15},{17,16},{18,... | collective-permute-start | bytes 3145736 | tf_op jit(solution)/shard_map/ppermute | solution.py:40
  125.1 26.3 %collective-permute-start.12 = (f32[512,512]{1,0:T(8,128)}, f32[512,512]{1,0:T(8,128)}, u32[]{:S(2)}, u32[]{:S(2)}) collective-permute-start(f32[512,512]{1,0:T(8,128)} %collective-permute-done.9), channel_id=1, source_target_pairs={{1,2},{2,1},{5,6},{6,5},{9,10},{10,9},{13,14},{14,13},{17,18},{18,... | collective-permute-start | bytes 3145736 | tf_op jit(solution)/shard_map/ppermute | solution.py:40
  133.0 29.3 %collective-permute-start.11 = (f32[512,512]{1,0:T(8,128)S(1)}, f32[512,512]{1,0:T(8,128)S(1)}, u32[]{:S(2)}, u32[]{:S(2)}) collective-permute-start(f32[512,512]{1,0:T(8,128)S(1)} %get-tuple-element.210), channel_id=1, source_target_pairs={{0,1},{3,2},{4,5},{7,6},{8,9},{11,10},{12,13},{15,14},{16,17},{19,... | collective-permute-start | bytes 3145736 | tf_op jit(solution)/shard_map/ppermute | solution.py:40
  151.4 56.0 %collective-permute-start.16 = (f32[512,512]{1,0:T(8,128)}, f32[512,512]{1,0:T(8,128)}, u32[]{:S(2)}, u32[]{:S(2)}) collective-permute-start(f32[512,512]{1,0:T(8,128)} %collective-permute-done.12), channel_id=1, source_target_pairs={{1,0},{2,3},{5,4},{6,7},{9,8},{10,11},{13,12},{14,15},{17,16},{18,... | collective-permute-start | bytes 3145736 | tf_op jit(solution)/shard_map/ppermute | solution.py:40
  163.4 42.4 %collective-permute-start.15 = (f32[512,512]{1,0:T(8,128)}, f32[512,512]{1,0:T(8,128)}, u32[]{:S(2)}, u32[]{:S(2)}) collective-permute-start(f32[512,512]{1,0:T(8,128)} %add.271), channel_id=1, source_target_pairs={{1,2},{2,1},{5,6},{6,5},{9,10},{10,9},{13,14},{14,13},{17,18},{18,... | collective-permute-start | bytes 3145736 | tf_op jit(solution)/shard_map/ppermute | solution.py:40
  177.4 27.1 %collective-permute-start.14 = (f32[512,512]{1,0:T(8,128)S(1)}, f32[512,512]{1,0:T(8,128)}, u32[]{:S(2)}, u32[]{:S(2)}) collective-permute-start(f32[512,512]{1,0:T(8,128)S(1)} %get-tuple-element.98), channel_id=1, source_target_pairs={{0,1},{3,2},{4,5},{7,6},{8,9},{11,10},{12,13},{15,14},{16,17},{19,... | collective-permute-start | bytes 3145736 | tf_op jit(solution)/shard_map/ppermute | solution.py:40
  208.2 25.6 %collective-permute-start.18 = (f32[512,512]{1,0:T(8,128)S(1)}, f32[512,512]{1,0:T(8,128)S(1)}, u32[]{:S(2)}, u32[]{:S(2)}) collective-permute-start(f32[512,512]{1,0:T(8,128)S(1)} %dynamic-slice_add_fusion.3), channel_id=1, source_target_pairs={{0,1},{1,0},{2,3},{3,2},{4,5},{5,4},{6,7},{7,6},{8,9},{9,8},{10,11... | collective-permute-start | bytes 3145736 | tf_op jit(solution)/shard_map/ppermute | solution.py:40
  234.2 22.0 %collective-permute-start.21 = (f32[512,512]{1,0:T(8,128)S(1)}, f32[512,512]{1,0:T(8,128)S(1)}, u32[]{:S(2)}, u32[]{:S(2)}) collective-permute-start(f32[512,512]{1,0:T(8,128)S(1)} %get-tuple-element.198), channel_id=1, source_target_pairs={{0,1},{1,0},{2,3},{3,2},{4,5},{5,4},{6,7},{7,6},{8,9},{9,8},{10,11... | collective-permute-start | bytes 3145736 | tf_op jit(solution)/shard_map/ppermute | solution.py:40
  236.2 19.9 %collective-permute-start.22 = (f32[512,512]{1,0:T(8,128)S(1)}, f32[512,512]{1,0:T(8,128)S(1)}, u32[]{:S(2)}, u32[]{:S(2)}) collective-permute-start(f32[512,512]{1,0:T(8,128)S(1)} %get-tuple-element.198), channel_id=1, source_target_pairs={{1,2},{2,1},{5,6},{6,5},{9,10},{10,9},{13,14},{14,13},{17,18},{18,... | collective-permute-start | bytes 3145736 | tf_op jit(solution)/shard_map/ppermute | solution.py:40
  256.1 23.6 %collective-permute-start.23 = (f32[512,512]{1,0:T(8,128)S(1)}, f32[512,512]{1,0:T(8,128)S(1)}, u32[]{:S(2)}, u32[]{:S(2)}) collective-permute-start(f32[512,512]{1,0:T(8,128)S(1)} %collective-permute-done.22), channel_id=1, source_target_pairs={{1,0},{2,3},{5,4},{6,7},{9,8},{10,11},{13,12},{14,15},{17,16},{18,... | collective-permute-start | bytes 3145736 | tf_op jit(solution)/shard_map/ppermute | solution.py:40
  257.4 22.3 %collective-permute-start.24 = (f32[512,512]{1,0:T(8,128)S(1)}, f32[512,512]{1,0:T(8,128)S(1)}, u32[]{:S(2)}, u32[]{:S(2)}) collective-permute-start(f32[512,512]{1,0:T(8,128)S(1)} %collective-permute-done.21), channel_id=1, source_target_pairs={{1,2},{2,1},{5,6},{6,5},{9,10},{10,9},{13,14},{14,13},{17,18},{18,... | collective-permute-start | bytes 3145736 | tf_op jit(solution)/shard_map/ppermute | solution.py:40
  258.2 21.5 %collective-permute-start.19 = (f32[512]{0:T(512)S(1)}, f32[512]{0:T(512)S(1)}, u32[]{:S(2)}, u32[]{:S(2)}) collective-permute-start(f32[512]{0:T(512)S(1)} %get-tuple-element.197), channel_id=1, source_target_pairs={{0,1},{1,0},{2,3},{3,2},{4,5},{5,4},{6,7},{7,6},{8,9},{9,8},{10,11... | collective-permute-start | bytes 6152 | tf_op jit(solution)/shard_map/ppermute | solution.py:40
  279.7 22.7 %collective-permute-start.25 = (f32[512,512]{1,0:T(8,128)S(1)}, f32[512,512]{1,0:T(8,128)S(1)}, u32[]{:S(2)}, u32[]{:S(2)}) collective-permute-start(f32[512,512]{1,0:T(8,128)S(1)} %collective-permute-done.24), channel_id=1, source_target_pairs={{1,0},{2,3},{5,4},{6,7},{9,8},{10,11},{13,12},{14,15},{17,16},{18,... | collective-permute-start | bytes 3145736 | tf_op jit(solution)/shard_map/ppermute | solution.py:40
  331.5 242.4 %reduce-scatter.7.cloned.1.call-start = ((), (), s32[]{:S(2)}) async-start(), calls=%async_computation.5 | async-start | bytes 28311552 | tf_op jit(solution)/shard_map/reduce_scatter | solution.py:479
  350.5 312.0 %reduce-scatter.9.cloned.1.call-start = ((), (), s32[]{:S(2)}) async-start(), calls=%async_computation.6 | async-start | bytes 11796480 | tf_op jit(solution)/shard_map/reduce_scatter | solution.py:479
  352.4 19.7 %collective-permute-start.26 = (f32[512,512]{1,0:T(8,128)S(1)}, f32[512,512]{1,0:T(8,128)S(1)}, u32[]{:S(2)}, u32[]{:S(2)}) collective-permute-start(f32[512,512]{1,0:T(8,128)S(1)} %get-tuple-element.209), channel_id=1, source_target_pairs={{0,1},{3,2},{4,5},{7,6},{8,9},{11,10},{12,13},{15,14},{16,17},{19,... | collective-permute-start | bytes 3145736 | tf_op jit(solution)/shard_map/ppermute | solution.py:40
  372.3 25.3 %collective-permute-start.28 = (f32[512,512]{1,0:T(8,128)S(1)}, f32[512,512]{1,0:T(8,128)S(1)}, u32[]{:S(2)}, u32[]{:S(2)}) collective-permute-start(f32[512,512]{1,0:T(8,128)S(1)} %get-tuple-element.111), channel_id=1, source_target_pairs={{0,1},{3,2},{4,5},{7,6},{8,9},{11,10},{12,13},{15,14},{16,17},{19,... | collective-permute-start | bytes 3145736 | tf_op jit(solution)/shard_map/ppermute | solution.py:40
  377.2 20.7 %collective-permute-start.27 = (f32[512,512]{1,0:T(8,128)S(1)}, f32[512,512]{1,0:T(8,128)S(1)}, u32[]{:S(2)}, u32[]{:S(2)}) collective-permute-start(f32[512,512]{1,0:T(8,128)S(1)} %add.288), channel_id=1, source_target_pairs={{1,2},{2,1},{5,6},{6,5},{9,10},{10,9},{13,14},{14,13},{17,18},{18,... | collective-permute-start | bytes 3145736 | tf_op jit(solution)/shard_map/ppermute | solution.py:40
  398.9 22.3 %collective-permute-start.32 = (f32[512,512]{1,0:T(8,128)S(1)}, f32[512,512]{1,0:T(8,128)S(1)}, u32[]{:S(2)}, u32[]{:S(2)}) collective-permute-start(f32[512,512]{1,0:T(8,128)S(1)} %dynamic-slice_add_fusion.2), channel_id=1, source_target_pairs={{0,1},{1,0},{2,3},{3,2},{4,5},{5,4},{6,7},{7,6},{8,9},{9,8},{10,11... | collective-permute-start | bytes 3145736 | tf_op jit(solution)/shard_map/ppermute | solution.py:40
  422.6 24.1 %collective-permute-start.34 = (f32[512,512]{1,0:T(8,128)S(1)}, f32[512,512]{1,0:T(8,128)S(1)}, u32[]{:S(2)}, u32[]{:S(2)}) collective-permute-start(f32[512,512]{1,0:T(8,128)S(1)} %get-tuple-element.116), channel_id=1, source_target_pairs={{0,1},{1,0},{2,3},{3,2},{4,5},{5,4},{6,7},{7,6},{8,9},{9,8},{10,11... | collective-permute-start | bytes 3145736 | tf_op jit(solution)/shard_map/ppermute | solution.py:40
  446.7 22.6 %collective-permute-start.35 = (f32[512,512]{1,0:T(8,128)S(1)}, f32[512,512]{1,0:T(8,128)S(1)}, u32[]{:S(2)}, u32[]{:S(2)}) collective-permute-start(f32[512,512]{1,0:T(8,128)S(1)} %get-tuple-element.117), channel_id=1, source_target_pairs={{0,1},{3,2},{4,5},{7,6},{8,9},{11,10},{12,13},{15,14},{16,17},{19,... | collective-permute-start | bytes 3145736 | tf_op jit(solution)/shard_map/ppermute | solution.py:40
  451.2 20.3 %collective-permute-start.36 = (f32[512,512]{1,0:T(8,128)S(1)}, f32[512,512]{1,0:T(8,128)S(1)}, u32[]{:S(2)}, u32[]{:S(2)}) collective-permute-start(f32[512,512]{1,0:T(8,128)S(1)} %collective-permute-done.33), channel_id=1, source_target_pairs={{1,0},{2,3},{5,4},{6,7},{9,8},{10,11},{13,12},{14,15},{17,16},{18,... | collective-permute-start | bytes 3145736 | tf_op jit(solution)/shard_map/ppermute | solution.py:40
  452.5 25.2 %collective-permute-start.41 = (f32[512,512]{1,0:T(8,128)S(1)}, f32[512,512]{1,0:T(8,128)}, u32[]{:S(2)}, u32[]{:S(2)}) collective-permute-start(f32[512,512]{1,0:T(8,128)S(1)} %collective-permute-done.34), channel_id=1, source_target_pairs={{1,2},{2,1},{5,6},{6,5},{9,10},{10,9},{13,14},{14,13},{17,18},{18,... | collective-permute-start | bytes 3145736 | tf_op jit(solution)/shard_map/ppermute | solution.py:40
  471.5 16.1 %collective-permute-start.37 = (f32[512,512]{1,0:T(8,128)}, f32[512,512]{1,0:T(8,128)}, u32[]{:S(2)}, u32[]{:S(2)}) collective-permute-start(f32[512,512]{1,0:T(8,128)} %get-tuple-element.119), channel_id=1, source_target_pairs={{0,1},{3,2},{4,5},{7,6},{8,9},{11,10},{12,13},{15,14},{16,17},{19,... | collective-permute-start | bytes 3145736 | tf_op jit(solution)/shard_map/ppermute | solution.py:40
  477.6 26.0 %collective-permute-start.42 = (f32[512,512]{1,0:T(8,128)}, f32[512,512]{1,0:T(8,128)S(1)}, u32[]{:S(2)}, u32[]{:S(2)}) collective-permute-start(f32[512,512]{1,0:T(8,128)} %collective-permute-done.41), channel_id=1, source_target_pairs={{1,0},{2,3},{5,4},{6,7},{9,8},{10,11},{13,12},{14,15},{17,16},{18,... | collective-permute-start | bytes 3145736 | tf_op jit(solution)/shard_map/ppermute | solution.py:40
  493.0 45.1 %collective-permute-start.39 = (f32[512,512]{1,0:T(8,128)}, f32[512,512]{1,0:T(8,128)}, u32[]{:S(2)}, u32[]{:S(2)}) collective-permute-start(f32[512,512]{1,0:T(8,128)} %add.297), channel_id=1, source_target_pairs={{1,2},{2,1},{5,6},{6,5},{9,10},{10,9},{13,14},{14,13},{17,18},{18,... | collective-permute-start | bytes 3145736 | tf_op jit(solution)/shard_map/ppermute | solution.py:40
  494.7 43.4 %collective-permute-start.40 = (f32[512,512]{1,0:T(8,128)}, f32[512,512]{1,0:T(8,128)}, u32[]{:S(2)}, u32[]{:S(2)}) collective-permute-start(f32[512,512]{1,0:T(8,128)} %dynamic-slice_add_fusion.1), channel_id=1, source_target_pairs={{0,1},{1,0},{2,3},{3,2},{4,5},{5,4},{6,7},{7,6},{8,9},{9,8},{10,11... | collective-permute-start | bytes 3145736 | tf_op jit(solution)/shard_map/ppermute | solution.py:40
  550.1 137.2 %reduce-scatter.11.cloned.1.call-start = ((), (), s32[]{:S(2)}) async-start(), calls=%async_computation.7 | async-start | bytes 5898240 | tf_op jit(solution)/shard_map/reduce_scatter | solution.py:479
  572.1 36.4 %collective-permute-start.57 = (f32[656,320]{0,1:T(8,128)}, f32[656,320]{0,1:T(8,128)}, u32[]{:S(2)}, u32[]{:S(2)}) collective-permute-start(f32[656,320]{0,1:T(8,128)} %fusion.53), channel_id=1, source_target_pairs={{0,8},{4,12},{8,0},{12,4},{16,24},{20,28},{24,16},{28,20},{1,9},{5... | collective-permute-start | bytes 2519048 | tf_op jit(solution)/shard_map/ppermute | solution.py:113
  573.9 41.9 %collective-permute-start.44 = (f32[512,512]{1,0:T(8,128)}, f32[512,512]{1,0:T(8,128)S(1)}, u32[]{:S(2)}, u32[]{:S(2)}) collective-permute-start(f32[512,512]{1,0:T(8,128)} %get-tuple-element.141), channel_id=1, source_target_pairs={{0,1},{3,2},{4,5},{7,6},{8,9},{11,10},{12,13},{15,14},{16,17},{19,... | collective-permute-start | bytes 3145736 | tf_op jit(solution)/shard_map/ppermute | solution.py:40
  577.7 23.2 %collective-permute-start.51 = (f32[2,2048]{1,0:T(2,128)S(1)}, f32[2,2048]{1,0:T(2,128)S(1)}, u32[]{:S(2)}, u32[]{:S(2)}) collective-permute-start(f32[2,2048]{1,0:T(2,128)S(1)} %fusion.52), channel_id=1, source_target_pairs={{0,2},{1,3},{2,0},{3,1},{4,6},{5,7},{6,4},{7,5},{8,10},{9,11},{10,... | collective-permute-start | bytes 49160 | tf_op jit(solution)/shard_map/ppermute | solution.py:113
  605.1 18.1 %collective-permute-start.48 = (f32[512]{0:T(512)S(1)}, f32[512]{0:T(512)S(1)}, u32[]{:S(2)}, u32[]{:S(2)}) collective-permute-start(f32[512]{0:T(512)S(1)} %add.309), channel_id=1, source_target_pairs={{0,2},{2,0},{1,3},{3,1},{4,6},{6,4},{5,7},{7,5},{8,10},{10,8},{9,1... | collective-permute-start | bytes 6152 | tf_op jit(solution)/shard_map/ppermute | solution.py:40
  610.1 32.0 %collective-permute-start.58 = (f32[656,320]{0,1:T(8,128)S(1)}, f32[656,320]{0,1:T(8,128)S(1)}, u32[]{:S(2)}, u32[]{:S(2)}) collective-permute-start(f32[656,320]{0,1:T(8,128)S(1)} %add.320), channel_id=1, source_target_pairs={{0,16},{4,20},{8,24},{12,28},{16,0},{20,4},{24,8},{28,12},{1,17},{... | collective-permute-start | bytes 2519048 | tf_op jit(solution)/shard_map/ppermute | solution.py:113
  615.5 25.9 %collective-permute-start.56 = (f32[2,2048]{1,0:T(2,128)S(1)}, f32[2,2048]{1,0:T(2,128)S(1)}, u32[]{:S(2)}, u32[]{:S(2)}) collective-permute-start(f32[2,2048]{1,0:T(2,128)S(1)} %add.318), channel_id=1, source_target_pairs={{0,16},{4,20},{8,24},{12,28},{16,0},{20,4},{24,8},{28,12},{1,17},{... | collective-permute-start | bytes 49160 | tf_op jit(solution)/shard_map/ppermute | solution.py:113
  616.9 37.8 %collective-permute-start.46 = (f32[512,512]{1,0:T(8,128)}, f32[512,512]{1,0:T(8,128)}, u32[]{:S(2)}, u32[]{:S(2)}) collective-permute-start(f32[512,512]{1,0:T(8,128)} %add.306), channel_id=1, source_target_pairs={{1,2},{2,1},{5,6},{6,5},{9,10},{10,9},{13,14},{14,13},{17,18},{18,... | collective-permute-start | bytes 3145736 | tf_op jit(solution)/shard_map/ppermute | solution.py:40
  618.6 33.4 %collective-permute-start.45 = (f32[512,512]{1,0:T(8,128)}, f32[512,512]{1,0:T(8,128)}, u32[]{:S(2)}, u32[]{:S(2)}) collective-permute-start(f32[512,512]{1,0:T(8,128)} %get-tuple-element.149), channel_id=1, source_target_pairs={{0,1},{3,2},{4,5},{7,6},{8,9},{11,10},{12,13},{15,14},{16,17},{19,... | collective-permute-start | bytes 3145736 | tf_op jit(solution)/shard_map/ppermute | solution.py:40
  659.1 25.0 %collective-permute-start.53 = (f32[512,512]{1,0:T(8,128)}, f32[512,512]{1,0:T(8,128)}, u32[]{:S(2)}, u32[]{:S(2)}) collective-permute-start(f32[512,512]{1,0:T(8,128)} %dynamic-slice_add_fusion), channel_id=1, source_target_pairs={{0,1},{1,0},{2,3},{3,2},{4,5},{5,4},{6,7},{7,6},{8,9},{9,8},{10,11... | collective-permute-start | bytes 3145736 | tf_op jit(solution)/shard_map/ppermute | solution.py:40
  (87 other events, 1535.8 us)
Sparse Core Ops, SparseCore 0:
  331.6 67.6 reduce-scatter.4
  401.7 128.1 reduce-scatter.6
  550.3 86.2 reduce-scatter.8
  639.3 38.8 reduce-scatter.10

commit v3 on v2

--- a/solution.py
+++ b/solution.py
@@ -111,6 +111,15 @@
 def swapped(value, axis, bit):
     count = lax.axis_size(axis)
     return lax.ppermute(value, axis, [(d, d ^ bit) for d in range(count)])
+
+
+def over_chips(value, bit):
+    devices = lax.axis_size("seq")
+    value = value + swapped(value, "seq", bit)
+    while bit > 2 and 2 * bit < devices:
+        bit *= 2
+        value = value + swapped(value, "seq", bit)
+    return value
 
 
 def sum_over(value, axis):
@@ -267,8 +276,8 @@
 def backward_kernel(
     mine_ref, ends_ref, dstates_ref, alpha_ref, states_ref, enter_ref, conv_ref, rg_ref, ig_ref,
     factor_ref, valid_ref, inner_ref, halo_ref, row_ref, gate_ref,
-    dinner_ref, tail_ref, head_ref, drec_ref, sums_ref,
-    dconv_ref, ext_ref,
+    dinner_ref, tail_ref, head_ref, small_ref,
+    dconv_ref, ext_ref, drec_ref, whole_ref, *, groups,
 ):
     devices = ends_ref.shape[0]
     count, width = alpha_ref.shape
@@ -280,11 +289,11 @@
     dconv_ref[pl.ds(0, SUB), :] = jnp.zeros((SUB, width), f32)
     dconv_ref[pl.ds(count + SUB, SUB), :] = jnp.zeros((SUB, width), f32)
     ext_ref[pl.ds(0, SUB), :] = halo_ref[...]
-    groups = (ROWS // SUB, SUB, width)
+    parts = (ROWS // SUB, SUB, width)
     place = lax.broadcasted_iota(jnp.int32, (SUB, width), 0)
 
     def fold(value):
-        return jnp.sum(value.reshape(groups), axis=0)
+        return jnp.sum(value.reshape(parts), axis=0)
 
     def back(step, carry):
         flow, decay, bias_r, bias_i = carry
@@ -294,8 +303,8 @@
         ext_ref[pl.ds(r + SUB, ROWS), :] = inner_ref[here, :]
         alpha = alpha_ref[here, :]
         dstates = dstates_ref[here, :]
-        a3, b3 = group_scan_back(alpha.reshape(groups), (alpha * dstates).reshape(groups))
-        d3 = dstates.reshape(groups)
+        a3, b3 = group_scan_back(alpha.reshape(parts), (alpha * dstates).reshape(parts))
+        d3 = dstates.reshape(parts)
         totals = [None] * (ROWS // SUB)
         for g in reversed(range(ROWS // SUB)):
             flows = b3[g] + a3[g] * flow
@@ -360,9 +369,28 @@
         return tuple(c + s for c, s in zip(carry, sums))
 
     sums = lax.fori_loop(0, blocks, finish, (zero,) * 5)
-    sums_ref[...] = jnp.concatenate(
+    sums = jnp.concatenate(
         [jnp.sum(s, axis=0, keepdims=True) for s in (*sums, bias_r, bias_i, decay)], 0
     )
+    whole_ref[...] = lax.dot_general(
+        conv_ref[...].astype(bf16), drec_ref[...], (((0,), (0,)), ((), ())),
+        preferred_element_type=f32,
+    )
+    block = width // groups
+    left = lax.broadcasted_iota(jnp.int32, (block, width), 1) < block
+
+    def turned(value, shift):
+        return pltpu.roll(value, shift % width, 1) if shift % width else value
+
+    for b in range(groups):
+        here = slice(b * block, (b + 1) * block)
+        recur = turned(whole_ref[here, :width], -b * block)
+        entry = turned(whole_ref[here, width:], block - b * block)
+        small_ref[here, :] = jnp.where(left, recur, entry)[:, : 2 * block]
+    for b in range(groups // 2):
+        small_ref[width + b * SUB : width + (b + 1) * SUB, :] = turned(
+            sums, -2 * b * block
+        )[:, : 2 * block]
 
 
 def vmem(count=1):
@@ -435,19 +463,21 @@
     )(dmixed, gate_pre, states, span)
 
 
-def run_backward(mine, ends, dstates, saved, enter, valid, inner, halo, rows, gates):
+def run_backward(mine, ends, dstates, saved, enter, valid, inner, halo, rows, gates, groups):
     count, width = dstates.shape
     return pl.pallas_call(
-        backward_kernel,
+        partial(backward_kernel, groups=groups),
         out_shape=(
             shape((count, width), bf16), shape((2 * SUB, width)), shape((SUB, width)),
-            shape((count, 2 * width), bf16), shape((SUB, width)),
+            shape((width + SUB * groups // 2, 2 * width // groups)),
         ),
         in_specs=[pl.BlockSpec(memory_space=pltpu.SMEM)] + vmem(14),
-        out_specs=tuple(vmem(5)),
+        out_specs=tuple(vmem(4)),
         scratch_shapes=[
             pltpu.VMEM((count + 2 * SUB, width), f32),
             pltpu.VMEM((count + SUB, width), f32),
+            pltpu.VMEM((count, 2 * width), bf16),
+            pltpu.VMEM((width, 2 * width), f32),
         ],
         compiler_params=pltpu.CompilerParams(vmem_limit_bytes=VMEM_LIMIT),
         cost_estimate=small_cost(),
@@ -538,17 +568,6 @@
     return jnp.concatenate(rows, 0)
 
 
-def diagonal_blocks(whole, groups):
-    width = whole.shape[0] // groups
-    return jnp.stack(
-        [
-            whole[b * width : (b + 1) * width, b * width : (b + 1) * width]
-            for b in range(groups)
-        ],
-        0,
-    )
-
-
 def row_scale(squares, features):
     return lax.rsqrt(squares / features + norm_eps)[:, None]
 
@@ -638,14 +657,16 @@
     ffn_up = ffn[:, ffn_width:]
     hidden_low = (act * ffn_up).astype(bf16)
     d_pair_low = jnp.concatenate([d_hidden * ffn_up * slope, d_hidden * act], 1).astype(bf16)
+    whole_down = rows_product(hidden_low, cot_low, own_width)
+    grad_down = ring_scatter(whole_down)
+    d_pair_low = after(d_pair_low, whole_down)
     d_second_part = matmul_nt(d_pair_low, ffn_weight)
 
     turned = LineScatter(d_second_part, own_width)
     turned.first()
-    whole_down = rows_product(after(hidden_low, d_second_part), cot_low, own_width)
     whole_pair = columns_product(after(second_low, d_second_part), [d_pair_low])
-    turned.second(whole_down, whole_pair)
-    grad_down = ring_scatter(whole_down)
+    turned.second(whole_pair)
+    whole_pair = after(whole_pair, turned.far_one)
     grad_pair = ring_scatter(whole_pair)
     second_product = after(d_second_part, turned.far_one) * second_low.astype(f32)
     second_mean = line_sum(jnp.sum(second_product, axis=1)) / features
@@ -660,7 +681,8 @@
     )
     gathered = LineGather(own_d_resid)
     gathered.first(mlp_part)
-    gathered.second()
+    d_gain_second = sum_over(sum_over(after(d_gain_second, own_d_resid), "mp"), "seq")
+    gathered.second(d_gain_second)
     sent = LineScatter(mlp_part, own_width)
     sent.first(gathered.near_in, gathered.beside)
     gathered.third(sent.far_one, grad_down)
@@ -669,12 +691,14 @@
 
     d_mixed = matmul_nt(after(branch_low, sent.far_two, sent.near_one), proj_out)
     d_states, d_gate_low, outgoing = run_turn(d_mixed, gate_pre, states, span)
-    leaving = jnp.stack([last[0], jnp.sum(outgoing, axis=0)], 0)
+    whole_out = rows_product(after(mixed_low, d_states), branch_low, 2 * own_width)
+    grad_out = ring_scatter(whole_out)
+    leaving = jnp.stack([last[0], jnp.sum(after(outgoing, whole_out), axis=0)], 0)
     back_ends = lax.all_gather(leaving, "seq")
-    sent.third()
+    sent.third(outgoing)
     saved = dict(alpha=alpha, states=states, conv=conv, rg=rg, ig=ig, factor=factor)
-    d_inner_low, tail, head, d_rec_low, sums = run_backward(
-        seq_at, back_ends, d_states, saved, enter, valid, inner, halo, rows, gates
+    d_inner_low, tail, head, small = run_backward(
+        seq_at, back_ends, d_states, saved, enter, valid, inner, halo, rows, gates, groups
     )
     returned = lax.ppermute(head, "seq", backward)
     d_first_gate = matmul_nt(after(d_gate_low, head), proj_gate)
@@ -688,45 +712,37 @@
     whole_first = columns_product(
         after(first_low, d_first_part), [d_inner_low, d_gate_low]
     )
-    grad_first = ring_scatter(whole_first)
     first_product = after(d_first_part, whole_first) * first_low.astype(f32)
     first_mean = jnp.sum(first_product, axis=1)
-    gains = jnp.stack([jnp.sum(first_product, axis=0) / gain_first, d_gain_second], 0)
-    gate_grads = matmul_tn(conv_low, after(d_rec_low, whole_first))
-    block_width = inner_width // groups
-    small = jnp.concatenate(
-        [
-            jnp.concatenate(
-                [
-                    diagonal_blocks(gate_grads[:, :inner_width], groups),
-                    diagonal_blocks(gate_grads[:, inner_width:], groups),
-                ],
-                2,
-            ).reshape(inner_width, 2 * block_width),
-            sums.reshape(-1, 2 * block_width),
-        ],
-        0,
-    )
-    whole_out = rows_product(after(mixed_low, whole_first), branch_low, 2 * own_width)
-    grad_out = ring_scatter(whole_out)
-    final.second(small, gains, first_mean, whole_out)
+    d_gain_first = jnp.sum(first_product, axis=0) / gain_first
+    output = own_resid + sent.result()
     small = small + swapped(small, "seq", 1)
-    gains = sum_over(gains, "mp")
-    first_mean = line_sum(first_mean) / features
-    output = own_resid + sent.result()
-    final.third(output, first_mean, small, gains)
-    bit = 2
-    while bit < devices:
-        small = small + swapped(small, "seq", bit)
-        bit *= 2
-    gains = sum_over(gains, "seq")
+    half = small.shape[0] // 2
+    small = lax.dynamic_slice_in_dim(small, (lax.axis_index("seq") & 1) * half, half, 0)
+    final.second(whole_first, first_mean, d_gain_first, output, small, grad_out)
+    whole_first, first_mean, d_gain_first = after(
+        (whole_first, first_mean, d_gain_first), final.far_one
+    )
+    grad_first = ring_scatter(whole_first)
+    first_sums = line_sum(jnp.concatenate([first_mean, d_gain_first]))
+    first_mean, d_gain_first = first_sums[:count] / features, first_sums[count:]
+    small = over_chips(after(small, final.far_one), 2)
+    final.third(first_mean, d_gain_first, small)
+    small = over_chips(small, 4)
+    d_gain_first = sum_over(d_gain_first, "seq")
+    small, d_gain_first = after((small, d_gain_first), final.last)
+    other = swapped(small, "seq", 1)
+    lower = lax.axis_index("seq") & 1 == 0
+    small = jnp.concatenate([jnp.where(lower, small, other), jnp.where(lower, other, small)], 0)
     own_d_first = final.result()
     grad_stream = (
         own_d_resid
         + first_scale * (own_first * own_d_first)
         - stream * (first_scale * first_scale * first_mean[:, None])
     )
-    sums = small[inner_width:].reshape(SUB, inner_width)
+    block_width = inner_width // groups
+    sums = small[inner_width:].reshape(groups // 2, SUB, 2 * block_width)
+    sums = sums.transpose(1, 0, 2).reshape(SUB, inner_width)
     grad_gates = [
         small[:inner_width, g * block_width : (g + 1) * block_width].reshape(
             groups, block_width, block_width
@@ -737,7 +753,7 @@
     return (
         output,
         grad_stream,
-        gains[0],
+        d_gain_first,
         grad_first[:, :inner_width],
         grad_first[:, inner_width:],
         sums[:4],
@@ -748,7 +764,7 @@
         sums[6],
         grad_decay,
         grad_out,
-        gains[1],
+        d_gain_second,
         grad_pair[:, :ffn_width],
         grad_pair[:, ffn_width:],
         grad_down,

time: 699 us -> 691 us (0.989)
  waiting for transfers between devices: 287 us -> 259 us
  starting transfers between devices: 149 us -> 157 us
    ppermute x48, waiting for transfers between devices: 245 us -> 228 us  [over_mp(): return lax.ppermute(value, 'mp', list(pairs))]
    ppermute x8 -> x12, waiting for transfers between devices: 41.4 us -> 31.4 us  [swapped(): return lax.ppermute(value, axis, [(d, d ^ bit) for d in range(count)])]
    ppermute x8 -> x12, starting transfers between devices: 5.92 us -> 13.4 us  [swapped(): return lax.ppermute(value, axis, [(d, d ^ bit) for d in range(count)])]
    unnamed x145 -> x147, local copies, waits for them, and re-layouts: 15.6 us -> 20.6 us
  transfers between devices with their start and end apart: 63 -> 67, of which waited for: 25 -> 32; matrix products, arithmetic and copies ran while one was open for 19% -> 20% of each run, Pallas kernels for 8% -> 8%
where the time goes in v3:
time: 691 us; the launch traced here: 683 us
  waiting for transfers between devices  259 us (37%)
  starting transfers between devices  157 us (23%)
  other arithmetic  75 us (11%)
  Pallas kernels  63.4 us (9%)
  local copies, waits for them, and re-layouts  46.8 us (7%)
  matrix products  45.5 us (7%)
  blocking collectives  20.3 us (3%)
  between operations  15.3 us (2%)
    ppermute x48, waiting for transfers between devices, over_mp(): return lax.ppermute(value, 'mp', list(pairs))  228 us
    ppermute x48, starting transfers between devices, over_mp(): return lax.ppermute(value, 'mp', list(pairs))  139 us
    ppermute x12, waiting for transfers between devices, swapped(): return lax.ppermute(value, axis, [(d, d ^ bit) for d in range(count)])  31.4 us
    dot_general x5, matrix products, matmul_nt(): lax.dot_general(left, right, (((1,), (1,)), ((), ())), preferred_element_...  26.8 us
    pallas_call x2, Pallas kernels, columns_product(): pl.pallas_call(columns_product_kernel, grid_spec=pltpu.PrefetchScalarGrid...  22.6 us
    unnamed x147, local copies, waits for them, and re-layouts  20.6 us
    dot_general x5, matrix products, matmul(): return jnp.dot(left, right, preferred_element_type=f32)  18.7 us
    dynamic_update_slice x16, other arithmetic, assemble(): lax.dynamic_update_slice(whole, turn(piece, start).astype(bf16), (0, start))  14.9 us
  transfers between devices with their start and end apart: 67, of which 32 were waited for; matrix products, arithmetic and copies ran while one was open for 20% of the time, Pallas kernels for 8%

profile of v3, /device:TPU:0, one launch (start us, length us, event | category | flops | bytes accessed | tf_op | source)
XLA Modules:
  0.0 682.8 jit_solution(6690184132606542531)
XLA Ops:
  9.0 5.0 collective-permute-start.2
  18.9 18.3 %collective-permute-done.2 = f32[512,512]{1,0:T(8,128)} collective-permute-done((f32[512,512]{1,0:T(8,128)}, f32[512,512]{1,0:T(8,128)}, u32[]{:S(2)}, u32[]{:S(2)}) %collective-permute-start.2) | collective-permute-done | bytes 1048608 | tf_op jit(solution)/shard_map/ppermute | solution.py:40
  40.1 8.5 %fusion.29.gate_ref = bf16[640,1280]{1,0:T(8,128)(2,1)} fusion(bf16[160,160]{1,0:T(8,128)(2,1)S(1)} %get-tuple-element.206, bf16[160,160]{1,0:T(8,128)(2,1)S(1)} %get-tuple-element.207, bf16[160,160]{1,0:T(8,128)(2,1)S(1)} %get-tuple-element.205, bf16[160,160]{1,0:T(8,128)(2,1)S(1)} %get-tuple-element.204, bf16[160,160]{1,0:T(8,128)(2,1)S(1)} %get-tuple-element.218, ...), kind=kLoop, calls=%fused_computation.47 | loop fusion | flops 40960000 | bytes 2048000 | tf_op jit(solution)/shard_map/concatenate | solution.py:614
  50.2 5.4 collective-permute-start.1
  55.6 7.8 %collective-permute-done.4 = f32[512,512]{1,0:T(8,128)} collective-permute-done((f32[512,512]{1,0:T(8,128)}, f32[512,512]{1,0:T(8,128)}, u32[]{:S(2)}, u32[]{:S(2)}) %collective-permute-start.4) | collective-permute-done | bytes 1048608 | tf_op jit(solution)/shard_map/ppermute | solution.py:40
  71.3 19.4 %collective-permute-done.7 = f32[512,512]{1,0:T(8,128)} collective-permute-done((f32[512,512]{1,0:T(8,128)}, f32[512,512]{1,0:T(8,128)}, u32[]{:S(2)}, u32[]{:S(2)}) %collective-permute-start.7) | collective-permute-done | bytes 1048608 | tf_op jit(solution)/shard_map/ppermute | solution.py:40
  101.5 11.2 %recurrence_forward.1 = (f32[512,640]{1,0:T(8,128)S(1)}, bf16[512,640]{1,0:T(8,128)(2,1)}, f32[512,640]{1,0:T(8,128)}, f32[512,640]{1,0:T(8,128)}, f32[512,640]{...) custom-call(f32[512,640]{1,0:T(8,128)} %copy-done.27, ...), custom_call_target="tpu_custom_call" | custom-call | flops 1000 | bytes 1000 | tf_op jit(solution)/shard_map/recurrence_forward/pallas_call | solution.py:411
  113.7 11.0 %all-gather = f32[64,640]{1,0:T(8,128)S(1)} all-gather(f32[8,640]{1,0:T(8,128)S(1)} %get-tuple-element.96), channel_id=2, replica_groups=mesh['seq'=8,'mp'=4] {'seq'}, dimensions={0}, use_global_device_ids=true | all-gather | bytes 184320 | tf_op jit(solution)/shard_map/all_gather | solution.py:631
  133.8 5.9 collective-permute-start.11
  139.7 14.2 %collective-permute-done.13 = f32[512,512]{1,0:T(8,128)} collective-permute-done((f32[512,512]{1,0:T(8,128)}, f32[512,512]{1,0:T(8,128)}, u32[]{:S(2)}, u32[]{:S(2)}) %collective-permute-start.13) | collective-permute-done | bytes 1048608 | tf_op jit(solution)/shard_map/ppermute | solution.py:40
  155.3 7.0 %collective-permute-done.11 = f32[512,512]{1,0:T(8,128)S(1)} collective-permute-done((f32[512,512]{1,0:T(8,128)S(1)}, f32[512,512]{1,0:T(8,128)S(1)}, u32[]{:S(2)}, u32[]{:S(2)}) %collective-permute-start.11) | collective-permute-done | bytes 1048608 | tf_op jit(solution)/shard_map/ppermute | solution.py:40
  163.5 17.6 %collective-permute-start.14 = (f32[512,512]{1,0:T(8,128)S(1)}, f32[512,512]{1,0:T(8,128)}, u32[]{:S(2)}, u32[]{:S(2)}) collective-permute-start(f32[512,512]{1,0:T(8,128)S(1)} %get-tuple-element.104), channel_id=1, source_target_pairs={{0,1},{3,2},{4,5},{7,6},{8,9},{11,10},{12,13},{15,14},{16,17},{19,... | collective-permute-start | bytes 3145736 | tf_op jit(solution)/shard_map/ppermute | solution.py:40
  193.6 16.7 %collective-permute-start.18 = (f32[512,512]{1,0:T(8,128)S(1)}, f32[512,512]{1,0:T(8,128)S(1)}, u32[]{:S(2)}, u32[]{:S(2)}) collective-permute-start(f32[512,512]{1,0:T(8,128)S(1)} %dynamic-slice_add_fusion.3), channel_id=1, source_target_pairs={{0,1},{1,0},{2,3},{3,2},{4,5},{5,4},{6,7},{7,6},{8,9},{9,8},{10,11... | collective-permute-start | bytes 3145736 | tf_op jit(solution)/shard_map/ppermute | solution.py:40
  213.7 18.0 %collective-permute-done.18 = f32[512,512]{1,0:T(8,128)S(1)} collective-permute-done((f32[512,512]{1,0:T(8,128)S(1)}, f32[512,512]{1,0:T(8,128)S(1)}, u32[]{:S(2)}, u32[]{:S(2)}) %collective-permute-start.18) | collective-permute-done | bytes 1048608 | tf_op jit(solution)/shard_map/ppermute | solution.py:40
  232.8 4.2 collective-permute-start.21
  238.8 5.8 fusion.60
  244.6 12.5 %collective-permute-done.21 = f32[512,512]{1,0:T(8,128)S(1)} collective-permute-done((f32[512,512]{1,0:T(8,128)S(1)}, f32[512,512]{1,0:T(8,128)S(1)}, u32[]{:S(2)}, u32[]{:S(2)}) %collective-permute-start.21) | collective-permute-done | bytes 1048608 | tf_op jit(solution)/shard_map/ppermute | solution.py:40
  259.1 4.8 collective-permute-start.19
  263.9 16.4 %collective-permute-done.19 = f32[512]{0:T(512)S(1)} collective-permute-done((f32[512]{0:T(512)S(1)}, f32[512]{0:T(512)S(1)}, u32[]{:S(2)}, u32[]{:S(2)}) %collective-permute-start.19) | collective-permute-done | bytes 2080 | tf_op jit(solution)/shard_map/ppermute | solution.py:40
  285.7 17.9 %collective-permute-done.25 = f32[512,512]{1,0:T(8,128)S(1)} collective-permute-done((f32[512,512]{1,0:T(8,128)S(1)}, f32[512,512]{1,0:T(8,128)S(1)}, u32[]{:S(2)}, u32[]{:S(2)}) %collective-permute-start.25) | collective-permute-done | bytes 1048608 | tf_op jit(solution)/shard_map/ppermute | solution.py:40
  303.8 6.8 fusion.61
  310.5 3.6 multiply_convert_fusion.1
  314.1 6.7 rows_product.2
  324.4 11.8 %fusion.62 = f32[512,2048]{1,0:T(8,128)S(1)} fusion(bf16[512,3072]{1,0:T(8,128)(2,1)S(1)} %pad_maximum_fusion.refs_0_, bf16[2048,3072]{1,0:T(8,128)(2,1)} %constant_dynamic-update-slice_fusion), kind=kOutput, calls=%fused_computation.153 | convolution fusion | flops 6442450944 | bytes 19922944 | tf_op jit(solution)/shard_map/dot_general | solution.py:25
  342.0 14.5 %columns_product.2 = f32[2048,3072]{1,0:T(8,128)} custom-call(s32[8]{0:T(128)S(1)} %copy-done.18, bf16[512,2048]{1,0:T(8,128)(2,1)S(1)} %copy-done.2, bf16[512,3072]{1,0:T(8,128)(2,1)} %copy-done.26), custom_call_target="tpu_custom_call" | custom-call | flops 1000 | bytes 1000 | tf_op jit(solution)/shard_map/columns_product/pallas_call | solution.py:522
  360.1 4.5 collective-permute-start.28
  369.8 10.2 %collective-permute-done.29 = f32[512]{0:T(512)S(1)} collective-permute-done((f32[512]{0:T(512)S(1)}, f32[512]{0:T(512)S(1)}, u32[]{:S(2)}, u32[]{:S(2)}) %collective-permute-start.29) | collective-permute-done | bytes 2080 | tf_op jit(solution)/shard_map/ppermute | solution.py:40
  386.2 4.6 collective-permute-start.32
  390.8 5.5 fusion.63
  396.3 12.9 %collective-permute-done.32 = f32[512,512]{1,0:T(8,128)S(1)} collective-permute-done((f32[512,512]{1,0:T(8,128)S(1)}, f32[512,512]{1,0:T(8,128)S(1)}, u32[]{:S(2)}, u32[]{:S(2)}) %collective-permute-start.32) | collective-permute-done | bytes 1048608 | tf_op jit(solution)/shard_map/ppermute | solution.py:40
  416.1 12.0 %collective-permute-done.36 = f32[2048]{0:T(1024)S(1)} collective-permute-done((f32[2048]{0:T(1024)S(1)}, f32[2048]{0:T(1024)S(1)}, u32[]{:S(2)}, u32[]{:S(2)}) %collective-permute-start.36) | collective-permute-done | bytes 8224 | tf_op jit(solution)/shard_map/ppermute | solution.py:113
  444.3 7.1 %collective-permute-start.35 = (f32[512,512]{1,0:T(8,128)S(1)}, f32[512,512]{1,0:T(8,128)}, u32[]{:S(2)}, u32[]{:S(2)}) collective-permute-start(f32[512,512]{1,0:T(8,128)S(1)} %get-tuple-element.123), channel_id=1, source_target_pairs={{0,1},{3,2},{4,5},{7,6},{8,9},{11,10},{12,13},{15,14},{16,17},{19,... | collective-permute-start | bytes 3145736 | tf_op jit(solution)/shard_map/ppermute | solution.py:40
  451.4 16.8 %collective-permute-done.41 = f32[512,512]{1,0:T(8,128)S(1)} collective-permute-done((f32[512,512]{1,0:T(8,128)S(1)}, f32[512,512]{1,0:T(8,128)S(1)}, u32[]{:S(2)}, u32[]{:S(2)}) %collective-permute-start.41) | collective-permute-done | bytes 1048608 | tf_op jit(solution)/shard_map/ppermute | solution.py:40
  474.8 4.8 collective-permute-start.42
  483.2 13.3 %collective-permute-done.45 = f32[512,512]{1,0:T(8,128)S(1)} collective-permute-done((f32[512,512]{1,0:T(8,128)}, f32[512,512]{1,0:T(8,128)S(1)}, u32[]{:S(2)}, u32[]{:S(2)}) %collective-permute-start.45) | collective-permute-done | bytes 1048608 | tf_op jit(solution)/shard_map/ppermute | solution.py:40
  509.2 4.5 rows_product.3
  520.9 5.0 collective-permute-start.47
  525.9 9.3 %all-gather.2.ends_ref = f32[8,2,640]{2,1,0:T(2,128)S(1)} all-gather(f32[1,2,640]{2,1,0:T(2,128)S(1)} %maximum_bitcast_fusion), channel_id=3, replica_groups=mesh['seq'=8,'mp'=4] {'seq'}, dimensions={0}, use_global_device_ids=true | all-gather | bytes 46080 | tf_op jit(solution)/shard_map/all_gather | solution.py:697
  536.4 12.3 %recurrence_backward.1 = (bf16[512,640]{1,0:T(8,128)(2,1)S(1)}, f32[16,640]{1,0:T(8,128)S(1)}, f32[8,640]{1,0:T(8,128)S(1)}, f32[656,320]{1,0:T(8,128)S(1)}) custom-call(s32[1]{0:T(128)} %bitcast.mine_ref, f32[8,2,640]{2,1,0:T(2,128)S(1)} %all-gather.2.ends_ref, f32[512,640]{1,0:T(8,128)} %copy-done.13, f32[512,640]{1,0:T(8,128)} %get-tuple-element.138.alpha_ref, ...), custom_call_target="tpu_custom_call" | custom-call | flops 1000 | bytes 1000 | tf_op jit(solution)/shard_map/recurrence_backward/pallas_call | solution.py:468
  550.1 3.8 fusion.65
  564.9 8.2 %columns_product.3 = f32[2048,1280]{1,0:T(8,128)} custom-call(s32[8]{0:T(128)S(1)} %copy-done.18, bf16[512,2048]{1,0:T(8,128)(2,1)S(1)} %copy-done.5, bf16[512,640]{1,0:T(8,128)(2,1)S(1)} %fusion.51.refs_0_, bf16[512,640]{1,0:T(8,128)(2,1)S(1)} %copy-done.17), custom_call_target="tpu_custom_call" | custom-call | flops 1000 | bytes 1000 | tf_op jit(solution)/shard_map/columns_product/pallas_call | solution.py:522
  573.1 3.6 fusion.25
  576.7 8.3 %collective-permute-done.49 = f32[512,512]{1,0:T(8,128)} collective-permute-done((f32[512,512]{1,0:T(8,128)}, f32[512,512]{1,0:T(8,128)}, u32[]{:S(2)}, u32[]{:S(2)}) %collective-permute-start.49) | collective-permute-done | bytes 1048608 | tf_op jit(solution)/shard_map/ppermute | solution.py:40
  594.2 3.8 add_add_fusion
  600.4 5.4 collective-permute-start.51
  609.6 18.4 %collective-permute-done.53 = f32[2560]{0:T(1024)S(1)} collective-permute-done((f32[2560]{0:T(1024)S(1)}, f32[2560]{0:T(1024)S(1)}, u32[]{:S(2)}, u32[]{:S(2)}) %collective-permute-start.53) | collective-permute-done | bytes 10272 | tf_op jit(solution)/shard_map/ppermute | solution.py:40
  649.6 3.7 fusion.53
  654.0 8.1 %collective-permute-done.58 = f32[328,320]{1,0:T(8,128)S(1)} collective-permute-done((f32[328,320]{1,0:T(8,128)S(1)}, f32[328,320]{1,0:T(8,128)S(1)}, u32[]{:S(2)}, u32[]{:S(2)}) %collective-permute-start.58) | collective-permute-done | bytes 419872 | tf_op jit(solution)/shard_map/ppermute | solution.py:113
  (369 shorter events, 210.7 us)
Async XLA Ops:
  7.2 464.1 %reduce-scatter.5.cloned.1.call-start = ((), (), s32[]{:S(2)}) async-start(), calls=%async_computation.4 | async-start | bytes 14155776 | tf_op jit(solution)/shard_map/reduce_scatter | solution.py:509
  9.0 28.2 %collective-permute-start.2 = (f32[512,512]{1,0:T(8,128)}, f32[512,512]{1,0:T(8,128)}, u32[]{:S(2)}, u32[]{:S(2)}) collective-permute-start(f32[512,512]{1,0:T(8,128)} %param.20), channel_id=1, source_target_pairs={{0,1},{1,0},{2,3},{3,2},{4,5},{5,4},{6,7},{7,6},{8,9},{9,8},{10,11... | collective-permute-start | bytes 3145736 | tf_op jit(solution)/shard_map/ppermute | solution.py:40
  14.7 33.9 %collective-permute-start.6 = (f32[8]{0:T(128)S(1)}, f32[8]{0:T(128)S(1)}, u32[]{:S(2)}, u32[]{:S(2)}) collective-permute-start(f32[8]{0:T(128)S(1)} %slice.111), channel_id=1, source_target_pairs={{0,4},{4,8},{8,12},{12,16},{16,20},{20,24},{24,28},{1,5},{5,9},{9,... | collective-permute-start | bytes 104 | tf_op jit(solution)/shard_map/ppermute | solution.py:598
  17.4 32.8 %collective-permute-start = (f32[512]{0:T(512)S(1)}, f32[512]{0:T(512)S(1)}, u32[]{:S(2)}, u32[]{:S(2)}) collective-permute-start(f32[512]{0:T(512)S(1)} %multiply_reduce_fusion.1), channel_id=1, source_target_pairs={{0,1},{1,0},{2,3},{3,2},{4,5},{5,4},{6,7},{7,6},{8,9},{9,8},{10,11... | collective-permute-start | bytes 6152 | tf_op jit(solution)/shard_map/ppermute | solution.py:40
  37.2 26.2 %collective-permute-start.4 = (f32[512,512]{1,0:T(8,128)}, f32[512,512]{1,0:T(8,128)}, u32[]{:S(2)}, u32[]{:S(2)}) collective-permute-start(f32[512,512]{1,0:T(8,128)} %collective-permute-done.3), channel_id=1, source_target_pairs={{1,0},{2,3},{5,4},{6,7},{9,8},{10,11},{13,12},{14,15},{17,16},{18,... | collective-permute-start | bytes 3145736 | tf_op jit(solution)/shard_map/ppermute | solution.py:40
  38.5 24.9 %collective-permute-start.5 = (f32[512,512]{1,0:T(8,128)}, f32[512,512]{1,0:T(8,128)}, u32[]{:S(2)}, u32[]{:S(2)}) collective-permute-start(f32[512,512]{1,0:T(8,128)} %collective-permute-done.2), channel_id=1, source_target_pairs={{1,2},{2,1},{5,6},{6,5},{9,10},{10,9},{13,14},{14,13},{17,18},{18,... | collective-permute-start | bytes 3145736 | tf_op jit(solution)/shard_map/ppermute | solution.py:40
  50.2 17.2 %collective-permute-start.1 = (f32[512]{0:T(512)S(1)}, f32[512]{0:T(512)S(1)}, u32[]{:S(2)}, u32[]{:S(2)}) collective-permute-start(f32[512]{0:T(512)S(1)} %add.273), channel_id=1, source_target_pairs={{0,2},{2,0},{1,3},{3,1},{4,6},{6,4},{5,7},{7,5},{8,10},{10,8},{9,1... | collective-permute-start | bytes 6152 | tf_op jit(solution)/shard_map/ppermute | solution.py:40
  63.4 27.3 %collective-permute-start.7 = (f32[512,512]{1,0:T(8,128)}, f32[512,512]{1,0:T(8,128)}, u32[]{:S(2)}, u32[]{:S(2)}) collective-permute-start(f32[512,512]{1,0:T(8,128)} %collective-permute-done.5), channel_id=1, source_target_pairs={{1,0},{2,3},{5,4},{6,7},{9,8},{10,11},{13,12},{14,15},{17,16},{18,... | collective-permute-start | bytes 3145736 | tf_op jit(solution)/shard_map/ppermute | solution.py:40
  90.7 34.0 %collective-permute-start.10 = (f32[512,512]{1,0:T(8,128)S(1)}, f32[512,512]{1,0:T(8,128)}, u32[]{:S(2)}, u32[]{:S(2)}) collective-permute-start(f32[512,512]{1,0:T(8,128)S(1)} %copy-done.35), channel_id=1, source_target_pairs={{1,2},{2,1},{5,6},{6,5},{9,10},{10,9},{13,14},{14,13},{17,18},{18,... | collective-permute-start | bytes 3145736 | tf_op jit(solution)/shard_map/ppermute | solution.py:40
  92.3 32.4 %collective-permute-start.9 = (f32[512,512]{1,0:T(8,128)S(1)}, f32[512,512]{1,0:T(8,128)}, u32[]{:S(2)}, u32[]{:S(2)}) collective-permute-start(f32[512,512]{1,0:T(8,128)S(1)} %copy-done.35), channel_id=1, source_target_pairs={{0,1},{1,0},{2,3},{3,2},{4,5},{5,4},{6,7},{7,6},{8,9},{9,8},{10,11... | collective-permute-start | bytes 3145736 | tf_op jit(solution)/shard_map/ppermute | solution.py:40
  124.7 15.0 %collective-permute-start.12 = (f32[512,512]{1,0:T(8,128)}, f32[512,512]{1,0:T(8,128)}, u32[]{:S(2)}, u32[]{:S(2)}) collective-permute-start(f32[512,512]{1,0:T(8,128)} %collective-permute-done.9), channel_id=1, source_target_pairs={{1,2},{2,1},{5,6},{6,5},{9,10},{10,9},{13,14},{14,13},{17,18},{18,... | collective-permute-start | bytes 3145736 | tf_op jit(solution)/shard_map/ppermute | solution.py:40
  126.4 27.6 %collective-permute-start.13 = (f32[512,512]{1,0:T(8,128)}, f32[512,512]{1,0:T(8,128)}, u32[]{:S(2)}, u32[]{:S(2)}) collective-permute-start(f32[512,512]{1,0:T(8,128)} %collective-permute-done.10), channel_id=1, source_target_pairs={{1,0},{2,3},{5,4},{6,7},{9,8},{10,11},{13,12},{14,15},{17,16},{18,... | collective-permute-start | bytes 3145736 | tf_op jit(solution)/shard_map/ppermute | solution.py:40
  133.8 28.5 %collective-permute-start.11 = (f32[512,512]{1,0:T(8,128)S(1)}, f32[512,512]{1,0:T(8,128)S(1)}, u32[]{:S(2)}, u32[]{:S(2)}) collective-permute-start(f32[512,512]{1,0:T(8,128)S(1)} %get-tuple-element.190), channel_id=1, source_target_pairs={{0,1},{3,2},{4,5},{7,6},{8,9},{11,10},{12,13},{15,14},{16,17},{19,... | collective-permute-start | bytes 3145736 | tf_op jit(solution)/shard_map/ppermute | solution.py:40
  154.0 38.9 %collective-permute-start.16 = (f32[512,512]{1,0:T(8,128)}, f32[512,512]{1,0:T(8,128)}, u32[]{:S(2)}, u32[]{:S(2)}) collective-permute-start(f32[512,512]{1,0:T(8,128)} %collective-permute-done.12), channel_id=1, source_target_pairs={{1,0},{2,3},{5,4},{6,7},{9,8},{10,11},{13,12},{14,15},{17,16},{18,... | collective-permute-start | bytes 3145736 | tf_op jit(solution)/shard_map/ppermute | solution.py:40
  163.5 26.4 %collective-permute-start.14 = (f32[512,512]{1,0:T(8,128)S(1)}, f32[512,512]{1,0:T(8,128)}, u32[]{:S(2)}, u32[]{:S(2)}) collective-permute-start(f32[512,512]{1,0:T(8,128)S(1)} %get-tuple-element.104), channel_id=1, source_target_pairs={{0,1},{3,2},{4,5},{7,6},{8,9},{11,10},{12,13},{15,14},{16,17},{19,... | collective-permute-start | bytes 3145736 | tf_op jit(solution)/shard_map/ppermute | solution.py:40
  192.9 20.8 %collective-permute-start.17 = (f32[512,512]{1,0:T(8,128)S(1)}, f32[512,512]{1,0:T(8,128)S(1)}, u32[]{:S(2)}, u32[]{:S(2)}) collective-permute-start(f32[512,512]{1,0:T(8,128)S(1)} %add.284), channel_id=1, source_target_pairs={{1,2},{2,1},{5,6},{6,5},{9,10},{10,9},{13,14},{14,13},{17,18},{18,... | collective-permute-start | bytes 3145736 | tf_op jit(solution)/shard_map/ppermute | solution.py:40
  193.6 38.0 %collective-permute-start.18 = (f32[512,512]{1,0:T(8,128)S(1)}, f32[512,512]{1,0:T(8,128)S(1)}, u32[]{:S(2)}, u32[]{:S(2)}) collective-permute-start(f32[512,512]{1,0:T(8,128)S(1)} %dynamic-slice_add_fusion.3), channel_id=1, source_target_pairs={{0,1},{1,0},{2,3},{3,2},{4,5},{5,4},{6,7},{7,6},{8,9},{9,8},{10,11... | collective-permute-start | bytes 3145736 | tf_op jit(solution)/shard_map/ppermute | solution.py:40
  232.8 24.3 %collective-permute-start.21 = (f32[512,512]{1,0:T(8,128)S(1)}, f32[512,512]{1,0:T(8,128)S(1)}, u32[]{:S(2)}, u32[]{:S(2)}) collective-permute-start(f32[512,512]{1,0:T(8,128)S(1)} %get-tuple-element.178), channel_id=1, source_target_pairs={{0,1},{1,0},{2,3},{3,2},{4,5},{5,4},{6,7},{7,6},{8,9},{9,8},{10,11... | collective-permute-start | bytes 3145736 | tf_op jit(solution)/shard_map/ppermute | solution.py:40
  257.1 23.2 %collective-permute-start.23 = (f32[512,512]{1,0:T(8,128)S(1)}, f32[512,512]{1,0:T(8,128)S(1)}, u32[]{:S(2)}, u32[]{:S(2)}) collective-permute-start(f32[512,512]{1,0:T(8,128)S(1)} %collective-permute-done.22), channel_id=1, source_target_pairs={{1,0},{2,3},{5,4},{6,7},{9,8},{10,11},{13,12},{14,15},{17,16},{18,... | collective-permute-start | bytes 3145736 | tf_op jit(solution)/shard_map/ppermute | solution.py:40
  258.4 21.9 %collective-permute-start.24 = (f32[512,512]{1,0:T(8,128)S(1)}, f32[512,512]{1,0:T(8,128)S(1)}, u32[]{:S(2)}, u32[]{:S(2)}) collective-permute-start(f32[512,512]{1,0:T(8,128)S(1)} %collective-permute-done.21), channel_id=1, source_target_pairs={{1,2},{2,1},{5,6},{6,5},{9,10},{10,9},{13,14},{14,13},{17,18},{18,... | collective-permute-start | bytes 3145736 | tf_op jit(solution)/shard_map/ppermute | solution.py:40
  259.1 21.2 %collective-permute-start.19 = (f32[512]{0:T(512)S(1)}, f32[512]{0:T(512)S(1)}, u32[]{:S(2)}, u32[]{:S(2)}) collective-permute-start(f32[512]{0:T(512)S(1)} %get-tuple-element.177), channel_id=1, source_target_pairs={{0,1},{1,0},{2,3},{3,2},{4,5},{5,4},{6,7},{7,6},{8,9},{9,8},{10,11... | collective-permute-start | bytes 6152 | tf_op jit(solution)/shard_map/ppermute | solution.py:40
  280.3 23.2 %collective-permute-start.25 = (f32[512,512]{1,0:T(8,128)S(1)}, f32[512,512]{1,0:T(8,128)S(1)}, u32[]{:S(2)}, u32[]{:S(2)}) collective-permute-start(f32[512,512]{1,0:T(8,128)S(1)} %collective-permute-done.24), channel_id=1, source_target_pairs={{1,0},{2,3},{5,4},{6,7},{9,8},{10,11},{13,12},{14,15},{17,16},{18,... | collective-permute-start | bytes 3145736 | tf_op jit(solution)/shard_map/ppermute | solution.py:40
  322.1 237.2 %reduce-scatter.7.cloned.1.call-start = ((), (), s32[]{:S(2)}) async-start(), calls=%async_computation.5 | async-start | bytes 28311552 | tf_op jit(solution)/shard_map/reduce_scatter | solution.py:509
  339.7 18.0 %collective-permute-start.26 = (f32[512,512]{1,0:T(8,128)}, f32[512,512]{1,0:T(8,128)}, u32[]{:S(2)}, u32[]{:S(2)}) collective-permute-start(f32[512,512]{1,0:T(8,128)} %get-tuple-element.189), channel_id=1, source_target_pairs={{0,1},{3,2},{4,5},{7,6},{8,9},{11,10},{12,13},{15,14},{16,17},{19,... | collective-permute-start | bytes 3145736 | tf_op jit(solution)/shard_map/ppermute | solution.py:40
  357.7 242.6 %reduce-scatter.9.cloned.1.call-start = ((), (), s32[]{:S(2)}) async-start(), calls=%async_computation.6 | async-start | bytes 5898240 | tf_op jit(solution)/shard_map/reduce_scatter | solution.py:509
  360.1 24.7 %collective-permute-start.28 = (f32[512,512]{1,0:T(8,128)S(1)}, f32[512,512]{1,0:T(8,128)S(1)}, u32[]{:S(2)}, u32[]{:S(2)}) collective-permute-start(f32[512,512]{1,0:T(8,128)S(1)} %copy-done.30), channel_id=1, source_target_pairs={{0,1},{3,2},{4,5},{7,6},{8,9},{11,10},{12,13},{15,14},{16,17},{19,... | collective-permute-start | bytes 3145736 | tf_op jit(solution)/shard_map/ppermute | solution.py:40
  364.7 20.4 %collective-permute-start.27 = (f32[512,512]{1,0:T(8,128)S(1)}, f32[512,512]{1,0:T(8,128)S(1)}, u32[]{:S(2)}, u32[]{:S(2)}) collective-permute-start(f32[512,512]{1,0:T(8,128)S(1)} %add.300), channel_id=1, source_target_pairs={{1,2},{2,1},{5,6},{6,5},{9,10},{10,9},{13,14},{14,13},{17,18},{18,... | collective-permute-start | bytes 3145736 | tf_op jit(solution)/shard_map/ppermute | solution.py:40
  386.2 23.1 %collective-permute-start.32 = (f32[512,512]{1,0:T(8,128)S(1)}, f32[512,512]{1,0:T(8,128)S(1)}, u32[]{:S(2)}, u32[]{:S(2)}) collective-permute-start(f32[512,512]{1,0:T(8,128)S(1)} %dynamic-slice_add_fusion.2), channel_id=1, source_target_pairs={{0,1},{1,0},{2,3},{3,2},{4,5},{5,4},{6,7},{7,6},{8,9},{9,8},{10,11... | collective-permute-start | bytes 3145736 | tf_op jit(solution)/shard_map/ppermute | solution.py:40
  412.1 30.2 %collective-permute-start.34 = (f32[512,512]{1,0:T(8,128)S(1)}, f32[512,512]{1,0:T(8,128)S(1)}, u32[]{:S(2)}, u32[]{:S(2)}) collective-permute-start(f32[512,512]{1,0:T(8,128)S(1)} %get-tuple-element.122), channel_id=1, source_target_pairs={{0,1},{1,0},{2,3},{3,2},{4,5},{5,4},{6,7},{7,6},{8,9},{9,8},{10,11... | collective-permute-start | bytes 3145736 | tf_op jit(solution)/shard_map/ppermute | solution.py:40
  414.1 28.1 %collective-permute-start.33 = (f32[512,512]{1,0:T(8,128)S(1)}, f32[512,512]{1,0:T(8,128)S(1)}, u32[]{:S(2)}, u32[]{:S(2)}) collective-permute-start(f32[512,512]{1,0:T(8,128)S(1)} %get-tuple-element.122), channel_id=1, source_target_pairs={{1,2},{2,1},{5,6},{6,5},{9,10},{10,9},{13,14},{14,13},{17,18},{18,... | collective-permute-start | bytes 3145736 | tf_op jit(solution)/shard_map/ppermute | solution.py:40
  414.8 13.3 %collective-permute-start.36 = (f32[2048]{0:T(1024)S(1)}, f32[2048]{0:T(1024)S(1)}, u32[]{:S(2)}, u32[]{:S(2)}) collective-permute-start(f32[2048]{0:T(1024)S(1)} %div.23), channel_id=1, source_target_pairs={{0,1},{1,0},{2,3},{3,2},{4,5},{5,4},{6,7},{7,6},{8,9},{9,8},{10,11... | collective-permute-start | bytes 24584 | tf_op jit(solution)/shard_map/ppermute | solution.py:113
  442.3 25.9 %collective-permute-start.41 = (f32[512,512]{1,0:T(8,128)S(1)}, f32[512,512]{1,0:T(8,128)S(1)}, u32[]{:S(2)}, u32[]{:S(2)}) collective-permute-start(f32[512,512]{1,0:T(8,128)S(1)} %collective-permute-done.33), channel_id=1, source_target_pairs={{1,0},{2,3},{5,4},{6,7},{9,8},{10,11},{13,12},{14,15},{17,16},{18,... | collective-permute-start | bytes 3145736 | tf_op jit(solution)/shard_map/ppermute | solution.py:40
  443.6 24.6 %collective-permute-start.44 = (f32[512,512]{1,0:T(8,128)S(1)}, f32[512,512]{1,0:T(8,128)S(1)}, u32[]{:S(2)}, u32[]{:S(2)}) collective-permute-start(f32[512,512]{1,0:T(8,128)S(1)} %collective-permute-done.34), channel_id=1, source_target_pairs={{1,2},{2,1},{5,6},{6,5},{9,10},{10,9},{13,14},{14,13},{17,18},{18,... | collective-permute-start | bytes 3145736 | tf_op jit(solution)/shard_map/ppermute | solution.py:40
  444.3 27.0 %collective-permute-start.35 = (f32[512,512]{1,0:T(8,128)S(1)}, f32[512,512]{1,0:T(8,128)}, u32[]{:S(2)}, u32[]{:S(2)}) collective-permute-start(f32[512,512]{1,0:T(8,128)S(1)} %get-tuple-element.123), channel_id=1, source_target_pairs={{0,1},{3,2},{4,5},{7,6},{8,9},{11,10},{12,13},{15,14},{16,17},{19,... | collective-permute-start | bytes 3145736 | tf_op jit(solution)/shard_map/ppermute | solution.py:40
  471.4 25.1 %collective-permute-start.45 = (f32[512,512]{1,0:T(8,128)}, f32[512,512]{1,0:T(8,128)S(1)}, u32[]{:S(2)}, u32[]{:S(2)}) collective-permute-start(f32[512,512]{1,0:T(8,128)} %copy-done.48), channel_id=1, source_target_pairs={{1,0},{2,3},{5,4},{6,7},{9,8},{10,11},{13,12},{14,15},{17,16},{18,... | collective-permute-start | bytes 3145736 | tf_op jit(solution)/shard_map/ppermute | solution.py:40
  474.8 24.6 %collective-permute-start.42 = (f32[512,512]{1,0:T(8,128)S(1)}, f32[512,512]{1,0:T(8,128)S(1)}, u32[]{:S(2)}, u32[]{:S(2)}) collective-permute-start(f32[512,512]{1,0:T(8,128)S(1)} %copy-done.28), channel_id=1, source_target_pairs={{0,1},{3,2},{4,5},{7,6},{8,9},{11,10},{12,13},{15,14},{16,17},{19,... | collective-permute-start | bytes 3145736 | tf_op jit(solution)/shard_map/ppermute | solution.py:40
  479.7 20.8 %collective-permute-start.43 = (f32[512,512]{1,0:T(8,128)S(1)}, f32[512,512]{1,0:T(8,128)}, u32[]{:S(2)}, u32[]{:S(2)}) collective-permute-start(f32[512,512]{1,0:T(8,128)S(1)} %add.308), channel_id=1, source_target_pairs={{1,2},{2,1},{5,6},{6,5},{9,10},{10,9},{13,14},{14,13},{17,18},{18,... | collective-permute-start | bytes 3145736 | tf_op jit(solution)/shard_map/ppermute | solution.py:40
  513.7 160.0 %reduce-scatter.11.cloned.1.call-start = ((), (), s32[]{:S(2)}) async-start(), calls=%async_computation.7 | async-start | bytes 11796480 | tf_op jit(solution)/shard_map/reduce_scatter | solution.py:509
  519.2 34.6 %collective-permute-start.46 = (f32[512,512]{1,0:T(8,128)}, f32[512,512]{1,0:T(8,128)}, u32[]{:S(2)}, u32[]{:S(2)}) collective-permute-start(f32[512,512]{1,0:T(8,128)} %add.314), channel_id=1, source_target_pairs={{1,2},{2,1},{5,6},{6,5},{9,10},{10,9},{13,14},{14,13},{17,18},{18,... | collective-permute-start | bytes 3145736 | tf_op jit(solution)/shard_map/ppermute | solution.py:40
  520.9 33.0 %collective-permute-start.47 = (f32[512,512]{1,0:T(8,128)}, f32[512,512]{1,0:T(8,128)}, u32[]{:S(2)}, u32[]{:S(2)}) collective-permute-start(f32[512,512]{1,0:T(8,128)} %dynamic-slice_add_fusion.1), channel_id=1, source_target_pairs={{0,1},{1,0},{2,3},{3,2},{4,5},{5,4},{6,7},{7,6},{8,9},{9,8},{10,11... | collective-permute-start | bytes 3145736 | tf_op jit(solution)/shard_map/ppermute | solution.py:40
  559.3 25.7 %collective-permute-start.49 = (f32[512,512]{1,0:T(8,128)}, f32[512,512]{1,0:T(8,128)}, u32[]{:S(2)}, u32[]{:S(2)}) collective-permute-start(f32[512,512]{1,0:T(8,128)} %get-tuple-element.151), channel_id=1, source_target_pairs={{0,1},{3,2},{4,5},{7,6},{8,9},{11,10},{12,13},{15,14},{16,17},{19,... | collective-permute-start | bytes 3145736 | tf_op jit(solution)/shard_map/ppermute | solution.py:40
  600.4 33.5 %collective-permute-start.51 = (f32[512,512]{1,0:T(8,128)}, f32[512,512]{1,0:T(8,128)}, u32[]{:S(2)}, u32[]{:S(2)}) collective-permute-start(f32[512,512]{1,0:T(8,128)} %get-tuple-element.155), channel_id=1, source_target_pairs={{0,1},{3,2},{4,5},{7,6},{8,9},{11,10},{12,13},{15,14},{16,17},{19,... | collective-permute-start | bytes 3145736 | tf_op jit(solution)/shard_map/ppermute | solution.py:40
  605.7 31.0 %collective-permute-start.52 = (f32[512,512]{1,0:T(8,128)}, f32[512,512]{1,0:T(8,128)}, u32[]{:S(2)}, u32[]{:S(2)}) collective-permute-start(f32[512,512]{1,0:T(8,128)} %add.323), channel_id=1, source_target_pairs={{1,2},{2,1},{5,6},{6,5},{9,10},{10,9},{13,14},{14,13},{17,18},{18,... | collective-permute-start | bytes 3145736 | tf_op jit(solution)/shard_map/ppermute | solution.py:40
  607.4 25.2 %collective-permute-start.55 = (f32[328,320]{1,0:T(8,128)S(1)}, f32[328,320]{1,0:T(8,128)}, u32[]{:S(2)}, u32[]{:S(2)}) collective-permute-start(f32[328,320]{1,0:T(8,128)S(1)} %dynamic-slice_add_fusion.4), channel_id=1, source_target_pairs={{0,8},{4,12},{8,0},{12,4},{16,24},{20,28},{24,16},{28,20},{1,9},{5... | collective-permute-start | bytes 1259528 | tf_op jit(solution)/shard_map/ppermute | solution.py:113
  609.5 18.4 %collective-permute-start.53 = (f32[2560]{0:T(1024)S(1)}, f32[2560]{0:T(1024)S(1)}, u32[]{:S(2)}, u32[]{:S(2)}) collective-permute-start(f32[2560]{0:T(1024)S(1)} %constant_dynamic-update-slice_fusion.3), channel_id=1, source_target_pairs={{0,1},{1,0},{2,3},{3,2},{4,5},{5,4},{6,7},{7,6},{8,9},{9,8},{10,11... | collective-permute-start | bytes 30728 | tf_op jit(solution)/shard_map/ppermute | solution.py:40
  639.4 24.4 %collective-permute-start.57 = (f32[512,512]{1,0:T(8,128)}, f32[512,512]{1,0:T(8,128)}, u32[]{:S(2)}, u32[]{:S(2)}) collective-permute-start(f32[512,512]{1,0:T(8,128)} %dynamic-slice_add_fusion), channel_id=1, source_target_pairs={{0,1},{1,0},{2,3},{3,2},{4,5},{5,4},{6,7},{7,6},{8,9},{9,8},{10,11... | collective-permute-start | bytes 3145736 | tf_op jit(solution)/shard_map/ppermute | solution.py:40
  641.9 21.9 %collective-permute-start.56 = (f32[512,512]{1,0:T(8,128)}, f32[512,512]{1,0:T(8,128)}, u32[]{:S(2)}, u32[]{:S(2)}) collective-permute-start(f32[512,512]{1,0:T(8,128)} %add.326), channel_id=1, source_target_pairs={{1,2},{2,1},{5,6},{6,5},{9,10},{10,9},{13,14},{14,13},{17,18},{18,... | collective-permute-start | bytes 3145736 | tf_op jit(solution)/shard_map/ppermute | solution.py:40
  649.1 12.9 %collective-permute-start.58 = (f32[328,320]{1,0:T(8,128)S(1)}, f32[328,320]{1,0:T(8,128)S(1)}, u32[]{:S(2)}, u32[]{:S(2)}) collective-permute-start(f32[328,320]{1,0:T(8,128)S(1)} %add.330), channel_id=1, source_target_pairs={{0,16},{4,20},{8,24},{12,28},{16,0},{20,4},{24,8},{28,12},{1,17},{... | collective-permute-start | bytes 1259528 | tf_op jit(solution)/shard_map/ppermute | solution.py:113
  (91 other events, 1407.6 us)
Sparse Core Ops, SparseCore 0:
  322.2 67.3 reduce-scatter.4
  392.0 128.1 reduce-scatter.6
  523.1 35.7 reduce-scatter.8
  585.1 63.6 reduce-scatter.10

commit v4 on v3

--- a/solution.py
+++ b/solution.py
@@ -14,7 +14,7 @@
 LANES = 128
 SUB = 8
 ROWS = 32
-VMEM_LIMIT = 50 * 1024 * 1024
+VMEM_LIMIT = 56 * 1024 * 1024
 
 
 def matmul(left, right):
@@ -74,33 +74,34 @@
 
 
 class LineScatter:
-    def __init__(self, whole, width):
-        self.whole, self.width = whole, width
-        self.mine, self.beside, self.near, self.far = line_places()
-
-    def piece(self, place):
-        return lax.dynamic_slice_in_dim(self.whole, place * self.width, self.width, 1)
+    def __init__(self, blocks):
+        self.far, self.near, self.beside, self.own = blocks
 
     def first(self, *needed):
-        self.far_one = over_mp(after(self.piece(self.far), *needed), INWARD)
+        self.far_one = over_mp(after(self.far, *needed), INWARD)
         return self.far_one
 
     def second(self, *needed):
-        far, near = after(
-            (self.piece(self.far) + self.far_one, self.piece(self.near)), *needed
-        )
+        far, near = after((self.far + self.far_one, self.near), *needed)
         self.far_two, self.near_one = over_mp(far, MIDDLE), over_mp(near, INWARD)
         return self.far_two, self.near_one
 
+    def prepare(self):
+        self.parts = (self.near + self.near_one, self.beside + self.far_two)
+        return self.parts
+
     def third(self, *needed):
-        near, last = after(
-            (self.piece(self.near) + self.near_one, self.piece(self.beside) + self.far_two), *needed
-        )
+        near, last = after(self.prepare(), *needed)
         self.near_two, self.last = over_mp(near, MIDDLE), over_mp(last, PAIRS)
         return self.near_two, self.last
 
     def result(self):
-        return self.piece(self.mine) + self.near_two + self.last
+        return self.own + self.near_two + self.last
+
+
+def block_order():
+    mine, beside, near, far = line_places()
+    return jnp.stack([far, near, beside, mine]).astype(jnp.int32)
 
 
 def line_sum(value):
@@ -241,7 +242,8 @@
 
 
 def state_kernel(
-    mine_ref, ends_ref, part_ref, span_ref, gate_ref, states_ref, mixed_ref, enter_ref
+    mine_ref, order_ref, ends_ref, part_ref, span_ref, gate_ref, weight_ref,
+    states_ref, mixed_ref, enter_ref, *block_refs,
 ):
     devices = ends_ref.shape[0]
     width = part_ref.shape[1]
@@ -251,15 +253,22 @@
         entering = jnp.where(d < mine_ref[0], ends[0:1, :] * entering + ends[1:2, :], entering)
     states = span_ref[...] * entering + part_ref[...]
     states_ref[...] = states
-    mixed_ref[...] = (gelu_parts(gate_ref[...])[0] * states).astype(bf16)
+    mixed = (gelu_parts(gate_ref[...])[0] * states).astype(bf16)
+    mixed_ref[...] = mixed
     enter_ref[...] = jnp.broadcast_to(entering, enter_ref.shape)
+    for k, block_ref in enumerate(block_refs):
+        block = block_ref.shape[1]
+        columns = pl.ds(pl.multiple_of(order_ref[k] * block, block), block)
+        block_ref[...] = jnp.dot(mixed, weight_ref[:, columns], preferred_element_type=f32)
 
 
 def turn_kernel(
-    dmixed_ref, gate_ref, states_ref, span_ref, dstates_ref, dgate_ref, out_ref
+    branch_ref, weight_ref, gate_ref, states_ref, span_ref, dstates_ref, dgate_ref, out_ref
 ):
     act, slope = gelu_parts(gate_ref[...])
-    dmixed = dmixed_ref[...]
+    dmixed = lax.dot_general(
+        branch_ref[...], weight_ref[...], (((1,), (1,)), ((), ())), preferred_element_type=f32
+    )
     dstates = dmixed * act
     dstates_ref[...] = dstates
     dgate_ref[...] = (dmixed * states_ref[...] * slope).astype(bf16)
@@ -270,6 +279,71 @@
 
     out_ref[...] += jnp.sum(
         (dstates * span_ref[...]).reshape(-1, SUB, dstates.shape[1]), axis=0
+    )
+
+
+def feed_forward_kernel(
+    order_ref, low_ref, gate_ref, up_ref, dhidden_ref, hidden_ref, dgate_ref, dup_ref, *block_refs
+):
+    step = pl.program_id(0)
+    low = low_ref[...]
+    gate = jnp.dot(low, gate_ref[...], preferred_element_type=f32)
+    up = jnp.dot(low, up_ref[...], preferred_element_type=f32)
+    act, slope = gelu_parts(gate)
+    dhidden = dhidden_ref[...]
+    hidden_ref[...] = (act * up).astype(bf16)
+    dgate_ref[...] = (dhidden * up * slope).astype(bf16)
+    dup_ref[...] = (dhidden * act).astype(bf16)
+    contract = (((1,), (1,)), ((), ()))
+    for k, block_ref in enumerate(block_refs):
+        block = block_ref.shape[1]
+        rows = pl.ds(pl.multiple_of(order_ref[k] * block, block), block)
+        part = lax.dot_general(
+            dgate_ref[...], gate_ref[rows, :], contract, preferred_element_type=f32
+        ) + lax.dot_general(dup_ref[...], up_ref[rows, :], contract, preferred_element_type=f32)
+
+        @pl.when(step == 0)
+        def _():
+            block_ref[...] = part
+
+        @pl.when(step > 0)
+        def _():
+            block_ref[...] += part
+
+
+def blocks_kernel(order_ref, *refs, pairs, transposed):
+    for k, block_ref in enumerate(refs[2 * pairs :]):
+        block = block_ref.shape[1]
+        here = pl.ds(pl.multiple_of(order_ref[k] * block, block), block)
+        total = None
+        for left_ref, right_ref in zip(refs[:pairs], refs[pairs : 2 * pairs]):
+            if transposed:
+                part = lax.dot_general(
+                    left_ref[...], right_ref[here, :], (((1,), (1,)), ((), ())),
+                    preferred_element_type=f32,
+                )
+            else:
+                part = jnp.dot(left_ref[...], right_ref[:, here], preferred_element_type=f32)
+            total = part if total is None else total + part
+        block_ref[...] = total
+
+
+def sums_kernel(order_ref, low_ref, *refs):
+    row_ref, column_ref = refs[-2:]
+    rows = 0.0
+    for k, block_ref in enumerate(refs[:-2]):
+        block = block_ref.shape[1]
+        here = pl.ds(pl.multiple_of(order_ref[k] * block, block), block)
+        product = block_ref[...] * low_ref[:, here].astype(f32)
+        rows = rows + jnp.sum(product, axis=1, keepdims=True)
+        column_ref[:, here] = jnp.sum(product, axis=0, keepdims=True)
+    row_ref[...] = rows
+
+
+def product_kernel(left_ref, right_ref, out_ref, *, transposed):
+    contract = (((1,), (1,)), ((), ())) if transposed else (((1,), (0,)), ((), ()))
+    out_ref[...] = lax.dot_general(
+        left_ref[...], right_ref[...], contract, preferred_element_type=f32
     )
 
 
@@ -386,11 +460,14 @@
         here = slice(b * block, (b + 1) * block)
         recur = turned(whole_ref[here, :width], -b * block)
         entry = turned(whole_ref[here, width:], block - b * block)
-        small_ref[here, :] = jnp.where(left, recur, entry)[:, : 2 * block]
-    for b in range(groups // 2):
-        small_ref[width + b * SUB : width + (b + 1) * SUB, :] = turned(
-            sums, -2 * b * block
-        )[:, : 2 * block]
+        small_ref[2 * b // groups, b % (groups // 2) * block : (b % (groups // 2) + 1) * block, :] = (
+            jnp.where(left, recur, entry)[:, : 2 * block]
+        )
+    for h in range(2):
+        for b in range(groups // 4):
+            small_ref[h, width // 2 + b * SUB : width // 2 + (b + 1) * SUB, :] = turned(
+                sums, -2 * (h * (groups // 4) + b) * block
+            )[:, : 2 * block]
 
 
 def vmem(count=1):
@@ -423,30 +500,36 @@
     )(inner, halo, valid, rows, gates)
 
 
-def run_states(mine, ends, part, span, gate_pre):
+def run_states(mine, order, ends, part, span, gate_pre, weight):
     count, width = part.shape
+    features = weight.shape[1]
     block = count // 4
-    tile = pl.BlockSpec((block, width), lambda i: (i, 0))
+    tile = pl.BlockSpec((block, width), lambda i, m, o: (i, 0))
+    out = pl.BlockSpec((block, features // 4), lambda i, m, o: (i, 0))
     return pl.pallas_call(
         state_kernel,
-        grid=(4,),
+        grid_spec=pltpu.PrefetchScalarGridSpec(
+            num_scalar_prefetch=2,
+            grid=(4,),
+            in_specs=[
+                pl.BlockSpec(ends.shape, lambda i, m, o: (0, 0, 0)),
+                tile, tile, tile,
+                pl.BlockSpec(weight.shape, lambda i, m, o: (0, 0)),
+            ],
+            out_specs=(tile, tile, pl.BlockSpec((SUB, width), lambda i, m, o: (0, 0))) + (out,) * 4,
+        ),
         out_shape=(
             shape((count, width)), shape((count, width), bf16), shape((SUB, width)),
-        ),
-        in_specs=[
-            pl.BlockSpec(memory_space=pltpu.SMEM),
-            pl.BlockSpec(ends.shape, lambda i: (0, 0, 0)),
-            tile, tile, tile,
-        ],
-        out_specs=(tile, tile, pl.BlockSpec((SUB, width), lambda i: (0, 0))),
+        ) + (shape((count, features // 4)),) * 4,
         compiler_params=pltpu.CompilerParams(vmem_limit_bytes=VMEM_LIMIT),
         cost_estimate=small_cost(),
         name="recurrence_states",
-    )(mine, ends, part, span, gate_pre)
-
-
-def run_turn(dmixed, gate_pre, states, span):
-    count, width = dmixed.shape
+    )(mine, order, ends, part, span, gate_pre, weight)
+
+
+def run_turn(branch, weight, gate_pre, states, span):
+    count, width = states.shape
+    features = branch.shape[1]
     block = count // 4
     tile = pl.BlockSpec((block, width), lambda i: (i, 0))
     return pl.pallas_call(
@@ -455,12 +538,87 @@
         out_shape=(
             shape((count, width)), shape((count, width), bf16), shape((SUB, width)),
         ),
-        in_specs=[tile] * 4,
+        in_specs=[
+            pl.BlockSpec((block, features), lambda i: (i, 0)),
+            pl.BlockSpec(weight.shape, lambda i: (0, 0)),
+        ] + [tile] * 3,
         out_specs=(tile, tile, pl.BlockSpec((SUB, width), lambda i: (0, 0))),
         compiler_params=pltpu.CompilerParams(vmem_limit_bytes=VMEM_LIMIT),
         cost_estimate=small_cost(),
         name="recurrence_turn",
-    )(dmixed, gate_pre, states, span)
+    )(branch, weight, gate_pre, states, span)
+
+
+def feed_forward(order, low, gate, up, dhidden):
+    count, features = low.shape
+    hidden = gate.shape[1]
+    block = 512
+    tile = pl.BlockSpec((count, block), lambda i, o: (0, i))
+    weight = pl.BlockSpec((features, block), lambda i, o: (0, i))
+    out = pl.BlockSpec((count, features // 4), lambda i, o: (0, 0))
+    return pl.pallas_call(
+        feed_forward_kernel,
+        grid_spec=pltpu.PrefetchScalarGridSpec(
+            num_scalar_prefetch=1,
+            grid=(hidden // block,),
+            in_specs=[
+                pl.BlockSpec((count, features), lambda i, o: (0, 0)), weight, weight, tile,
+            ],
+            out_specs=(tile,) * 3 + (out,) * 4,
+        ),
+        out_shape=(shape((count, hidden), bf16),) * 3 + (shape((count, features // 4)),) * 4,
+        compiler_params=pltpu.CompilerParams(vmem_limit_bytes=VMEM_LIMIT),
+        cost_estimate=small_cost(),
+        name="feed_forward",
+    )(order, low, gate, up, dhidden)
+
+
+def product_blocks(order, lefts, rights, transposed):
+    count = lefts[0].shape[0]
+    features = rights[0].shape[0 if transposed else 1]
+    return pl.pallas_call(
+        partial(blocks_kernel, pairs=len(lefts), transposed=transposed),
+        out_shape=(shape((count, features // 4)),) * 4,
+        in_specs=[pl.BlockSpec(memory_space=pltpu.SMEM)] + vmem(2 * len(lefts)),
+        out_specs=tuple(vmem(4)),
+        compiler_params=pltpu.CompilerParams(vmem_limit_bytes=VMEM_LIMIT),
+        cost_estimate=small_cost(),
+        name="product_blocks",
+    )(order, *lefts, *rights)
+
+
+def product_sums(order, low, blocks):
+    count, features = low.shape
+    row, column = pl.pallas_call(
+        sums_kernel,
+        out_shape=(shape((count, 1)), shape((1, features))),
+        in_specs=[pl.BlockSpec(memory_space=pltpu.SMEM)] + vmem(5),
+        out_specs=tuple(vmem(2)),
+        compiler_params=pltpu.CompilerParams(vmem_limit_bytes=VMEM_LIMIT),
+        cost_estimate=small_cost(),
+        name="product_sums",
+    )(order, low, *blocks)
+    return row[:, 0], column[0]
+
+
+def product(left, right, block, transposed=False):
+    count, inner = left.shape
+    width = right.shape[0 if transposed else 1]
+    right_tile = (
+        pl.BlockSpec((block, inner), lambda i: (i, 0))
+        if transposed
+        else pl.BlockSpec((inner, block), lambda i: (0, i))
+    )
+    return pl.pallas_call(
+        partial(product_kernel, transposed=transposed),
+        grid=(width // block,),
+        in_specs=[pl.BlockSpec(left.shape, lambda i: (0, 0)), right_tile],
+        out_specs=pl.BlockSpec((count, block), lambda i: (0, i)),
+        out_shape=shape((count, width)),
+        compiler_params=pltpu.CompilerParams(vmem_limit_bytes=VMEM_LIMIT),
+        cost_estimate=small_cost(),
+        name="product",
+    )(left, right)
 
 
 def run_backward(mine, ends, dstates, saved, enter, valid, inner, halo, rows, gates, groups):
@@ -469,7 +627,7 @@
         partial(backward_kernel, groups=groups),
         out_shape=(
             shape((count, width), bf16), shape((2 * SUB, width)), shape((SUB, width)),
-            shape((width + SUB * groups // 2, 2 * width // groups)),
+            shape((2, width // 2 + SUB * groups // 4, 2 * width // groups)),
         ),
         in_specs=[pl.BlockSpec(memory_space=pltpu.SMEM)] + vmem(14),
         out_specs=tuple(vmem(4)),
@@ -587,6 +745,7 @@
     column = lax.axis_index("mp") * own_width
     own_first = lax.dynamic_slice_in_dim(gain_first, column, own_width)
     own_second = lax.dynamic_slice_in_dim(gain_second, column, own_width)
+    order = block_order()
     onward = [(s, s + 1) for s in range(devices - 1)]
     backward = [(s + 1, s) for s in range(devices - 1)]
 
@@ -630,16 +789,17 @@
     )
     ends = after(lax.all_gather(last, "seq"), cot.beside, cot.near_in)
     cot.second()
-    states, mixed_low, enter = run_states(seq_at, ends, part, span, gate_pre)
-
-    branch = LineScatter(matmul(mixed_low, proj_out), own_width)
+    states, mixed_low, enter, *blocks = run_states(
+        seq_at, order, ends, part, span, gate_pre, proj_out
+    )
+
+    branch = LineScatter(blocks)
     branch.first()
     branch.second(cot.far_in, cot.near_out)
     cot.third()
-    ffn_weight = jnp.concatenate(after((mlp_gate, mlp_up), branch.far_one), 1)
-    branch.third(cot.far_out, ffn_weight)
+    branch.third(cot.far_out)
     cot_low = assemble(cot.pieces(), features, lambda piece, start: piece)
-    d_hidden = matmul_nt(cot_low, mlp_down)
+    d_hidden = product(cot_low, mlp_down, 2 * LANES, True)
     own_resid = stream + branch.result()
 
     second = LineGather(own_resid)
@@ -652,27 +812,26 @@
         return piece * second_scale * lax.dynamic_slice_in_dim(gain_second, start, own_width)
 
     second_low = assemble(second.pieces(), features, second_turn)
-    ffn = matmul(second_low, ffn_weight)
-    act, slope = gelu_parts(ffn[:, :ffn_width])
-    ffn_up = ffn[:, ffn_width:]
-    hidden_low = (act * ffn_up).astype(bf16)
-    d_pair_low = jnp.concatenate([d_hidden * ffn_up * slope, d_hidden * act], 1).astype(bf16)
+    hidden_low, d_gate_ffn, d_up_ffn, *d_second_blocks = feed_forward(
+        order, second_low, mlp_gate, mlp_up, d_hidden
+    )
+    turned = LineScatter(d_second_blocks)
     whole_down = rows_product(hidden_low, cot_low, own_width)
     grad_down = ring_scatter(whole_down)
-    d_pair_low = after(d_pair_low, whole_down)
-    d_second_part = matmul_nt(d_pair_low, ffn_weight)
-
-    turned = LineScatter(d_second_part, own_width)
-    turned.first()
-    whole_pair = columns_product(after(second_low, d_second_part), [d_pair_low])
+    turned.first(whole_down)
+    whole_pair = columns_product(after(second_low, turned.own), [d_gate_ffn, d_up_ffn])
     turned.second(whole_pair)
     whole_pair = after(whole_pair, turned.far_one)
     grad_pair = ring_scatter(whole_pair)
-    second_product = after(d_second_part, turned.far_one) * second_low.astype(f32)
-    second_mean = line_sum(jnp.sum(second_product, axis=1)) / features
-    d_gain_second = jnp.sum(second_product, axis=0) / gain_second
+    second_sums, gain_sums = product_sums(
+        order, second_low, after(d_second_blocks, turned.far_one)
+    )
+    second_mean = line_sum(second_sums) / features
+    d_gain_second = gain_sums / gain_second
     turned.third(d_gain_second, second_mean)
-    mlp_part = matmul(after(hidden_low, turned.far_two, turned.near_one), mlp_down)
+    mlp_blocks = product_blocks(
+        order, [after(hidden_low, turned.far_two, turned.near_one)], [mlp_down], False
+    )
     own_d_second = turned.result()
     own_d_resid = (
         cotangent
@@ -680,60 +839,65 @@
         - own_resid * (second_scale * second_scale * second_mean[:, None])
     )
     gathered = LineGather(own_d_resid)
-    gathered.first(mlp_part)
-    d_gain_second = sum_over(sum_over(after(d_gain_second, own_d_resid), "mp"), "seq")
-    gathered.second(d_gain_second)
-    sent = LineScatter(mlp_part, own_width)
+    gathered.first(mlp_blocks)
+    gathered.second()
+    sent = LineScatter(mlp_blocks)
     sent.first(gathered.near_in, gathered.beside)
     gathered.third(sent.far_one, grad_down)
     sent.second(gathered.near_out)
     branch_low = assemble(gathered.pieces(), features, lambda piece, start: piece)
 
-    d_mixed = matmul_nt(after(branch_low, sent.far_two, sent.near_one), proj_out)
-    d_states, d_gate_low, outgoing = run_turn(d_mixed, gate_pre, states, span)
-    whole_out = rows_product(after(mixed_low, d_states), branch_low, 2 * own_width)
-    grad_out = ring_scatter(whole_out)
-    leaving = jnp.stack([last[0], jnp.sum(after(outgoing, whole_out), axis=0)], 0)
-    back_ends = lax.all_gather(leaving, "seq")
-    sent.third(outgoing)
+    d_states, d_gate_low, outgoing = run_turn(
+        after(branch_low, sent.far_two, sent.near_one), proj_out, gate_pre, states, span
+    )
+    leaving = jnp.stack([last[0], jnp.sum(outgoing, axis=0)], 0)
+    leaving = after(leaving, sent.prepare())
+    sent.third()
+    back_ends = after(lax.all_gather(leaving, "seq"), sent.last, sent.near_two)
     saved = dict(alpha=alpha, states=states, conv=conv, rg=rg, ig=ig, factor=factor)
     d_inner_low, tail, head, small = run_backward(
         seq_at, back_ends, d_states, saved, enter, valid, inner, halo, rows, gates, groups
     )
     returned = lax.ppermute(head, "seq", backward)
-    d_first_gate = matmul_nt(after(d_gate_low, head), proj_gate)
-    returned = after(returned, d_first_gate, sent.last, sent.near_two)
+    whole_out = rows_product(after(mixed_low, head), branch_low, 2 * own_width)
+    grad_out = ring_scatter(whole_out)
+    returned = after(returned, whole_out)
     tail = tail + jnp.concatenate([jnp.zeros_like(returned), returned], 0)
     d_inner_low = lax.dynamic_update_slice(d_inner_low, tail.astype(bf16), (count - 2 * SUB, 0))
-    d_first_part = matmul_nt(d_inner_low, proj_inner) + d_first_gate
-
-    final = LineScatter(d_first_part, own_width)
+    d_first_blocks = product_blocks(
+        order, [d_inner_low, d_gate_low], [proj_inner, proj_gate], True
+    )
+
+    final = LineScatter(d_first_blocks)
     final.first(grad_pair)
     whole_first = columns_product(
-        after(first_low, d_first_part), [d_inner_low, d_gate_low]
-    )
-    first_product = after(d_first_part, whole_first) * first_low.astype(f32)
-    first_mean = jnp.sum(first_product, axis=1)
-    d_gain_first = jnp.sum(first_product, axis=0) / gain_first
-    output = own_resid + sent.result()
-    small = small + swapped(small, "seq", 1)
-    half = small.shape[0] // 2
-    small = lax.dynamic_slice_in_dim(small, (lax.axis_index("seq") & 1) * half, half, 0)
-    final.second(whole_first, first_mean, d_gain_first, output, small, grad_out)
+        after(first_low, final.own), [d_inner_low, d_gate_low]
+    )
+    first_mean, gain_sums = product_sums(
+        order, after(first_low, whole_first), d_first_blocks
+    )
+    d_gain_first = gain_sums / gain_first
+    output = after(own_resid, final.own) + sent.result()
+    core = lax.axis_index("seq") & 1
+    other = swapped(lax.dynamic_index_in_dim(small, 1 - core, 0, False), "seq", 1)
+    small = lax.dynamic_index_in_dim(small, core, 0, False) + other
+    final.second(whole_first, first_mean, d_gain_first, grad_out, output, small)
     whole_first, first_mean, d_gain_first = after(
         (whole_first, first_mean, d_gain_first), final.far_one
     )
     grad_first = ring_scatter(whole_first)
-    first_sums = line_sum(jnp.concatenate([first_mean, d_gain_first]))
-    first_mean, d_gain_first = first_sums[:count] / features, first_sums[count:]
-    small = over_chips(after(small, final.far_one), 2)
-    final.third(first_mean, d_gain_first, small)
+    small = over_chips(small, 2)
+    first_sums = jnp.concatenate([first_mean, d_gain_first, d_gain_second])
+    first_sums = first_sums + over_mp(first_sums, PAIRS)
+    final.third(first_sums, small)
+    first_sums, small = after((first_sums, small), final.far_two, final.near_one)
+    first_sums = first_sums + over_mp(first_sums, CROSS)
+    first_mean = first_sums[:count] / features
     small = over_chips(small, 4)
-    d_gain_first = sum_over(d_gain_first, "seq")
-    small, d_gain_first = after((small, d_gain_first), final.last)
+    gains = sum_over(first_sums[count:], "seq")
+    small, gains = after((small, gains), final.last)
     other = swapped(small, "seq", 1)
-    lower = lax.axis_index("seq") & 1 == 0
-    small = jnp.concatenate([jnp.where(lower, small, other), jnp.where(lower, other, small)], 0)
+    small = [jnp.where(core == 0, small, other), jnp.where(core == 0, other, small)]
     own_d_first = final.result()
     grad_stream = (
         own_d_resid
@@ -741,19 +905,22 @@
         - stream * (first_scale * first_scale * first_mean[:, None])
     )
     block_width = inner_width // groups
-    sums = small[inner_width:].reshape(groups // 2, SUB, 2 * block_width)
-    sums = sums.transpose(1, 0, 2).reshape(SUB, inner_width)
+    half = inner_width // 2
+    sums = [
+        part[half + b * SUB : half + (b + 1) * SUB] for part in small for b in range(groups // 4)
+    ]
+    sums = jnp.concatenate(sums, 1)
     grad_gates = [
-        small[:inner_width, g * block_width : (g + 1) * block_width].reshape(
-            groups, block_width, block_width
-        )
+        jnp.concatenate(
+            [part[:half, g * block_width : (g + 1) * block_width] for part in small], 0
+        ).reshape(groups, block_width, block_width)
         for g in range(2)
     ]
     grad_decay = sums[7] * (recur_scale * jax.nn.sigmoid(-decay_param))
     return (
         output,
         grad_stream,
-        d_gain_first,
+        gains[:features],
         grad_first[:, :inner_width],
         grad_first[:, inner_width:],
         sums[:4],
@@ -764,7 +931,7 @@
         sums[6],
         grad_decay,
         grad_out,
-        d_gain_second,
+        gains[features:],
         grad_pair[:, :ffn_width],
         grad_pair[:, ffn_width:],
         grad_down,

time: 691 us -> 657 us (0.951)
  Pallas kernels: 63.4 us -> 136 us
  matrix products: 45.5 us -> 4.66 us
  starting transfers between devices: 157 us -> 119 us
  local copies, waits for them, and re-layouts: 46.8 us -> 23 us
  other arithmetic: 75 us -> 57.2 us
  waiting for transfers between devices: 259 us -> 269 us
    pallas_call x1 -> x7, Pallas kernels: 2.8 us -> 63.7 us  [the longest x1 23.5 us: feed_forward(): pl.pallas_call(feed_forward_kernel, grid_spec=pltpu.PrefetchScalarGridSpe...]
    ppermute x48, starting transfers between devices: 139 us -> 108 us  [over_mp(): return lax.ppermute(value, 'mp', list(pairs))]
    dot_general x5 -> x0, matrix products: 26.8 us -> none  [matmul_nt(): lax.dot_general(left, right, (((1,), (1,)), ((), ())), preferred_element_...]
    dot_general x5 -> x2, matrix products: 18.7 us -> 4.66 us  [matmul(): return jnp.dot(left, right, preferred_element_type=f32)]
    ppermute x48, waiting for transfers between devices: 228 us -> 241 us  [over_mp(): return lax.ppermute(value, 'mp', list(pairs))]
    unnamed x147 -> x102, local copies, waits for them, and re-layouts: 20.6 us -> 10.7 us
    ppermute x12 -> x7, waiting for transfers between devices: 31.4 us -> 26.1 us  [swapped(): return lax.ppermute(value, axis, [(d, d ^ bit) for d in range(count)])]
    add x15 -> x16, other arithmetic: 26.7 us -> 22.6 us  [the longest x8 11 us: prepare(): self.parts = (self.near + self.near_one, self.beside + self.far_two)]
  transfers between devices with their start and end apart: 67 -> 62, of which waited for: 32 -> 30; matrix products, arithmetic and copies ran while one was open for 20% -> 11% of each run, Pallas kernels for 8% -> 15%
where the time goes in v4:
time: 657 us; the launch traced here: 646 us
  waiting for transfers between devices  269 us (41%)
  Pallas kernels  136 us (21%)
  starting transfers between devices  119 us (18%)
  other arithmetic  57.2 us (9%)
  local copies, waits for them, and re-layouts  23 us (4%)
  blocking collectives  22.3 us (3%)
  between operations  15.2 us (2%)
    ppermute x48, waiting for transfers between devices, over_mp(): return lax.ppermute(value, 'mp', list(pairs))  241 us
    ppermute x48, starting transfers between devices, over_mp(): return lax.ppermute(value, 'mp', list(pairs))  108 us
    ppermute x7, waiting for transfers between devices, swapped(): return lax.ppermute(value, axis, [(d, d ^ bit) for d in range(count)])  26.1 us
    pallas_call x2, Pallas kernels, columns_product(): pl.pallas_call(columns_product_kernel, grid_spec=pltpu.PrefetchScalarGrid...  25.7 us
    pallas_call x1, Pallas kernels, feed_forward(): pl.pallas_call(feed_forward_kernel, grid_spec=pltpu.PrefetchScalarGridSpe...  23.5 us
    pallas_call x2, Pallas kernels, product_blocks(): pl.pallas_call(partial(blocks_kernel, pairs=len(lefts), transposed=transp...  15.2 us
    pallas_call x1, Pallas kernels, run_backward(): pl.pallas_call(partial(backward_kernel, groups=groups), out_shape=(shape(...  13.7 us
    pallas_call x2, Pallas kernels, rows_product(): pl.pallas_call(partial(rows_product_kernel, ring=ring_order()), grid=(rig...  13.2 us
  transfers between devices with their start and end apart: 62, of which 30 were waited for; matrix products, arithmetic and copies ran while one was open for 11% of the time, Pallas kernels for 15%

profile of v4, /device:TPU:0, one launch (start us, length us, event | category | flops | bytes accessed | tf_op | source)
XLA Modules:
  0.0 646.1 jit_solution(3433282485501279318)
XLA Ops:
  8.0 5.8 collective-permute-start.2
  18.9 18.1 %collective-permute-done.2 = f32[512,512]{1,0:T(8,128)S(1)} collective-permute-done((f32[512,512]{1,0:T(8,128)}, f32[512,512]{1,0:T(8,128)S(1)}, u32[]{:S(2)}, u32[]{:S(2)}) %collective-permute-start.2) | collective-permute-done | bytes 1048608 | tf_op jit(solution)/shard_map/ppermute | solution.py:40
  39.9 8.4 %fusion.24.gate_ref = bf16[640,1280]{1,0:T(8,128)(2,1)} fusion(bf16[160,160]{1,0:T(8,128)(2,1)S(1)} %get-tuple-element.243, bf16[160,160]{1,0:T(8,128)(2,1)S(1)} %get-tuple-element.244, bf16[160,160]{1,0:T(8,128)(2,1)S(1)} %get-tuple-element.242, bf16[160,160]{1,0:T(8,128)(2,1)S(1)} %get-tuple-element.241, bf16[160,160]{1,0:T(8,128)(2,1)S(1)} %get-tuple-element.257, ...), kind=kLoop, calls=%fused_computation.32 | loop fusion | flops 40960000 | bytes 2048000 | tf_op jit(solution)/shard_map/concatenate | solution.py:773
  50.0 5.4 collective-permute-start.1
  55.4 7.5 %collective-permute-done.4 = f32[512,512]{1,0:T(8,128)} collective-permute-done((f32[512,512]{1,0:T(8,128)S(1)}, f32[512,512]{1,0:T(8,128)}, u32[]{:S(2)}, u32[]{:S(2)}) %collective-permute-start.4) | collective-permute-done | bytes 1048608 | tf_op jit(solution)/shard_map/ppermute | solution.py:40
  69.1 21.1 %collective-permute-done.7 = f32[512,512]{1,0:T(8,128)} collective-permute-done((f32[512,512]{1,0:T(8,128)}, f32[512,512]{1,0:T(8,128)}, u32[]{:S(2)}, u32[]{:S(2)}) %collective-permute-start.7) | collective-permute-done | bytes 1048608 | tf_op jit(solution)/shard_map/ppermute | solution.py:40
  100.6 11.8 %recurrence_forward.1 = (f32[512,640]{1,0:T(8,128)}, bf16[512,640]{1,0:T(8,128)(2,1)}, f32[512,640]{1,0:T(8,128)}, f32[512,640]{1,0:T(8,128)}, f32[512,640]{1,0:...) custom-call(f32[512,640]{1,0:T(8,128)} %copy-done.8, ...), custom_call_target="tpu_custom_call" | custom-call | flops 1000 | bytes 1000 | tf_op jit(solution)/shard_map/recurrence_forward/pallas_call | solution.py:488
  112.4 12.0 %all-gather = f32[64,640]{1,0:T(8,128)} all-gather(f32[8,640]{1,0:T(8,128)} %get-tuple-element.121), channel_id=2, replica_groups=mesh['seq'=8,'mp'=4] {'seq'}, dimensions={0}, use_global_device_ids=true | all-gather | bytes 184320 | tf_op jit(solution)/shard_map/all_gather | solution.py:790
  124.4 7.7 %recurrence_states.1 = (f32[512,640]{1,0:T(8,128)}, bf16[512,640]{1,0:T(8,128)(2,1)}, f32[8,640]{1,0:T(8,128)}, f32[512,512]{1,0:T(8,128)}, f32[512,512]{1,0:T(8...) custom-call(s32[1]{0:T(128)} %bitcast.mine_ref, s32[4]{0:T(128)} %pad_add_fusion.order_ref, f32[8,8,640]{2,1,0:T(8,128)} %bitcast.38, ...), custom_call_target="tpu_custom_call" | custom-call | flops 1000 | bytes 1000 | tf_op jit(solution)/shard_map/recurrence_states/pallas_call | solution.py:509
  137.1 21.1 %collective-permute-done.11 = f32[512,512]{1,0:T(8,128)S(1)} collective-permute-done((f32[512,512]{1,0:T(8,128)}, f32[512,512]{1,0:T(8,128)S(1)}, u32[]{:S(2)}, u32[]{:S(2)}) %collective-permute-start.11) | collective-permute-done | bytes 1048608 | tf_op jit(solution)/shard_map/ppermute | solution.py:40
  166.5 19.7 %collective-permute-done.14 = f32[512,512]{1,0:T(8,128)S(1)} collective-permute-done((f32[512,512]{1,0:T(8,128)S(1)}, f32[512,512]{1,0:T(8,128)S(1)}, u32[]{:S(2)}, u32[]{:S(2)}) %collective-permute-start.14) | collective-permute-done | bytes 1048608 | tf_op jit(solution)/shard_map/ppermute | solution.py:40
  186.7 4.5 collective-permute-done.16
  193.4 21.8 %collective-permute-done.18 = f32[512,512]{1,0:T(8,128)S(1)} collective-permute-done((f32[512,512]{1,0:T(8,128)S(1)}, f32[512,512]{1,0:T(8,128)S(1)}, u32[]{:S(2)}, u32[]{:S(2)}) %collective-permute-start.18) | collective-permute-done | bytes 1048608 | tf_op jit(solution)/shard_map/ppermute | solution.py:40
  222.1 8.8 %product.1.dhidden_ref = f32[512,1536]{1,0:T(8,128)} custom-call(bf16[512,2048]{1,0:T(8,128)(2,1)} %copy-done.3, bf16[1536,2048]{1,0:T(8,128)(2,1)} %refs_1_.1), custom_call_target="tpu_custom_call" | custom-call | flops 1000 | bytes 1000 | tf_op jit(solution)/shard_map/product/pallas_call | solution.py:612
  230.9 9.2 %collective-permute-done.21 = f32[512,512]{1,0:T(8,128)} collective-permute-done((f32[512,512]{1,0:T(8,128)S(1)}, f32[512,512]{1,0:T(8,128)}, u32[]{:S(2)}, u32[]{:S(2)}) %collective-permute-start.21) | collective-permute-done | bytes 1048608 | tf_op jit(solution)/shard_map/ppermute | solution.py:40
  242.1 4.7 collective-permute-start.19
  246.9 16.5 %collective-permute-done.19 = f32[512]{0:T(512)S(1)} collective-permute-done((f32[512]{0:T(512)S(1)}, f32[512]{0:T(512)S(1)}, u32[]{:S(2)}, u32[]{:S(2)}) %collective-permute-start.19) | collective-permute-done | bytes 2080 | tf_op jit(solution)/shard_map/ppermute | solution.py:40
  271.2 15.3 %collective-permute-done.25 = f32[512,512]{1,0:T(8,128)S(1)} collective-permute-done((f32[512,512]{1,0:T(8,128)S(1)}, f32[512,512]{1,0:T(8,128)S(1)}, u32[]{:S(2)}, u32[]{:S(2)}) %collective-permute-start.25) | collective-permute-done | bytes 1048608 | tf_op jit(solution)/shard_map/ppermute | solution.py:40
  288.1 23.5 %feed_forward.1 = (bf16[512,1536]{1,0:T(8,128)(2,1)}, bf16[512,1536]{1,0:T(8,128)(2,1)}, bf16[512,1536]{1,0:T(8,128)(2,1)}, f32[512,512]{1,0:T(8,128)}, f32[512,...) custom-call(s32[4]{0:T(128)} %pad_add_fusion.order_ref, bf16[512,2048]{1,0:T(8,128)(2,1)} %copy-done, ...), custom_call_target="tpu_custom_call" | custom-call | flops 1000 | bytes 1000 | tf_op jit(solution)/shard_map/feed_forward/pallas_call | solution.py:559
  311.6 8.5 %rows_product.2 = f32[1536,2048]{1,0:T(8,128)} custom-call(bf16[512,1536]{1,0:T(8,128)(2,1)} %get-tuple-element.159.left_ref.refs_0_, bf16[512,2048]{1,0:T(8,128)(2,1)} %copy-done.3), custom_call_target="tpu_custom_call" | custom-call | flops 1000 | bytes 1000 | tf_op jit(solution)/shard_map/rows_product/pallas_call | solution.py:705
  322.8 15.5 %columns_product.2 = f32[2048,3072]{1,0:T(8,128)} custom-call(s32[8]{0:T(128)} %constant.56.clone.ring_ref, bf16[512,2048]{1,0:T(8,128)(2,1)} %copy-done, bf16[512,1536]{1,0:T(8,128)(2,1)} %get-tuple-element.146.refs_0_, bf16[512,1536]{1,0:T(8,128)(2,1)} %get-tuple-element.147.refs_1_), custom_call_target="tpu_custom_call" | custom-call | flops 1000 | bytes 1000 | tf_op jit(solution)/shard_map/columns_product/pallas_call | solution.py:680
  342.1 5.3 collective-permute-start.27
  349.0 4.3 product_sums.2
  354.6 8.3 %collective-permute-done.29 = f32[512]{0:T(512)S(1)} collective-permute-done((f32[512]{0:T(512)S(1)}, f32[512]{0:T(512)S(1)}, u32[]{:S(2)}, u32[]{:S(2)}) %collective-permute-start.29) | collective-permute-done | bytes 2080 | tf_op jit(solution)/shard_map/ppermute | solution.py:40
  371.6 4.7 collective-permute-start.32
  376.3 7.8 %product_blocks.2 = (f32[512,512]{1,0:T(8,128)}, f32[512,512]{1,0:T(8,128)}, f32[512,512]{1,0:T(8,128)}, f32[512,512]{1,0:T(8,128)}) custom-call(s32[4]{0:T(128)} %pad_add_fusion.order_ref, bf16[512,1536]{1,0:T(8,128)(2,1)} %get-tuple-element.159.left_ref.refs_0_, bf16[1536,2048]{1,0:T(8,128)(2,1)} %refs_1_.1), custom_call_target="tpu_custom_call" | custom-call | flops 1000 | bytes 1000 | tf_op jit(solution)/shard_map/product_blocks/pallas_call | solution.py:579
  385.1 7.4 %collective-permute-done.32 = f32[512,512]{1,0:T(8,128)} collective-permute-done((f32[512,512]{1,0:T(8,128)S(1)}, f32[512,512]{1,0:T(8,128)}, u32[]{:S(2)}, u32[]{:S(2)}) %collective-permute-start.32) | collective-permute-done | bytes 1048608 | tf_op jit(solution)/shard_map/ppermute | solution.py:40
  395.9 3.8 collective-permute-start.33
  399.7 18.8 %collective-permute-done.33 = f32[512,512]{1,0:T(8,128)S(1)} collective-permute-done((f32[512,512]{1,0:T(8,128)S(1)}, f32[512,512]{1,0:T(8,128)S(1)}, u32[]{:S(2)}, u32[]{:S(2)}) %collective-permute-start.33) | collective-permute-done | bytes 1048608 | tf_op jit(solution)/shard_map/ppermute | solution.py:40
  418.5 4.4 collective-permute-start.37
  425.9 11.8 %collective-permute-done.37 = f32[512,512]{1,0:T(8,128)S(1)} collective-permute-done((f32[512,512]{1,0:T(8,128)S(1)}, f32[512,512]{1,0:T(8,128)S(1)}, u32[]{:S(2)}, u32[]{:S(2)}) %collective-permute-start.37) | collective-permute-done | bytes 1048608 | tf_op jit(solution)/shard_map/ppermute | solution.py:40
  443.2 4.1 collective-permute-start.40
  451.3 7.6 %collective-permute-done.40 = f32[512,512]{1,0:T(8,128)} collective-permute-done((f32[512,512]{1,0:T(8,128)}, f32[512,512]{1,0:T(8,128)}, u32[]{:S(2)}, u32[]{:S(2)}) %collective-permute-start.40) | collective-permute-done | bytes 1048608 | tf_op jit(solution)/shard_map/ppermute | solution.py:40
  461.7 10.5 %collective-permute-start.41 = (f32[512,512]{1,0:T(8,128)}, f32[512,512]{1,0:T(8,128)}, u32[]{:S(2)}, u32[]{:S(2)}) collective-permute-start(f32[512,512]{1,0:T(8,128)} %add.261), channel_id=1, source_target_pairs={{0,1},{1,0},{2,3},{3,2},{4,5},{5,4},{6,7},{7,6},{8,9},{9,8},{10,11... | collective-permute-start | bytes 3145736 | tf_op jit(solution)/shard_map/ppermute | solution.py:40
  479.0 7.9 %recurrence_turn.1 = (f32[512,640]{1,0:T(8,128)}, bf16[512,640]{1,0:T(8,128)(2,1)}, f32[8,640]{1,0:T(8,128)}) custom-call(bf16[512,2048]{1,0:T(8,128)(2,1)} %copy-done.2, bf16[640,2048]{1,0:T(8,128)(2,1)} %weight_ref.3, f32[512,640]{1,0:T(8,128)} %fusion.65.gate_ref, f32[512,640]{1,0:T(8,128)} %get-tuple-element.172.states_ref, ...), custom_call_target="tpu_custom_call" | custom-call | flops 1000 | bytes 1000 | tf_op jit(solution)/shard_map/recurrence_turn/pallas_call | solution.py:535
  487.7 10.2 %all-gather.2.ends_ref = f32[8,2,640]{2,1,0:T(2,128)} all-gather(f32[1,2,640]{2,1,0:T(2,128)S(1)} %bitcast.41), channel_id=3, replica_groups=mesh['seq'=8,'mp'=4] {'seq'}, dimensions={0}, use_global_device_ids=true | all-gather | bytes 46080 | tf_op jit(solution)/shard_map/all_gather | solution.py:856
  497.9 13.7 %recurrence_backward.1 = (bf16[512,640]{1,0:T(8,128)(2,1)}, f32[16,640]{1,0:T(8,128)}, f32[8,640]{1,0:T(8,128)}, f32[2,328,320]{2,1,0:T(8,128)}) custom-call(s32[1]{0:T(128)} %bitcast.mine_ref, f32[8,2,640]{2,1,0:T(2,128)} %all-gather.2.ends_ref, f32[512,640]{1,0:T(8,128)} %get-tuple-element.178.dstates_ref, f32[512,640]{1,0:T(8,128)} %get-tuple-element.179.alpha_ref, ...), custom_call_target="tpu_custom_call" | custom-call | flops 1000 | bytes 1000 | tf_op jit(solution)/shard_map/recurrence_backward/pallas_call | solution.py:626
  511.7 4.8 rows_product.3
  520.8 7.4 %product_blocks.3 = (f32[512,512]{1,0:T(8,128)}, f32[512,512]{1,0:T(8,128)}, f32[512,512]{1,0:T(8,128)}, f32[512,512]{1,0:T(8,128)}) custom-call(s32[4]{0:T(128)} %pad_add_fusion.order_ref, bf16[512,640]{1,0:T(8,128)(2,1)} %fusion.45.refs_0_, bf16[512,640]{1,0:T(8,128)(2,1)} %get-tuple-element.191.refs_1_, bf16[2048,640]{1,0:T(8,128)(2,1)} %refs_2_.1, ...), custom_call_target="tpu_custom_call" | custom-call | flops 1000 | bytes 1000 | tf_op jit(solution)/shard_map/product_blocks/pallas_call | solution.py:579
  531.0 10.2 %columns_product.3 = f32[2048,1280]{1,0:T(8,128)} custom-call(s32[8]{0:T(128)} %constant.56.clone.ring_ref, bf16[512,2048]{1,0:T(8,128)(2,1)} %copy-done.1, bf16[512,640]{1,0:T(8,128)(2,1)} %fusion.45.refs_0_, bf16[512,640]{1,0:T(8,128)(2,1)} %get-tuple-element.191.refs_1_), custom_call_target="tpu_custom_call" | custom-call | flops 1000 | bytes 1000 | tf_op jit(solution)/shard_map/columns_product/pallas_call | solution.py:680
  541.1 4.3 product_sums.3
  547.2 4.8 collective-permute-done.44
  563.2 4.4 collective-permute-start.46
  572.5 15.7 %collective-permute-done.49 = f32[328,320]{1,0:T(8,128)S(1)} collective-permute-done((f32[328,320]{1,0:T(8,128)}, f32[328,320]{1,0:T(8,128)S(1)}, u32[]{:S(2)}, u32[]{:S(2)}) %collective-permute-start.49) | collective-permute-done | bytes 419872 | tf_op jit(solution)/shard_map/ppermute | solution.py:114
  592.5 3.3 collective-permute-start.52
  602.6 4.8 collective-permute-start.51
  611.6 8.5 %collective-permute-done.56 = f32[4096]{0:T(1024)S(1)} collective-permute-done((f32[4096]{0:T(1024)S(1)}, f32[4096]{0:T(1024)S(1)}, u32[]{:S(2)}, u32[]{:S(2)}) %collective-permute-start.56) | collective-permute-done | bytes 16416 | tf_op jit(solution)/shard_map/ppermute | solution.py:114
  620.2 10.4 %collective-permute-done.51 = f32[512,512]{1,0:T(8,128)S(1)} collective-permute-done((f32[512,512]{1,0:T(8,128)S(1)}, f32[512,512]{1,0:T(8,128)S(1)}, u32[]{:S(2)}, u32[]{:S(2)}) %collective-permute-start.51) | collective-permute-done | bytes 1048608 | tf_op jit(solution)/shard_map/ppermute | solution.py:40
  (295 shorter events, 154.7 us)
Async XLA Ops:
  7.2 440.1 %reduce-scatter.5.cloned.1.call-start = ((), (), s32[]{:S(2)}) async-start(), calls=%async_computation.4 | async-start | bytes 14155776 | tf_op jit(solution)/shard_map/reduce_scatter | solution.py:667
  7.2 11.6 %collective-permute-start.3 = (f32[512,512]{1,0:T(8,128)}, f32[512,512]{1,0:T(8,128)S(1)}, u32[]{:S(2)}, u32[]{:S(2)}) collective-permute-start(f32[512,512]{1,0:T(8,128)} %param.20), channel_id=1, source_target_pairs={{1,2},{2,1},{5,6},{6,5},{9,10},{10,9},{13,14},{14,13},{17,18},{18,... | collective-permute-start | bytes 3145736 | tf_op jit(solution)/shard_map/ppermute | solution.py:40
  8.0 29.0 %collective-permute-start.2 = (f32[512,512]{1,0:T(8,128)}, f32[512,512]{1,0:T(8,128)S(1)}, u32[]{:S(2)}, u32[]{:S(2)}) collective-permute-start(f32[512,512]{1,0:T(8,128)} %param.20), channel_id=1, source_target_pairs={{0,1},{1,0},{2,3},{3,2},{4,5},{5,4},{6,7},{7,6},{8,9},{9,8},{10,11... | collective-permute-start | bytes 3145736 | tf_op jit(solution)/shard_map/ppermute | solution.py:40
  14.6 33.8 %collective-permute-start.6 = (f32[8]{0:T(128)S(1)}, f32[8]{0:T(128)S(1)}, u32[]{:S(2)}, u32[]{:S(2)}) collective-permute-start(f32[8]{0:T(128)S(1)} %slice.113), channel_id=1, source_target_pairs={{0,4},{4,8},{8,12},{12,16},{16,20},{20,24},{24,28},{1,5},{5,9},{9,... | collective-permute-start | bytes 104 | tf_op jit(solution)/shard_map/ppermute | solution.py:757
  17.4 32.7 %collective-permute-start = (f32[512]{0:T(512)S(1)}, f32[512]{0:T(512)S(1)}, u32[]{:S(2)}, u32[]{:S(2)}) collective-permute-start(f32[512]{0:T(512)S(1)} %multiply_reduce_fusion.1), channel_id=1, source_target_pairs={{0,1},{1,0},{2,3},{3,2},{4,5},{5,4},{6,7},{7,6},{8,9},{9,8},{10,11... | collective-permute-start | bytes 6152 | tf_op jit(solution)/shard_map/ppermute | solution.py:40
  36.9 26.0 %collective-permute-start.4 = (f32[512,512]{1,0:T(8,128)S(1)}, f32[512,512]{1,0:T(8,128)}, u32[]{:S(2)}, u32[]{:S(2)}) collective-permute-start(f32[512,512]{1,0:T(8,128)S(1)} %collective-permute-done.3), channel_id=1, source_target_pairs={{1,0},{2,3},{5,4},{6,7},{9,8},{10,11},{13,12},{14,15},{17,16},{18,... | collective-permute-start | bytes 3145736 | tf_op jit(solution)/shard_map/ppermute | solution.py:40
  38.2 24.7 %collective-permute-start.5 = (f32[512,512]{1,0:T(8,128)S(1)}, f32[512,512]{1,0:T(8,128)}, u32[]{:S(2)}, u32[]{:S(2)}) collective-permute-start(f32[512,512]{1,0:T(8,128)S(1)} %collective-permute-done.2), channel_id=1, source_target_pairs={{1,2},{2,1},{5,6},{6,5},{9,10},{10,9},{13,14},{14,13},{17,18},{18,... | collective-permute-start | bytes 3145736 | tf_op jit(solution)/shard_map/ppermute | solution.py:40
  50.0 16.9 %collective-permute-start.1 = (f32[512]{0:T(512)S(1)}, f32[512]{0:T(512)S(1)}, u32[]{:S(2)}, u32[]{:S(2)}) collective-permute-start(f32[512]{0:T(512)S(1)} %add.226), channel_id=1, source_target_pairs={{0,2},{2,0},{1,3},{3,1},{4,6},{6,4},{5,7},{7,5},{8,10},{10,8},{9,1... | collective-permute-start | bytes 6152 | tf_op jit(solution)/shard_map/ppermute | solution.py:40
  62.9 27.3 %collective-permute-start.7 = (f32[512,512]{1,0:T(8,128)}, f32[512,512]{1,0:T(8,128)}, u32[]{:S(2)}, u32[]{:S(2)}) collective-permute-start(f32[512,512]{1,0:T(8,128)} %collective-permute-done.5), channel_id=1, source_target_pairs={{1,0},{2,3},{5,4},{6,7},{9,8},{10,11},{13,12},{14,15},{17,16},{18,... | collective-permute-start | bytes 3145736 | tf_op jit(solution)/shard_map/ppermute | solution.py:40
  90.2 34.2 %collective-permute-start.10 = (f32[512,512]{1,0:T(8,128)S(1)}, f32[512,512]{1,0:T(8,128)S(1)}, u32[]{:S(2)}, u32[]{:S(2)}) collective-permute-start(f32[512,512]{1,0:T(8,128)S(1)} %copy-done.18), channel_id=1, source_target_pairs={{1,2},{2,1},{5,6},{6,5},{9,10},{10,9},{13,14},{14,13},{17,18},{18,... | collective-permute-start | bytes 3145736 | tf_op jit(solution)/shard_map/ppermute | solution.py:40
  91.0 33.4 %collective-permute-start.9 = (f32[512,512]{1,0:T(8,128)S(1)}, f32[512,512]{1,0:T(8,128)S(1)}, u32[]{:S(2)}, u32[]{:S(2)}) collective-permute-start(f32[512,512]{1,0:T(8,128)S(1)} %copy-done.18), channel_id=1, source_target_pairs={{0,1},{1,0},{2,3},{3,2},{4,5},{5,4},{6,7},{7,6},{8,9},{9,8},{10,11... | collective-permute-start | bytes 3145736 | tf_op jit(solution)/shard_map/ppermute | solution.py:40
  132.1 26.1 %collective-permute-start.11 = (f32[512,512]{1,0:T(8,128)}, f32[512,512]{1,0:T(8,128)S(1)}, u32[]{:S(2)}, u32[]{:S(2)}) collective-permute-start(f32[512,512]{1,0:T(8,128)} %get-tuple-element.128), channel_id=1, source_target_pairs={{0,1},{3,2},{4,5},{7,6},{8,9},{11,10},{12,13},{15,14},{16,17},{19,... | collective-permute-start | bytes 3145736 | tf_op jit(solution)/shard_map/ppermute | solution.py:40
  135.0 24.6 %collective-permute-start.12 = (f32[512,512]{1,0:T(8,128)S(1)}, f32[512,512]{1,0:T(8,128)S(1)}, u32[]{:S(2)}, u32[]{:S(2)}) collective-permute-start(f32[512,512]{1,0:T(8,128)S(1)} %collective-permute-done.9), channel_id=1, source_target_pairs={{1,2},{2,1},{5,6},{6,5},{9,10},{10,9},{13,14},{14,13},{17,18},{18,... | collective-permute-start | bytes 3145736 | tf_op jit(solution)/shard_map/ppermute | solution.py:40
  135.8 27.0 %collective-permute-start.13 = (f32[512,512]{1,0:T(8,128)S(1)}, f32[512,512]{1,0:T(8,128)S(1)}, u32[]{:S(2)}, u32[]{:S(2)}) collective-permute-start(f32[512,512]{1,0:T(8,128)S(1)} %collective-permute-done.10), channel_id=1, source_target_pairs={{1,0},{2,3},{5,4},{6,7},{9,8},{10,11},{13,12},{14,15},{17,16},{18,... | collective-permute-start | bytes 3145736 | tf_op jit(solution)/shard_map/ppermute | solution.py:40
  162.8 23.4 %collective-permute-start.14 = (f32[512,512]{1,0:T(8,128)S(1)}, f32[512,512]{1,0:T(8,128)S(1)}, u32[]{:S(2)}, u32[]{:S(2)}) collective-permute-start(f32[512,512]{1,0:T(8,128)S(1)} %copy-done.31), channel_id=1, source_target_pairs={{0,1},{3,2},{4,5},{7,6},{8,9},{11,10},{12,13},{15,14},{16,17},{19,... | collective-permute-start | bytes 3145736 | tf_op jit(solution)/shard_map/ppermute | solution.py:40
  164.3 22.1 %collective-permute-start.15 = (f32[512,512]{1,0:T(8,128)S(1)}, f32[512,512]{1,0:T(8,128)S(1)}, u32[]{:S(2)}, u32[]{:S(2)}) collective-permute-start(f32[512,512]{1,0:T(8,128)S(1)} %add.236), channel_id=1, source_target_pairs={{1,2},{2,1},{5,6},{6,5},{9,10},{10,9},{13,14},{14,13},{17,18},{18,... | collective-permute-start | bytes 3145736 | tf_op jit(solution)/shard_map/ppermute | solution.py:40
  165.0 26.1 %collective-permute-start.16 = (f32[512,512]{1,0:T(8,128)S(1)}, f32[512,512]{1,0:T(8,128)S(1)}, u32[]{:S(2)}, u32[]{:S(2)}) collective-permute-start(f32[512,512]{1,0:T(8,128)S(1)} %collective-permute-done.12), channel_id=1, source_target_pairs={{1,0},{2,3},{5,4},{6,7},{9,8},{10,11},{13,12},{14,15},{17,16},{18,... | collective-permute-start | bytes 3145736 | tf_op jit(solution)/shard_map/ppermute | solution.py:40
  191.8 23.3 %collective-permute-start.18 = (f32[512,512]{1,0:T(8,128)S(1)}, f32[512,512]{1,0:T(8,128)S(1)}, u32[]{:S(2)}, u32[]{:S(2)}) collective-permute-start(f32[512,512]{1,0:T(8,128)S(1)} %add.238), channel_id=1, source_target_pairs={{0,1},{1,0},{2,3},{3,2},{4,5},{5,4},{6,7},{7,6},{8,9},{9,8},{10,11... | collective-permute-start | bytes 3145736 | tf_op jit(solution)/shard_map/ppermute | solution.py:40
  215.5 15.4 %collective-permute-start.22 = (f32[512,512]{1,0:T(8,128)S(1)}, f32[512,512]{1,0:T(8,128)}, u32[]{:S(2)}, u32[]{:S(2)}) collective-permute-start(f32[512,512]{1,0:T(8,128)S(1)} %get-tuple-element.193), channel_id=1, source_target_pairs={{1,2},{2,1},{5,6},{6,5},{9,10},{10,9},{13,14},{14,13},{17,18},{18,... | collective-permute-start | bytes 3145736 | tf_op jit(solution)/shard_map/ppermute | solution.py:40
  217.2 22.9 %collective-permute-start.21 = (f32[512,512]{1,0:T(8,128)S(1)}, f32[512,512]{1,0:T(8,128)}, u32[]{:S(2)}, u32[]{:S(2)}) collective-permute-start(f32[512,512]{1,0:T(8,128)S(1)} %get-tuple-element.193), channel_id=1, source_target_pairs={{0,1},{1,0},{2,3},{3,2},{4,5},{5,4},{6,7},{7,6},{8,9},{9,8},{10,11... | collective-permute-start | bytes 3145736 | tf_op jit(solution)/shard_map/ppermute | solution.py:40
  240.1 23.3 %collective-permute-start.23 = (f32[512,512]{1,0:T(8,128)}, f32[512,512]{1,0:T(8,128)S(1)}, u32[]{:S(2)}, u32[]{:S(2)}) collective-permute-start(f32[512,512]{1,0:T(8,128)} %collective-permute-done.22), channel_id=1, source_target_pairs={{1,0},{2,3},{5,4},{6,7},{9,8},{10,11},{13,12},{14,15},{17,16},{18,... | collective-permute-start | bytes 3145736 | tf_op jit(solution)/shard_map/ppermute | solution.py:40
  241.4 22.0 %collective-permute-start.24 = (f32[512,512]{1,0:T(8,128)}, f32[512,512]{1,0:T(8,128)S(1)}, u32[]{:S(2)}, u32[]{:S(2)}) collective-permute-start(f32[512,512]{1,0:T(8,128)} %collective-permute-done.21), channel_id=1, source_target_pairs={{1,2},{2,1},{5,6},{6,5},{9,10},{10,9},{13,14},{14,13},{17,18},{18,... | collective-permute-start | bytes 3145736 | tf_op jit(solution)/shard_map/ppermute | solution.py:40
  242.1 21.3 %collective-permute-start.19 = (f32[512]{0:T(512)S(1)}, f32[512]{0:T(512)S(1)}, u32[]{:S(2)}, u32[]{:S(2)}) collective-permute-start(f32[512]{0:T(512)S(1)} %get-tuple-element.223), channel_id=1, source_target_pairs={{0,1},{1,0},{2,3},{3,2},{4,5},{5,4},{6,7},{7,6},{8,9},{9,8},{10,11... | collective-permute-start | bytes 6152 | tf_op jit(solution)/shard_map/ppermute | solution.py:40
  263.4 23.1 %collective-permute-start.25 = (f32[512,512]{1,0:T(8,128)S(1)}, f32[512,512]{1,0:T(8,128)S(1)}, u32[]{:S(2)}, u32[]{:S(2)}) collective-permute-start(f32[512,512]{1,0:T(8,128)S(1)} %collective-permute-done.24), channel_id=1, source_target_pairs={{1,0},{2,3},{5,4},{6,7},{9,8},{10,11},{13,12},{14,15},{17,16},{18,... | collective-permute-start | bytes 3145736 | tf_op jit(solution)/shard_map/ppermute | solution.py:40
  320.1 208.2 %reduce-scatter.7.cloned.1.call-start = ((), (), s32[]{:S(2)}) async-start(), calls=%async_computation.5 | async-start | bytes 28311552 | tf_op jit(solution)/shard_map/reduce_scatter | solution.py:667
  321.3 18.4 %collective-permute-start.26 = (f32[512,512]{1,0:T(8,128)S(1)}, f32[512,512]{1,0:T(8,128)S(1)}, u32[]{:S(2)}, u32[]{:S(2)}) collective-permute-start(f32[512,512]{1,0:T(8,128)S(1)} %copy-done.14), channel_id=1, source_target_pairs={{0,1},{3,2},{4,5},{7,6},{8,9},{11,10},{12,13},{15,14},{16,17},{19,... | collective-permute-start | bytes 3145736 | tf_op jit(solution)/shard_map/ppermute | solution.py:40
  340.6 222.6 %reduce-scatter.9.cloned.1.call-start = ((), (), s32[]{:S(2)}) async-start(), calls=%async_computation.6 | async-start | bytes 5898240 | tf_op jit(solution)/shard_map/reduce_scatter | solution.py:667
  342.1 25.3 %collective-permute-start.27 = (f32[512,512]{1,0:T(8,128)}, f32[512,512]{1,0:T(8,128)}, u32[]{:S(2)}, u32[]{:S(2)}) collective-permute-start(f32[512,512]{1,0:T(8,128)} %get-tuple-element.148.refs_1_), channel_id=1, source_target_pairs={{0,1},{3,2},{4,5},{7,6},{8,9},{11,10},{12,13},{15,14},{16,17},{19,... | collective-permute-start | bytes 3145736 | tf_op jit(solution)/shard_map/ppermute | solution.py:40
  347.4 21.8 %collective-permute-start.28 = (f32[512,512]{1,0:T(8,128)S(1)}, f32[512,512]{1,0:T(8,128)}, u32[]{:S(2)}, u32[]{:S(2)}) collective-permute-start(f32[512,512]{1,0:T(8,128)S(1)} %add.249), channel_id=1, source_target_pairs={{1,2},{2,1},{5,6},{6,5},{9,10},{10,9},{13,14},{14,13},{17,18},{18,... | collective-permute-start | bytes 3145736 | tf_op jit(solution)/shard_map/ppermute | solution.py:40
  370.6 13.5 %collective-permute-start.31 = (f32[512,512]{1,0:T(8,128)S(1)}, f32[512,512]{1,0:T(8,128)S(1)}, u32[]{:S(2)}, u32[]{:S(2)}) collective-permute-start(f32[512,512]{1,0:T(8,128)S(1)} %add.250), channel_id=1, source_target_pairs={{1,2},{2,1},{5,6},{6,5},{9,10},{10,9},{13,14},{14,13},{17,18},{18,... | collective-permute-start | bytes 3145736 | tf_op jit(solution)/shard_map/ppermute | solution.py:40
  371.6 21.0 %collective-permute-start.32 = (f32[512,512]{1,0:T(8,128)S(1)}, f32[512,512]{1,0:T(8,128)}, u32[]{:S(2)}, u32[]{:S(2)}) collective-permute-start(f32[512,512]{1,0:T(8,128)S(1)} %add.251), channel_id=1, source_target_pairs={{0,1},{1,0},{2,3},{3,2},{4,5},{5,4},{6,7},{7,6},{8,9},{9,8},{10,11... | collective-permute-start | bytes 3145736 | tf_op jit(solution)/shard_map/ppermute | solution.py:40
  395.9 22.7 %collective-permute-start.33 = (f32[512,512]{1,0:T(8,128)S(1)}, f32[512,512]{1,0:T(8,128)S(1)}, u32[]{:S(2)}, u32[]{:S(2)}) collective-permute-start(f32[512,512]{1,0:T(8,128)S(1)} %get-tuple-element.164), channel_id=1, source_target_pairs={{0,1},{1,0},{2,3},{3,2},{4,5},{5,4},{6,7},{7,6},{8,9},{9,8},{10,11... | collective-permute-start | bytes 3145736 | tf_op jit(solution)/shard_map/ppermute | solution.py:40
  418.5 19.2 %collective-permute-start.37 = (f32[512,512]{1,0:T(8,128)S(1)}, f32[512,512]{1,0:T(8,128)S(1)}, u32[]{:S(2)}, u32[]{:S(2)}) collective-permute-start(f32[512,512]{1,0:T(8,128)S(1)} %copy-done.26), channel_id=1, source_target_pairs={{0,1},{3,2},{4,5},{7,6},{8,9},{11,10},{12,13},{15,14},{16,17},{19,... | collective-permute-start | bytes 3145736 | tf_op jit(solution)/shard_map/ppermute | solution.py:40
  423.0 18.6 %collective-permute-start.35 = (f32[512,512]{1,0:T(8,128)S(1)}, f32[512,512]{1,0:T(8,128)S(1)}, u32[]{:S(2)}, u32[]{:S(2)}) collective-permute-start(f32[512,512]{1,0:T(8,128)S(1)} %collective-permute-done.34), channel_id=1, source_target_pairs={{1,0},{2,3},{5,4},{6,7},{9,8},{10,11},{13,12},{14,15},{17,16},{18,... | collective-permute-start | bytes 3145736 | tf_op jit(solution)/shard_map/ppermute | solution.py:40
  424.3 23.0 %collective-permute-start.36 = (f32[512,512]{1,0:T(8,128)S(1)}, f32[512,512]{1,0:T(8,128)}, u32[]{:S(2)}, u32[]{:S(2)}) collective-permute-start(f32[512,512]{1,0:T(8,128)S(1)} %collective-permute-done.33), channel_id=1, source_target_pairs={{1,2},{2,1},{5,6},{6,5},{9,10},{10,9},{13,14},{14,13},{17,18},{18,... | collective-permute-start | bytes 3145736 | tf_op jit(solution)/shard_map/ppermute | solution.py:40
  443.2 15.7 %collective-permute-start.40 = (f32[512,512]{1,0:T(8,128)}, f32[512,512]{1,0:T(8,128)}, u32[]{:S(2)}, u32[]{:S(2)}) collective-permute-start(f32[512,512]{1,0:T(8,128)} %get-tuple-element.170), channel_id=1, source_target_pairs={{0,1},{3,2},{4,5},{7,6},{8,9},{11,10},{12,13},{15,14},{16,17},{19,... | collective-permute-start | bytes 3145736 | tf_op jit(solution)/shard_map/ppermute | solution.py:40
  447.3 29.1 %collective-permute-start.38 = (f32[512,512]{1,0:T(8,128)}, f32[512,512]{1,0:T(8,128)S(1)}, u32[]{:S(2)}, u32[]{:S(2)}) collective-permute-start(f32[512,512]{1,0:T(8,128)} %collective-permute-done.36), channel_id=1, source_target_pairs={{1,0},{2,3},{5,4},{6,7},{9,8},{10,11},{13,12},{14,15},{17,16},{18,... | collective-permute-start | bytes 3145736 | tf_op jit(solution)/shard_map/ppermute | solution.py:40
  461.7 36.3 %collective-permute-start.41 = (f32[512,512]{1,0:T(8,128)}, f32[512,512]{1,0:T(8,128)}, u32[]{:S(2)}, u32[]{:S(2)}) collective-permute-start(f32[512,512]{1,0:T(8,128)} %add.261), channel_id=1, source_target_pairs={{0,1},{1,0},{2,3},{3,2},{4,5},{5,4},{6,7},{7,6},{8,9},{9,8},{10,11... | collective-permute-start | bytes 3145736 | tf_op jit(solution)/shard_map/ppermute | solution.py:40
  472.2 25.7 %collective-permute-start.42 = (f32[512,512]{1,0:T(8,128)}, f32[512,512]{1,0:T(8,128)}, u32[]{:S(2)}, u32[]{:S(2)}) collective-permute-start(f32[512,512]{1,0:T(8,128)} %add.260), channel_id=1, source_target_pairs={{1,2},{2,1},{5,6},{6,5},{9,10},{10,9},{13,14},{14,13},{17,18},{18,... | collective-permute-start | bytes 3145736 | tf_op jit(solution)/shard_map/ppermute | solution.py:40
  516.5 120.2 %reduce-scatter.11.cloned.1.call-start = ((), (), s32[]{:S(2)}) async-start(), calls=%async_computation.7 | async-start | bytes 11796480 | tf_op jit(solution)/shard_map/reduce_scatter | solution.py:667
  528.2 23.8 %collective-permute-start.44 = (f32[512,512]{1,0:T(8,128)}, f32[512,512]{1,0:T(8,128)}, u32[]{:S(2)}, u32[]{:S(2)}) collective-permute-start(f32[512,512]{1,0:T(8,128)} %get-tuple-element.197.refs_0_), channel_id=1, source_target_pairs={{0,1},{3,2},{4,5},{7,6},{8,9},{11,10},{12,13},{15,14},{16,17},{19,... | collective-permute-start | bytes 3145736 | tf_op jit(solution)/shard_map/ppermute | solution.py:40
  563.2 27.4 %collective-permute-start.46 = (f32[512,512]{1,0:T(8,128)S(1)}, f32[512,512]{1,0:T(8,128)S(1)}, u32[]{:S(2)}, u32[]{:S(2)}) collective-permute-start(f32[512,512]{1,0:T(8,128)S(1)} %copy-done.11), channel_id=1, source_target_pairs={{0,1},{3,2},{4,5},{7,6},{8,9},{11,10},{12,13},{15,14},{16,17},{19,... | collective-permute-start | bytes 3145736 | tf_op jit(solution)/shard_map/ppermute | solution.py:40
  567.6 23.9 %collective-permute-start.47 = (f32[512,512]{1,0:T(8,128)}, f32[512,512]{1,0:T(8,128)S(1)}, u32[]{:S(2)}, u32[]{:S(2)}) collective-permute-start(f32[512,512]{1,0:T(8,128)} %add.266), channel_id=1, source_target_pairs={{1,2},{2,1},{5,6},{6,5},{9,10},{10,9},{13,14},{14,13},{17,18},{18,... | collective-permute-start | bytes 3145736 | tf_op jit(solution)/shard_map/ppermute | solution.py:40
  568.3 19.9 %collective-permute-start.49 = (f32[328,320]{1,0:T(8,128)}, f32[328,320]{1,0:T(8,128)S(1)}, u32[]{:S(2)}, u32[]{:S(2)}) collective-permute-start(f32[328,320]{1,0:T(8,128)} %bitcast_add_fusion), channel_id=1, source_target_pairs={{0,8},{4,12},{8,0},{12,4},{16,24},{20,28},{24,16},{28,20},{1,9},{5... | collective-permute-start | bytes 1259528 | tf_op jit(solution)/shard_map/ppermute | solution.py:114
  570.7 19.8 %collective-permute-start.48 = (f32[4608]{0:T(1024)S(1)}, f32[4608]{0:T(1024)S(1)}, u32[]{:S(2)}, u32[]{:S(2)}) collective-permute-start(f32[4608]{0:T(1024)S(1)} %pad_maximum_fusion.2), channel_id=1, source_target_pairs={{0,1},{1,0},{2,3},{3,2},{4,5},{5,4},{6,7},{7,6},{8,9},{9,8},{10,11... | collective-permute-start | bytes 55304 | tf_op jit(solution)/shard_map/ppermute | solution.py:40
  599.6 20.5 %collective-permute-start.53 = (f32[328,320]{1,0:T(8,128)S(1)}, f32[328,320]{1,0:T(8,128)S(1)}, u32[]{:S(2)}, u32[]{:S(2)}) collective-permute-start(f32[328,320]{1,0:T(8,128)S(1)} %copy-done.23), channel_id=1, source_target_pairs={{0,16},{4,20},{8,24},{12,28},{16,0},{20,4},{24,8},{28,12},{1,17},{... | collective-permute-start | bytes 1259528 | tf_op jit(solution)/shard_map/ppermute | solution.py:114
  601.9 29.3 %collective-permute-start.50 = (f32[512,512]{1,0:T(8,128)S(1)}, f32[512,512]{1,0:T(8,128)S(1)}, u32[]{:S(2)}, u32[]{:S(2)}) collective-permute-start(f32[512,512]{1,0:T(8,128)S(1)} %add.270), channel_id=1, source_target_pairs={{1,2},{2,1},{5,6},{6,5},{9,10},{10,9},{13,14},{14,13},{17,18},{18,... | collective-permute-start | bytes 3145736 | tf_op jit(solution)/shard_map/ppermute | solution.py:40
  602.6 28.0 %collective-permute-start.51 = (f32[512,512]{1,0:T(8,128)S(1)}, f32[512,512]{1,0:T(8,128)S(1)}, u32[]{:S(2)}, u32[]{:S(2)}) collective-permute-start(f32[512,512]{1,0:T(8,128)S(1)} %add.271), channel_id=1, source_target_pairs={{0,1},{1,0},{2,3},{3,2},{4,5},{5,4},{6,7},{7,6},{8,9},{9,8},{10,11... | collective-permute-start | bytes 3145736 | tf_op jit(solution)/shard_map/ppermute | solution.py:40
  (65 other events, 803.7 us)
Sparse Core Ops, SparseCore 0:
  320.2 67.3 reduce-scatter.4
  389.9 128.0 reduce-scatter.6
  520.9 35.6 reduce-scatter.8
  558.8 73.4 reduce-scatter.10

commit v5 on v4

--- a/solution.py
+++ b/solution.py
@@ -15,6 +15,7 @@
 SUB = 8
 ROWS = 32
 VMEM_LIMIT = 56 * 1024 * 1024
+VMEM_SMALL = 24 * 1024 * 1024
 
 
 def matmul(left, right):
@@ -283,9 +284,8 @@
 
 
 def feed_forward_kernel(
-    order_ref, low_ref, gate_ref, up_ref, dhidden_ref, hidden_ref, dgate_ref, dup_ref, *block_refs
+    low_ref, gate_ref, up_ref, dhidden_ref, hidden_ref, dgate_ref, dup_ref
 ):
-    step = pl.program_id(0)
     low = low_ref[...]
     gate = jnp.dot(low, gate_ref[...], preferred_element_type=f32)
     up = jnp.dot(low, up_ref[...], preferred_element_type=f32)
@@ -294,21 +294,6 @@
     hidden_ref[...] = (act * up).astype(bf16)
     dgate_ref[...] = (dhidden * up * slope).astype(bf16)
     dup_ref[...] = (dhidden * act).astype(bf16)
-    contract = (((1,), (1,)), ((), ()))
-    for k, block_ref in enumerate(block_refs):
-        block = block_ref.shape[1]
-        rows = pl.ds(pl.multiple_of(order_ref[k] * block, block), block)
-        part = lax.dot_general(
-            dgate_ref[...], gate_ref[rows, :], contract, preferred_element_type=f32
-        ) + lax.dot_general(dup_ref[...], up_ref[rows, :], contract, preferred_element_type=f32)
-
-        @pl.when(step == 0)
-        def _():
-            block_ref[...] = part
-
-        @pl.when(step > 0)
-        def _():
-            block_ref[...] += part
 
 
 def blocks_kernel(order_ref, *refs, pairs, transposed):
@@ -521,7 +506,7 @@
         out_shape=(
             shape((count, width)), shape((count, width), bf16), shape((SUB, width)),
         ) + (shape((count, features // 4)),) * 4,
-        compiler_params=pltpu.CompilerParams(vmem_limit_bytes=VMEM_LIMIT),
+        compiler_params=pltpu.CompilerParams(vmem_limit_bytes=VMEM_SMALL),
         cost_estimate=small_cost(),
         name="recurrence_states",
     )(mine, order, ends, part, span, gate_pre, weight)
@@ -543,34 +528,28 @@
             pl.BlockSpec(weight.shape, lambda i: (0, 0)),
         ] + [tile] * 3,
         out_specs=(tile, tile, pl.BlockSpec((SUB, width), lambda i: (0, 0))),
-        compiler_params=pltpu.CompilerParams(vmem_limit_bytes=VMEM_LIMIT),
+        compiler_params=pltpu.CompilerParams(vmem_limit_bytes=VMEM_SMALL),
         cost_estimate=small_cost(),
         name="recurrence_turn",
     )(branch, weight, gate_pre, states, span)
 
 
-def feed_forward(order, low, gate, up, dhidden):
+def feed_forward(low, gate, up, dhidden):
     count, features = low.shape
     hidden = gate.shape[1]
     block = 512
-    tile = pl.BlockSpec((count, block), lambda i, o: (0, i))
-    weight = pl.BlockSpec((features, block), lambda i, o: (0, i))
-    out = pl.BlockSpec((count, features // 4), lambda i, o: (0, 0))
+    tile = pl.BlockSpec((count, block), lambda i: (0, i))
+    weight = pl.BlockSpec((features, block), lambda i: (0, i))
     return pl.pallas_call(
         feed_forward_kernel,
-        grid_spec=pltpu.PrefetchScalarGridSpec(
-            num_scalar_prefetch=1,
-            grid=(hidden // block,),
-            in_specs=[
-                pl.BlockSpec((count, features), lambda i, o: (0, 0)), weight, weight, tile,
-            ],
-            out_specs=(tile,) * 3 + (out,) * 4,
-        ),
-        out_shape=(shape((count, hidden), bf16),) * 3 + (shape((count, features // 4)),) * 4,
+        grid=(hidden // block,),
+        in_specs=[pl.BlockSpec((count, features), lambda i: (0, 0)), weight, weight, tile],
+        out_specs=(tile,) * 3,
+        out_shape=(shape((count, hidden), bf16),) * 3,
         compiler_params=pltpu.CompilerParams(vmem_limit_bytes=VMEM_LIMIT),
         cost_estimate=small_cost(),
         name="feed_forward",
-    )(order, low, gate, up, dhidden)
+    )(low, gate, up, dhidden)
 
 
 def product_blocks(order, lefts, rights, transposed):
@@ -812,13 +791,13 @@
         return piece * second_scale * lax.dynamic_slice_in_dim(gain_second, start, own_width)
 
     second_low = assemble(second.pieces(), features, second_turn)
-    hidden_low, d_gate_ffn, d_up_ffn, *d_second_blocks = feed_forward(
-        order, second_low, mlp_gate, mlp_up, d_hidden
-    )
-    turned = LineScatter(d_second_blocks)
+    hidden_low, d_gate_ffn, d_up_ffn = feed_forward(second_low, mlp_gate, mlp_up, d_hidden)
     whole_down = rows_product(hidden_low, cot_low, own_width)
     grad_down = ring_scatter(whole_down)
-    turned.first(whole_down)
+    d_pair = after((d_gate_ffn, d_up_ffn), whole_down)
+    d_second_blocks = product_blocks(order, d_pair, [mlp_gate, mlp_up], True)
+    turned = LineScatter(d_second_blocks)
+    turned.first()
     whole_pair = columns_product(after(second_low, turned.own), [d_gate_ffn, d_up_ffn])
     turned.second(whole_pair)
     whole_pair = after(whole_pair, turned.far_one)
@@ -877,23 +856,22 @@
         order, after(first_low, whole_first), d_first_blocks
     )
     d_gain_first = gain_sums / gain_first
-    output = after(own_resid, final.own) + sent.result()
+    first_sums = jnp.concatenate([first_mean, d_gain_first, d_gain_second])
+    first_sums = first_sums + over_mp(first_sums, PAIRS)
+    final.second(whole_first, first_sums, grad_out)
+    whole_first = after(whole_first, final.far_one)
+    grad_first = ring_scatter(whole_first)
     core = lax.axis_index("seq") & 1
+    small = after(small, final.far_one)
     other = swapped(lax.dynamic_index_in_dim(small, 1 - core, 0, False), "seq", 1)
     small = lax.dynamic_index_in_dim(small, core, 0, False) + other
-    final.second(whole_first, first_mean, d_gain_first, grad_out, output, small)
-    whole_first, first_mean, d_gain_first = after(
-        (whole_first, first_mean, d_gain_first), final.far_one
-    )
-    grad_first = ring_scatter(whole_first)
     small = over_chips(small, 2)
-    first_sums = jnp.concatenate([first_mean, d_gain_first, d_gain_second])
-    first_sums = first_sums + over_mp(first_sums, PAIRS)
-    final.third(first_sums, small)
+    final.third(small)
     first_sums, small = after((first_sums, small), final.far_two, final.near_one)
     first_sums = first_sums + over_mp(first_sums, CROSS)
     first_mean = first_sums[:count] / features
     small = over_chips(small, 4)
+    output = after(own_resid, final.far_two) + sent.result()
     gains = sum_over(first_sums[count:], "seq")
     small, gains = after((small, gains), final.last)
     other = swapped(small, "seq", 1)

time: 657 us -> 649 us (0.988)
    pallas_call x2 -> x3, Pallas kernels: 15.2 us -> 29.6 us  [product_blocks(): pl.pallas_call(partial(blocks_kernel, pairs=len(lefts), transposed=transp...]
    pallas_call x1, Pallas kernels: 23.5 us -> 13 us  [feed_forward(): pl.pallas_call(feed_forward_kernel, grid=(hidden // block,), in_specs=[pl...]
  transfers between devices with their start and end apart: 62 -> 62, of which waited for: 30 -> 28; matrix products, arithmetic and copies ran while one was open for 11% -> 10% of each run, Pallas kernels for 15% -> 17%
where the time goes in v5:
time: 649 us; the launch traced here: 638 us
  waiting for transfers between devices  272 us (42%)
  Pallas kernels  131 us (20%)
  starting transfers between devices  118 us (18%)
  other arithmetic  53.4 us (8%)
  local copies, waits for them, and re-layouts  23 us (4%)
  blocking collectives  22.4 us (3%)
  between operations  15.4 us (2%)
    ppermute x48, waiting for transfers between devices, over_mp(): return lax.ppermute(value, 'mp', list(pairs))  238 us
    ppermute x48, starting transfers between devices, over_mp(): return lax.ppermute(value, 'mp', list(pairs))  108 us
    ppermute x7, waiting for transfers between devices, swapped(): return lax.ppermute(value, axis, [(d, d ^ bit) for d in range(count)])  31.6 us
    pallas_call x3, Pallas kernels, product_blocks(): pl.pallas_call(partial(blocks_kernel, pairs=len(lefts), transposed=transp...  29.6 us
    pallas_call x2, Pallas kernels, columns_product(): pl.pallas_call(columns_product_kernel, grid_spec=pltpu.PrefetchScalarGrid...  24.8 us
    pallas_call x1, Pallas kernels, run_backward(): pl.pallas_call(partial(backward_kernel, groups=groups), out_shape=(shape(...  13.6 us
    pallas_call x2, Pallas kernels, rows_product(): pl.pallas_call(partial(rows_product_kernel, ring=ring_order()), grid=(rig...  13.2 us
    pallas_call x1, Pallas kernels, feed_forward(): pl.pallas_call(feed_forward_kernel, grid=(hidden // block,), in_specs=[pl...  13 us
  transfers between devices with their start and end apart: 62, of which 28 were waited for; matrix products, arithmetic and copies ran while one was open for 10% of the time, Pallas kernels for 17%

profile of v5, /device:TPU:0, one launch (start us, length us, event | category | flops | bytes accessed | tf_op | source)
XLA Modules:
  0.0 638.4 jit_solution(7217970469593237455)
XLA Ops:
  8.0 5.8 collective-permute-start.2
  18.9 18.1 %collective-permute-done.2 = f32[512,512]{1,0:T(8,128)S(1)} collective-permute-done((f32[512,512]{1,0:T(8,128)}, f32[512,512]{1,0:T(8,128)S(1)}, u32[]{:S(2)}, u32[]{:S(2)}) %collective-permute-start.2) | collective-permute-done | bytes 1048608 | tf_op jit(solution)/shard_map/ppermute | solution.py:41
  39.9 8.4 %fusion.24.gate_ref = bf16[640,1280]{1,0:T(8,128)(2,1)} fusion(bf16[160,160]{1,0:T(8,128)(2,1)S(1)} %get-tuple-element.243, bf16[160,160]{1,0:T(8,128)(2,1)S(1)} %get-tuple-element.244, bf16[160,160]{1,0:T(8,128)(2,1)S(1)} %get-tuple-element.242, bf16[160,160]{1,0:T(8,128)(2,1)S(1)} %get-tuple-element.241, bf16[160,160]{1,0:T(8,128)(2,1)S(1)} %get-tuple-element.257, ...), kind=kLoop, calls=%fused_computation.32 | loop fusion | flops 40960000 | bytes 2048000 | tf_op jit(solution)/shard_map/concatenate | solution.py:752
  50.0 5.4 collective-permute-start.1
  55.5 7.5 %collective-permute-done.4 = f32[512,512]{1,0:T(8,128)} collective-permute-done((f32[512,512]{1,0:T(8,128)S(1)}, f32[512,512]{1,0:T(8,128)}, u32[]{:S(2)}, u32[]{:S(2)}) %collective-permute-start.4) | collective-permute-done | bytes 1048608 | tf_op jit(solution)/shard_map/ppermute | solution.py:41
  69.1 21.1 %collective-permute-done.7 = f32[512,512]{1,0:T(8,128)} collective-permute-done((f32[512,512]{1,0:T(8,128)}, f32[512,512]{1,0:T(8,128)}, u32[]{:S(2)}, u32[]{:S(2)}) %collective-permute-start.7) | collective-permute-done | bytes 1048608 | tf_op jit(solution)/shard_map/ppermute | solution.py:41
  99.6 12.4 %recurrence_forward.1 = (f32[512,640]{1,0:T(8,128)}, bf16[512,640]{1,0:T(8,128)(2,1)}, f32[512,640]{1,0:T(8,128)}, f32[512,640]{1,0:T(8,128)}, f32[512,640]{1,0:...) custom-call(f32[512,640]{1,0:T(8,128)} %copy-done.23, ...), custom_call_target="tpu_custom_call" | custom-call | flops 1000 | bytes 1000 | tf_op jit(solution)/shard_map/recurrence_forward/pallas_call | solution.py:473
  112.0 11.4 %all-gather = f32[64,640]{1,0:T(8,128)S(1)} all-gather(f32[8,640]{1,0:T(8,128)} %get-tuple-element.121), channel_id=2, replica_groups=mesh['seq'=8,'mp'=4] {'seq'}, dimensions={0}, use_global_device_ids=true | all-gather | bytes 184320 | tf_op jit(solution)/shard_map/all_gather | solution.py:769
  126.1 3.3 recurrence_states.1
  129.4 3.7 collective-permute-start.11
  135.2 20.8 %collective-permute-done.11 = f32[512,512]{1,0:T(8,128)S(1)} collective-permute-done((f32[512,512]{1,0:T(8,128)S(1)}, f32[512,512]{1,0:T(8,128)S(1)}, u32[]{:S(2)}, u32[]{:S(2)}) %collective-permute-start.11) | collective-permute-done | bytes 1048608 | tf_op jit(solution)/shard_map/ppermute | solution.py:41
  156.2 4.9 collective-permute-done.13
  164.8 19.7 %collective-permute-done.14 = f32[512,512]{1,0:T(8,128)S(1)} collective-permute-done((f32[512,512]{1,0:T(8,128)S(1)}, f32[512,512]{1,0:T(8,128)S(1)}, u32[]{:S(2)}, u32[]{:S(2)}) %collective-permute-start.14) | collective-permute-done | bytes 1048608 | tf_op jit(solution)/shard_map/ppermute | solution.py:41
  184.9 4.4 collective-permute-done.16
  191.5 21.9 %collective-permute-done.18 = f32[512,512]{1,0:T(8,128)S(1)} collective-permute-done((f32[512,512]{1,0:T(8,128)S(1)}, f32[512,512]{1,0:T(8,128)S(1)}, u32[]{:S(2)}, u32[]{:S(2)}) %collective-permute-start.18) | collective-permute-done | bytes 1048608 | tf_op jit(solution)/shard_map/ppermute | solution.py:41
  214.6 3.7 collective-permute-start.21
  224.1 8.8 %product.1.dhidden_ref = f32[512,1536]{1,0:T(8,128)} custom-call(bf16[512,2048]{1,0:T(8,128)(2,1)} %copy-done.16, bf16[1536,2048]{1,0:T(8,128)(2,1)} %refs_1_.1), custom_call_target="tpu_custom_call" | custom-call | flops 1000 | bytes 1000 | tf_op jit(solution)/shard_map/product/pallas_call | solution.py:591
  232.8 5.4 collective-permute-done.21
  240.2 4.4 collective-permute-start.19
  244.7 16.5 %collective-permute-done.19 = f32[512]{0:T(512)S(1)} collective-permute-done((f32[512]{0:T(512)S(1)}, f32[512]{0:T(512)S(1)}, u32[]{:S(2)}, u32[]{:S(2)}) %collective-permute-start.19) | collective-permute-done | bytes 2080 | tf_op jit(solution)/shard_map/ppermute | solution.py:41
  267.3 16.8 %collective-permute-done.25 = f32[512,512]{1,0:T(8,128)S(1)} collective-permute-done((f32[512,512]{1,0:T(8,128)S(1)}, f32[512,512]{1,0:T(8,128)S(1)}, u32[]{:S(2)}, u32[]{:S(2)}) %collective-permute-start.25) | collective-permute-done | bytes 1048608 | tf_op jit(solution)/shard_map/ppermute | solution.py:41
  285.7 13.0 %feed_forward.1 = (bf16[512,1536]{1,0:T(8,128)(2,1)}, bf16[512,1536]{1,0:T(8,128)(2,1)}, bf16[512,1536]{1,0:T(8,128)(2,1)}) custom-call(bf16[512,2048]{1,0:T(8,128)(2,1)} %copy-done.14, bf16[2048,1536]{1,0:T(8,128)(2,1)} %refs_2_.2, bf16[2048,1536]{1,0:T(8,128)(2,1)} %refs_3_.2, f32[512,1536]{1,0:T(8,128)} %product.1.dhidden_ref), custom_call_target="tpu_custom_call" | custom-call | flops 1000 | bytes 1000 | tf_op jit(solution)/shard_map/feed_forward/pallas_call | solution.py:543
  298.7 8.5 %rows_product.2 = f32[1536,2048]{1,0:T(8,128)} custom-call(bf16[512,1536]{1,0:T(8,128)(2,1)} %get-tuple-element.160.left_ref.refs_0_, bf16[512,2048]{1,0:T(8,128)(2,1)} %copy-done.16), custom_call_target="tpu_custom_call" | custom-call | flops 1000 | bytes 1000 | tf_op jit(solution)/shard_map/rows_product/pallas_call | solution.py:684
  307.3 14.4 %product_blocks.3 = (f32[512,512]{1,0:T(8,128)}, f32[512,512]{1,0:T(8,128)}, f32[512,512]{1,0:T(8,128)}, f32[512,512]{1,0:T(8,128)}) custom-call(s32[4]{0:T(128)} %copy-done.12, bf16[512,1536]{1,0:T(8,128)(2,1)} %get-tuple-element.143.refs_0_, bf16[512,1536]{1,0:T(8,128)(2,1)} %get-tuple-element.144.refs_1_, bf16[2048,1536]{1,0:T(8,128)(2,1)} %refs_2_.2, ...), custom_call_target="tpu_custom_call" | custom-call | flops 1000 | bytes 1000 | tf_op jit(solution)/shard_map/product_blocks/pallas_call | solution.py:558
  323.0 14.6 %columns_product.2 = f32[2048,3072]{1,0:T(8,128)} custom-call(s32[8]{0:T(128)} %constant.56.clone.ring_ref, bf16[512,2048]{1,0:T(8,128)(2,1)} %copy-done.14, bf16[512,1536]{1,0:T(8,128)(2,1)} %get-tuple-element.143.refs_0_, bf16[512,1536]{1,0:T(8,128)(2,1)} %get-tuple-element.144.refs_1_), custom_call_target="tpu_custom_call" | custom-call | flops 1000 | bytes 1000 | tf_op jit(solution)/shard_map/columns_product/pallas_call | solution.py:659
  341.9 5.2 collective-permute-start.27
  349.0 4.3 product_sums.2
  354.5 7.1 %collective-permute-done.29 = f32[512]{0:T(512)S(1)} collective-permute-done((f32[512]{0:T(512)S(1)}, f32[512]{0:T(512)S(1)}, u32[]{:S(2)}, u32[]{:S(2)}) %collective-permute-start.29) | collective-permute-done | bytes 2080 | tf_op jit(solution)/shard_map/ppermute | solution.py:41
  370.0 4.8 collective-permute-start.32
  374.9 7.7 %product_blocks.4 = (f32[512,512]{1,0:T(8,128)}, f32[512,512]{1,0:T(8,128)}, f32[512,512]{1,0:T(8,128)}, f32[512,512]{1,0:T(8,128)}) custom-call(s32[4]{0:T(128)} %copy-done.12, bf16[512,1536]{1,0:T(8,128)(2,1)} %get-tuple-element.160.left_ref.refs_0_, bf16[1536,2048]{1,0:T(8,128)(2,1)} %refs_1_.1), custom_call_target="tpu_custom_call" | custom-call | flops 1000 | bytes 1000 | tf_op jit(solution)/shard_map/product_blocks/pallas_call | solution.py:558
  382.6 9.6 %collective-permute-done.32 = f32[512,512]{1,0:T(8,128)S(1)} collective-permute-done((f32[512,512]{1,0:T(8,128)S(1)}, f32[512,512]{1,0:T(8,128)S(1)}, u32[]{:S(2)}, u32[]{:S(2)}) %collective-permute-start.32) | collective-permute-done | bytes 1048608 | tf_op jit(solution)/shard_map/ppermute | solution.py:41
  398.2 18.8 %collective-permute-done.33 = f32[512,512]{1,0:T(8,128)S(1)} collective-permute-done((f32[512,512]{1,0:T(8,128)S(1)}, f32[512,512]{1,0:T(8,128)S(1)}, u32[]{:S(2)}, u32[]{:S(2)}) %collective-permute-start.33) | collective-permute-done | bytes 1048608 | tf_op jit(solution)/shard_map/ppermute | solution.py:41
  417.0 4.4 collective-permute-start.37
  424.4 11.6 %collective-permute-done.37 = f32[512,512]{1,0:T(8,128)S(1)} collective-permute-done((f32[512,512]{1,0:T(8,128)S(1)}, f32[512,512]{1,0:T(8,128)S(1)}, u32[]{:S(2)}, u32[]{:S(2)}) %collective-permute-start.37) | collective-permute-done | bytes 1048608 | tf_op jit(solution)/shard_map/ppermute | solution.py:41
  441.5 7.1 %collective-permute-start.40 = (f32[512,512]{1,0:T(8,128)}, f32[512,512]{1,0:T(8,128)}, u32[]{:S(2)}, u32[]{:S(2)}) collective-permute-start(f32[512,512]{1,0:T(8,128)} %get-tuple-element.171), channel_id=1, source_target_pairs={{0,1},{3,2},{4,5},{7,6},{8,9},{11,10},{12,13},{15,14},{16,17},{19,... | collective-permute-start | bytes 3145736 | tf_op jit(solution)/shard_map/ppermute | solution.py:41
  452.7 8.8 %collective-permute-done.40 = f32[512,512]{1,0:T(8,128)} collective-permute-done((f32[512,512]{1,0:T(8,128)}, f32[512,512]{1,0:T(8,128)}, u32[]{:S(2)}, u32[]{:S(2)}) %collective-permute-start.40) | collective-permute-done | bytes 1048608 | tf_op jit(solution)/shard_map/ppermute | solution.py:41
  464.3 7.0 %collective-permute-start.41 = (f32[512,512]{1,0:T(8,128)}, f32[512,512]{1,0:T(8,128)}, u32[]{:S(2)}, u32[]{:S(2)}) collective-permute-start(f32[512,512]{1,0:T(8,128)} %add.261), channel_id=1, source_target_pairs={{0,1},{1,0},{2,3},{3,2},{4,5},{5,4},{6,7},{7,6},{8,9},{9,8},{10,11... | collective-permute-start | bytes 3145736 | tf_op jit(solution)/shard_map/ppermute | solution.py:41
  476.9 4.1 recurrence_turn.1
  483.0 11.0 %all-gather.2.ends_ref = f32[8,2,640]{2,1,0:T(2,128)} all-gather(f32[1,2,640]{2,1,0:T(2,128)S(1)} %bitcast.41), channel_id=3, replica_groups=mesh['seq'=8,'mp'=4] {'seq'}, dimensions={0}, use_global_device_ids=true | all-gather | bytes 46080 | tf_op jit(solution)/shard_map/all_gather | solution.py:835
  494.0 13.6 %recurrence_backward.1 = (bf16[512,640]{1,0:T(8,128)(2,1)}, f32[16,640]{1,0:T(8,128)}, f32[8,640]{1,0:T(8,128)}, f32[2,328,320]{2,1,0:T(8,128)}) custom-call(s32[1]{0:T(128)} %bitcast.mine_ref, f32[8,2,640]{2,1,0:T(2,128)} %all-gather.2.ends_ref, f32[512,640]{1,0:T(8,128)} %copy-done.9, f32[512,640]{1,0:T(8,128)} %get-tuple-element.180.alpha_ref, ...), custom_call_target="tpu_custom_call" | custom-call | flops 1000 | bytes 1000 | tf_op jit(solution)/shard_map/recurrence_backward/pallas_call | solution.py:605
  507.6 4.7 rows_product.3
  516.6 7.6 %product_blocks.5 = (f32[512,512]{1,0:T(8,128)}, f32[512,512]{1,0:T(8,128)}, f32[512,512]{1,0:T(8,128)}, f32[512,512]{1,0:T(8,128)}) custom-call(s32[4]{0:T(128)} %copy-done.12, bf16[512,640]{1,0:T(8,128)(2,1)} %fusion.45.refs_0_, bf16[512,640]{1,0:T(8,128)(2,1)} %copy-done.8, bf16[2048,640]{1,0:T(8,128)(2,1)} %refs_2_.3, bf16[2048,640]{1,0:T(8,128)(2,1)} %refs_3_.3), custom_call_target="tpu_custom_call" | custom-call | flops 1000 | bytes 1000 | tf_op jit(solution)/shard_map/product_blocks/pallas_call | solution.py:558
  527.3 10.2 %columns_product.3 = f32[2048,1280]{1,0:T(8,128)} custom-call(s32[8]{0:T(128)} %constant.56.clone.ring_ref, bf16[512,2048]{1,0:T(8,128)(2,1)} %copy-done.15, bf16[512,640]{1,0:T(8,128)(2,1)} %fusion.45.refs_0_, bf16[512,640]{1,0:T(8,128)(2,1)} %copy-done.8), custom_call_target="tpu_custom_call" | custom-call | flops 1000 | bytes 1000 | tf_op jit(solution)/shard_map/columns_product/pallas_call | solution.py:659
  537.5 12.7 %collective-permute-done.44 = f32[512,512]{1,0:T(8,128)S(1)} collective-permute-done((f32[512,512]{1,0:T(8,128)}, f32[512,512]{1,0:T(8,128)S(1)}, u32[]{:S(2)}, u32[]{:S(2)}) %collective-permute-start.44) | collective-permute-done | bytes 1048608 | tf_op jit(solution)/shard_map/ppermute | solution.py:41
  550.2 4.2 product_sums.3
  564.1 6.3 collective-permute-start.47
  573.1 17.8 %collective-permute-done.49 = f32[328,320]{1,0:T(8,128)S(1)} collective-permute-done((f32[328,320]{1,0:T(8,128)S(1)}, f32[328,320]{1,0:T(8,128)S(1)}, u32[]{:S(2)}, u32[]{:S(2)}) %collective-permute-start.49) | collective-permute-done | bytes 419872 | tf_op jit(solution)/shard_map/ppermute | solution.py:115
  609.6 13.0 %collective-permute-done.56 = f32[4096]{0:T(1024)S(1)} collective-permute-done((f32[4096]{0:T(1024)S(1)}, f32[4096]{0:T(1024)S(1)}, u32[]{:S(2)}, u32[]{:S(2)}) %collective-permute-start.56) | collective-permute-done | bytes 16416 | tf_op jit(solution)/shard_map/ppermute | solution.py:115
  (312 shorter events, 146.4 us)
Async XLA Ops:
  7.2 441.5 %reduce-scatter.5.cloned.1.call-start = ((), (), s32[]{:S(2)}) async-start(), calls=%async_computation.4 | async-start | bytes 14155776 | tf_op jit(solution)/shard_map/reduce_scatter | solution.py:646
  7.2 11.6 %collective-permute-start.3 = (f32[512,512]{1,0:T(8,128)}, f32[512,512]{1,0:T(8,128)S(1)}, u32[]{:S(2)}, u32[]{:S(2)}) collective-permute-start(f32[512,512]{1,0:T(8,128)} %param.20), channel_id=1, source_target_pairs={{1,2},{2,1},{5,6},{6,5},{9,10},{10,9},{13,14},{14,13},{17,18},{18,... | collective-permute-start | bytes 3145736 | tf_op jit(solution)/shard_map/ppermute | solution.py:41
  8.0 29.0 %collective-permute-start.2 = (f32[512,512]{1,0:T(8,128)}, f32[512,512]{1,0:T(8,128)S(1)}, u32[]{:S(2)}, u32[]{:S(2)}) collective-permute-start(f32[512,512]{1,0:T(8,128)} %param.20), channel_id=1, source_target_pairs={{0,1},{1,0},{2,3},{3,2},{4,5},{5,4},{6,7},{7,6},{8,9},{9,8},{10,11... | collective-permute-start | bytes 3145736 | tf_op jit(solution)/shard_map/ppermute | solution.py:41
  14.6 33.9 %collective-permute-start.6 = (f32[8]{0:T(128)S(1)}, f32[8]{0:T(128)S(1)}, u32[]{:S(2)}, u32[]{:S(2)}) collective-permute-start(f32[8]{0:T(128)S(1)} %slice.113), channel_id=1, source_target_pairs={{0,4},{4,8},{8,12},{12,16},{16,20},{20,24},{24,28},{1,5},{5,9},{9,... | collective-permute-start | bytes 104 | tf_op jit(solution)/shard_map/ppermute | solution.py:736
  17.4 32.7 %collective-permute-start = (f32[512]{0:T(512)S(1)}, f32[512]{0:T(512)S(1)}, u32[]{:S(2)}, u32[]{:S(2)}) collective-permute-start(f32[512]{0:T(512)S(1)} %multiply_reduce_fusion.1), channel_id=1, source_target_pairs={{0,1},{1,0},{2,3},{3,2},{4,5},{5,4},{6,7},{7,6},{8,9},{9,8},{10,11... | collective-permute-start | bytes 6152 | tf_op jit(solution)/shard_map/ppermute | solution.py:41
  36.9 26.0 %collective-permute-start.4 = (f32[512,512]{1,0:T(8,128)S(1)}, f32[512,512]{1,0:T(8,128)}, u32[]{:S(2)}, u32[]{:S(2)}) collective-permute-start(f32[512,512]{1,0:T(8,128)S(1)} %collective-permute-done.3), channel_id=1, source_target_pairs={{1,0},{2,3},{5,4},{6,7},{9,8},{10,11},{13,12},{14,15},{17,16},{18,... | collective-permute-start | bytes 3145736 | tf_op jit(solution)/shard_map/ppermute | solution.py:41
  38.2 24.7 %collective-permute-start.5 = (f32[512,512]{1,0:T(8,128)S(1)}, f32[512,512]{1,0:T(8,128)}, u32[]{:S(2)}, u32[]{:S(2)}) collective-permute-start(f32[512,512]{1,0:T(8,128)S(1)} %collective-permute-done.2), channel_id=1, source_target_pairs={{1,2},{2,1},{5,6},{6,5},{9,10},{10,9},{13,14},{14,13},{17,18},{18,... | collective-permute-start | bytes 3145736 | tf_op jit(solution)/shard_map/ppermute | solution.py:41
  50.0 16.9 %collective-permute-start.1 = (f32[512]{0:T(512)S(1)}, f32[512]{0:T(512)S(1)}, u32[]{:S(2)}, u32[]{:S(2)}) collective-permute-start(f32[512]{0:T(512)S(1)} %add.226), channel_id=1, source_target_pairs={{0,2},{2,0},{1,3},{3,1},{4,6},{6,4},{5,7},{7,5},{8,10},{10,8},{9,1... | collective-permute-start | bytes 6152 | tf_op jit(solution)/shard_map/ppermute | solution.py:41
  62.9 27.3 %collective-permute-start.7 = (f32[512,512]{1,0:T(8,128)}, f32[512,512]{1,0:T(8,128)}, u32[]{:S(2)}, u32[]{:S(2)}) collective-permute-start(f32[512,512]{1,0:T(8,128)} %collective-permute-done.5), channel_id=1, source_target_pairs={{1,0},{2,3},{5,4},{6,7},{9,8},{10,11},{13,12},{14,15},{17,16},{18,... | collective-permute-start | bytes 3145736 | tf_op jit(solution)/shard_map/ppermute | solution.py:41
  90.2 33.2 %collective-permute-start.10 = (f32[512,512]{1,0:T(8,128)}, f32[512,512]{1,0:T(8,128)}, u32[]{:S(2)}, u32[]{:S(2)}) collective-permute-start(f32[512,512]{1,0:T(8,128)} %param.37), channel_id=1, source_target_pairs={{1,2},{2,1},{5,6},{6,5},{9,10},{10,9},{13,14},{14,13},{17,18},{18,... | collective-permute-start | bytes 3145736 | tf_op jit(solution)/shard_map/ppermute | solution.py:41
  91.9 31.6 %collective-permute-start.9 = (f32[512,512]{1,0:T(8,128)}, f32[512,512]{1,0:T(8,128)}, u32[]{:S(2)}, u32[]{:S(2)}) collective-permute-start(f32[512,512]{1,0:T(8,128)} %param.37), channel_id=1, source_target_pairs={{0,1},{1,0},{2,3},{3,2},{4,5},{5,4},{6,7},{7,6},{8,9},{9,8},{10,11... | collective-permute-start | bytes 3145736 | tf_op jit(solution)/shard_map/ppermute | solution.py:41
  129.4 26.5 %collective-permute-start.11 = (f32[512,512]{1,0:T(8,128)S(1)}, f32[512,512]{1,0:T(8,128)S(1)}, u32[]{:S(2)}, u32[]{:S(2)}) collective-permute-start(f32[512,512]{1,0:T(8,128)S(1)} %get-tuple-element.128), channel_id=1, source_target_pairs={{0,1},{3,2},{4,5},{7,6},{8,9},{11,10},{12,13},{15,14},{16,17},{19,... | collective-permute-start | bytes 3145736 | tf_op jit(solution)/shard_map/ppermute | solution.py:41
  133.1 23.1 %collective-permute-start.12 = (f32[512,512]{1,0:T(8,128)}, f32[512,512]{1,0:T(8,128)S(1)}, u32[]{:S(2)}, u32[]{:S(2)}) collective-permute-start(f32[512,512]{1,0:T(8,128)} %collective-permute-done.9), channel_id=1, source_target_pairs={{1,2},{2,1},{5,6},{6,5},{9,10},{10,9},{13,14},{14,13},{17,18},{18,... | collective-permute-start | bytes 3145736 | tf_op jit(solution)/shard_map/ppermute | solution.py:41
  133.9 27.2 %collective-permute-start.13 = (f32[512,512]{1,0:T(8,128)}, f32[512,512]{1,0:T(8,128)S(1)}, u32[]{:S(2)}, u32[]{:S(2)}) collective-permute-start(f32[512,512]{1,0:T(8,128)} %collective-permute-done.10), channel_id=1, source_target_pairs={{1,0},{2,3},{5,4},{6,7},{9,8},{10,11},{13,12},{14,15},{17,16},{18,... | collective-permute-start | bytes 3145736 | tf_op jit(solution)/shard_map/ppermute | solution.py:41
  161.1 23.4 %collective-permute-start.14 = (f32[512,512]{1,0:T(8,128)S(1)}, f32[512,512]{1,0:T(8,128)S(1)}, u32[]{:S(2)}, u32[]{:S(2)}) collective-permute-start(f32[512,512]{1,0:T(8,128)S(1)} %get-tuple-element.131), channel_id=1, source_target_pairs={{0,1},{3,2},{4,5},{7,6},{8,9},{11,10},{12,13},{15,14},{16,17},{19,... | collective-permute-start | bytes 3145736 | tf_op jit(solution)/shard_map/ppermute | solution.py:41
  162.7 22.0 %collective-permute-start.15 = (f32[512,512]{1,0:T(8,128)S(1)}, f32[512,512]{1,0:T(8,128)S(1)}, u32[]{:S(2)}, u32[]{:S(2)}) collective-permute-start(f32[512,512]{1,0:T(8,128)S(1)} %add.236), channel_id=1, source_target_pairs={{1,2},{2,1},{5,6},{6,5},{9,10},{10,9},{13,14},{14,13},{17,18},{18,... | collective-permute-start | bytes 3145736 | tf_op jit(solution)/shard_map/ppermute | solution.py:41
  163.5 25.9 %collective-permute-start.16 = (f32[512,512]{1,0:T(8,128)S(1)}, f32[512,512]{1,0:T(8,128)S(1)}, u32[]{:S(2)}, u32[]{:S(2)}) collective-permute-start(f32[512,512]{1,0:T(8,128)S(1)} %collective-permute-done.12), channel_id=1, source_target_pairs={{1,0},{2,3},{5,4},{6,7},{9,8},{10,11},{13,12},{14,15},{17,16},{18,... | collective-permute-start | bytes 3145736 | tf_op jit(solution)/shard_map/ppermute | solution.py:41
  190.3 23.2 %collective-permute-start.18 = (f32[512,512]{1,0:T(8,128)S(1)}, f32[512,512]{1,0:T(8,128)S(1)}, u32[]{:S(2)}, u32[]{:S(2)}) collective-permute-start(f32[512,512]{1,0:T(8,128)S(1)} %add.238), channel_id=1, source_target_pairs={{0,1},{1,0},{2,3},{3,2},{4,5},{5,4},{6,7},{7,6},{8,9},{9,8},{10,11... | collective-permute-start | bytes 3145736 | tf_op jit(solution)/shard_map/ppermute | solution.py:41
  213.9 18.9 %collective-permute-start.22 = (f32[512,512]{1,0:T(8,128)S(1)}, f32[512,512]{1,0:T(8,128)S(1)}, u32[]{:S(2)}, u32[]{:S(2)}) collective-permute-start(f32[512,512]{1,0:T(8,128)S(1)} %get-tuple-element.204), channel_id=1, source_target_pairs={{1,2},{2,1},{5,6},{6,5},{9,10},{10,9},{13,14},{14,13},{17,18},{18,... | collective-permute-start | bytes 3145736 | tf_op jit(solution)/shard_map/ppermute | solution.py:41
  214.6 23.6 %collective-permute-start.21 = (f32[512,512]{1,0:T(8,128)S(1)}, f32[512,512]{1,0:T(8,128)S(1)}, u32[]{:S(2)}, u32[]{:S(2)}) collective-permute-start(f32[512,512]{1,0:T(8,128)S(1)} %get-tuple-element.204), channel_id=1, source_target_pairs={{0,1},{1,0},{2,3},{3,2},{4,5},{5,4},{6,7},{7,6},{8,9},{9,8},{10,11... | collective-permute-start | bytes 3145736 | tf_op jit(solution)/shard_map/ppermute | solution.py:41
  238.2 22.9 %collective-permute-start.23 = (f32[512,512]{1,0:T(8,128)S(1)}, f32[512,512]{1,0:T(8,128)S(1)}, u32[]{:S(2)}, u32[]{:S(2)}) collective-permute-start(f32[512,512]{1,0:T(8,128)S(1)} %collective-permute-done.22), channel_id=1, source_target_pairs={{1,0},{2,3},{5,4},{6,7},{9,8},{10,11},{13,12},{14,15},{17,16},{18,... | collective-permute-start | bytes 3145736 | tf_op jit(solution)/shard_map/ppermute | solution.py:41
  239.5 21.7 %collective-permute-start.24 = (f32[512,512]{1,0:T(8,128)S(1)}, f32[512,512]{1,0:T(8,128)S(1)}, u32[]{:S(2)}, u32[]{:S(2)}) collective-permute-start(f32[512,512]{1,0:T(8,128)S(1)} %collective-permute-done.21), channel_id=1, source_target_pairs={{1,2},{2,1},{5,6},{6,5},{9,10},{10,9},{13,14},{14,13},{17,18},{18,... | collective-permute-start | bytes 3145736 | tf_op jit(solution)/shard_map/ppermute | solution.py:41
  240.2 20.9 %collective-permute-start.19 = (f32[512]{0:T(512)S(1)}, f32[512]{0:T(512)S(1)}, u32[]{:S(2)}, u32[]{:S(2)}) collective-permute-start(f32[512]{0:T(512)S(1)} %get-tuple-element.223), channel_id=1, source_target_pairs={{0,1},{1,0},{2,3},{3,2},{4,5},{5,4},{6,7},{7,6},{8,9},{9,8},{10,11... | collective-permute-start | bytes 6152 | tf_op jit(solution)/shard_map/ppermute | solution.py:41
  261.1 23.0 %collective-permute-start.25 = (f32[512,512]{1,0:T(8,128)S(1)}, f32[512,512]{1,0:T(8,128)S(1)}, u32[]{:S(2)}, u32[]{:S(2)}) collective-permute-start(f32[512,512]{1,0:T(8,128)S(1)} %collective-permute-done.24), channel_id=1, source_target_pairs={{1,0},{2,3},{5,4},{6,7},{9,8},{10,11},{13,12},{14,15},{17,16},{18,... | collective-permute-start | bytes 3145736 | tf_op jit(solution)/shard_map/ppermute | solution.py:41
  307.3 217.0 %reduce-scatter.7.cloned.1.call-start = ((), (), s32[]{:S(2)}) async-start(), calls=%async_computation.5 | async-start | bytes 28311552 | tf_op jit(solution)/shard_map/reduce_scatter | solution.py:646
  321.7 17.8 %collective-permute-start.26 = (f32[512,512]{1,0:T(8,128)}, f32[512,512]{1,0:T(8,128)S(1)}, u32[]{:S(2)}, u32[]{:S(2)}) collective-permute-start(f32[512,512]{1,0:T(8,128)} %get-tuple-element.152.refs_0_), channel_id=1, source_target_pairs={{0,1},{3,2},{4,5},{7,6},{8,9},{11,10},{12,13},{15,14},{16,17},{19,... | collective-permute-start | bytes 3145736 | tf_op jit(solution)/shard_map/ppermute | solution.py:41
  340.4 221.9 %reduce-scatter.9.cloned.1.call-start = ((), (), s32[]{:S(2)}) async-start(), calls=%async_computation.6 | async-start | bytes 5898240 | tf_op jit(solution)/shard_map/reduce_scatter | solution.py:646
  341.9 24.2 %collective-permute-start.27 = (f32[512,512]{1,0:T(8,128)}, f32[512,512]{1,0:T(8,128)}, u32[]{:S(2)}, u32[]{:S(2)}) collective-permute-start(f32[512,512]{1,0:T(8,128)} %get-tuple-element.149.refs_1_), channel_id=1, source_target_pairs={{0,1},{3,2},{4,5},{7,6},{8,9},{11,10},{12,13},{15,14},{16,17},{19,... | collective-permute-start | bytes 3145736 | tf_op jit(solution)/shard_map/ppermute | solution.py:41
  347.1 20.7 %collective-permute-start.28 = (f32[512,512]{1,0:T(8,128)S(1)}, f32[512,512]{1,0:T(8,128)}, u32[]{:S(2)}, u32[]{:S(2)}) collective-permute-start(f32[512,512]{1,0:T(8,128)S(1)} %add.249), channel_id=1, source_target_pairs={{1,2},{2,1},{5,6},{6,5},{9,10},{10,9},{13,14},{14,13},{17,18},{18,... | collective-permute-start | bytes 3145736 | tf_op jit(solution)/shard_map/ppermute | solution.py:41
  369.3 13.3 %collective-permute-start.31 = (f32[512,512]{1,0:T(8,128)S(1)}, f32[512,512]{1,0:T(8,128)S(1)}, u32[]{:S(2)}, u32[]{:S(2)}) collective-permute-start(f32[512,512]{1,0:T(8,128)S(1)} %add.250), channel_id=1, source_target_pairs={{1,2},{2,1},{5,6},{6,5},{9,10},{10,9},{13,14},{14,13},{17,18},{18,... | collective-permute-start | bytes 3145736 | tf_op jit(solution)/shard_map/ppermute | solution.py:41
  370.0 22.2 %collective-permute-start.32 = (f32[512,512]{1,0:T(8,128)S(1)}, f32[512,512]{1,0:T(8,128)S(1)}, u32[]{:S(2)}, u32[]{:S(2)}) collective-permute-start(f32[512,512]{1,0:T(8,128)S(1)} %add.251), channel_id=1, source_target_pairs={{0,1},{1,0},{2,3},{3,2},{4,5},{5,4},{6,7},{7,6},{8,9},{9,8},{10,11... | collective-permute-start | bytes 3145736 | tf_op jit(solution)/shard_map/ppermute | solution.py:41
  395.2 21.8 %collective-permute-start.33 = (f32[512,512]{1,0:T(8,128)S(1)}, f32[512,512]{1,0:T(8,128)S(1)}, u32[]{:S(2)}, u32[]{:S(2)}) collective-permute-start(f32[512,512]{1,0:T(8,128)S(1)} %get-tuple-element.165), channel_id=1, source_target_pairs={{0,1},{1,0},{2,3},{3,2},{4,5},{5,4},{6,7},{7,6},{8,9},{9,8},{10,11... | collective-permute-start | bytes 3145736 | tf_op jit(solution)/shard_map/ppermute | solution.py:41
  417.0 19.0 %collective-permute-start.37 = (f32[512,512]{1,0:T(8,128)S(1)}, f32[512,512]{1,0:T(8,128)S(1)}, u32[]{:S(2)}, u32[]{:S(2)}) collective-permute-start(f32[512,512]{1,0:T(8,128)S(1)} %copy-done.37), channel_id=1, source_target_pairs={{0,1},{3,2},{4,5},{7,6},{8,9},{11,10},{12,13},{15,14},{16,17},{19,... | collective-permute-start | bytes 3145736 | tf_op jit(solution)/shard_map/ppermute | solution.py:41
  421.5 18.4 %collective-permute-start.35 = (f32[512,512]{1,0:T(8,128)S(1)}, f32[512,512]{1,0:T(8,128)S(1)}, u32[]{:S(2)}, u32[]{:S(2)}) collective-permute-start(f32[512,512]{1,0:T(8,128)S(1)} %collective-permute-done.34), channel_id=1, source_target_pairs={{1,0},{2,3},{5,4},{6,7},{9,8},{10,11},{13,12},{14,15},{17,16},{18,... | collective-permute-start | bytes 3145736 | tf_op jit(solution)/shard_map/ppermute | solution.py:41
  422.8 25.9 %collective-permute-start.36 = (f32[512,512]{1,0:T(8,128)S(1)}, f32[512,512]{1,0:T(8,128)}, u32[]{:S(2)}, u32[]{:S(2)}) collective-permute-start(f32[512,512]{1,0:T(8,128)S(1)} %collective-permute-done.33), channel_id=1, source_target_pairs={{1,2},{2,1},{5,6},{6,5},{9,10},{10,9},{13,14},{14,13},{17,18},{18,... | collective-permute-start | bytes 3145736 | tf_op jit(solution)/shard_map/ppermute | solution.py:41
  441.5 20.0 %collective-permute-start.40 = (f32[512,512]{1,0:T(8,128)}, f32[512,512]{1,0:T(8,128)}, u32[]{:S(2)}, u32[]{:S(2)}) collective-permute-start(f32[512,512]{1,0:T(8,128)} %get-tuple-element.171), channel_id=1, source_target_pairs={{0,1},{3,2},{4,5},{7,6},{8,9},{11,10},{12,13},{15,14},{16,17},{19,... | collective-permute-start | bytes 3145736 | tf_op jit(solution)/shard_map/ppermute | solution.py:41
  448.6 26.7 %collective-permute-start.38 = (f32[512,512]{1,0:T(8,128)}, f32[512,512]{1,0:T(8,128)S(1)}, u32[]{:S(2)}, u32[]{:S(2)}) collective-permute-start(f32[512,512]{1,0:T(8,128)} %collective-permute-done.36), channel_id=1, source_target_pairs={{1,0},{2,3},{5,4},{6,7},{9,8},{10,11},{13,12},{14,15},{17,16},{18,... | collective-permute-start | bytes 3145736 | tf_op jit(solution)/shard_map/ppermute | solution.py:41
  464.3 29.7 %collective-permute-start.41 = (f32[512,512]{1,0:T(8,128)}, f32[512,512]{1,0:T(8,128)}, u32[]{:S(2)}, u32[]{:S(2)}) collective-permute-start(f32[512,512]{1,0:T(8,128)} %add.261), channel_id=1, source_target_pairs={{0,1},{1,0},{2,3},{3,2},{4,5},{5,4},{6,7},{7,6},{8,9},{9,8},{10,11... | collective-permute-start | bytes 3145736 | tf_op jit(solution)/shard_map/ppermute | solution.py:41
  471.3 22.7 %collective-permute-start.42 = (f32[512,512]{1,0:T(8,128)}, f32[512,512]{1,0:T(8,128)}, u32[]{:S(2)}, u32[]{:S(2)}) collective-permute-start(f32[512,512]{1,0:T(8,128)} %add.260), channel_id=1, source_target_pairs={{1,2},{2,1},{5,6},{6,5},{9,10},{10,9},{13,14},{14,13},{17,18},{18,... | collective-permute-start | bytes 3145736 | tf_op jit(solution)/shard_map/ppermute | solution.py:41
  512.3 116.8 %reduce-scatter.11.cloned.1.call-start = ((), (), s32[]{:S(2)}) async-start(), calls=%async_computation.7 | async-start | bytes 11796480 | tf_op jit(solution)/shard_map/reduce_scatter | solution.py:646
  524.2 26.0 %collective-permute-start.44 = (f32[512,512]{1,0:T(8,128)}, f32[512,512]{1,0:T(8,128)S(1)}, u32[]{:S(2)}, u32[]{:S(2)}) collective-permute-start(f32[512,512]{1,0:T(8,128)} %get-tuple-element.195.refs_0_), channel_id=1, source_target_pairs={{0,1},{3,2},{4,5},{7,6},{8,9},{11,10},{12,13},{15,14},{16,17},{19,... | collective-permute-start | bytes 3145736 | tf_op jit(solution)/shard_map/ppermute | solution.py:41
  562.3 28.7 %collective-permute-start.46 = (f32[512,512]{1,0:T(8,128)}, f32[512,512]{1,0:T(8,128)}, u32[]{:S(2)}, u32[]{:S(2)}) collective-permute-start(f32[512,512]{1,0:T(8,128)} %add.263), channel_id=1, source_target_pairs={{1,2},{2,1},{5,6},{6,5},{9,10},{10,9},{13,14},{14,13},{17,18},{18,... | collective-permute-start | bytes 3145736 | tf_op jit(solution)/shard_map/ppermute | solution.py:41
  564.1 27.6 %collective-permute-start.47 = (f32[512,512]{1,0:T(8,128)S(1)}, f32[512,512]{1,0:T(8,128)}, u32[]{:S(2)}, u32[]{:S(2)}) collective-permute-start(f32[512,512]{1,0:T(8,128)S(1)} %copy-done.25), channel_id=1, source_target_pairs={{0,1},{3,2},{4,5},{7,6},{8,9},{11,10},{12,13},{15,14},{16,17},{19,... | collective-permute-start | bytes 3145736 | tf_op jit(solution)/shard_map/ppermute | solution.py:41
  571.7 19.2 %collective-permute-start.49 = (f32[328,320]{1,0:T(8,128)S(1)}, f32[328,320]{1,0:T(8,128)S(1)}, u32[]{:S(2)}, u32[]{:S(2)}) collective-permute-start(f32[328,320]{1,0:T(8,128)S(1)} %bitcast_add_fusion), channel_id=1, source_target_pairs={{0,8},{4,12},{8,0},{12,4},{16,24},{20,28},{24,16},{28,20},{1,9},{5... | collective-permute-start | bytes 1259528 | tf_op jit(solution)/shard_map/ppermute | solution.py:115
  597.1 26.6 %collective-permute-start.50 = (f32[512,512]{1,0:T(8,128)S(1)}, f32[512,512]{1,0:T(8,128)S(1)}, u32[]{:S(2)}, u32[]{:S(2)}) collective-permute-start(f32[512,512]{1,0:T(8,128)S(1)} %add.268), channel_id=1, source_target_pairs={{1,2},{2,1},{5,6},{6,5},{9,10},{10,9},{13,14},{14,13},{17,18},{18,... | collective-permute-start | bytes 3145736 | tf_op jit(solution)/shard_map/ppermute | solution.py:41
  597.8 24.9 %collective-permute-start.51 = (f32[512,512]{1,0:T(8,128)S(1)}, f32[512,512]{1,0:T(8,128)S(1)}, u32[]{:S(2)}, u32[]{:S(2)}) collective-permute-start(f32[512,512]{1,0:T(8,128)S(1)} %add.269), channel_id=1, source_target_pairs={{0,1},{1,0},{2,3},{3,2},{4,5},{5,4},{6,7},{7,6},{8,9},{9,8},{10,11... | collective-permute-start | bytes 3145736 | tf_op jit(solution)/shard_map/ppermute | solution.py:41
  602.2 20.5 %collective-permute-start.53 = (f32[328,320]{1,0:T(8,128)S(1)}, f32[328,320]{1,0:T(8,128)S(1)}, u32[]{:S(2)}, u32[]{:S(2)}) collective-permute-start(f32[328,320]{1,0:T(8,128)S(1)} %add.273), channel_id=1, source_target_pairs={{0,16},{4,20},{8,24},{12,28},{16,0},{20,4},{24,8},{28,12},{1,17},{... | collective-permute-start | bytes 1259528 | tf_op jit(solution)/shard_map/ppermute | solution.py:115
  608.7 14.0 %collective-permute-start.56 = (f32[4096]{0:T(1024)S(1)}, f32[4096]{0:T(1024)S(1)}, u32[]{:S(2)}, u32[]{:S(2)}) collective-permute-start(f32[4096]{0:T(1024)S(1)} %add.280), channel_id=1, source_target_pairs={{0,16},{4,20},{8,24},{12,28},{16,0},{20,4},{24,8},{28,12},{1,17},{... | collective-permute-start | bytes 49160 | tf_op jit(solution)/shard_map/ppermute | solution.py:115
  (73 other events, 1312.5 us)
Sparse Core Ops, SparseCore 0:
  307.4 67.0 reduce-scatter.4
  376.8 128.1 reduce-scatter.6
  512.4 34.4 reduce-scatter.8
  550.3 75.2 reduce-scatter.10

commit v6 on v5

--- a/solution.py
+++ b/solution.py
@@ -13,6 +13,7 @@
 f32 = jnp.float32
 LANES = 128
 SUB = 8
+STEPS = 4
 ROWS = 32
 VMEM_LIMIT = 56 * 1024 * 1024
 VMEM_SMALL = 24 * 1024 * 1024
@@ -186,7 +187,16 @@
     ext_ref, pre_ref,
 ):
     count, width = inner_ref.shape
-    ext_ref[pl.ds(0, SUB), :] = halo_ref[...]
+
+    @pl.when(pl.program_id(0) == 0)
+    def _():
+        ext_ref[pl.ds(0, SUB), :] = halo_ref[...]
+        start = lax.broadcasted_iota(jnp.int32, (SUB, width), 0) == 0
+        last_ref[...] = jnp.where(start, 1.0, 0.0)
+
+    @pl.when(pl.program_id(0) > 0)
+    def _():
+        ext_ref[pl.ds(0, SUB), :] = ext_ref[pl.ds(count, SUB), :]
 
     def fill(i, _):
         r = pl.multiple_of(i * ROWS, ROWS)
@@ -200,7 +210,7 @@
         window = ext_ref[pl.ds(r, ROWS + SUB), :]
         total = row_ref[0:1, :] * window[SUB:]
         for k in range(1, 4):
-            valid = wide(valid_ref[k, pl.ds(r + SUB, ROWS), :], width)
+            valid = wide(valid_ref[k, pl.ds(r, ROWS), :], width)
             total = total + row_ref[k : k + 1, :] * window[SUB - k : SUB - k + ROWS] * valid
         total = total + row_ref[4:5, :]
         conv_ref[pl.ds(r, ROWS), :] = total
@@ -216,7 +226,7 @@
         rg = jax.nn.sigmoid(pre_ref[here, :width] + row_ref[5:6, :])
         ig = jax.nn.sigmoid(pre_ref[here, width:] + row_ref[6:7, :])
         log_a = row_ref[7:8, :] * rg
-        keep = wide(valid_ref[0, pl.ds(r + SUB, ROWS), :], width)
+        keep = wide(valid_ref[0, here, :], width)
         a = jnp.exp(log_a)
         root = jnp.sqrt(neg_expm1(2.0 * log_a, a * a))
         factor = (1.0 - keep) + keep * root
@@ -237,8 +247,9 @@
             state, product = part[SUB - 1 : SUB, :], span[SUB - 1 : SUB, :]
         return state, product
 
-    zero = jnp.zeros((1, width), f32)
-    state, product = lax.fori_loop(0, count // ROWS, scan, (zero, zero + 1.0))
+    state, product = lax.fori_loop(
+        0, count // ROWS, scan, (last_ref[1:2, :], last_ref[0:1, :])
+    )
     last_ref[...] = jnp.concatenate([product, state, jnp.zeros((SUB - 2, width), f32)], 0)
 
 
@@ -333,33 +344,42 @@
 
 
 def backward_kernel(
-    mine_ref, ends_ref, dstates_ref, alpha_ref, states_ref, enter_ref, conv_ref, rg_ref, ig_ref,
-    factor_ref, valid_ref, inner_ref, halo_ref, row_ref, gate_ref,
+    mine_ref, ends_ref, dstates_ref, alpha_ref, states_ref, before_ref, enter_ref, conv_ref,
+    rg_ref, ig_ref, factor_ref, valid_ref, inner_ref, halo_ref, row_ref, gate_ref,
     dinner_ref, tail_ref, head_ref, small_ref,
-    dconv_ref, ext_ref, drec_ref, whole_ref, *, groups,
+    dconv_ref, ext_ref, drec_ref, low_ref, whole_ref, flow_ref, sum_ref, *, groups,
 ):
     devices = ends_ref.shape[0]
-    count, width = alpha_ref.shape
-    blocks = count // ROWS
-    incoming = jnp.zeros((1, width), f32)
-    for d in reversed(range(devices)):
-        ends = ends_ref[d]
-        incoming = jnp.where(d > mine_ref[0], ends[0:1, :] * incoming + ends[1:2, :], incoming)
-    dconv_ref[pl.ds(0, SUB), :] = jnp.zeros((SUB, width), f32)
-    dconv_ref[pl.ds(count + SUB, SUB), :] = jnp.zeros((SUB, width), f32)
-    ext_ref[pl.ds(0, SUB), :] = halo_ref[...]
+    tile, width = alpha_ref.shape
+    step = pl.program_id(0)
+    base = pl.multiple_of((STEPS - 1 - step) * tile, tile)
+
+    @pl.when(step == 0)
+    def _():
+        incoming = jnp.zeros((1, width), f32)
+        for d in reversed(range(devices)):
+            ends = ends_ref[d]
+            incoming = jnp.where(d > mine_ref[0], ends[0:1, :] * incoming + ends[1:2, :], incoming)
+        flow_ref[...] = jnp.broadcast_to(incoming, (SUB, width))
+        sum_ref[...] = jnp.zeros_like(sum_ref)
+        dconv_ref[pl.ds(0, SUB), :] = jnp.zeros((SUB, width), f32)
+        dconv_ref[pl.ds(STEPS * tile + SUB, SUB), :] = jnp.zeros((SUB, width), f32)
+        ext_ref[pl.ds(0, SUB), :] = halo_ref[...]
+
     parts = (ROWS // SUB, SUB, width)
     place = lax.broadcasted_iota(jnp.int32, (SUB, width), 0)
 
     def fold(value):
         return jnp.sum(value.reshape(parts), axis=0)
 
-    def back(step, carry):
+    def back(turn, carry):
         flow, decay, bias_r, bias_i = carry
-        i = blocks - 1 - step
+        i = tile // ROWS - 1 - turn
         r = pl.multiple_of(i * ROWS, ROWS)
         here = pl.ds(r, ROWS)
-        ext_ref[pl.ds(r + SUB, ROWS), :] = inner_ref[here, :]
+        there = pl.ds(pl.multiple_of(base + r, ROWS), ROWS)
+        padded = pl.ds(pl.multiple_of(base + r + SUB, SUB), ROWS)
+        ext_ref[padded, :] = inner_ref[here, :]
         alpha = alpha_ref[here, :]
         dstates = dstates_ref[here, :]
         a3, b3 = group_scan_back(alpha.reshape(parts), (alpha * dstates).reshape(parts))
@@ -371,21 +391,22 @@
             totals[g] = d3[g] + later
             flow = flows[0:1, :]
         total = jnp.concatenate(totals, 0)
-        before = pl.multiple_of(jnp.maximum(r - SUB, 0), SUB)
-        first = jnp.where(i == 0, enter_ref[...], states_ref[pl.ds(before, SUB), :])
-        window = jnp.concatenate([first, states_ref[here, :]], 0)
+        earlier = jnp.where(step == STEPS - 1, enter_ref[...], before_ref[...])
+        inside = states_ref[pl.ds(pl.multiple_of(jnp.maximum(r - SUB, 0), SUB), SUB), :]
+        window = jnp.concatenate([jnp.where(i == 0, earlier, inside), states_ref[here, :]], 0)
         prior = window[SUB - 1 : SUB - 1 + ROWS]
         rg = rg_ref[here, :]
         ig = ig_ref[here, :]
         factor = factor_ref[here, :]
         conv = conv_ref[here, :]
+        low_ref[there, :] = conv.astype(bf16)
         gain = total * factor
-        dconv_ref[pl.ds(r + SUB, ROWS), :] = gain * ig
+        dconv_ref[padded, :] = gain * ig
         dinput = (gain * conv * ig * (1.0 - ig)).astype(bf16)
         dlog = alpha * (total * prior - total * ig * conv * alpha / factor)
         drecur = (dlog * row_ref[7:8, :] * rg * (1.0 - rg)).astype(bf16)
-        drec_ref[here, :width] = drecur
-        drec_ref[here, width:] = dinput
+        drec_ref[there, :width] = drecur
+        drec_ref[there, width:] = dinput
         return (
             flow,
             decay + fold(dlog * rg),
@@ -393,11 +414,35 @@
             bias_i + fold(dinput.astype(f32)),
         )
 
+    flow, *totals = lax.fori_loop(
+        0, tile // ROWS, back, (flow_ref[0:1, :], sum_ref[0], sum_ref[1], sum_ref[2])
+    )
+    flow_ref[...] = jnp.broadcast_to(flow, (SUB, width))
+    for k in range(3):
+        sum_ref[k] = totals[k]
+    dconv_ref[pl.ds(pl.multiple_of(base + SUB, SUB), tile), :] += lax.dot_general(
+        drec_ref[pl.ds(base, tile), :], gate_ref[...], (((1,), (1,)), ((), ())),
+        preferred_element_type=f32,
+    )
+
+    @pl.when(step == STEPS - 1)
+    def _():
+        backward_end(
+            valid_ref, row_ref, dinner_ref, tail_ref, head_ref, small_ref, dconv_ref, ext_ref,
+            drec_ref, low_ref, whole_ref, sum_ref, groups,
+        )
+
+
+def backward_end(
+    valid_ref, row_ref, dinner_ref, tail_ref, head_ref, small_ref, dconv_ref, ext_ref,
+    drec_ref, low_ref, whole_ref, sum_ref, groups,
+):
+    count, width = dinner_ref.shape
+    blocks = count // ROWS
     zero = jnp.zeros((SUB, width), f32)
-    _, decay, bias_r, bias_i = lax.fori_loop(0, blocks, back, (incoming, zero, zero, zero))
-    dconv_ref[pl.ds(SUB, count), :] += lax.dot_general(
-        drec_ref[...], gate_ref[...], (((1,), (1,)), ((), ())), preferred_element_type=f32
-    )
+
+    def fold(value):
+        return jnp.sum(value.reshape(ROWS // SUB, SUB, width), axis=0)
 
     def spread_back(window, r, rows):
         total = row_ref[0:1, :] * window[:rows]
@@ -429,10 +474,10 @@
 
     sums = lax.fori_loop(0, blocks, finish, (zero,) * 5)
     sums = jnp.concatenate(
-        [jnp.sum(s, axis=0, keepdims=True) for s in (*sums, bias_r, bias_i, decay)], 0
+        [jnp.sum(s, axis=0, keepdims=True) for s in (*sums, sum_ref[1], sum_ref[2], sum_ref[0])], 0
     )
     whole_ref[...] = lax.dot_general(
-        conv_ref[...].astype(bf16), drec_ref[...], (((0,), (0,)), ((), ())),
+        low_ref[...], drec_ref[...], (((0,), (0,)), ((), ())),
         preferred_element_type=f32,
     )
     block = width // groups
@@ -469,15 +514,24 @@
 
 def run_forward(inner, halo, valid, rows, gates):
     count, width = inner.shape
+    block = count // STEPS
     full = shape((count, width))
+    tile = pl.BlockSpec((block, width), lambda i: (i, 0))
+    small = pl.BlockSpec((SUB, width), lambda i: (0, 0))
     return pl.pallas_call(
         forward_kernel,
+        grid=(STEPS,),
         out_shape=(full, shape((count, width), bf16)) + (full,) * 6 + (shape((SUB, width)),),
-        in_specs=vmem(5),
-        out_specs=tuple(vmem(9)),
+        in_specs=[
+            tile, small,
+            pl.BlockSpec((4, block, LANES), lambda i: (0, i, 0)),
+            small,
+            pl.BlockSpec(gates.shape, lambda i: (0, 0)),
+        ],
+        out_specs=(tile,) * 8 + (small,),
         scratch_shapes=[
-            pltpu.VMEM((count + SUB, width), f32),
-            pltpu.VMEM((count, 2 * width), f32),
+            pltpu.VMEM((block + SUB, width), f32),
+            pltpu.VMEM((block, 2 * width), f32),
         ],
         compiler_params=pltpu.CompilerParams(vmem_limit_bytes=VMEM_LIMIT),
         cost_estimate=small_cost(),
@@ -602,26 +656,48 @@
 
 def run_backward(mine, ends, dstates, saved, enter, valid, inner, halo, rows, gates, groups):
     count, width = dstates.shape
+    block = count // STEPS
+    groups_of_rows = block // SUB
+    tile = pl.BlockSpec((block, width), lambda j, m: (STEPS - 1 - j, 0))
+    before = pl.BlockSpec(
+        (SUB, width), lambda j, m: (jnp.maximum((STEPS - 1 - j) * groups_of_rows - 1, 0), 0)
+    )
+
+    def whole(dims):
+        return pl.BlockSpec(dims, lambda j, m: (0,) * len(dims))
+
+    small = whole((SUB, width))
+    outs = (
+        ((count, width), bf16), ((2 * SUB, width), f32), ((SUB, width), f32),
+        ((2, width // 2 + SUB * groups // 4, 2 * width // groups), f32),
+    )
     return pl.pallas_call(
         partial(backward_kernel, groups=groups),
-        out_shape=(
-            shape((count, width), bf16), shape((2 * SUB, width)), shape((SUB, width)),
-            shape((2, width // 2 + SUB * groups // 4, 2 * width // groups)),
+        grid_spec=pltpu.PrefetchScalarGridSpec(
+            num_scalar_prefetch=1,
+            grid=(STEPS,),
+            in_specs=[
+                whole(ends.shape), tile, tile, tile, before, small, tile, tile, tile, tile,
+                whole(valid.shape), tile, small, small, whole(gates.shape),
+            ],
+            out_specs=tuple(whole(dims) for dims, _ in outs),
+            scratch_shapes=[
+                pltpu.VMEM((count + 2 * SUB, width), f32),
+                pltpu.VMEM((count + SUB, width), f32),
+                pltpu.VMEM((count, 2 * width), bf16),
+                pltpu.VMEM((count, width), bf16),
+                pltpu.VMEM((width, 2 * width), f32),
+                pltpu.VMEM((SUB, width), f32),
+                pltpu.VMEM((3, SUB, width), f32),
+            ],
         ),
-        in_specs=[pl.BlockSpec(memory_space=pltpu.SMEM)] + vmem(14),
-        out_specs=tuple(vmem(4)),
-        scratch_shapes=[
-            pltpu.VMEM((count + 2 * SUB, width), f32),
-            pltpu.VMEM((count + SUB, width), f32),
-            pltpu.VMEM((count, 2 * width), bf16),
-            pltpu.VMEM((width, 2 * width), f32),
-        ],
+        out_shape=tuple(shape(*out) for out in outs),
         compiler_params=pltpu.CompilerParams(vmem_limit_bytes=VMEM_LIMIT),
         cost_estimate=small_cost(),
         name="recurrence_backward",
     )(
-        mine, ends, dstates, saved["alpha"], saved["states"], enter, saved["conv"], saved["rg"],
-        saved["ig"], saved["factor"], valid, inner, halo, rows, gates,
+        mine, ends, dstates, saved["alpha"], saved["states"], saved["states"], enter,
+        saved["conv"], saved["rg"], saved["ig"], saved["factor"], valid, inner, halo, rows, gates,
     )
 
 
@@ -741,7 +817,7 @@
             (reach[-1] if k > 1 else 1.0) * keep_ext[SUB - k + 1 : SUB - k + 1 + count]
         )
     valid = jnp.broadcast_to(jnp.stack(reach, 0)[:, :, None], (4, count, LANES))
-    valid = jnp.pad(valid, ((0, 0), (SUB, SUB), (0, 0)))
+    valid_pad = jnp.pad(valid, ((0, 0), (SUB, SUB), (0, 0)))
     rows = jnp.stack(
         [
             conv_weight[0], conv_weight[1], conv_weight[2], conv_weight[3], conv_bias, bias_recur,
@@ -751,7 +827,7 @@
     )
     gates = jnp.concatenate([block_diagonal(gate_recur), block_diagonal(gate_input)], 1)
     first.second()
-    first.third(gates, valid)
+    first.third(gates, valid, valid_pad)
 
     def first_turn(piece, start):
         return piece * first_scale * lax.dynamic_slice_in_dim(gain_first, start, own_width)
@@ -835,7 +911,7 @@
     back_ends = after(lax.all_gather(leaving, "seq"), sent.last, sent.near_two)
     saved = dict(alpha=alpha, states=states, conv=conv, rg=rg, ig=ig, factor=factor)
     d_inner_low, tail, head, small = run_backward(
-        seq_at, back_ends, d_states, saved, enter, valid, inner, halo, rows, gates, groups
+        seq_at, back_ends, d_states, saved, enter, valid_pad, inner, halo, rows, gates, groups
     )
     returned = lax.ppermute(head, "seq", backward)
     whole_out = rows_product(after(mixed_low, head), branch_low, 2 * own_width)
@@ -857,14 +933,16 @@
     )
     d_gain_first = gain_sums / gain_first
     first_sums = jnp.concatenate([first_mean, d_gain_first, d_gain_second])
+    core = lax.axis_index("seq") & 1
+    other = lax.dynamic_index_in_dim(small, 1 - core, 0, False)
+    small = lax.dynamic_index_in_dim(small, core, 0, False)
+    whole_first, first_sums, other, small = after(
+        (whole_first, first_sums, other, small), final.far_one
+    )
+    grad_first = ring_scatter(whole_first)
     first_sums = first_sums + over_mp(first_sums, PAIRS)
-    final.second(whole_first, first_sums, grad_out)
-    whole_first = after(whole_first, final.far_one)
-    grad_first = ring_scatter(whole_first)
-    core = lax.axis_index("seq") & 1
-    small = after(small, final.far_one)
-    other = swapped(lax.dynamic_index_in_dim(small, 1 - core, 0, False), "seq", 1)
-    small = lax.dynamic_index_in_dim(small, core, 0, False) + other
+    final.second(first_sums, grad_out)
+    small = small + swapped(other, "seq", 1)
     small = over_chips(small, 2)
     final.third(small)
     first_sums, small = after((first_sums, small), final.far_two, final.near_one)

time: 649 us -> 644 us (level)
    ppermute x48, waiting for transfers between devices: 238 us -> 231 us  [over_mp(): return lax.ppermute(value, 'mp', list(pairs))]
  transfers between devices with their start and end apart: 62 -> 62, of which waited for: 28 -> 30; matrix products, arithmetic and copies ran while one was open for 10% -> 10% of each run, Pallas kernels for 17% -> 16%
where the time goes in v6:
time: 644 us; the launch traced here: 633 us
  waiting for transfers between devices  269 us (42%)
  Pallas kernels  129 us (20%)
  starting transfers between devices  118 us (18%)
  other arithmetic  53.3 us (8%)
  blocking collectives  22.6 us (4%)
  local copies, waits for them, and re-layouts  22.3 us (3%)
  between operations  15.5 us (2%)
    ppermute x48, waiting for transfers between devices, over_mp(): return lax.ppermute(value, 'mp', list(pairs))  231 us
    ppermute x48, starting transfers between devices, over_mp(): return lax.ppermute(value, 'mp', list(pairs))  108 us
    ppermute x7, waiting for transfers between devices, swapped(): return lax.ppermute(value, axis, [(d, d ^ bit) for d in range(count)])  34.1 us
    pallas_call x3, Pallas kernels, product_blocks(): pl.pallas_call(partial(blocks_kernel, pairs=len(lefts), transposed=transp...  29.7 us
    pallas_call x2, Pallas kernels, columns_product(): pl.pallas_call(columns_product_kernel, grid_spec=pltpu.PrefetchScalarGrid...  24.7 us
    pallas_call x1, Pallas kernels, run_backward(): pl.pallas_call(partial(backward_kernel, groups=groups), grid_spec=pltpu.P...  13.5 us
    dynamic_update_slice x16, other arithmetic, assemble(): lax.dynamic_update_slice(whole, turn(piece, start).astype(bf16), (0, start))  13.2 us
    pallas_call x1, Pallas kernels, feed_forward(): pl.pallas_call(feed_forward_kernel, grid=(hidden // block,), in_specs=[pl...  13 us
  transfers between devices with their start and end apart: 62, of which 30 were waited for; matrix products, arithmetic and copies ran while one was open for 10% of the time, Pallas kernels for 16%

profile of v6, /device:TPU:0, one launch (start us, length us, event | category | flops | bytes accessed | tf_op | source)
XLA Modules:
  0.0 633.3 jit_solution(14685268214204309647)
XLA Ops:
  8.0 5.8 collective-permute-start.2
  18.9 18.2 %collective-permute-done.2 = f32[512,512]{1,0:T(8,128)} collective-permute-done((f32[512,512]{1,0:T(8,128)}, f32[512,512]{1,0:T(8,128)}, u32[]{:S(2)}, u32[]{:S(2)}) %collective-permute-start.2) | collective-permute-done | bytes 1048608 | tf_op jit(solution)/shard_map/ppermute | solution.py:42
  40.0 8.4 %fusion.24.gate_ref = bf16[640,1280]{1,0:T(8,128)(2,1)} fusion(bf16[160,160]{1,0:T(8,128)(2,1)S(1)} %get-tuple-element.249, bf16[160,160]{1,0:T(8,128)(2,1)S(1)} %get-tuple-element.250, bf16[160,160]{1,0:T(8,128)(2,1)S(1)} %get-tuple-element.248, bf16[160,160]{1,0:T(8,128)(2,1)S(1)} %get-tuple-element.247, bf16[160,160]{1,0:T(8,128)(2,1)S(1)} %get-tuple-element.263, ...), kind=kLoop, calls=%fused_computation.32 | loop fusion | flops 40960000 | bytes 2048000 | tf_op jit(solution)/shard_map/concatenate | solution.py:828
  50.1 5.4 collective-permute-start.1
  55.6 7.4 %collective-permute-done.4 = f32[512,512]{1,0:T(8,128)} collective-permute-done((f32[512,512]{1,0:T(8,128)S(1)}, f32[512,512]{1,0:T(8,128)}, u32[]{:S(2)}, u32[]{:S(2)}) %collective-permute-start.4) | collective-permute-done | bytes 1048608 | tf_op jit(solution)/shard_map/ppermute | solution.py:42
  70.9 19.7 %collective-permute-done.7 = f32[512,512]{1,0:T(8,128)} collective-permute-done((f32[512,512]{1,0:T(8,128)}, f32[512,512]{1,0:T(8,128)}, u32[]{:S(2)}, u32[]{:S(2)}) %collective-permute-start.7) | collective-permute-done | bytes 1048608 | tf_op jit(solution)/shard_map/ppermute | solution.py:42
  99.9 10.4 %recurrence_forward.1 = (f32[512,640]{1,0:T(8,128)}, bf16[512,640]{1,0:T(8,128)(2,1)}, f32[512,640]{1,0:T(8,128)}, f32[512,640]{1,0:T(8,128)}, f32[512,640]{1,0:...) custom-call(f32[512,640]{1,0:T(8,128)} %copy-done.24, ...), custom_call_target="tpu_custom_call" | custom-call | flops 1000 | bytes 1000 | tf_op jit(solution)/shard_map/recurrence_forward/pallas_call | solution.py:521
  110.3 11.5 %all-gather = f32[64,640]{1,0:T(8,128)S(1)} all-gather(f32[8,640]{1,0:T(8,128)} %get-tuple-element.123), channel_id=2, replica_groups=mesh['seq'=8,'mp'=4] {'seq'}, dimensions={0}, use_global_device_ids=true | all-gather | bytes 184320 | tf_op jit(solution)/shard_map/all_gather | solution.py:845
  127.8 3.7 collective-permute-start.11
  133.5 20.8 %collective-permute-done.11 = f32[512,512]{1,0:T(8,128)S(1)} collective-permute-done((f32[512,512]{1,0:T(8,128)S(1)}, f32[512,512]{1,0:T(8,128)S(1)}, u32[]{:S(2)}, u32[]{:S(2)}) %collective-permute-start.11) | collective-permute-done | bytes 1048608 | tf_op jit(solution)/shard_map/ppermute | solution.py:42
  154.5 4.9 collective-permute-done.13
  163.1 19.7 %collective-permute-done.14 = f32[512,512]{1,0:T(8,128)S(1)} collective-permute-done((f32[512,512]{1,0:T(8,128)S(1)}, f32[512,512]{1,0:T(8,128)S(1)}, u32[]{:S(2)}, u32[]{:S(2)}) %collective-permute-start.14) | collective-permute-done | bytes 1048608 | tf_op jit(solution)/shard_map/ppermute | solution.py:42
  183.3 4.4 collective-permute-done.16
  189.9 21.9 %collective-permute-done.18 = f32[512,512]{1,0:T(8,128)S(1)} collective-permute-done((f32[512,512]{1,0:T(8,128)S(1)}, f32[512,512]{1,0:T(8,128)S(1)}, u32[]{:S(2)}, u32[]{:S(2)}) %collective-permute-start.18) | collective-permute-done | bytes 1048608 | tf_op jit(solution)/shard_map/ppermute | solution.py:42
  213.0 3.7 collective-permute-start.21
  222.5 8.8 %product.1.dhidden_ref = f32[512,1536]{1,0:T(8,128)} custom-call(bf16[512,2048]{1,0:T(8,128)(2,1)} %copy-done.16, bf16[1536,2048]{1,0:T(8,128)(2,1)} %refs_1_.1), custom_call_target="tpu_custom_call" | custom-call | flops 1000 | bytes 1000 | tf_op jit(solution)/shard_map/product/pallas_call | solution.py:645
  231.3 5.3 collective-permute-done.21
  238.6 4.4 collective-permute-start.19
  243.0 16.5 %collective-permute-done.19 = f32[512]{0:T(512)S(1)} collective-permute-done((f32[512]{0:T(512)S(1)}, f32[512]{0:T(512)S(1)}, u32[]{:S(2)}, u32[]{:S(2)}) %collective-permute-start.19) | collective-permute-done | bytes 2080 | tf_op jit(solution)/shard_map/ppermute | solution.py:42
  265.7 16.8 %collective-permute-done.25 = f32[512,512]{1,0:T(8,128)S(1)} collective-permute-done((f32[512,512]{1,0:T(8,128)S(1)}, f32[512,512]{1,0:T(8,128)S(1)}, u32[]{:S(2)}, u32[]{:S(2)}) %collective-permute-start.25) | collective-permute-done | bytes 1048608 | tf_op jit(solution)/shard_map/ppermute | solution.py:42
  284.1 13.0 %feed_forward.1 = (bf16[512,1536]{1,0:T(8,128)(2,1)}, bf16[512,1536]{1,0:T(8,128)(2,1)}, bf16[512,1536]{1,0:T(8,128)(2,1)}) custom-call(bf16[512,2048]{1,0:T(8,128)(2,1)} %copy-done.14, bf16[2048,1536]{1,0:T(8,128)(2,1)} %refs_2_.2, bf16[2048,1536]{1,0:T(8,128)(2,1)} %refs_3_.2, f32[512,1536]{1,0:T(8,128)} %product.1.dhidden_ref), custom_call_target="tpu_custom_call" | custom-call | flops 1000 | bytes 1000 | tf_op jit(solution)/shard_map/feed_forward/pallas_call | solution.py:597
  297.1 8.4 %rows_product.2 = f32[1536,2048]{1,0:T(8,128)} custom-call(bf16[512,1536]{1,0:T(8,128)(2,1)} %get-tuple-element.162.left_ref.refs_0_, bf16[512,2048]{1,0:T(8,128)(2,1)} %copy-done.16), custom_call_target="tpu_custom_call" | custom-call | flops 1000 | bytes 1000 | tf_op jit(solution)/shard_map/rows_product/pallas_call | solution.py:760
  305.6 14.4 %product_blocks.3 = (f32[512,512]{1,0:T(8,128)}, f32[512,512]{1,0:T(8,128)}, f32[512,512]{1,0:T(8,128)}, f32[512,512]{1,0:T(8,128)}) custom-call(s32[4]{0:T(128)} %copy-done.12, bf16[512,1536]{1,0:T(8,128)(2,1)} %get-tuple-element.145.refs_0_, bf16[512,1536]{1,0:T(8,128)(2,1)} %get-tuple-element.146.refs_1_, bf16[2048,1536]{1,0:T(8,128)(2,1)} %refs_2_.2, ...), custom_call_target="tpu_custom_call" | custom-call | flops 1000 | bytes 1000 | tf_op jit(solution)/shard_map/product_blocks/pallas_call | solution.py:612
  321.3 14.6 %columns_product.2 = f32[2048,3072]{1,0:T(8,128)} custom-call(s32[8]{0:T(128)} %constant.56.clone.ring_ref, bf16[512,2048]{1,0:T(8,128)(2,1)} %copy-done.14, bf16[512,1536]{1,0:T(8,128)(2,1)} %get-tuple-element.145.refs_0_, bf16[512,1536]{1,0:T(8,128)(2,1)} %get-tuple-element.146.refs_1_), custom_call_target="tpu_custom_call" | custom-call | flops 1000 | bytes 1000 | tf_op jit(solution)/shard_map/columns_product/pallas_call | solution.py:735
  340.2 5.3 collective-permute-start.27
  347.3 4.3 product_sums.2
  352.8 7.0 %collective-permute-done.29 = f32[512]{0:T(512)S(1)} collective-permute-done((f32[512]{0:T(512)S(1)}, f32[512]{0:T(512)S(1)}, u32[]{:S(2)}, u32[]{:S(2)}) %collective-permute-start.29) | collective-permute-done | bytes 2080 | tf_op jit(solution)/shard_map/ppermute | solution.py:42
  368.3 4.8 collective-permute-start.32
  373.1 7.7 %product_blocks.4 = (f32[512,512]{1,0:T(8,128)}, f32[512,512]{1,0:T(8,128)}, f32[512,512]{1,0:T(8,128)}, f32[512,512]{1,0:T(8,128)}) custom-call(s32[4]{0:T(128)} %copy-done.12, bf16[512,1536]{1,0:T(8,128)(2,1)} %get-tuple-element.162.left_ref.refs_0_, bf16[1536,2048]{1,0:T(8,128)(2,1)} %refs_1_.1), custom_call_target="tpu_custom_call" | custom-call | flops 1000 | bytes 1000 | tf_op jit(solution)/shard_map/product_blocks/pallas_call | solution.py:612
  380.7 9.7 %collective-permute-done.32 = f32[512,512]{1,0:T(8,128)S(1)} collective-permute-done((f32[512,512]{1,0:T(8,128)S(1)}, f32[512,512]{1,0:T(8,128)S(1)}, u32[]{:S(2)}, u32[]{:S(2)}) %collective-permute-start.32) | collective-permute-done | bytes 1048608 | tf_op jit(solution)/shard_map/ppermute | solution.py:42
  396.4 18.8 %collective-permute-done.33 = f32[512,512]{1,0:T(8,128)S(1)} collective-permute-done((f32[512,512]{1,0:T(8,128)S(1)}, f32[512,512]{1,0:T(8,128)S(1)}, u32[]{:S(2)}, u32[]{:S(2)}) %collective-permute-start.33) | collective-permute-done | bytes 1048608 | tf_op jit(solution)/shard_map/ppermute | solution.py:42
  415.2 4.4 collective-permute-start.37
  422.6 11.6 %collective-permute-done.37 = f32[512,512]{1,0:T(8,128)S(1)} collective-permute-done((f32[512,512]{1,0:T(8,128)S(1)}, f32[512,512]{1,0:T(8,128)S(1)}, u32[]{:S(2)}, u32[]{:S(2)}) %collective-permute-start.37) | collective-permute-done | bytes 1048608 | tf_op jit(solution)/shard_map/ppermute | solution.py:42
  439.8 7.0 %collective-permute-start.40 = (f32[512,512]{1,0:T(8,128)}, f32[512,512]{1,0:T(8,128)}, u32[]{:S(2)}, u32[]{:S(2)}) collective-permute-start(f32[512,512]{1,0:T(8,128)} %get-tuple-element.173), channel_id=1, source_target_pairs={{0,1},{3,2},{4,5},{7,6},{8,9},{11,10},{12,13},{15,14},{16,17},{19,... | collective-permute-start | bytes 3145736 | tf_op jit(solution)/shard_map/ppermute | solution.py:42
  450.9 8.8 %collective-permute-done.40 = f32[512,512]{1,0:T(8,128)} collective-permute-done((f32[512,512]{1,0:T(8,128)}, f32[512,512]{1,0:T(8,128)}, u32[]{:S(2)}, u32[]{:S(2)}) %collective-permute-start.40) | collective-permute-done | bytes 1048608 | tf_op jit(solution)/shard_map/ppermute | solution.py:42
  462.4 7.1 %collective-permute-start.41 = (f32[512,512]{1,0:T(8,128)}, f32[512,512]{1,0:T(8,128)}, u32[]{:S(2)}, u32[]{:S(2)}) collective-permute-start(f32[512,512]{1,0:T(8,128)} %add.261), channel_id=1, source_target_pairs={{0,1},{1,0},{2,3},{3,2},{4,5},{5,4},{6,7},{7,6},{8,9},{9,8},{10,11... | collective-permute-start | bytes 3145736 | tf_op jit(solution)/shard_map/ppermute | solution.py:42
  475.1 4.1 recurrence_turn.1
  481.2 11.1 %all-gather.2.ends_ref = f32[8,2,640]{2,1,0:T(2,128)} all-gather(f32[1,2,640]{2,1,0:T(2,128)S(1)} %bitcast.41), channel_id=3, replica_groups=mesh['seq'=8,'mp'=4] {'seq'}, dimensions={0}, use_global_device_ids=true | all-gather | bytes 46080 | tf_op jit(solution)/shard_map/all_gather | solution.py:911
  492.2 13.5 %recurrence_backward.1 = (bf16[512,640]{1,0:T(8,128)(2,1)}, f32[16,640]{1,0:T(8,128)}, f32[8,640]{1,0:T(8,128)}, f32[2,328,320]{2,1,0:T(8,128)}) custom-call(s32[1]{0:T(128)} %bitcast.mine_ref, f32[8,2,640]{2,1,0:T(2,128)} %all-gather.2.ends_ref, f32[512,640]{1,0:T(8,128)} %copy-done.9, f32[512,640]{1,0:T(8,128)} %get-tuple-element.182.alpha_ref, ...), custom_call_target="tpu_custom_call" | custom-call | flops 1000 | bytes 1000 | tf_op jit(solution)/shard_map/recurrence_backward/pallas_call | solution.py:674
  505.7 4.6 rows_product.3
  514.8 7.7 %product_blocks.5 = (f32[512,512]{1,0:T(8,128)}, f32[512,512]{1,0:T(8,128)}, f32[512,512]{1,0:T(8,128)}, f32[512,512]{1,0:T(8,128)}) custom-call(s32[4]{0:T(128)} %copy-done.12, bf16[512,640]{1,0:T(8,128)(2,1)} %fusion.45.refs_0_, bf16[512,640]{1,0:T(8,128)(2,1)} %copy-done.8, bf16[2048,640]{1,0:T(8,128)(2,1)} %refs_2_.3, bf16[2048,640]{1,0:T(8,128)(2,1)} %refs_3_.3), custom_call_target="tpu_custom_call" | custom-call | flops 1000 | bytes 1000 | tf_op jit(solution)/shard_map/product_blocks/pallas_call | solution.py:612
  522.5 3.9 collective-permute-start.44
  526.5 10.1 %columns_product.3 = f32[2048,1280]{1,0:T(8,128)} custom-call(s32[8]{0:T(128)} %constant.56.clone.ring_ref, bf16[512,2048]{1,0:T(8,128)(2,1)} %copy-done.15, bf16[512,640]{1,0:T(8,128)(2,1)} %fusion.45.refs_0_, bf16[512,640]{1,0:T(8,128)(2,1)} %copy-done.8), custom_call_target="tpu_custom_call" | custom-call | flops 1000 | bytes 1000 | tf_op jit(solution)/shard_map/columns_product/pallas_call | solution.py:735
  536.7 4.3 product_sums.3
  542.8 5.6 collective-permute-done.44
  554.2 6.6 %collective-permute-start.47 = (f32[512,512]{1,0:T(8,128)S(1)}, f32[512,512]{1,0:T(8,128)S(1)}, u32[]{:S(2)}, u32[]{:S(2)}) collective-permute-start(f32[512,512]{1,0:T(8,128)S(1)} %copy-done.26), channel_id=1, source_target_pairs={{0,1},{3,2},{4,5},{7,6},{8,9},{11,10},{12,13},{15,14},{16,17},{19,... | collective-permute-start | bytes 3145736 | tf_op jit(solution)/shard_map/ppermute | solution.py:42
  564.2 18.0 %collective-permute-done.49 = f32[328,320]{1,0:T(8,128)S(1)} collective-permute-done((f32[328,320]{1,0:T(8,128)S(1)}, f32[328,320]{1,0:T(8,128)S(1)}, u32[]{:S(2)}, u32[]{:S(2)}) %collective-permute-start.49) | collective-permute-done | bytes 419872 | tf_op jit(solution)/shard_map/ppermute | solution.py:116
  601.2 13.8 %collective-permute-done.56 = f32[4096]{0:T(1024)S(1)} collective-permute-done((f32[4096]{0:T(1024)S(1)}, f32[4096]{0:T(1024)S(1)}, u32[]{:S(2)}, u32[]{:S(2)}) %collective-permute-start.56) | collective-permute-done | bytes 16416 | tf_op jit(solution)/shard_map/ppermute | solution.py:116
  (322 shorter events, 149.8 us)
Async XLA Ops:
  7.2 439.6 %reduce-scatter.5.cloned.1.call-start = ((), (), s32[]{:S(2)}) async-start(), calls=%async_computation.4 | async-start | bytes 14155776 | tf_op jit(solution)/shard_map/reduce_scatter | solution.py:722
  7.2 11.6 %collective-permute-start.3 = (f32[512,512]{1,0:T(8,128)}, f32[512,512]{1,0:T(8,128)S(1)}, u32[]{:S(2)}, u32[]{:S(2)}) collective-permute-start(f32[512,512]{1,0:T(8,128)} %param.20), channel_id=1, source_target_pairs={{1,2},{2,1},{5,6},{6,5},{9,10},{10,9},{13,14},{14,13},{17,18},{18,... | collective-permute-start | bytes 3145736 | tf_op jit(solution)/shard_map/ppermute | solution.py:42
  8.0 29.1 %collective-permute-start.2 = (f32[512,512]{1,0:T(8,128)}, f32[512,512]{1,0:T(8,128)}, u32[]{:S(2)}, u32[]{:S(2)}) collective-permute-start(f32[512,512]{1,0:T(8,128)} %param.20), channel_id=1, source_target_pairs={{0,1},{1,0},{2,3},{3,2},{4,5},{5,4},{6,7},{7,6},{8,9},{9,8},{10,11... | collective-permute-start | bytes 3145736 | tf_op jit(solution)/shard_map/ppermute | solution.py:42
  14.6 33.9 %collective-permute-start.6 = (f32[8]{0:T(128)S(1)}, f32[8]{0:T(128)S(1)}, u32[]{:S(2)}, u32[]{:S(2)}) collective-permute-start(f32[8]{0:T(128)S(1)} %slice.113), channel_id=1, source_target_pairs={{0,4},{4,8},{8,12},{12,16},{16,20},{20,24},{24,28},{1,5},{5,9},{9,... | collective-permute-start | bytes 104 | tf_op jit(solution)/shard_map/ppermute | solution.py:812
  17.4 32.8 %collective-permute-start = (f32[512]{0:T(512)S(1)}, f32[512]{0:T(512)S(1)}, u32[]{:S(2)}, u32[]{:S(2)}) collective-permute-start(f32[512]{0:T(512)S(1)} %multiply_reduce_fusion.1), channel_id=1, source_target_pairs={{0,1},{1,0},{2,3},{3,2},{4,5},{5,4},{6,7},{7,6},{8,9},{9,8},{10,11... | collective-permute-start | bytes 6152 | tf_op jit(solution)/shard_map/ppermute | solution.py:42
  37.0 26.0 %collective-permute-start.4 = (f32[512,512]{1,0:T(8,128)S(1)}, f32[512,512]{1,0:T(8,128)}, u32[]{:S(2)}, u32[]{:S(2)}) collective-permute-start(f32[512,512]{1,0:T(8,128)S(1)} %collective-permute-done.3), channel_id=1, source_target_pairs={{1,0},{2,3},{5,4},{6,7},{9,8},{10,11},{13,12},{14,15},{17,16},{18,... | collective-permute-start | bytes 3145736 | tf_op jit(solution)/shard_map/ppermute | solution.py:42
  38.3 24.7 %collective-permute-start.5 = (f32[512,512]{1,0:T(8,128)}, f32[512,512]{1,0:T(8,128)}, u32[]{:S(2)}, u32[]{:S(2)}) collective-permute-start(f32[512,512]{1,0:T(8,128)} %collective-permute-done.2), channel_id=1, source_target_pairs={{1,2},{2,1},{5,6},{6,5},{9,10},{10,9},{13,14},{14,13},{17,18},{18,... | collective-permute-start | bytes 3145736 | tf_op jit(solution)/shard_map/ppermute | solution.py:42
  50.1 17.1 %collective-permute-start.1 = (f32[512]{0:T(512)S(1)}, f32[512]{0:T(512)S(1)}, u32[]{:S(2)}, u32[]{:S(2)}) collective-permute-start(f32[512]{0:T(512)S(1)} %add.226), channel_id=1, source_target_pairs={{0,2},{2,0},{1,3},{3,1},{4,6},{6,4},{5,7},{7,5},{8,10},{10,8},{9,1... | collective-permute-start | bytes 6152 | tf_op jit(solution)/shard_map/ppermute | solution.py:42
  63.0 27.5 %collective-permute-start.7 = (f32[512,512]{1,0:T(8,128)}, f32[512,512]{1,0:T(8,128)}, u32[]{:S(2)}, u32[]{:S(2)}) collective-permute-start(f32[512,512]{1,0:T(8,128)} %collective-permute-done.5), channel_id=1, source_target_pairs={{1,0},{2,3},{5,4},{6,7},{9,8},{10,11},{13,12},{14,15},{17,16},{18,... | collective-permute-start | bytes 3145736 | tf_op jit(solution)/shard_map/ppermute | solution.py:42
  90.5 31.3 %collective-permute-start.10 = (f32[512,512]{1,0:T(8,128)}, f32[512,512]{1,0:T(8,128)}, u32[]{:S(2)}, u32[]{:S(2)}) collective-permute-start(f32[512,512]{1,0:T(8,128)} %param.37), channel_id=1, source_target_pairs={{1,2},{2,1},{5,6},{6,5},{9,10},{10,9},{13,14},{14,13},{17,18},{18,... | collective-permute-start | bytes 3145736 | tf_op jit(solution)/shard_map/ppermute | solution.py:42
  92.2 29.6 %collective-permute-start.9 = (f32[512,512]{1,0:T(8,128)}, f32[512,512]{1,0:T(8,128)}, u32[]{:S(2)}, u32[]{:S(2)}) collective-permute-start(f32[512,512]{1,0:T(8,128)} %param.37), channel_id=1, source_target_pairs={{0,1},{1,0},{2,3},{3,2},{4,5},{5,4},{6,7},{7,6},{8,9},{9,8},{10,11... | collective-permute-start | bytes 3145736 | tf_op jit(solution)/shard_map/ppermute | solution.py:42
  127.8 26.5 %collective-permute-start.11 = (f32[512,512]{1,0:T(8,128)S(1)}, f32[512,512]{1,0:T(8,128)S(1)}, u32[]{:S(2)}, u32[]{:S(2)}) collective-permute-start(f32[512,512]{1,0:T(8,128)S(1)} %get-tuple-element.130), channel_id=1, source_target_pairs={{0,1},{3,2},{4,5},{7,6},{8,9},{11,10},{12,13},{15,14},{16,17},{19,... | collective-permute-start | bytes 3145736 | tf_op jit(solution)/shard_map/ppermute | solution.py:42
  131.5 23.1 %collective-permute-start.12 = (f32[512,512]{1,0:T(8,128)}, f32[512,512]{1,0:T(8,128)S(1)}, u32[]{:S(2)}, u32[]{:S(2)}) collective-permute-start(f32[512,512]{1,0:T(8,128)} %collective-permute-done.9), channel_id=1, source_target_pairs={{1,2},{2,1},{5,6},{6,5},{9,10},{10,9},{13,14},{14,13},{17,18},{18,... | collective-permute-start | bytes 3145736 | tf_op jit(solution)/shard_map/ppermute | solution.py:42
  132.2 27.2 %collective-permute-start.13 = (f32[512,512]{1,0:T(8,128)}, f32[512,512]{1,0:T(8,128)S(1)}, u32[]{:S(2)}, u32[]{:S(2)}) collective-permute-start(f32[512,512]{1,0:T(8,128)} %collective-permute-done.10), channel_id=1, source_target_pairs={{1,0},{2,3},{5,4},{6,7},{9,8},{10,11},{13,12},{14,15},{17,16},{18,... | collective-permute-start | bytes 3145736 | tf_op jit(solution)/shard_map/ppermute | solution.py:42
  159.5 23.4 %collective-permute-start.14 = (f32[512,512]{1,0:T(8,128)S(1)}, f32[512,512]{1,0:T(8,128)S(1)}, u32[]{:S(2)}, u32[]{:S(2)}) collective-permute-start(f32[512,512]{1,0:T(8,128)S(1)} %get-tuple-element.133), channel_id=1, source_target_pairs={{0,1},{3,2},{4,5},{7,6},{8,9},{11,10},{12,13},{15,14},{16,17},{19,... | collective-permute-start | bytes 3145736 | tf_op jit(solution)/shard_map/ppermute | solution.py:42
  161.1 22.0 %collective-permute-start.15 = (f32[512,512]{1,0:T(8,128)S(1)}, f32[512,512]{1,0:T(8,128)S(1)}, u32[]{:S(2)}, u32[]{:S(2)}) collective-permute-start(f32[512,512]{1,0:T(8,128)S(1)} %add.236), channel_id=1, source_target_pairs={{1,2},{2,1},{5,6},{6,5},{9,10},{10,9},{13,14},{14,13},{17,18},{18,... | collective-permute-start | bytes 3145736 | tf_op jit(solution)/shard_map/ppermute | solution.py:42
  161.8 25.9 %collective-permute-start.16 = (f32[512,512]{1,0:T(8,128)S(1)}, f32[512,512]{1,0:T(8,128)S(1)}, u32[]{:S(2)}, u32[]{:S(2)}) collective-permute-start(f32[512,512]{1,0:T(8,128)S(1)} %collective-permute-done.12), channel_id=1, source_target_pairs={{1,0},{2,3},{5,4},{6,7},{9,8},{10,11},{13,12},{14,15},{17,16},{18,... | collective-permute-start | bytes 3145736 | tf_op jit(solution)/shard_map/ppermute | solution.py:42
  188.6 23.2 %collective-permute-start.18 = (f32[512,512]{1,0:T(8,128)S(1)}, f32[512,512]{1,0:T(8,128)S(1)}, u32[]{:S(2)}, u32[]{:S(2)}) collective-permute-start(f32[512,512]{1,0:T(8,128)S(1)} %add.238), channel_id=1, source_target_pairs={{0,1},{1,0},{2,3},{3,2},{4,5},{5,4},{6,7},{7,6},{8,9},{9,8},{10,11... | collective-permute-start | bytes 3145736 | tf_op jit(solution)/shard_map/ppermute | solution.py:42
  212.3 19.0 %collective-permute-start.22 = (f32[512,512]{1,0:T(8,128)S(1)}, f32[512,512]{1,0:T(8,128)S(1)}, u32[]{:S(2)}, u32[]{:S(2)}) collective-permute-start(f32[512,512]{1,0:T(8,128)S(1)} %get-tuple-element.208), channel_id=1, source_target_pairs={{1,2},{2,1},{5,6},{6,5},{9,10},{10,9},{13,14},{14,13},{17,18},{18,... | collective-permute-start | bytes 3145736 | tf_op jit(solution)/shard_map/ppermute | solution.py:42
  213.0 23.6 %collective-permute-start.21 = (f32[512,512]{1,0:T(8,128)S(1)}, f32[512,512]{1,0:T(8,128)S(1)}, u32[]{:S(2)}, u32[]{:S(2)}) collective-permute-start(f32[512,512]{1,0:T(8,128)S(1)} %get-tuple-element.208), channel_id=1, source_target_pairs={{0,1},{1,0},{2,3},{3,2},{4,5},{5,4},{6,7},{7,6},{8,9},{9,8},{10,11... | collective-permute-start | bytes 3145736 | tf_op jit(solution)/shard_map/ppermute | solution.py:42
  236.6 22.9 %collective-permute-start.23 = (f32[512,512]{1,0:T(8,128)S(1)}, f32[512,512]{1,0:T(8,128)S(1)}, u32[]{:S(2)}, u32[]{:S(2)}) collective-permute-start(f32[512,512]{1,0:T(8,128)S(1)} %collective-permute-done.22), channel_id=1, source_target_pairs={{1,0},{2,3},{5,4},{6,7},{9,8},{10,11},{13,12},{14,15},{17,16},{18,... | collective-permute-start | bytes 3145736 | tf_op jit(solution)/shard_map/ppermute | solution.py:42
  237.9 21.7 %collective-permute-start.24 = (f32[512,512]{1,0:T(8,128)S(1)}, f32[512,512]{1,0:T(8,128)S(1)}, u32[]{:S(2)}, u32[]{:S(2)}) collective-permute-start(f32[512,512]{1,0:T(8,128)S(1)} %collective-permute-done.21), channel_id=1, source_target_pairs={{1,2},{2,1},{5,6},{6,5},{9,10},{10,9},{13,14},{14,13},{17,18},{18,... | collective-permute-start | bytes 3145736 | tf_op jit(solution)/shard_map/ppermute | solution.py:42
  238.6 20.9 %collective-permute-start.19 = (f32[512]{0:T(512)S(1)}, f32[512]{0:T(512)S(1)}, u32[]{:S(2)}, u32[]{:S(2)}) collective-permute-start(f32[512]{0:T(512)S(1)} %get-tuple-element.227), channel_id=1, source_target_pairs={{0,1},{1,0},{2,3},{3,2},{4,5},{5,4},{6,7},{7,6},{8,9},{9,8},{10,11... | collective-permute-start | bytes 6152 | tf_op jit(solution)/shard_map/ppermute | solution.py:42
  259.6 23.0 %collective-permute-start.25 = (f32[512,512]{1,0:T(8,128)S(1)}, f32[512,512]{1,0:T(8,128)S(1)}, u32[]{:S(2)}, u32[]{:S(2)}) collective-permute-start(f32[512,512]{1,0:T(8,128)S(1)} %collective-permute-done.24), channel_id=1, source_target_pairs={{1,0},{2,3},{5,4},{6,7},{9,8},{10,11},{13,12},{14,15},{17,16},{18,... | collective-permute-start | bytes 3145736 | tf_op jit(solution)/shard_map/ppermute | solution.py:42
  305.5 217.0 %reduce-scatter.7.cloned.1.call-start = ((), (), s32[]{:S(2)}) async-start(), calls=%async_computation.5 | async-start | bytes 28311552 | tf_op jit(solution)/shard_map/reduce_scatter | solution.py:722
  319.9 17.8 %collective-permute-start.26 = (f32[512,512]{1,0:T(8,128)}, f32[512,512]{1,0:T(8,128)S(1)}, u32[]{:S(2)}, u32[]{:S(2)}) collective-permute-start(f32[512,512]{1,0:T(8,128)} %get-tuple-element.154.refs_0_), channel_id=1, source_target_pairs={{0,1},{3,2},{4,5},{7,6},{8,9},{11,10},{12,13},{15,14},{16,17},{19,... | collective-permute-start | bytes 3145736 | tf_op jit(solution)/shard_map/ppermute | solution.py:42
  338.7 214.7 %reduce-scatter.9.cloned.1.call-start = ((), (), s32[]{:S(2)}) async-start(), calls=%async_computation.6 | async-start | bytes 5898240 | tf_op jit(solution)/shard_map/reduce_scatter | solution.py:722
  340.2 24.2 %collective-permute-start.27 = (f32[512,512]{1,0:T(8,128)}, f32[512,512]{1,0:T(8,128)}, u32[]{:S(2)}, u32[]{:S(2)}) collective-permute-start(f32[512,512]{1,0:T(8,128)} %get-tuple-element.151.refs_1_), channel_id=1, source_target_pairs={{0,1},{3,2},{4,5},{7,6},{8,9},{11,10},{12,13},{15,14},{16,17},{19,... | collective-permute-start | bytes 3145736 | tf_op jit(solution)/shard_map/ppermute | solution.py:42
  345.4 20.7 %collective-permute-start.28 = (f32[512,512]{1,0:T(8,128)S(1)}, f32[512,512]{1,0:T(8,128)}, u32[]{:S(2)}, u32[]{:S(2)}) collective-permute-start(f32[512,512]{1,0:T(8,128)S(1)} %add.249), channel_id=1, source_target_pairs={{1,2},{2,1},{5,6},{6,5},{9,10},{10,9},{13,14},{14,13},{17,18},{18,... | collective-permute-start | bytes 3145736 | tf_op jit(solution)/shard_map/ppermute | solution.py:42
  367.5 13.2 %collective-permute-start.31 = (f32[512,512]{1,0:T(8,128)S(1)}, f32[512,512]{1,0:T(8,128)S(1)}, u32[]{:S(2)}, u32[]{:S(2)}) collective-permute-start(f32[512,512]{1,0:T(8,128)S(1)} %add.250), channel_id=1, source_target_pairs={{1,2},{2,1},{5,6},{6,5},{9,10},{10,9},{13,14},{14,13},{17,18},{18,... | collective-permute-start | bytes 3145736 | tf_op jit(solution)/shard_map/ppermute | solution.py:42
  368.3 22.1 %collective-permute-start.32 = (f32[512,512]{1,0:T(8,128)S(1)}, f32[512,512]{1,0:T(8,128)S(1)}, u32[]{:S(2)}, u32[]{:S(2)}) collective-permute-start(f32[512,512]{1,0:T(8,128)S(1)} %add.251), channel_id=1, source_target_pairs={{0,1},{1,0},{2,3},{3,2},{4,5},{5,4},{6,7},{7,6},{8,9},{9,8},{10,11... | collective-permute-start | bytes 3145736 | tf_op jit(solution)/shard_map/ppermute | solution.py:42
  393.5 21.8 %collective-permute-start.33 = (f32[512,512]{1,0:T(8,128)S(1)}, f32[512,512]{1,0:T(8,128)S(1)}, u32[]{:S(2)}, u32[]{:S(2)}) collective-permute-start(f32[512,512]{1,0:T(8,128)S(1)} %get-tuple-element.167), channel_id=1, source_target_pairs={{0,1},{1,0},{2,3},{3,2},{4,5},{5,4},{6,7},{7,6},{8,9},{9,8},{10,11... | collective-permute-start | bytes 3145736 | tf_op jit(solution)/shard_map/ppermute | solution.py:42
  415.2 19.0 %collective-permute-start.37 = (f32[512,512]{1,0:T(8,128)S(1)}, f32[512,512]{1,0:T(8,128)S(1)}, u32[]{:S(2)}, u32[]{:S(2)}) collective-permute-start(f32[512,512]{1,0:T(8,128)S(1)} %copy-done.38), channel_id=1, source_target_pairs={{0,1},{3,2},{4,5},{7,6},{8,9},{11,10},{12,13},{15,14},{16,17},{19,... | collective-permute-start | bytes 3145736 | tf_op jit(solution)/shard_map/ppermute | solution.py:42
  419.7 18.4 %collective-permute-start.35 = (f32[512,512]{1,0:T(8,128)S(1)}, f32[512,512]{1,0:T(8,128)S(1)}, u32[]{:S(2)}, u32[]{:S(2)}) collective-permute-start(f32[512,512]{1,0:T(8,128)S(1)} %collective-permute-done.34), channel_id=1, source_target_pairs={{1,0},{2,3},{5,4},{6,7},{9,8},{10,11},{13,12},{14,15},{17,16},{18,... | collective-permute-start | bytes 3145736 | tf_op jit(solution)/shard_map/ppermute | solution.py:42
  421.0 25.8 %collective-permute-start.36 = (f32[512,512]{1,0:T(8,128)S(1)}, f32[512,512]{1,0:T(8,128)}, u32[]{:S(2)}, u32[]{:S(2)}) collective-permute-start(f32[512,512]{1,0:T(8,128)S(1)} %collective-permute-done.33), channel_id=1, source_target_pairs={{1,2},{2,1},{5,6},{6,5},{9,10},{10,9},{13,14},{14,13},{17,18},{18,... | collective-permute-start | bytes 3145736 | tf_op jit(solution)/shard_map/ppermute | solution.py:42
  439.8 19.9 %collective-permute-start.40 = (f32[512,512]{1,0:T(8,128)}, f32[512,512]{1,0:T(8,128)}, u32[]{:S(2)}, u32[]{:S(2)}) collective-permute-start(f32[512,512]{1,0:T(8,128)} %get-tuple-element.173), channel_id=1, source_target_pairs={{0,1},{3,2},{4,5},{7,6},{8,9},{11,10},{12,13},{15,14},{16,17},{19,... | collective-permute-start | bytes 3145736 | tf_op jit(solution)/shard_map/ppermute | solution.py:42
  446.8 26.8 %collective-permute-start.38 = (f32[512,512]{1,0:T(8,128)}, f32[512,512]{1,0:T(8,128)S(1)}, u32[]{:S(2)}, u32[]{:S(2)}) collective-permute-start(f32[512,512]{1,0:T(8,128)} %collective-permute-done.36), channel_id=1, source_target_pairs={{1,0},{2,3},{5,4},{6,7},{9,8},{10,11},{13,12},{14,15},{17,16},{18,... | collective-permute-start | bytes 3145736 | tf_op jit(solution)/shard_map/ppermute | solution.py:42
  462.4 29.8 %collective-permute-start.41 = (f32[512,512]{1,0:T(8,128)}, f32[512,512]{1,0:T(8,128)}, u32[]{:S(2)}, u32[]{:S(2)}) collective-permute-start(f32[512,512]{1,0:T(8,128)} %add.261), channel_id=1, source_target_pairs={{0,1},{1,0},{2,3},{3,2},{4,5},{5,4},{6,7},{7,6},{8,9},{9,8},{10,11... | collective-permute-start | bytes 3145736 | tf_op jit(solution)/shard_map/ppermute | solution.py:42
  469.5 22.7 %collective-permute-start.42 = (f32[512,512]{1,0:T(8,128)}, f32[512,512]{1,0:T(8,128)}, u32[]{:S(2)}, u32[]{:S(2)}) collective-permute-start(f32[512,512]{1,0:T(8,128)} %add.260), channel_id=1, source_target_pairs={{1,2},{2,1},{5,6},{6,5},{9,10},{10,9},{13,14},{14,13},{17,18},{18,... | collective-permute-start | bytes 3145736 | tf_op jit(solution)/shard_map/ppermute | solution.py:42
  510.4 113.5 %reduce-scatter.11.cloned.1.call-start = ((), (), s32[]{:S(2)}) async-start(), calls=%async_computation.7 | async-start | bytes 11796480 | tf_op jit(solution)/shard_map/reduce_scatter | solution.py:722
  522.5 25.9 %collective-permute-start.44 = (f32[512,512]{1,0:T(8,128)}, f32[512,512]{1,0:T(8,128)}, u32[]{:S(2)}, u32[]{:S(2)}) collective-permute-start(f32[512,512]{1,0:T(8,128)} %get-tuple-element.197.refs_0_), channel_id=1, source_target_pairs={{0,1},{3,2},{4,5},{7,6},{8,9},{11,10},{12,13},{15,14},{16,17},{19,... | collective-permute-start | bytes 3145736 | tf_op jit(solution)/shard_map/ppermute | solution.py:42
  553.4 28.9 %collective-permute-start.46 = (f32[512,512]{1,0:T(8,128)}, f32[512,512]{1,0:T(8,128)S(1)}, u32[]{:S(2)}, u32[]{:S(2)}) collective-permute-start(f32[512,512]{1,0:T(8,128)} %add.263), channel_id=1, source_target_pairs={{1,2},{2,1},{5,6},{6,5},{9,10},{10,9},{13,14},{14,13},{17,18},{18,... | collective-permute-start | bytes 3145736 | tf_op jit(solution)/shard_map/ppermute | solution.py:42
  554.2 29.2 %collective-permute-start.47 = (f32[512,512]{1,0:T(8,128)S(1)}, f32[512,512]{1,0:T(8,128)S(1)}, u32[]{:S(2)}, u32[]{:S(2)}) collective-permute-start(f32[512,512]{1,0:T(8,128)S(1)} %copy-done.26), channel_id=1, source_target_pairs={{0,1},{3,2},{4,5},{7,6},{8,9},{11,10},{12,13},{15,14},{16,17},{19,... | collective-permute-start | bytes 3145736 | tf_op jit(solution)/shard_map/ppermute | solution.py:42
  562.8 19.4 %collective-permute-start.49 = (f32[328,320]{1,0:T(8,128)S(1)}, f32[328,320]{1,0:T(8,128)S(1)}, u32[]{:S(2)}, u32[]{:S(2)}) collective-permute-start(f32[328,320]{1,0:T(8,128)S(1)} %add.272), channel_id=1, source_target_pairs={{0,8},{4,12},{8,0},{12,4},{16,24},{20,28},{24,16},{28,20},{1,9},{5... | collective-permute-start | bytes 1259528 | tf_op jit(solution)/shard_map/ppermute | solution.py:116
  588.4 27.4 %collective-permute-start.50 = (f32[512,512]{1,0:T(8,128)S(1)}, f32[512,512]{1,0:T(8,128)S(1)}, u32[]{:S(2)}, u32[]{:S(2)}) collective-permute-start(f32[512,512]{1,0:T(8,128)S(1)} %add.270), channel_id=1, source_target_pairs={{1,2},{2,1},{5,6},{6,5},{9,10},{10,9},{13,14},{14,13},{17,18},{18,... | collective-permute-start | bytes 3145736 | tf_op jit(solution)/shard_map/ppermute | solution.py:42
  589.2 25.8 %collective-permute-start.51 = (f32[512,512]{1,0:T(8,128)S(1)}, f32[512,512]{1,0:T(8,128)S(1)}, u32[]{:S(2)}, u32[]{:S(2)}) collective-permute-start(f32[512,512]{1,0:T(8,128)S(1)} %add.271), channel_id=1, source_target_pairs={{0,1},{1,0},{2,3},{3,2},{4,5},{5,4},{6,7},{7,6},{8,9},{9,8},{10,11... | collective-permute-start | bytes 3145736 | tf_op jit(solution)/shard_map/ppermute | solution.py:42
  593.7 21.2 %collective-permute-start.53 = (f32[328,320]{1,0:T(8,128)S(1)}, f32[328,320]{1,0:T(8,128)S(1)}, u32[]{:S(2)}, u32[]{:S(2)}) collective-permute-start(f32[328,320]{1,0:T(8,128)S(1)} %add.273), channel_id=1, source_target_pairs={{0,16},{4,20},{8,24},{12,28},{16,0},{20,4},{24,8},{28,12},{1,17},{... | collective-permute-start | bytes 1259528 | tf_op jit(solution)/shard_map/ppermute | solution.py:116
  600.8 14.1 %collective-permute-start.56 = (f32[4096]{0:T(1024)S(1)}, f32[4096]{0:T(1024)S(1)}, u32[]{:S(2)}, u32[]{:S(2)}) collective-permute-start(f32[4096]{0:T(1024)S(1)} %add.280), channel_id=1, source_target_pairs={{0,16},{4,20},{8,24},{12,28},{16,0},{20,4},{24,8},{28,12},{1,17},{... | collective-permute-start | bytes 49160 | tf_op jit(solution)/shard_map/ppermute | solution.py:116
  (78 other events, 1346.5 us)
Sparse Core Ops, SparseCore 0:
  305.6 66.9 reduce-scatter.4
  375.0 128.1 reduce-scatter.6
  510.5 34.5 reduce-scatter.8
  548.5 75.3 reduce-scatter.10
